TPU v7x, 32 devices: a whole 2x2x4 slice. The times are simulated.
32 devices in a mesh: user: 4 (over y, core), pool: 8 (over z, x).
Axes of the slice: x: 2, y: 2, z: 4, core: 2. Of those that a mesh axis runs over, the one named last changes fastest.
Arguments:
- item_feats: bfloat16 [16384, 512], P(('user', 'pool')), may hold values from -6 to 6
- w_in: bfloat16 [512, 2048], replicated, may hold values from -0.25 to 0.25
- bias_in: float32 [2048], replicated, may hold values from -3 to 3
- w_out: bfloat16 [2048, 512], replicated, may hold values from -0.125 to 0.125
- bilinear: bfloat16 [512, 512], replicated, may hold values from -0.25 to 0.25
- fetch_table: int32 [32, 32, 16], P(None, ('user', 'pool')), may hold values from 0 to 511, as said below
- hist_index: int32 [1024, 256], P(('user', 'pool')), may hold values from 0 to 511
- hist_len: int32 [1024], P(('user', 'pool')), may hold values from 32 to 256
- route_init: float32 [1024, 4, 256], P(('user', 'pool')), may hold values from -6 to 6
- label_index: int32 [1024], P(('user', 'pool')), may hold values from 0 to 511
- label_ids: int32 [1024], P(('user', 'pool')), may hold values from 0 to 1048575
- label_counts: int32 [1024], P(('user', 'pool')), may hold values from 1 to 15
- neg_feats: bfloat16 [4096, 512], P(('user', 'pool')), may hold values from -6 to 6
- neg_ids: int32 [4096], P(('user', 'pool')), may hold values from 0 to 1048575
- neg_counts: int32 [4096], P(('user', 'pool')), may hold values from 1 to 15
Outputs:
- interests: float32 [1024, 2048], P(('user', 'pool'))
- user_loss: float32 [1024], P(('user', 'pool'))
Inputs may be any that keep to these rules, and one draw needn't show every extreme that they name: fetch_table[b, s, :] names 16 different rows of item block s.
All inputs are finite; a program needn't handle non-finite values.
Results may differ from a plain program's by a relative error of at most 0.0011.
Values may be sent and summed in bfloat16 or wider, within the bound.
No kernel may reach another device: no remote copies, remote signals or barrier semaphores. Data moves between devices by JAX's collectives and lax.ppermute only.
A program may use at most 192 MiB of HBM per device.

v0:
```python
import jax
import jax.numpy as jnp
from jax import lax
from jax.sharding import PartitionSpec as P

INTERESTS = 4
ITERS = 3


norm_epsilon = 1e-06
attend_scale = 8.0
logit_scale = 20.0


def item_tower(features, w_in, bias_in, w_out):
    hidden = jnp.dot(features, w_in, preferred_element_type=jnp.float32) + bias_in
    hidden = jnp.maximum(hidden, 0.0).astype(jnp.bfloat16)
    embedding = jnp.dot(hidden, w_out, preferred_element_type=jnp.float32)
    inverse_norm = lax.rsqrt(jnp.sum(embedding * embedding, axis=-1, keepdims=True) + norm_epsilon)
    return (embedding * inverse_norm).astype(jnp.bfloat16)


def scatter_weights(weights, hist_index, slot_count):

    def one_user(user_weights, user_index):
        empty = jnp.zeros((user_weights.shape[0], slot_count), jnp.float32)
        return empty.at[:, user_index].add(user_weights)

    return jax.vmap(one_user)(weights, hist_index)


def dynamic_route(mapped, hist_index, hist_len, route_init):
    user_count = hist_index.shape[0]
    slot_count = mapped.shape[0]
    width = mapped.shape[1]
    mapped_wide = mapped.astype(jnp.float32)
    live_mask = (lax.broadcasted_iota(jnp.int32, hist_index.shape, 1) < hist_len[:, None]).astype(
        jnp.float32
    )
    route_logits = route_init
    capsules = jnp.zeros((user_count, INTERESTS, width), jnp.float32)
    for iteration in range(ITERS):
        raised = jnp.exp(route_logits)
        weights = (raised / jnp.sum(raised, axis=1, keepdims=True) * live_mask[:, None, :]).astype(
            jnp.bfloat16
        )
        slot_weights = scatter_weights(weights.astype(jnp.float32), hist_index, slot_count)
        capsule_sums = jnp.dot(
            slot_weights.reshape(user_count * INTERESTS, slot_count),
            mapped_wide,
            precision=lax.Precision.HIGHEST,
            preferred_element_type=jnp.float32,
        )
        capsule_sums = capsule_sums.reshape(user_count, INTERESTS, width)
        norm_sq = jnp.sum(capsule_sums * capsule_sums, axis=-1, keepdims=True)
        capsules = capsule_sums * jnp.sqrt(norm_sq) / (1.0 + norm_sq)
        if iteration + 1 < ITERS:
            capsule_half = capsules.astype(jnp.bfloat16).reshape(user_count * INTERESTS, width)
            slot_scores = lax.dot_general(
                capsule_half, mapped, (((1,), (1,)), ((), ())), preferred_element_type=jnp.float32
            )
            slot_scores = slot_scores.reshape(user_count, INTERESTS, slot_count)
            agreement = jnp.take_along_axis(slot_scores, hist_index[:, None, :], axis=2)
            route_logits = route_logits + agreement
    return capsules


def label_attention(capsules, label_rows, label_counts):
    scores = attend_scale * jnp.sum(capsules * label_rows[:, None, :], axis=-1)
    raised = jnp.exp(scores)
    attention = raised / jnp.sum(raised, axis=1, keepdims=True)
    user_vec = jnp.sum(attention[:, :, None] * capsules, axis=1).astype(jnp.bfloat16)
    positive = logit_scale * jnp.sum(user_vec.astype(jnp.float32) * label_rows, axis=-1) - jnp.log(
        label_counts.astype(jnp.float32)
    )
    return (user_vec, positive)


def exp_terms(user_vec, label_ids, neg_unit, neg_ids, neg_counts):
    logits = logit_scale * jnp.einsum(
        "ud,nd->un", user_vec, neg_unit, preferred_element_type=jnp.float32
    )
    logits = logits - jnp.log(neg_counts.astype(jnp.float32))[None, :]
    keep_mask = neg_ids[None, :] != label_ids[:, None]
    return jnp.sum(jnp.where(keep_mask, jnp.exp(logits), 0.0), axis=1)


def on_device(
    item_feats,
    w_in,
    bias_in,
    w_out,
    bilinear,
    fetch_table,
    hist_index,
    hist_len,
    route_init,
    label_index,
    label_ids,
    label_counts,
    neg_feats,
    neg_ids,
    neg_counts,
):
    unit = item_tower(item_feats, w_in, bias_in, w_out)
    outgoing = jnp.take(unit, fetch_table[:, 0, :], axis=0)
    item_rows = lax.all_to_all(outgoing, ("user", "pool"), split_axis=0, concat_axis=0, tiled=True)
    mapped_rows = jnp.dot(item_rows, bilinear, preferred_element_type=jnp.float32).astype(
        jnp.bfloat16
    )
    received = item_rows.reshape(-1, item_rows.shape[-1])
    mapped = mapped_rows.reshape(-1, mapped_rows.shape[-1])
    capsules = dynamic_route(mapped, hist_index, hist_len, route_init)
    label_rows = jnp.take(received, label_index, axis=0).astype(jnp.float32)
    user_vec, positive = label_attention(capsules, label_rows, label_counts)
    neg_unit = item_tower(neg_feats, w_in, bias_in, w_out)
    block_unit, block_ids, block_counts = (
        lax.all_gather(neg_unit, "user", axis=0, tiled=True),
        lax.all_gather(neg_ids, "user", axis=0, tiled=True),
        lax.all_gather(neg_counts, "user", axis=0, tiled=True),
    )
    all_vec, all_labels = (
        lax.all_gather(user_vec, "pool", axis=0, tiled=True),
        lax.all_gather(label_ids, "pool", axis=0, tiled=True),
    )
    negative_sum = lax.psum_scatter(
        exp_terms(all_vec, all_labels, block_unit, block_ids, block_counts),
        "pool",
        scatter_dimension=0,
        tiled=True,
    )
    partition = jnp.exp(positive) + negative_sum
    user_loss = jnp.log(partition) - positive
    return (capsules.reshape(capsules.shape[0], -1), user_loss)


def solution(mesh):
    in_specs = (
        P(("user", "pool"), None),
        P(),
        P(),
        P(),
        P(),
        P(None, ("user", "pool"), None),
        P(("user", "pool"), None),
        P(("user", "pool")),
        P(("user", "pool"), None, None),
        P(("user", "pool")),
        P(("user", "pool")),
        P(("user", "pool")),
        P(("user", "pool"), None),
        P(("user", "pool")),
        P(("user", "pool")),
    )
    out_specs = (P(("user", "pool"), None), P(("user", "pool")))
    return jax.shard_map(
        on_device, mesh=mesh, in_specs=in_specs, out_specs=out_specs, check_vma=False
    )
```

profile of v0, /device:TPU:0, one launch (start us, length us, event | category | flops | bytes accessed | tf_op | source)
XLA Modules:
  0.0 533.0 jit_solution(9652071260504484841)
XLA Ops:
  0.6 0.8 compare_select_fusion.2
  1.5 0.7 compare_and_fusion
  2.2 5.0 multiply_reduce_fusion
  7.3 1.3 multiply_convert_fusion
  8.7 0.2 copy.52
  9.2 2.0 gather_fusion
  11.2 1.0 broadcast_select_fusion
  12.2 7.3 %all-to-all-start = ((bf16[32,16,512]{2,1,0:T(8,128)(2,1)}), bf16[32,16,512]{2,1,0:T(8,128)(2,1)S(1)}, u32[]{:S(2)}, u32[]{:S(2)}) async-start(bf16[32,16,512]{2,1,0:T(8,128)(2,1)} %broadcast_select_fusion), calls=%async_computation | async-start | bytes 1048576 | tf_op jit(solution)/shard_map/all_to_all | solution.py:107
  19.8 2.4 multiply_reduce_fusion.1
  22.2 0.1 fusion.23
  22.5 2.7 copy.48
  25.2 48.0 %scatter_custom_fusion = f32[16384,4]{1,0:T(8,128)} fusion(s32[8192]{0:T(1024)S(1)} %bitcast.118, f32[8192,4]{1,0:T(8,128)} %copy.48, f32[]{:T(128)} %constant.17.clone.1), kind=kCustom, calls=%fused_computation.12 | custom fusion | flops 32768 | bytes 262656
  73.2 5.3 copy.49
  78.6 0.6 fusion.63
  80.5 0.2 dynamic-update-slice
  80.7 11.6 %all-reduce = s32[256]{0:T(256)S(1)} all-reduce(s32[256]{0:T(256)S(1)} %dynamic-update-slice), channel_id=1, replica_groups=mesh['user'=4,'pool'=8] {'pool'}, use_global_device_ids=true, to_apply=%add | all-reduce | flops 256 | bytes 2048
  92.4 5.0 all-gather.1
  97.4 5.0 all-gather
  102.5 7.9 %all_gather.18 = bf16[512,512]{1,0:T(8,128)(2,1)} all-gather(bf16[128,512]{1,0:T(8,128)(2,1)S(1)} %multiply_convert_fusion.1), channel_id=1, replica_groups=mesh['user'=4,'pool'=8] {'user'}, dimensions={0}, use_global_device_ids=true | all-gather | bytes 655360 | tf_op jit(solution)/shard_map/all_gather | solution.py:118
  110.4 0.4 convolution_convert_fusion
  110.9 0.5 multiply_reduce_fusion.6
  111.3 0.3 fusion.38
  111.7 4.7 copy.53
  116.3 118.6 %gather_fusion.2 = f32[8192,4]{1,0:T(8,128)} fusion(f32[32,4,512]{1,2,0:T(8,128)} %copy.53, s32[8192]{0:T(1024)S(1)} %bitcast.100), kind=kCustom, calls=%fused_computation.clone | custom fusion | bytes 327680 | tf_op jit(solution)/shard_map/jit(take_along_axis)/gather | solution.py:63
  235.0 2.8 copy.54
  237.9 0.1 fusion.25
  238.0 2.7 copy.55
  240.7 48.0 %scatter_custom_fusion.1 = f32[16384,4]{1,0:T(8,128)} fusion(s32[8192]{0:T(1024)S(1)} %bitcast.119, f32[8192,4]{1,0:T(8,128)} %copy.55, f32[]{:T(128)} %constant.17.clone.1), kind=kCustom, calls=%fused_computation.10 | custom fusion | flops 32768 | bytes 262656
  288.7 5.2 copy.56
  293.9 0.5 multiply_reduce_fusion.5
  294.4 0.3 fusion.39
  294.7 4.7 copy.57
  299.4 118.6 %gather_fusion.3 = f32[8192,4]{1,0:T(8,128)} fusion(f32[32,4,512]{1,2,0:T(8,128)} %copy.57, s32[8192]{0:T(1024)S(1)} %bitcast.101), kind=kCustom, calls=%fused_computation.1.clone | custom fusion | bytes 327680 | tf_op jit(solution)/shard_map/jit(take_along_axis)/gather | solution.py:63
  418.0 2.8 copy.58
  420.9 0.2 fusion.27
  421.0 2.7 copy.59
  423.7 48.0 %scatter_custom_fusion.2 = f32[16384,4]{1,0:T(8,128)} fusion(s32[8192]{0:T(1024)S(1)} %bitcast.120, f32[8192,4]{1,0:T(8,128)} %copy.59, f32[]{:T(128)} %constant.17.clone.1), kind=kCustom, calls=%fused_computation.14 | custom fusion | flops 32768 | bytes 262656
  471.7 6.0 %copy.60 = f32[32,512,4]{1,0,2:T(8,128)} copy(f32[32,512,4]{2,1,0:T(8,128)} %bitcast.102) | data formatting | bytes 524288
  477.7 1.4 multiply_reduce_fusion.4
  479.2 0.6 gather_fusion.1
  479.9 0.2 multiply_reduce_fusion.3
  480.1 0.1 multiply_reduce_fusion.2
  480.3 30.7 %all_gather.17 = bf16[256,512]{1,0:T(8,128)(2,1)S(1)} all-gather(bf16[32,512]{1,0:T(8,128)(2,1)S(1)} %get-tuple-element.3), channel_id=1, replica_groups=mesh['user'=4,'pool'=8] {'pool'}, dimensions={0}, use_global_device_ids=true | all-gather | bytes 294912 | tf_op jit(solution)/shard_map/all_gather | solution.py:123
  511.0 0.2 multiply_reduce_fusion.8
  511.2 0.7 copy.62
  511.9 1.5 fusion.15
  513.4 18.9 %all-reduce.1 = f32[256]{0:T(256)S(1)} all-reduce(f32[256]{0:T(256)S(1)} %fusion.15), channel_id=2, replica_groups=mesh['user'=4,'pool'=8] {'pool'}, use_global_device_ids=true, to_apply=%region_16.18.clone | all-reduce | flops 256 | bytes 2048
  532.4 0.6 fusion.57
  (62 shorter events, 1.0 us)
Async XLA Ops:
  0.6 1.6 copy-start
  8.6 10.9 %copy-start.3 = (s32[32,256]{1,0:T(8,128)S(1)}, s32[32,256]{1,0:T(8,128)}, u32[]{:S(2)}) copy-start(s32[32,256]{1,0:T(8,128)} %param.23) | copy-start | bytes 98308
  8.6 10.9 %copy-start.9 = (s32[2]{0:T(128)S(1)}, s32[2]{0:T(128)}, u32[]{:S(2)}) copy-start(s32[2]{0:T(128)} %constant.41) | copy-start | bytes 28
  8.6 11.0 %copy-start.10 = (s32[2]{0:T(128)S(1)}, s32[2]{0:T(128)}, u32[]{:S(2)}) copy-start(s32[2]{0:T(128)} %constant.38) | copy-start | bytes 28
  8.7 11.1 %copy-start.8 = (s32[32]{0:T(128)S(1)}, s32[32]{0:T(128)}, u32[]{:S(2)}) copy-start(s32[32]{0:T(128)} %param.24) | copy-start | bytes 388
  8.7 11.1 %copy-start.4 = (bf16[128,512]{1,0:T(8,128)(2,1)S(1)}, bf16[128,512]{1,0:T(8,128)(2,1)}, u32[]{:S(2)}) copy-start(bf16[128,512]{1,0:T(8,128)(2,1)} %param.29) | copy-start | bytes 393220
  8.7 11.1 %copy-start.6 = (f32[2048]{0:T(1024)S(1)}, f32[2048]{0:T(1024)}, u32[]{:S(2)}) copy-start(f32[2048]{0:T(1024)} %param.19) | copy-start | bytes 24580
  11.1 11.1 %copy-start.5 = (f32[32,4,256]{2,1,0:T(4,128)S(1)}, f32[32,4,256]{2,1,0:T(4,128)}, u32[]{:S(2)}) copy-start(f32[32,4,256]{2,1,0:T(4,128)} %param.25) | copy-start | bytes 393220
  11.2 11.3 %copy-start.15 = (s32[32]{0:T(128)S(1)}, s32[32]{0:T(128)}, u32[]{:S(2)}) copy-start(s32[32]{0:T(128)} %param.26) | copy-start | bytes 388
  12.2 98.2 %all-to-all-start = ((bf16[32,16,512]{2,1,0:T(8,128)(2,1)}), bf16[32,16,512]{2,1,0:T(8,128)(2,1)S(1)}, u32[]{:S(2)}, u32[]{:S(2)}) async-start(bf16[32,16,512]{2,1,0:T(8,128)(2,1)} %broadcast_select_fusion), calls=%async_computation | async-start | bytes 1048576 | tf_op jit(solution)/shard_map/all_to_all | solution.py:107
  73.2 5.4 %copy-start.7 = (u32[32]{0:T(128)S(1)}, u32[32]{0:T(128)}, u32[]{:S(2)}) copy-start(u32[32]{0:T(128)} %constant.106) | copy-start | bytes 388
  73.2 7.3 %copy-start.14 = (s32[32]{0:T(128)S(1)}, s32[32]{0:T(128)}, u32[]{:S(2)}) copy-start(s32[32]{0:T(128)} %param.27) | copy-start | bytes 388
  73.2 19.2 %copy-start.11 = (s32[128]{0:T(128)S(1)}, s32[128]{0:T(128)}, u32[]{:S(2)}) copy-start(s32[128]{0:T(128)} %param.31) | copy-start | bytes 1540
  73.2 24.2 %copy-start.12 = (s32[128]{0:T(128)S(1)}, s32[128]{0:T(128)}, u32[]{:S(2)}) copy-start(s32[128]{0:T(128)} %param.30) | copy-start | bytes 1540
  73.2 37.2 %copy-start.2 = (bf16[512,512]{1,0:T(8,128)(2,1)S(1)}, bf16[512,512]{1,0:T(8,128)(2,1)}, u32[]{:S(2)}) copy-start(bf16[512,512]{1,0:T(8,128)(2,1)} %param.21) | copy-start | bytes 1572868
  471.7 61.3 %copy-start.1 = (bf16[2048,512]{1,0:T(8,128)(2,1)S(1)}, bf16[2048,512]{1,0:T(8,128)(2,1)}, u32[]{:S(2)}) copy-start(bf16[2048,512]{1,0:T(8,128)(2,1)} %param.20) | copy-start | bytes 6291460
  477.7 54.6 %copy-start.13 = (s32[32]{0:T(128)S(1)}, s32[32]{0:T(128)}, u32[]{:S(2)}) copy-start(s32[32]{0:T(128)} %param.28) | copy-start | bytes 388
where the time goes:
time: 535 us; the launch traced here: 533 us
  local copies, waits for them, and re-layouts  282 us (53%)
  other arithmetic  150 us (28%)
  blocking collectives  79.3 us (15%)
  matrix products  12.3 us (2%)
  starting transfers between devices  7.33 us (1%)
    gather x4, local copies, waits for them, and re-layouts, dynamic_route(): agreement = jnp.take_along_axis(slot_scores, hist_index[:, None, :], axis=2)  243 us
    unnamed x7, other arithmetic  144 us
    all_gather x1, blocking collectives, on_device(): lax.all_gather(user_vec, 'pool', axis=0, tiled=True)  30.7 us
    unnamed x2, blocking collectives  30.6 us
    unnamed x41, local copies, waits for them, and re-layouts  17.6 us
  transfers between devices with their start and end apart: 1, of which 0 were waited for; matrix products, arithmetic and copies ran while one was open for 11% of the time, Pallas kernels for 0%

commit v1 on v0

v1 whole, which is shorter than its diff:
```python
import functools

import jax
import jax.numpy as jnp
from jax import lax
from jax.experimental import pallas as pl
from jax.experimental.pallas import tpu as pltpu
from jax.sharding import PartitionSpec as P

INTERESTS = 4
ITERS = 3
LANES = 128
SUB = 8
GROUP_USERS = 8

norm_epsilon = 1e-06
attend_scale = 8.0
logit_scale = 20.0

f32 = jnp.float32
bf16 = jnp.bfloat16
i32 = jnp.int32


def mm(a, b):
    return jnp.dot(a, b, preferred_element_type=f32)


def mm_nt(a, b):
    return lax.dot_general(a, b, (((1,), (1,)), ((), ())), preferred_element_type=f32)


def iota(shape, axis):
    return lax.broadcasted_iota(i32, shape, axis)


def to_column(row):
    n = row.shape[1]
    eye = iota((n, n), 0) == iota((n, n), 1)
    return jnp.sum(jnp.where(eye, row, 0.0), axis=1, keepdims=True)


def to_row(column):
    n = column.shape[0]
    eye = iota((n, n), 0) == iota((n, n), 1)
    return jnp.sum(jnp.where(eye, column, 0.0), axis=0, keepdims=True)


def id_digits(ids_row):
    low = to_column((ids_row & 255).astype(f32))
    mid = to_column(((ids_row >> 8) & 255).astype(f32))
    high = to_column((ids_row >> 16).astype(f32))
    return low, mid, high


def lane_columns(columns, rows):
    lane = iota((rows, LANES), 1)
    out = jnp.zeros((rows, LANES), f32)
    for at, column in enumerate(columns):
        out = jnp.where(lane == at, column, out)
    return out


def select_kernel(fetch_ref, rows_ref, out_ref):
    blocks, _, cap = fetch_ref.shape
    count = blocks * cap
    fetch = fetch_ref[:, 0, :]
    row = iota((count, blocks), 0)
    block = iota((count, blocks), 1)
    pick = jnp.where((row >= block * cap) & (row < block * cap + cap), 1.0, 0.0).astype(bf16)
    high = mm(pick, (fetch >> 7).astype(f32).astype(bf16))
    low = mm(pick, (fetch & 127).astype(f32).astype(bf16))
    place = iota((count, cap), 1) == lax.rem(iota((count, cap), 0), jnp.int32(cap))
    column = jnp.sum(jnp.where(place, high * 128.0 + low, 0.0), axis=1, keepdims=True)
    item = iota((count, rows_ref.shape[0]), 1).astype(f32)
    chosen = jnp.where(item == column, 1.0, 0.0).astype(bf16)
    out_ref[...] = mm(chosen, rows_ref[...]).astype(bf16)


def select_rows(fetch, rows):
    blocks, _, cap = fetch.shape
    return pl.pallas_call(
        select_kernel,
        out_shape=jax.ShapeDtypeStruct((blocks * cap, rows.shape[1]), bf16),
        name="select_rows",
    )(fetch, rows)


def tower_step(rows_ref, w_in_ref, bias_ref, w_out_ref, acc_ref):
    hidden = mm(rows_ref[...], w_in_ref[...]) + bias_ref[...]
    hidden = jnp.maximum(hidden, 0.0).astype(bf16)
    part = mm(hidden, w_out_ref[...])

    @pl.when(pl.program_id(0) == 0)
    def _():
        acc_ref[...] = part

    @pl.when(pl.program_id(0) > 0)
    def _():
        acc_ref[...] += part


def unit_of(acc_ref):
    embedding = acc_ref[...]
    total = jnp.sum(embedding * embedding, axis=1, keepdims=True)
    return (embedding * lax.rsqrt(total + norm_epsilon)).astype(bf16)


def item_kernel(rows_ref, w_in_ref, bias_ref, w_out_ref, bilinear_ref, unit_ref, mapped_ref, acc_ref):
    tower_step(rows_ref, w_in_ref, bias_ref, w_out_ref, acc_ref)

    @pl.when(pl.program_id(0) == pl.num_programs(0) - 1)
    def _():
        unit = unit_of(acc_ref)
        unit_ref[...] = unit
        mapped_ref[...] = mm(unit, bilinear_ref[...]).astype(bf16)


def neg_kernel(rows_ref, w_in_ref, bias_ref, w_out_ref, ids_ref, counts_ref, out_ref, acc_ref):
    tower_step(rows_ref, w_in_ref, bias_ref, w_out_ref, acc_ref)

    @pl.when(pl.program_id(0) == pl.num_programs(0) - 1)
    def _():
        width = acc_ref.shape[1]
        out_ref[:, :width] = unit_of(acc_ref)
        columns = id_digits(ids_ref[...]) + (to_column(counts_ref[...].astype(f32)),)
        out_ref[:, width:] = lane_columns(columns, acc_ref.shape[0]).astype(bf16)


def chunk_of(hidden_units):
    return 512 if hidden_units % 512 == 0 else hidden_units


def tower_specs(rows, w_in, w_out):
    chunk = chunk_of(w_in.shape[1])
    return chunk, [
        pl.BlockSpec(rows.shape, lambda i: (0, 0)),
        pl.BlockSpec((w_in.shape[0], chunk), lambda i: (0, i)),
        pl.BlockSpec((1, chunk), lambda i: (0, i)),
        pl.BlockSpec((chunk, w_out.shape[1]), lambda i: (i, 0)),
    ]


def whole(shape):
    return pl.BlockSpec(shape, lambda i: (0,) * len(shape))


def item_tower(rows, w_in, bias, w_out, bilinear):
    chunk, specs = tower_specs(rows, w_in, w_out)
    shape = (rows.shape[0], w_out.shape[1])
    return pl.pallas_call(
        item_kernel,
        grid=(w_in.shape[1] // chunk,),
        in_specs=specs + [whole(bilinear.shape)],
        out_specs=[whole(shape), whole((shape[0], bilinear.shape[1]))],
        out_shape=[
            jax.ShapeDtypeStruct(shape, bf16),
            jax.ShapeDtypeStruct((shape[0], bilinear.shape[1]), bf16),
        ],
        scratch_shapes=[pltpu.VMEM(shape, f32)],
        name="item_tower",
    )(rows, w_in, bias, w_out, bilinear)


def neg_tower(rows, w_in, bias, w_out, ids, counts):
    chunk, specs = tower_specs(rows, w_in, w_out)
    shape = (rows.shape[0], w_out.shape[1])
    return pl.pallas_call(
        neg_kernel,
        grid=(w_in.shape[1] // chunk,),
        in_specs=specs + [whole(ids.shape), whole(counts.shape)],
        out_specs=whole((shape[0], shape[1] + LANES)),
        out_shape=jax.ShapeDtypeStruct((shape[0], shape[1] + LANES), bf16),
        scratch_shapes=[pltpu.VMEM(shape, f32)],
        name="neg_tower",
    )(rows, w_in, bias, w_out, ids, counts)


def event_weights(logits, live):
    raised = [jnp.exp(one) for one in logits]
    total = functools.reduce(jnp.add, raised)
    return [(one / total * live).astype(bf16).astype(f32) for one in raised]


def scatter_weights(weights, upper, onehot_ref, slot_ref):
    users = weights[0].shape[0]
    pages = slot_ref.shape[1] // LANES
    count = pages * INTERESTS * SUB
    for group in range(users // GROUP_USERS):
        at = slice(group * GROUP_USERS, (group + 1) * GROUP_USERS)
        base = jnp.concatenate(
            [
                jnp.where(upper[at] == page, weights[k][at], 0.0)
                for page in range(pages)
                for k in range(INTERESTS)
            ],
            axis=0,
        )
        user = iota((count, 1), 0) & (GROUP_USERS - 1)
        left = jnp.concatenate(
            [
                jnp.where((user >> 1) == pair, base, 0.0).astype(bf16)
                for pair in range(GROUP_USERS // 2)
            ],
            axis=1,
        )
        both = mm_nt(left, onehot_ref[group])
        own = jnp.where((user & 1) == 0, both[:, :LANES], both[:, LANES:])
        for page in range(pages):
            for k in range(INTERESTS):
                source = (page * INTERESTS + k) * SUB
                target = k * users + group * GROUP_USERS
                slot_ref[target : target + SUB, page * LANES : (page + 1) * LANES] = own[
                    source : source + SUB
                ]


def live_mask(length_ref, shape):
    length = to_column(length_ref[...].astype(f32))
    return jnp.where(iota(shape, 1).astype(f32) < length, 1.0, 0.0)


def prepare_kernel(index_ref, length_ref, init_ref, onehot_ref, slot_ref):
    users, events = index_ref.shape
    index = index_ref[...]
    upper = index >> 7
    lower = index & (LANES - 1)
    lane_id = iota((LANES, events), 0)
    for user in range(users):
        group, within = divmod(user, GROUP_USERS)
        pair, side = divmod(within, 2)
        hit = jnp.where(lane_id == lower[user : user + 1], 1.0, 0.0).astype(bf16)
        onehot_ref[
            group, side * LANES : (side + 1) * LANES, pair * events : (pair + 1) * events
        ] = hit
    live = live_mask(length_ref, index.shape)
    weights = event_weights([init_ref[:, k, :] for k in range(INTERESTS)], live)
    scatter_weights(weights, upper, onehot_ref, slot_ref)


def prepare(index, length, init, slots):
    users, events = index.shape
    return pl.pallas_call(
        prepare_kernel,
        out_shape=[
            jax.ShapeDtypeStruct(
                (users // GROUP_USERS, 2 * LANES, GROUP_USERS // 2 * events), bf16
            ),
            jax.ShapeDtypeStruct((INTERESTS * users, slots), f32),
        ],
        name="prepare",
    )(index, length, init)


def route_kernel(
    unit_ref,
    mapped_ref,
    onehot_ref,
    first_ref,
    index_ref,
    length_ref,
    init_ref,
    label_ref,
    ids_ref,
    counts_ref,
    interests_ref,
    vec_ref,
    positive_ref,
    slot_ref,
):
    users, events = index_ref.shape
    slots, width = mapped_ref.shape
    index = index_ref[...]
    upper = index >> 7
    lower = index & (LANES - 1)
    live = live_mask(length_ref, index.shape)
    mapped = mapped_ref[...]
    logits = [init_ref[:, k, :] for k in range(INTERESTS)]
    capsules = None
    for iteration in range(ITERS):
        if iteration:
            scatter_weights(event_weights(logits, live), upper, onehot_ref, slot_ref)
        slot_weights = first_ref[...] if iteration == 0 else slot_ref[...]
        coarse = slot_weights.astype(bf16)
        rest = (slot_weights - coarse.astype(f32)).astype(bf16)
        sums = mm(coarse, mapped) + mm(rest, mapped)
        norm_sq = jnp.sum(sums * sums, axis=1, keepdims=True)
        capsules = sums * (jnp.sqrt(norm_sq) / (1.0 + norm_sq))
        if iteration + 1 < ITERS:
            scores = mm_nt(capsules.astype(bf16), mapped)
            for k in range(INTERESTS):
                chunks = []
                for at in range(0, events, LANES):
                    low = lower[:, at : at + LANES]
                    high = upper[:, at : at + LANES]
                    found = jnp.zeros((users, LANES), f32)
                    for page in range(slots // LANES):
                        piece = scores[
                            k * users : (k + 1) * users, page * LANES : (page + 1) * LANES
                        ]
                        taken = jnp.take_along_axis(
                            piece, low, axis=1, mode="promise_in_bounds"
                        )
                        found = jnp.where(high == page, taken, found)
                    chunks.append(found)
                logits[k] = logits[k] + jnp.concatenate(chunks, axis=1)
    each = [capsules[k * users : (k + 1) * users] for k in range(INTERESTS)]
    for k in range(INTERESTS):
        interests_ref[:, k * width : (k + 1) * width] = each[k]
    label = to_column(label_ref[...].astype(f32))
    chosen = jnp.where(iota((users, slots), 1).astype(f32) == label, 1.0, 0.0).astype(bf16)
    label_rows = mm(chosen, unit_ref[...])
    raised = [
        jnp.exp(attend_scale * jnp.sum(one * label_rows, axis=1, keepdims=True)) for one in each
    ]
    total = functools.reduce(jnp.add, raised)
    user_vec = functools.reduce(jnp.add, [(r / total) * one for r, one in zip(raised, each)])
    user_vec = user_vec.astype(bf16)
    vec_ref[:, :width] = user_vec
    vec_ref[:, width:] = lane_columns(id_digits(ids_ref[...]), users).astype(bf16)
    match = jnp.sum(user_vec.astype(f32) * label_rows, axis=1, keepdims=True)
    positive_ref[...] = logit_scale * to_row(match) - jnp.log(counts_ref[...].astype(f32))


def route(unit, mapped, onehot, first, index, length, init, label, ids, counts):
    users = index.shape[0]
    width = mapped.shape[1]
    return pl.pallas_call(
        route_kernel,
        out_shape=[
            jax.ShapeDtypeStruct((users, INTERESTS * width), f32),
            jax.ShapeDtypeStruct((users, width + LANES), bf16),
            jax.ShapeDtypeStruct((1, users), f32),
        ],
        scratch_shapes=[pltpu.VMEM(first.shape, f32)],
        name="route",
    )(unit, mapped, onehot, first, index, length, init, label, ids, counts)


def sums_kernel(parts, pieces, *refs):
    vec_refs = refs[:parts]
    neg_refs = refs[parts : parts + pieces]
    out_refs = refs[parts + pieces :]
    vec = jnp.concatenate([ref[...] for ref in vec_refs], axis=0)
    users = vec_refs[0].shape[0]
    width = vec.shape[1] - LANES
    place = iota((SUB, LANES), 1)
    scale = jnp.where(
        place == 0, 1.0, jnp.where(place == 1, 256.0, jnp.where(place == 2, 65536.0, 0.0))
    ).astype(bf16)
    label_ids = mm_nt(scale, vec[:, width:])[:1]
    row = iota((LANES, LANES), 0)
    to_id = jnp.where(
        row == 0, 1.0, jnp.where(row == 1, 256.0, jnp.where(row == 2, 65536.0, 0.0))
    ).astype(bf16)
    to_count = jnp.where(row == 3, 1.0, 0.0).astype(bf16)
    total = jnp.zeros((1, vec.shape[0]), f32)
    for ref in neg_refs:
        extra = ref[:, width:]
        ids = mm(extra, to_id)[:, :1]
        counts = mm(extra, to_count)[:, :1]
        dots = mm_nt(ref[:, :width], vec[:, :width])
        terms = jnp.exp(logit_scale * dots) * (1.0 / counts)
        total += jnp.sum(jnp.where(ids != label_ids, terms, 0.0), axis=0, keepdims=True)
    for part, ref in enumerate(out_refs):
        ref[...] = total[:, part * users : (part + 1) * users]


def negative_sums(vecs, negs):
    users = vecs[0].shape[0]
    return pl.pallas_call(
        functools.partial(sums_kernel, len(vecs), len(negs)),
        out_shape=[jax.ShapeDtypeStruct((1, users), f32) for _ in vecs],
        name="negative_sums",
    )(*vecs, *negs)


def swap(array, axis, size, bit):
    return lax.ppermute(array, axis, [(at, at ^ bit) for at in range(size)])


def rotate(array, axis, size, step):
    return lax.ppermute(array, axis, [(at, (at + step) % size) for at in range(size)])


def on_device(
    user_size,
    pool_size,
    item_feats,
    w_in,
    bias_in,
    w_out,
    bilinear,
    fetch_table,
    hist_index,
    hist_len,
    route_init,
    label_index,
    label_ids,
    label_counts,
    neg_feats,
    neg_ids,
    neg_counts,
):
    bias = bias_in.reshape(1, -1)
    outgoing = select_rows(fetch_table, item_feats)
    arrived = lax.all_to_all(
        outgoing.reshape(fetch_table.shape[0], fetch_table.shape[2], -1),
        ("user", "pool"),
        split_axis=0,
        concat_axis=0,
        tiled=True,
    )
    arrived = arrived.reshape(outgoing.shape)

    own_neg = neg_tower(
        neg_feats, w_in, bias, w_out, neg_ids.reshape(1, -1), neg_counts.reshape(1, -1)
    )
    length = hist_len.reshape(1, -1)
    onehot, first = prepare(hist_index, length, route_init, outgoing.shape[0])

    bits = [1 << at for at in range(pool_size.bit_length() - 1)]
    negs = [own_neg]
    for bit in bits[1:] + bits[:1]:
        held = negs[0] if len(negs) == 1 else jnp.concatenate(negs, axis=0)
        negs.append(swap(held, "pool", pool_size, bit))

    unit, mapped = item_tower(arrived, w_in, bias, w_out, bilinear)
    interests, vec, positive = route(
        unit,
        mapped,
        onehot,
        first,
        hist_index,
        length,
        route_init,
        label_index.reshape(1, -1),
        label_ids.reshape(1, -1),
        label_counts.reshape(1, -1),
    )
    vecs = [vec] + [rotate(vec, "user", user_size, step) for step in range(1, user_size)]
    sums = negative_sums(vecs, negs)
    partition = jnp.exp(positive) + sums[0]
    for step in range(1, user_size):
        partition += rotate(sums[step], "user", user_size, user_size - step)
    user_loss = jnp.log(partition) - positive
    return (interests, user_loss.reshape(-1))


def solution(mesh):
    both = ("user", "pool")
    in_specs = (
        P(both, None),
        P(),
        P(),
        P(),
        P(),
        P(None, both, None),
        P(both, None),
        P(both),
        P(both, None, None),
        P(both),
        P(both),
        P(both),
        P(both, None),
        P(both),
        P(both),
    )
    out_specs = (P(both, None), P(both))
    body = functools.partial(on_device, mesh.shape["user"], mesh.shape["pool"])
    return jax.shard_map(
        body, mesh=mesh, in_specs=in_specs, out_specs=out_specs, check_vma=False
    )
```

time: 535 us -> 71.6 us (0.13)
  local copies, waits for them, and re-layouts: 282 us -> 2.97 us
  other arithmetic: 150 us -> 2.26 us
  blocking collectives: 79.3 us -> 0 us
  Pallas kernels: 0 us -> 26.4 us
  waiting for transfers between devices: 0.01 us -> 22.4 us
  matrix products: 12.3 us -> 0 us
  starting transfers between devices: 7.33 us -> 16.5 us
    gather x6 -> x0, local copies, waits for them, and re-layouts: 246 us -> none  [the longest x4 243 us: dynamic_route(): agreement = jnp.take_along_axis(slot_scores, hist_index[:, None, :], axis=2)]
    unnamed x7 -> x0, other arithmetic: 144 us -> none
    all_gather x4 -> x0, blocking collectives: 48.7 us -> none  [the longest x1 30.7 us: on_device(): lax.all_gather(user_vec, 'pool', axis=0, tiled=True)]
    unnamed x2 -> x0, blocking collectives: 30.6 us -> none
    pallas_call x0 -> x6, Pallas kernels: none -> 26.4 us  [the longest x1 6.78 us: item_tower(): pl.pallas_call(item_kernel, grid=(w_in.shape[1] // chunk,), in_specs=spec...]
    ppermute x0 -> x9, waiting for transfers between devices: none -> 22.1 us  [the longest x3 18.1 us: swap(): return lax.ppermute(array, axis, [(at, at ^ bit) for at in range(size)])]
    unnamed x41 -> x21, local copies, waits for them, and re-layouts: 17.6 us -> 2.97 us
    ppermute x0 -> x9, starting transfers between devices: none -> 12.7 us  [the longest x3 7.36 us: swap(): return lax.ppermute(array, axis, [(at, at ^ bit) for at in range(size)])]
  transfers between devices with their start and end apart: 1 -> 10, of which waited for: 0 -> 8; matrix products, arithmetic and copies ran while one was open for 11% -> 1% of each run, Pallas kernels for 0% -> 27%
where the time goes in v1:
time: 71.6 us; the launch traced here: 71.2 us
  Pallas kernels  26.4 us (37%)
  waiting for transfers between devices  22.4 us (31%)
  starting transfers between devices  16.5 us (23%)
  local copies, waits for them, and re-layouts  2.97 us (4%)
  other arithmetic  2.26 us (3%)
    ppermute x3, waiting for transfers between devices, swap(): return lax.ppermute(array, axis, [(at, at ^ bit) for at in range(size)])  18.1 us
    ppermute x3, starting transfers between devices, swap(): return lax.ppermute(array, axis, [(at, at ^ bit) for at in range(size)])  7.36 us
    pallas_call x1, Pallas kernels, item_tower(): pl.pallas_call(item_kernel, grid=(w_in.shape[1] // chunk,), in_specs=spec...  6.78 us
    pallas_call x1, Pallas kernels, route(): pl.pallas_call(route_kernel, out_shape=[jax.ShapeDtypeStruct((users, INTE...  6.29 us
    ppermute x6, starting transfers between devices, rotate(): lax.ppermute(array, axis, [(at, (at + step) % size) for at in range(size)])  5.31 us
    pallas_call x1, Pallas kernels, neg_tower(): pl.pallas_call(neg_kernel, grid=(w_in.shape[1] // chunk,), in_specs=specs...  4.75 us
    ppermute x6, waiting for transfers between devices, rotate(): lax.ppermute(array, axis, [(at, (at + step) % size) for at in range(size)])  3.97 us
    all_to_all x1, starting transfers between devices, on_device(): lax.all_to_all(outgoing.reshape(fetch_table.shape[0], fetch_table.shape[2...  3.83 us
  transfers between devices with their start and end apart: 10, of which 8 were waited for; matrix products, arithmetic and copies ran while one was open for 1% of the time, Pallas kernels for 27%

profile of v1, /device:TPU:0, one launch (start us, length us, event | category | flops | bytes accessed | tf_op | source)
XLA Modules:
  0.0 71.2 jit_solution(12905614451894173160)
XLA Ops:
  0.6 0.0 copy-start.8
  0.6 4.7 %neg_tower.1.refs_4_ = bf16[128,640]{1,0:T(8,128)(2,1)} custom-call(bf16[128,512]{1,0:T(8,128)(2,1)} %rows_ref.3, bf16[512,2048]{1,0:T(8,128)(2,1)} %w_in_ref.3, f32[1,2048]{1,0:T(1,128)} %bitcast.13, bf16[2048,512]{1,0:T(8,128)(2,1)} %w_out_ref.3, s32[1,128]{1,0:T(1,128)} %bitcast.17, s32[1,128]{1,0:T(1,128)} %bitcast.18), custom_call_target="tpu_custom_call" | custom-call | tf_op jit(solution)/shard_map/neg_tower/pallas_call | solution.py:168
  5.4 0.0 copy-start
  5.4 3.0 %collective-permute-start.3 = (bf16[128,640]{1,0:T(8,128)(2,1)}, bf16[128,640]{1,0:T(8,128)(2,1)S(1)}, u32[]{:S(2)}, u32[]{:S(2)}) collective-permute-start(bf16[128,640]{1,0:T(8,128)(2,1)} %neg_tower.1.refs_4_), channel_id=1, source_target_pairs={{0,2},{1,3},{2,0},{3,1},{4,6},{5,7},{6,4},{7,5},{8,10},{9,11},{10,... | collective-permute-start | bytes 491528 | tf_op jit(solution)/shard_map/ppermute | solution.py:379
  8.4 4.5 %collective-permute-done.3.refs_5_ = bf16[128,640]{1,0:T(8,128)(2,1)S(1)} collective-permute-done((bf16[128,640]{1,0:T(8,128)(2,1)}, bf16[128,640]{1,0:T(8,128)(2,1)S(1)}, u32[]{:S(2)}, u32[]{:S(2)}) %collective-permute-start.3) | collective-permute-done | bytes 163872 | tf_op jit(solution)/shard_map/ppermute | solution.py:379
  12.9 0.0 copy-start.2
  12.9 1.0 %pad_maximum_fusion.1 = bf16[256,640]{1,0:T(8,128)(2,1)S(1)} fusion(bf16[128,640]{1,0:T(8,128)(2,1)S(1)} %collective-permute-done.3.refs_5_, bf16[128,640]{1,0:T(8,128)(2,1)} %neg_tower.1.refs_4_), kind=kLoop, calls=%fused_computation.1 | loop fusion | flops 655360 | bytes 655360 | tf_op jit(solution)/shard_map/concatenate | solution.py:425
  13.9 2.8 %collective-permute-start.4 = (bf16[256,640]{1,0:T(8,128)(2,1)S(1)}, bf16[256,640]{1,0:T(8,128)(2,1)S(1)}, u32[]{:S(2)}, u32[]{:S(2)}) collective-permute-start(bf16[256,640]{1,0:T(8,128)(2,1)S(1)} %pad_maximum_fusion.1), channel_id=1, source_target_pairs={{0,4},{1,5},{2,6},{3,7},{4,0},{5,1},{6,2},{7,3},{8,12},{9,13},{10,... | collective-permute-start | bytes 983048 | tf_op jit(solution)/shard_map/ppermute | solution.py:379
  16.7 0.0 copy-done.8
  16.7 0.7 copy.17.fetch_ref
  17.4 2.5 %select_rows.1 = bf16[512,512]{1,0:T(8,128)(2,1)} custom-call(s32[32,1,16]{2,1,0:T(1,128)} %copy.17.fetch_ref, bf16[512,512]{1,0:T(8,128)(2,1)} %rows_ref.2), custom_call_target="tpu_custom_call" | custom-call | tf_op jit(solution)/shard_map/select_rows/pallas_call | solution.py:82
  19.9 3.8 %all-to-all-start = ((bf16[32,16,512]{2,1,0:T(8,128)(2,1)}), bf16[32,16,512]{2,1,0:T(8,128)(2,1)S(1)}, u32[]{:S(2)}, u32[]{:S(2)}) async-start(bf16[32,16,512]{2,1,0:T(8,128)(2,1)} %bitcast.12), calls=%async_computation | async-start | bytes 1048576 | tf_op jit(solution)/shard_map/all_to_all | solution.py:407
  23.7 13.6 %collective-permute-done.4.refs_6_ = bf16[256,640]{1,0:T(8,128)(2,1)S(1)} collective-permute-done((bf16[256,640]{1,0:T(8,128)(2,1)S(1)}, bf16[256,640]{1,0:T(8,128)(2,1)S(1)}, u32[]{:S(2)}, u32[]{:S(2)}) %collective-permute-start.4) | collective-permute-done | bytes 327712 | tf_op jit(solution)/shard_map/ppermute | solution.py:379
  37.4 0.0 copy-done.2
  37.4 0.0 copy-done
  37.4 0.0 copy-start.3
  37.4 0.1 pad_maximum_fusion
  37.4 1.6 %collective-permute-start.5 = (bf16[512,640]{1,0:T(8,128)(2,1)S(1)}, bf16[512,640]{1,0:T(8,128)(2,1)S(1)}, u32[]{:S(2)}, u32[]{:S(2)}) collective-permute-start(bf16[512,640]{1,0:T(8,128)(2,1)S(1)} %pad_maximum_fusion), channel_id=1, source_target_pairs={{0,1},{1,0},{2,3},{3,2},{4,5},{5,4},{6,7},{7,6},{8,9},{9,8},{10,11... | collective-permute-start | bytes 1966088 | tf_op jit(solution)/shard_map/ppermute | solution.py:379
  39.0 3.3 %prepare.1 = (bf16[4,256,1024]{2,1,0:T(8,128)(2,1)}, f32[128,512]{1,0:T(8,128)}) custom-call(s32[32,256]{1,0:T(8,128)} %index_ref.3, s32[1,32]{1,0:T(1,128)} %bitcast.15, f32[32,4,256]{2,1,0:T(4,128)} %init_ref.3), custom_call_target="tpu_custom_call" | custom-call | tf_op jit(solution)/shard_map/prepare/pallas_call | solution.py:243
  42.3 0.3 all-to-all-done
  42.6 0.0 copy-start.1
  42.6 0.8 %copy-done.1 = bf16[32,16,512]{2,1,0:T(8,128)(2,1)} copy-done((bf16[32,16,512]{2,1,0:T(8,128)(2,1)}, bf16[32,16,512]{2,1,0:T(8,128)(2,1)S(1)}, u32[]{:S(2)}) %copy-start.1) | copy-done | bytes 524312
  43.4 6.8 %item_tower.1 = (bf16[512,512]{1,0:T(8,128)(2,1)}, bf16[512,512]{1,0:T(8,128)(2,1)}) custom-call(bf16[512,512]{1,0:T(8,128)(2,1)} %bitcast.11, bf16[512,2048]{1,0:T(8,128)(2,1)} %w_in_ref.3, f32[1,2048]{1,0:T(1,128)} %bitcast.14, bf16[2048,512]{1,0:T(8,128)(2,1)} %w_out_ref.3, bf16[512,512]{1,0:T(8,128)(2,1)} %bilinear_ref.1), custom_call_target="tpu_custom_call" | custom-call | tf_op jit(solution)/shard_map/item_tower/pallas_call | solution.py:151
  50.2 0.0 copy-done.3
  50.2 6.3 %route.1 = (f32[32,2048]{1,0:T(8,128)}, bf16[32,640]{1,0:T(8,128)(2,1)}, f32[1,32]{1,0:T(1,128)}) custom-call(bf16[512,512]{1,0:T(8,128)(2,1)} %get-tuple-element.13.unit_ref, bf16[512,512]{1,0:T(8,128)(2,1)} %get-tuple-element.14.mapped_ref, bf16[4,256,1024]{2,1,0:T(8,128)(2,1)} %get-tuple-element.15.onehot_ref, f32[128,512]{1,0:T(8,128)} %get-tuple-element.16.first_ref, ...), custom_call_target="tpu_custom_call" | custom-call | tf_op jit(solution)/shard_map/route/pallas_call | solution.py:328
  56.5 0.1 collective-permute-start
  56.6 1.5 %collective-permute-start.1 = (bf16[32,640]{1,0:T(8,128)(2,1)}, bf16[32,640]{1,0:T(8,128)(2,1)S(1)}, u32[]{:S(2)}, u32[]{:S(2)}) collective-permute-start(bf16[32,640]{1,0:T(8,128)(2,1)} %get-tuple-element.19.refs_0_), channel_id=1, source_target_pairs={{0,16},{8,24},{16,0},{24,8},{1,17},{9,25},{17,1},{25,9},{2,18},{10... | collective-permute-start | bytes 122888 | tf_op jit(solution)/shard_map/ppermute | solution.py:383
  58.1 1.0 %collective-permute-start.2 = (bf16[32,640]{1,0:T(8,128)(2,1)}, bf16[32,640]{1,0:T(8,128)(2,1)S(1)}, u32[]{:S(2)}, u32[]{:S(2)}) collective-permute-start(bf16[32,640]{1,0:T(8,128)(2,1)} %get-tuple-element.19.refs_0_), channel_id=1, source_target_pairs={{0,24},{8,0},{16,8},{24,16},{1,25},{9,1},{17,9},{25,17},{2,26},{10... | collective-permute-start | bytes 122888 | tf_op jit(solution)/shard_map/ppermute | solution.py:383
  59.2 1.0 %collective-permute-done.refs_1_ = bf16[32,640]{1,0:T(8,128)(2,1)S(1)} collective-permute-done((bf16[32,640]{1,0:T(8,128)(2,1)}, bf16[32,640]{1,0:T(8,128)(2,1)S(1)}, u32[]{:S(2)}, u32[]{:S(2)}) %collective-permute-start) | collective-permute-done | bytes 40992 | tf_op jit(solution)/shard_map/ppermute | solution.py:383
  60.2 0.0 copy-start.5
  60.2 0.9 %collective-permute-done.1.refs_2_ = bf16[32,640]{1,0:T(8,128)(2,1)S(1)} collective-permute-done((bf16[32,640]{1,0:T(8,128)(2,1)}, bf16[32,640]{1,0:T(8,128)(2,1)S(1)}, u32[]{:S(2)}, u32[]{:S(2)}) %collective-permute-start.1) | collective-permute-done | bytes 40992 | tf_op jit(solution)/shard_map/ppermute | solution.py:383
  61.1 0.0 copy-start.6
  61.1 0.1 collective-permute-done.2.refs_3_
  61.1 0.0 copy-start.7
  61.1 0.0 collective-permute-done.5.refs_7_
  61.1 0.0 copy-done.5
  61.2 0.5 copy-done.6
  61.7 0.1 copy-done.7
  61.8 0.9 %copy-done.4 = bf16[512,640]{1,0:T(8,128)(2,1)} copy-done((bf16[512,640]{1,0:T(8,128)(2,1)}, bf16[512,640]{1,0:T(8,128)(2,1)S(1)}, u32[]{:S(2)}) %copy-start.4) | copy-done | bytes 655384
  62.6 2.7 %negative_sums.1 = (f32[1,32]{1,0:T(1,128)}, f32[1,32]{1,0:T(1,128)}, f32[1,32]{1,0:T(1,128)}, f32[1,32]{1,0:T(1,128)}) custom-call(bf16[32,640]{1,0:T(8,128)(2,1)} %get-tuple-element.19.refs_0_, bf16[32,640]{1,0:T(8,128)(2,1)} %copy-done.5, bf16[32,640]{1,0:T(8,128)(2,1)} %copy-done.6, bf16[32,640]{1,0:T(8,128)(2,1)} %copy-done.7, ...), custom_call_target="tpu_custom_call" | custom-call | tf_op jit(solution)/shard_map/negative_sums/pallas_call | solution.py:371
  65.4 0.9 %collective-permute-start.8 = (f32[1,32]{1,0:T(1,128)}, f32[1,32]{1,0:T(1,128)S(1)}, u32[]{:S(2)}, u32[]{:S(2)}) collective-permute-start(f32[1,32]{1,0:T(1,128)} %get-tuple-element.23), channel_id=1, source_target_pairs={{0,8},{8,16},{16,24},{24,0},{1,9},{9,17},{17,25},{25,1},{2,10},{10... | collective-permute-start | bytes 392 | tf_op jit(solution)/shard_map/ppermute | solution.py:383
  66.2 1.2 %collective-permute-start.7 = (f32[1,32]{1,0:T(1,128)}, f32[1,32]{1,0:T(1,128)S(1)}, u32[]{:S(2)}, u32[]{:S(2)}) collective-permute-start(f32[1,32]{1,0:T(1,128)} %get-tuple-element.22), channel_id=1, source_target_pairs={{0,16},{8,24},{16,0},{24,8},{1,17},{9,25},{17,1},{25,9},{2,18},{10... | collective-permute-start | bytes 392 | tf_op jit(solution)/shard_map/ppermute | solution.py:383
  67.4 0.6 collective-permute-start.6
  68.0 0.5 collective-permute-done.8
  68.6 1.4 %collective-permute-done.7 = f32[1,32]{1,0:T(1,128)S(1)} collective-permute-done((f32[1,32]{1,0:T(1,128)}, f32[1,32]{1,0:T(1,128)S(1)}, u32[]{:S(2)}, u32[]{:S(2)}) %collective-permute-start.7) | collective-permute-done | bytes 160 | tf_op jit(solution)/shard_map/ppermute | solution.py:383
  70.0 0.0 collective-permute-done.6
  70.0 0.0 copy-done.9
  70.0 1.2 %subtract_bitcast_fusion = f32[32]{0:T(128)} fusion(f32[1,32]{1,0:T(1,128)S(1)} %copy-done.9, f32[1,32]{1,0:T(1,128)S(1)} %collective-permute-done.8, f32[1,32]{1,0:T(1,128)S(1)} %collective-permute-done.7, f32[1,32]{1,0:T(1,128)S(1)} %collective-permute-done.6, f32[1,32]{1,0:T(1,128)} %get-tuple-element.20), kind=kLoop, calls=%fused_computation.2 | loop fusion | flops 160 | bytes 768 | tf_op jit(solution)/shard_map/reshape | solution.py:447
  (2 shorter events, 0.0 us)
Async XLA Ops:
  0.6 16.0 %copy-start.8 = (s32[32,1,16]{0,2,1:T(8,128)S(1)}, s32[32,1,16]{0,2,1:T(8,128)}, u32[]{:S(2)}) copy-start(s32[32,1,16]{0,2,1:T(8,128)} %param.20) | copy-start | bytes 6148
  5.4 32.0 %copy-start = (bf16[128,640]{1,0:T(8,128)(2,1)S(1)}, bf16[128,640]{1,0:T(8,128)(2,1)}, u32[]{:S(2)}) copy-start(bf16[128,640]{1,0:T(8,128)(2,1)} %neg_tower.1.refs_4_) | copy-start | bytes 491524
  5.4 7.5 %collective-permute-start.3 = (bf16[128,640]{1,0:T(8,128)(2,1)}, bf16[128,640]{1,0:T(8,128)(2,1)S(1)}, u32[]{:S(2)}, u32[]{:S(2)}) collective-permute-start(bf16[128,640]{1,0:T(8,128)(2,1)} %neg_tower.1.refs_4_), channel_id=1, source_target_pairs={{0,2},{1,3},{2,0},{3,1},{4,6},{5,7},{6,4},{7,5},{8,10},{9,11},{10,... | collective-permute-start | bytes 491528 | tf_op jit(solution)/shard_map/ppermute | solution.py:379
  12.9 24.4 %copy-start.2 = (bf16[128,640]{1,0:T(8,128)(2,1)}, bf16[128,640]{1,0:T(8,128)(2,1)S(1)}, u32[]{:S(2)}) copy-start(bf16[128,640]{1,0:T(8,128)(2,1)S(1)} %collective-permute-done.3.refs_5_) | copy-start | bytes 491524
  13.9 23.4 %collective-permute-start.4 = (bf16[256,640]{1,0:T(8,128)(2,1)S(1)}, bf16[256,640]{1,0:T(8,128)(2,1)S(1)}, u32[]{:S(2)}, u32[]{:S(2)}) collective-permute-start(bf16[256,640]{1,0:T(8,128)(2,1)S(1)} %pad_maximum_fusion.1), channel_id=1, source_target_pairs={{0,4},{1,5},{2,6},{3,7},{4,0},{5,1},{6,2},{7,3},{8,12},{9,13},{10,... | collective-permute-start | bytes 983048 | tf_op jit(solution)/shard_map/ppermute | solution.py:379
  19.9 22.7 %all-to-all-start = ((bf16[32,16,512]{2,1,0:T(8,128)(2,1)}), bf16[32,16,512]{2,1,0:T(8,128)(2,1)S(1)}, u32[]{:S(2)}, u32[]{:S(2)}) async-start(bf16[32,16,512]{2,1,0:T(8,128)(2,1)} %bitcast.12), calls=%async_computation | async-start | bytes 1048576 | tf_op jit(solution)/shard_map/all_to_all | solution.py:407
  37.4 12.9 %copy-start.3 = (bf16[256,640]{1,0:T(8,128)(2,1)}, bf16[256,640]{1,0:T(8,128)(2,1)S(1)}, u32[]{:S(2)}) copy-start(bf16[256,640]{1,0:T(8,128)(2,1)S(1)} %collective-permute-done.4.refs_6_) | copy-start | bytes 983044
  37.4 23.7 %collective-permute-start.5 = (bf16[512,640]{1,0:T(8,128)(2,1)S(1)}, bf16[512,640]{1,0:T(8,128)(2,1)S(1)}, u32[]{:S(2)}, u32[]{:S(2)}) collective-permute-start(bf16[512,640]{1,0:T(8,128)(2,1)S(1)} %pad_maximum_fusion), channel_id=1, source_target_pairs={{0,1},{1,0},{2,3},{3,2},{4,5},{5,4},{6,7},{7,6},{8,9},{9,8},{10,11... | collective-permute-start | bytes 1966088 | tf_op jit(solution)/shard_map/ppermute | solution.py:379
  42.6 0.8 %copy-start.1 = (bf16[32,16,512]{2,1,0:T(8,128)(2,1)}, bf16[32,16,512]{2,1,0:T(8,128)(2,1)S(1)}, u32[]{:S(2)}) copy-start(bf16[32,16,512]{2,1,0:T(8,128)(2,1)S(1)} %all-to-all-done) | copy-start | bytes 1572868
  56.5 13.5 %copy-start.9 = (f32[1,32]{1,0:T(1,128)S(1)}, f32[1,32]{1,0:T(1,128)}, u32[]{:S(2)}) copy-start(f32[1,32]{1,0:T(1,128)} %get-tuple-element.18) | copy-start | bytes 388
  56.5 3.6 %collective-permute-start = (bf16[32,640]{1,0:T(8,128)(2,1)}, bf16[32,640]{1,0:T(8,128)(2,1)S(1)}, u32[]{:S(2)}, u32[]{:S(2)}) collective-permute-start(bf16[32,640]{1,0:T(8,128)(2,1)} %get-tuple-element.19.refs_0_), channel_id=1, source_target_pairs={{0,8},{8,16},{16,24},{24,0},{1,9},{9,17},{17,25},{25,1},{2,10},{10... | collective-permute-start | bytes 122888 | tf_op jit(solution)/shard_map/ppermute | solution.py:383
  56.6 4.4 %collective-permute-start.1 = (bf16[32,640]{1,0:T(8,128)(2,1)}, bf16[32,640]{1,0:T(8,128)(2,1)S(1)}, u32[]{:S(2)}, u32[]{:S(2)}) collective-permute-start(bf16[32,640]{1,0:T(8,128)(2,1)} %get-tuple-element.19.refs_0_), channel_id=1, source_target_pairs={{0,16},{8,24},{16,0},{24,8},{1,17},{9,25},{17,1},{25,9},{2,18},{10... | collective-permute-start | bytes 122888 | tf_op jit(solution)/shard_map/ppermute | solution.py:383
  58.1 3.0 %collective-permute-start.2 = (bf16[32,640]{1,0:T(8,128)(2,1)}, bf16[32,640]{1,0:T(8,128)(2,1)S(1)}, u32[]{:S(2)}, u32[]{:S(2)}) collective-permute-start(bf16[32,640]{1,0:T(8,128)(2,1)} %get-tuple-element.19.refs_0_), channel_id=1, source_target_pairs={{0,24},{8,0},{16,8},{24,16},{1,25},{9,1},{17,9},{25,17},{2,26},{10... | collective-permute-start | bytes 122888 | tf_op jit(solution)/shard_map/ppermute | solution.py:383
  60.2 1.0 %copy-start.5 = (bf16[32,640]{1,0:T(8,128)(2,1)}, bf16[32,640]{1,0:T(8,128)(2,1)S(1)}, u32[]{:S(2)}) copy-start(bf16[32,640]{1,0:T(8,128)(2,1)S(1)} %collective-permute-done.refs_1_) | copy-start | bytes 122884
  61.1 0.6 copy-start.6
  61.1 0.6 copy-start.7
  61.8 0.9 %copy-start.4 = (bf16[512,640]{1,0:T(8,128)(2,1)}, bf16[512,640]{1,0:T(8,128)(2,1)S(1)}, u32[]{:S(2)}) copy-start(bf16[512,640]{1,0:T(8,128)(2,1)S(1)} %collective-permute-done.5.refs_7_) | copy-start | bytes 1966084
  65.4 3.2 %collective-permute-start.8 = (f32[1,32]{1,0:T(1,128)}, f32[1,32]{1,0:T(1,128)S(1)}, u32[]{:S(2)}, u32[]{:S(2)}) collective-permute-start(f32[1,32]{1,0:T(1,128)} %get-tuple-element.23), channel_id=1, source_target_pairs={{0,8},{8,16},{16,24},{24,0},{1,9},{9,17},{17,25},{25,1},{2,10},{10... | collective-permute-start | bytes 392 | tf_op jit(solution)/shard_map/ppermute | solution.py:383
  66.2 3.8 %collective-permute-start.7 = (f32[1,32]{1,0:T(1,128)}, f32[1,32]{1,0:T(1,128)S(1)}, u32[]{:S(2)}, u32[]{:S(2)}) collective-permute-start(f32[1,32]{1,0:T(1,128)} %get-tuple-element.22), channel_id=1, source_target_pairs={{0,16},{8,24},{16,0},{24,8},{1,17},{9,25},{17,1},{25,9},{2,18},{10... | collective-permute-start | bytes 392 | tf_op jit(solution)/shard_map/ppermute | solution.py:383
  67.4 2.6 %collective-permute-start.6 = (f32[1,32]{1,0:T(1,128)}, f32[1,32]{1,0:T(1,128)S(1)}, u32[]{:S(2)}, u32[]{:S(2)}) collective-permute-start(f32[1,32]{1,0:T(1,128)} %get-tuple-element.21), channel_id=1, source_target_pairs={{0,24},{8,0},{16,8},{24,16},{1,25},{9,1},{17,9},{25,17},{2,26},{10... | collective-permute-start | bytes 392 | tf_op jit(solution)/shard_map/ppermute | solution.py:383

commit v2 on v1

--- a/solution.py
+++ b/solution.py
@@ -7,10 +7,12 @@
 from jax.experimental.pallas import tpu as pltpu
 from jax.sharding import PartitionSpec as P
 
+
 INTERESTS = 4
 ITERS = 3
 LANES = 128
 SUB = 8
+EXTRA = 16
 GROUP_USERS = 8
 
 norm_epsilon = 1e-06
@@ -47,9 +49,9 @@
 
 
 def id_digits(ids_row):
-    low = to_column((ids_row & 255).astype(f32))
-    mid = to_column(((ids_row >> 8) & 255).astype(f32))
-    high = to_column((ids_row >> 16).astype(f32))
+    low = (ids_row & 255).astype(f32)
+    mid = ((ids_row >> 8) & 255).astype(f32)
+    high = (ids_row >> 16).astype(f32)
     return low, mid, high
 
 
@@ -62,14 +64,14 @@
 
 
 def select_kernel(fetch_ref, rows_ref, out_ref):
-    blocks, _, cap = fetch_ref.shape
+    _, cap, blocks = fetch_ref.shape
     count = blocks * cap
-    fetch = fetch_ref[:, 0, :]
+    fetch = fetch_ref[0]
     row = iota((count, blocks), 0)
     block = iota((count, blocks), 1)
     pick = jnp.where((row >= block * cap) & (row < block * cap + cap), 1.0, 0.0).astype(bf16)
-    high = mm(pick, (fetch >> 7).astype(f32).astype(bf16))
-    low = mm(pick, (fetch & 127).astype(f32).astype(bf16))
+    high = mm_nt(pick, (fetch >> 7).astype(f32).astype(bf16))
+    low = mm_nt(pick, (fetch & 127).astype(f32).astype(bf16))
     place = iota((count, cap), 1) == lax.rem(iota((count, cap), 0), jnp.int32(cap))
     column = jnp.sum(jnp.where(place, high * 128.0 + low, 0.0), axis=1, keepdims=True)
     item = iota((count, rows_ref.shape[0]), 1).astype(f32)
@@ -81,9 +83,9 @@
     blocks, _, cap = fetch.shape
     return pl.pallas_call(
         select_kernel,
-        out_shape=jax.ShapeDtypeStruct((blocks * cap, rows.shape[1]), bf16),
+        out_shape=pltpu.VMEM((blocks * cap, rows.shape[1]), bf16),
         name="select_rows",
-    )(fetch, rows)
+    )(fetch.transpose(1, 2, 0), rows)
 
 
 def tower_step(rows_ref, w_in_ref, bias_ref, w_out_ref, acc_ref):
@@ -100,10 +102,10 @@
         acc_ref[...] += part
 
 
-def unit_of(acc_ref):
+def unit_of(acc_ref, kind):
     embedding = acc_ref[...]
     total = jnp.sum(embedding * embedding, axis=1, keepdims=True)
-    return (embedding * lax.rsqrt(total + norm_epsilon)).astype(bf16)
+    return (embedding * lax.rsqrt(total + norm_epsilon)).astype(kind)
 
 
 def item_kernel(rows_ref, w_in_ref, bias_ref, w_out_ref, bilinear_ref, unit_ref, mapped_ref, acc_ref):
@@ -111,7 +113,7 @@
 
     @pl.when(pl.program_id(0) == pl.num_programs(0) - 1)
     def _():
-        unit = unit_of(acc_ref)
+        unit = unit_of(acc_ref, bf16)
         unit_ref[...] = unit
         mapped_ref[...] = mm(unit, bilinear_ref[...]).astype(bf16)
 
@@ -121,10 +123,14 @@
 
     @pl.when(pl.program_id(0) == pl.num_programs(0) - 1)
     def _():
-        width = acc_ref.shape[1]
-        out_ref[:, :width] = unit_of(acc_ref)
-        columns = id_digits(ids_ref[...]) + (to_column(counts_ref[...].astype(f32)),)
-        out_ref[:, width:] = lane_columns(columns, acc_ref.shape[0]).astype(bf16)
+        count, width = acc_ref.shape
+        out_ref[:width, :] = unit_of(acc_ref, f32).T.astype(bf16)
+        rows = id_digits(ids_ref[...]) + (counts_ref[...].astype(f32),)
+        at = iota((EXTRA, count), 0)
+        extra = jnp.zeros((EXTRA, count), f32)
+        for place, row in enumerate(rows):
+            extra = jnp.where(at == place, row, extra)
+        out_ref[width:, :] = extra.astype(bf16)
 
 
 def chunk_of(hidden_units):
@@ -169,8 +175,8 @@
         neg_kernel,
         grid=(w_in.shape[1] // chunk,),
         in_specs=specs + [whole(ids.shape), whole(counts.shape)],
-        out_specs=whole((shape[0], shape[1] + LANES)),
-        out_shape=jax.ShapeDtypeStruct((shape[0], shape[1] + LANES), bf16),
+        out_specs=whole((shape[1] + EXTRA, shape[0])),
+        out_shape=jax.ShapeDtypeStruct((shape[1] + EXTRA, shape[0]), bf16),
         scratch_shapes=[pltpu.VMEM(shape, f32)],
         name="neg_tower",
     )(rows, w_in, bias, w_out, ids, counts)
@@ -317,7 +323,7 @@
     user_vec = functools.reduce(jnp.add, [(r / total) * one for r, one in zip(raised, each)])
     user_vec = user_vec.astype(bf16)
     vec_ref[:, :width] = user_vec
-    vec_ref[:, width:] = lane_columns(id_digits(ids_ref[...]), users).astype(bf16)
+    vec_ref[:, width:] = lane_columns([to_column(one) for one in id_digits(ids_ref[...])], users).astype(bf16)
     match = jnp.sum(user_vec.astype(f32) * label_rows, axis=1, keepdims=True)
     positive_ref[...] = logit_scale * to_row(match) - jnp.log(counts_ref[...].astype(f32))
 
@@ -344,24 +350,17 @@
     vec = jnp.concatenate([ref[...] for ref in vec_refs], axis=0)
     users = vec_refs[0].shape[0]
     width = vec.shape[1] - LANES
-    place = iota((SUB, LANES), 1)
-    scale = jnp.where(
-        place == 0, 1.0, jnp.where(place == 1, 256.0, jnp.where(place == 2, 65536.0, 0.0))
-    ).astype(bf16)
-    label_ids = mm_nt(scale, vec[:, width:])[:1]
-    row = iota((LANES, LANES), 0)
-    to_id = jnp.where(
-        row == 0, 1.0, jnp.where(row == 1, 256.0, jnp.where(row == 2, 65536.0, 0.0))
-    ).astype(bf16)
-    to_count = jnp.where(row == 3, 1.0, 0.0).astype(bf16)
-    total = jnp.zeros((1, vec.shape[0]), f32)
+    digits = vec[:, width:].astype(f32)
+    label_ids = digits[:, 0:1] + 256.0 * digits[:, 1:2] + 65536.0 * digits[:, 2:3]
+    vec = vec[:, :width]
+    total = None
     for ref in neg_refs:
-        extra = ref[:, width:]
-        ids = mm(extra, to_id)[:, :1]
-        counts = mm(extra, to_count)[:, :1]
-        dots = mm_nt(ref[:, :width], vec[:, :width])
-        terms = jnp.exp(logit_scale * dots) * (1.0 / counts)
-        total += jnp.sum(jnp.where(ids != label_ids, terms, 0.0), axis=0, keepdims=True)
+        extra = ref[width:, :].astype(f32)
+        ids = extra[0:1] + 256.0 * extra[1:2] + 65536.0 * extra[2:3]
+        terms = jnp.exp(logit_scale * mm(vec, ref[:width, :])) * (1.0 / extra[3:4])
+        terms = jnp.where(ids != label_ids, terms, 0.0)
+        total = terms if total is None else total + terms
+    total = to_row(jnp.sum(total, axis=1, keepdims=True))
     for part, ref in enumerate(out_refs):
         ref[...] = total[:, part * users : (part + 1) * users]
 
@@ -375,8 +374,14 @@
     )(*vecs, *negs)
 
 
-def swap(array, axis, size, bit):
-    return lax.ppermute(array, axis, [(at, at ^ bit) for at in range(size)])
+def gather_pool(own, size):
+    pieces = {0: own}
+    for mask in range(1, size):
+        bit = 1 << (mask.bit_length() - 1) if mask < 4 else mask & -mask
+        pieces[mask] = lax.ppermute(
+            pieces[mask ^ bit], "pool", [(at, at ^ bit) for at in range(size)]
+        )
+    return list(pieces.values())
 
 
 def rotate(array, axis, size, step):
@@ -418,12 +423,7 @@
     )
     length = hist_len.reshape(1, -1)
     onehot, first = prepare(hist_index, length, route_init, outgoing.shape[0])
-
-    bits = [1 << at for at in range(pool_size.bit_length() - 1)]
-    negs = [own_neg]
-    for bit in bits[1:] + bits[:1]:
-        held = negs[0] if len(negs) == 1 else jnp.concatenate(negs, axis=0)
-        negs.append(swap(held, "pool", pool_size, bit))
+    negs = gather_pool(own_neg, pool_size)
 
     unit, mapped = item_tower(arrived, w_in, bias, w_out, bilinear)
     interests, vec, positive = route(
@@ -438,7 +438,9 @@
         label_ids.reshape(1, -1),
         label_counts.reshape(1, -1),
     )
-    vecs = [vec] + [rotate(vec, "user", user_size, step) for step in range(1, user_size)]
+    vecs = [vec]
+    for step in range(1, user_size):
+        vecs.append(rotate(vec, "user", user_size, step))
     sums = negative_sums(vecs, negs)
     partition = jnp.exp(positive) + sums[0]
     for step in range(1, user_size):
@@ -467,7 +469,8 @@
         P(both),
     )
     out_specs = (P(both, None), P(both))
-    body = functools.partial(on_device, mesh.shape["user"], mesh.shape["pool"])
-    return jax.shard_map(
-        body, mesh=mesh, in_specs=in_specs, out_specs=out_specs, check_vma=False
-    )
+
+    def body(*args):
+        return on_device(mesh.shape["user"], mesh.shape["pool"], *args)
+
+    return jax.shard_map(body, mesh=mesh, in_specs=in_specs, out_specs=out_specs, check_vma=False)

time: 71.6 us -> 70.5 us (0.985)
  starting transfers between devices: 16.5 us -> 22.5 us
  waiting for transfers between devices: 22.4 us -> 18.2 us
  local copies, waits for them, and re-layouts: 2.97 us -> 1.44 us
  other arithmetic: 2.26 us -> 1.21 us
    all_to_all x1, starting transfers between devices: 3.83 us -> 7.32 us  [on_device(): lax.all_to_all(outgoing.reshape(fetch_table.shape[0], fetch_table.shape[2...]
    ppermute x3 -> x7, waiting for transfers between devices: 18.1 us -> 14.8 us  [gather_pool(): lax.ppermute(pieces[mask ^ bit], 'pool', [(at, at ^ bit) for at in range(...]
    ppermute x3 -> x7, starting transfers between devices: 7.36 us -> 9.17 us  [gather_pool(): lax.ppermute(pieces[mask ^ bit], 'pool', [(at, at ^ bit) for at in range(...]
    unnamed x21 -> x22, local copies, waits for them, and re-layouts: 2.97 us -> 1.44 us
    concatenate x2 -> x0, other arithmetic: 1.06 us -> none  [on_device(): held = negs[0] if len(negs) == 1 else jnp.concatenate(negs, axis=0)]
  transfers between devices with their start and end apart: 10 -> 14, of which waited for: 8 -> 7; matrix products, arithmetic and copies ran while one was open for 1% -> 0% of each run, Pallas kernels for 27% -> 30%
where the time goes in v2:
time: 70.5 us; the launch traced here: 70.1 us
  Pallas kernels  26.1 us (37%)
  starting transfers between devices  22.5 us (32%)
  waiting for transfers between devices  18.2 us (26%)
  local copies, waits for them, and re-layouts  1.44 us (2%)
  other arithmetic  1.21 us (2%)
  between operations  0.73 us (1%)
    ppermute x7, waiting for transfers between devices, gather_pool(): lax.ppermute(pieces[mask ^ bit], 'pool', [(at, at ^ bit) for at in range(...  14.8 us
    ppermute x7, starting transfers between devices, gather_pool(): lax.ppermute(pieces[mask ^ bit], 'pool', [(at, at ^ bit) for at in range(...  9.17 us
    all_to_all x1, starting transfers between devices, on_device(): lax.all_to_all(outgoing.reshape(fetch_table.shape[0], fetch_table.shape[2...  7.32 us
    pallas_call x1, Pallas kernels, item_tower(): pl.pallas_call(item_kernel, grid=(w_in.shape[1] // chunk,), in_specs=spec...  6.77 us
    pallas_call x1, Pallas kernels, route(): pl.pallas_call(route_kernel, out_shape=[jax.ShapeDtypeStruct((users, INTE...  6.29 us
    ppermute x6, starting transfers between devices, rotate(): lax.ppermute(array, axis, [(at, (at + step) % size) for at in range(size)])  6.01 us
    pallas_call x1, Pallas kernels, neg_tower(): pl.pallas_call(neg_kernel, grid=(w_in.shape[1] // chunk,), in_specs=specs...  4.76 us
    ppermute x6, waiting for transfers between devices, rotate(): lax.ppermute(array, axis, [(at, (at + step) % size) for at in range(size)])  3.39 us
  transfers between devices with their start and end apart: 14, of which 7 were waited for; matrix products, arithmetic and copies ran while one was open for 0% of the time, Pallas kernels for 30%

profile of v2, /device:TPU:0, one launch (start us, length us, event | category | flops | bytes accessed | tf_op | source)
XLA Modules:
  0.0 70.1 jit_solution(8012106266033455741)
XLA Ops:
  0.6 2.5 %select_rows.1 = bf16[512,512]{1,0:T(8,128)(2,1)} custom-call(s32[1,16,32]{2,1,0:T(8,128)} %bitcast.15, bf16[512,512]{1,0:T(8,128)(2,1)} %rows_ref.2), custom_call_target="tpu_custom_call" | custom-call | tf_op jit(solution)/shard_map/select_rows/pallas_call | solution.py:84
  3.1 7.3 %all-to-all-start = ((bf16[32,16,512]{2,1,0:T(8,128)(2,1)}), bf16[32,16,512]{2,1,0:T(8,128)(2,1)S(1)}, u32[]{:S(2)}, u32[]{:S(2)}) async-start(bf16[32,16,512]{2,1,0:T(8,128)(2,1)} %bitcast.1), calls=%async_computation | async-start | bytes 1048576 | tf_op jit(solution)/shard_map/all_to_all | solution.py:412
  10.5 4.8 %neg_tower.1.refs_4_ = bf16[528,128]{1,0:T(8,128)(2,1)} custom-call(bf16[128,512]{1,0:T(8,128)(2,1)} %rows_ref.3, bf16[512,2048]{1,0:T(8,128)(2,1)} %w_in_ref.3, f32[1,2048]{1,0:T(1,128)} %bitcast.13, bf16[2048,512]{1,0:T(8,128)(2,1)} %w_out_ref.3, s32[1,128]{1,0:T(1,128)} %bitcast.18, s32[1,128]{1,0:T(1,128)} %bitcast.19), custom_call_target="tpu_custom_call" | custom-call | tf_op jit(solution)/shard_map/neg_tower/pallas_call | solution.py:174
  15.2 2.7 %collective-permute-start.6 = (bf16[528,128]{1,0:T(8,128)(2,1)}, bf16[528,128]{1,0:T(8,128)(2,1)S(1)}, u32[]{:S(2)}, u32[]{:S(2)}) collective-permute-start(bf16[528,128]{1,0:T(8,128)(2,1)} %neg_tower.1.refs_4_), channel_id=1, source_target_pairs={{0,4},{1,5},{2,6},{3,7},{4,0},{5,1},{6,2},{7,3},{8,12},{9,13},{10,... | collective-permute-start | bytes 405512 | tf_op jit(solution)/shard_map/ppermute | solution.py:381
  17.9 1.5 %collective-permute-start.3 = (bf16[528,128]{1,0:T(8,128)(2,1)}, bf16[528,128]{1,0:T(8,128)(2,1)S(1)}, u32[]{:S(2)}, u32[]{:S(2)}) collective-permute-start(bf16[528,128]{1,0:T(8,128)(2,1)} %neg_tower.1.refs_4_), channel_id=1, source_target_pairs={{0,1},{1,0},{2,3},{3,2},{4,5},{5,4},{6,7},{7,6},{8,9},{9,8},{10,11... | collective-permute-start | bytes 405512 | tf_op jit(solution)/shard_map/ppermute | solution.py:381
  19.4 11.9 %collective-permute-done.6.refs_8_ = bf16[528,128]{1,0:T(8,128)(2,1)S(1)} collective-permute-done((bf16[528,128]{1,0:T(8,128)(2,1)}, bf16[528,128]{1,0:T(8,128)(2,1)S(1)}, u32[]{:S(2)}, u32[]{:S(2)}) %collective-permute-start.6) | collective-permute-done | bytes 135200 | tf_op jit(solution)/shard_map/ppermute | solution.py:381
  31.2 0.0 collective-permute-start.8
  31.2 2.0 %collective-permute-start.4 = (bf16[528,128]{1,0:T(8,128)(2,1)}, bf16[528,128]{1,0:T(8,128)(2,1)S(1)}, u32[]{:S(2)}, u32[]{:S(2)}) collective-permute-start(bf16[528,128]{1,0:T(8,128)(2,1)} %neg_tower.1.refs_4_), channel_id=1, source_target_pairs={{0,2},{1,3},{2,0},{3,1},{4,6},{5,7},{6,4},{7,5},{8,10},{9,11},{10,... | collective-permute-start | bytes 405512 | tf_op jit(solution)/shard_map/ppermute | solution.py:381
  33.3 0.0 collective-permute-done.3.refs_5_
  33.3 0.1 collective-permute-start.5
  33.3 1.5 %collective-permute-start.7 = (bf16[528,128]{1,0:T(8,128)(2,1)S(1)}, bf16[528,128]{1,0:T(8,128)(2,1)S(1)}, u32[]{:S(2)}, u32[]{:S(2)}) collective-permute-start(bf16[528,128]{1,0:T(8,128)(2,1)S(1)} %collective-permute-done.6.refs_8_), channel_id=1, source_target_pairs={{0,1},{1,0},{2,3},{3,2},{4,5},{5,4},{6,7},{7,6},{8,9},{9,8},{10,11... | collective-permute-start | bytes 405512 | tf_op jit(solution)/shard_map/ppermute | solution.py:381
  34.8 2.9 %collective-permute-done.8.refs_10_ = bf16[528,128]{1,0:T(8,128)(2,1)S(1)} collective-permute-done((bf16[528,128]{1,0:T(8,128)(2,1)S(1)}, bf16[528,128]{1,0:T(8,128)(2,1)S(1)}, u32[]{:S(2)}, u32[]{:S(2)}) %collective-permute-start.8) | collective-permute-done | bytes 135200 | tf_op jit(solution)/shard_map/ppermute | solution.py:381
  37.7 1.5 %collective-permute-start.9 = (bf16[528,128]{1,0:T(8,128)(2,1)S(1)}, bf16[528,128]{1,0:T(8,128)(2,1)S(1)}, u32[]{:S(2)}, u32[]{:S(2)}) collective-permute-start(bf16[528,128]{1,0:T(8,128)(2,1)S(1)} %collective-permute-done.8.refs_10_), channel_id=1, source_target_pairs={{0,1},{1,0},{2,3},{3,2},{4,5},{5,4},{6,7},{7,6},{8,9},{9,8},{10,11... | collective-permute-start | bytes 405512 | tf_op jit(solution)/shard_map/ppermute | solution.py:381
  39.2 3.3 %prepare.1 = (bf16[4,256,1024]{2,1,0:T(8,128)(2,1)}, f32[128,512]{1,0:T(8,128)}) custom-call(s32[32,256]{1,0:T(8,128)} %index_ref.3, s32[1,32]{1,0:T(1,128)} %bitcast.16, f32[32,4,256]{2,1,0:T(4,128)} %init_ref.3), custom_call_target="tpu_custom_call" | custom-call | tf_op jit(solution)/shard_map/prepare/pallas_call | solution.py:249
  42.4 0.0 all-to-all-done
  42.4 0.8 %copy-done = bf16[32,16,512]{2,1,0:T(8,128)(2,1)} copy-done((bf16[32,16,512]{2,1,0:T(8,128)(2,1)}, bf16[32,16,512]{2,1,0:T(8,128)(2,1)S(1)}, u32[]{:S(2)}) %copy-start) | copy-done | bytes 524312
  43.3 6.8 %item_tower.1 = (bf16[512,512]{1,0:T(8,128)(2,1)}, bf16[512,512]{1,0:T(8,128)(2,1)}) custom-call(bf16[512,512]{1,0:T(8,128)(2,1)} %bitcast.12, bf16[512,2048]{1,0:T(8,128)(2,1)} %w_in_ref.3, f32[1,2048]{1,0:T(1,128)} %bitcast.14, bf16[2048,512]{1,0:T(8,128)(2,1)} %w_out_ref.3, bf16[512,512]{1,0:T(8,128)(2,1)} %bilinear_ref.1), custom_call_target="tpu_custom_call" | custom-call | tf_op jit(solution)/shard_map/item_tower/pallas_call | solution.py:157
  50.0 0.0 copy-done.1
  50.0 6.3 %route.1 = (f32[32,2048]{1,0:T(8,128)}, bf16[32,640]{1,0:T(8,128)(2,1)}, f32[1,32]{1,0:T(1,128)}) custom-call(bf16[512,512]{1,0:T(8,128)(2,1)} %get-tuple-element.13.unit_ref, bf16[512,512]{1,0:T(8,128)(2,1)} %get-tuple-element.14.mapped_ref, bf16[4,256,1024]{2,1,0:T(8,128)(2,1)} %get-tuple-element.15.onehot_ref, f32[128,512]{1,0:T(8,128)} %get-tuple-element.16.first_ref, ...), custom_call_target="tpu_custom_call" | custom-call | tf_op jit(solution)/shard_map/route/pallas_call | solution.py:334
  56.3 0.0 collective-permute-start
  56.3 0.0 collective-permute-done.4.refs_6_
  56.3 0.0 copy-start.4
  56.3 1.6 %collective-permute-start.1 = (bf16[32,640]{1,0:T(8,128)(2,1)}, bf16[32,640]{1,0:T(8,128)(2,1)S(1)}, u32[]{:S(2)}, u32[]{:S(2)}) collective-permute-start(bf16[32,640]{1,0:T(8,128)(2,1)} %get-tuple-element.19.refs_0_), channel_id=1, source_target_pairs={{0,16},{8,24},{16,0},{24,8},{1,17},{9,25},{17,1},{25,9},{2,18},{10... | collective-permute-start | bytes 122888 | tf_op jit(solution)/shard_map/ppermute | solution.py:388
  57.9 0.0 collective-permute-done.5.refs_7_
  57.9 1.4 %collective-permute-start.2 = (bf16[32,640]{1,0:T(8,128)(2,1)}, bf16[32,640]{1,0:T(8,128)(2,1)S(1)}, u32[]{:S(2)}, u32[]{:S(2)}) collective-permute-start(bf16[32,640]{1,0:T(8,128)(2,1)} %get-tuple-element.19.refs_0_), channel_id=1, source_target_pairs={{0,24},{8,0},{16,8},{24,16},{1,25},{9,1},{17,9},{25,17},{2,26},{10... | collective-permute-start | bytes 122888 | tf_op jit(solution)/shard_map/ppermute | solution.py:388
  59.3 0.0 collective-permute-done.7.refs_9_
  59.3 0.0 collective-permute-done.9.refs_11_
  59.3 0.0 copy-start.7
  59.3 0.6 collective-permute-done.refs_1_
  60.0 0.7 collective-permute-done.1.refs_2_
  60.6 0.7 collective-permute-done.2.refs_3_
  61.3 0.0 copy-done.2
  61.3 0.0 copy-done.3
  61.3 0.0 copy-done.4
  61.3 0.0 copy-done.5
  61.3 0.0 copy-done.6
  61.3 0.0 copy-done.7
  61.3 0.0 copy-done.8
  61.3 0.0 copy-done.9
  61.3 0.6 copy-done.10
  61.9 2.5 %negative_sums.1 = (f32[1,32]{1,0:T(1,128)}, f32[1,32]{1,0:T(1,128)}, f32[1,32]{1,0:T(1,128)}, f32[1,32]{1,0:T(1,128)}) custom-call(bf16[32,640]{1,0:T(8,128)(2,1)} %get-tuple-element.19.refs_0_, bf16[32,640]{1,0:T(8,128)(2,1)} %copy-done.8, bf16[32,640]{1,0:T(8,128)(2,1)} %copy-done.9, bf16[32,640]{1,0:T(8,128)(2,1)} %copy-done.10, ...), custom_call_target="tpu_custom_call" | custom-call | tf_op jit(solution)/shard_map/negative_sums/pallas_call | solution.py:370
  64.4 0.6 collective-permute-start.12
  65.0 1.5 %collective-permute-start.11 = (f32[1,32]{1,0:T(1,128)}, f32[1,32]{1,0:T(1,128)S(1)}, u32[]{:S(2)}, u32[]{:S(2)}) collective-permute-start(f32[1,32]{1,0:T(1,128)} %get-tuple-element.22), channel_id=1, source_target_pairs={{0,16},{8,24},{16,0},{24,8},{1,17},{9,25},{17,1},{25,9},{2,18},{10... | collective-permute-start | bytes 392 | tf_op jit(solution)/shard_map/ppermute | solution.py:388
  66.5 1.0 %collective-permute-start.10 = (f32[1,32]{1,0:T(1,128)}, f32[1,32]{1,0:T(1,128)S(1)}, u32[]{:S(2)}, u32[]{:S(2)}) collective-permute-start(f32[1,32]{1,0:T(1,128)} %get-tuple-element.21), channel_id=1, source_target_pairs={{0,24},{8,0},{16,8},{24,16},{1,25},{9,1},{17,9},{25,17},{2,26},{10... | collective-permute-start | bytes 392 | tf_op jit(solution)/shard_map/ppermute | solution.py:388
  67.5 0.0 collective-permute-done.12
  67.5 1.3 %collective-permute-done.11 = f32[1,32]{1,0:T(1,128)S(1)} collective-permute-done((f32[1,32]{1,0:T(1,128)}, f32[1,32]{1,0:T(1,128)S(1)}, u32[]{:S(2)}, u32[]{:S(2)}) %collective-permute-start.11) | collective-permute-done | bytes 160 | tf_op jit(solution)/shard_map/ppermute | solution.py:388
  68.8 0.2 collective-permute-done.10
  68.9 1.2 %subtract_bitcast_fusion = f32[32]{0:T(128)} fusion(f32[1,32]{1,0:T(1,128)} %get-tuple-element.18, f32[1,32]{1,0:T(1,128)S(1)} %collective-permute-done.12, f32[1,32]{1,0:T(1,128)S(1)} %collective-permute-done.11, f32[1,32]{1,0:T(1,128)S(1)} %collective-permute-done.10, f32[1,32]{1,0:T(1,128)} %get-tuple-element.20), kind=kLoop, calls=%fused_computation | loop fusion | flops 160 | bytes 768 | tf_op jit(solution)/shard_map/reshape | solution.py:449
  (9 shorter events, 0.0 us)
Async XLA Ops:
  3.1 39.3 %all-to-all-start = ((bf16[32,16,512]{2,1,0:T(8,128)(2,1)}), bf16[32,16,512]{2,1,0:T(8,128)(2,1)S(1)}, u32[]{:S(2)}, u32[]{:S(2)}) async-start(bf16[32,16,512]{2,1,0:T(8,128)(2,1)} %bitcast.1), calls=%async_computation | async-start | bytes 1048576 | tf_op jit(solution)/shard_map/all_to_all | solution.py:412
  15.2 16.0 %collective-permute-start.6 = (bf16[528,128]{1,0:T(8,128)(2,1)}, bf16[528,128]{1,0:T(8,128)(2,1)S(1)}, u32[]{:S(2)}, u32[]{:S(2)}) collective-permute-start(bf16[528,128]{1,0:T(8,128)(2,1)} %neg_tower.1.refs_4_), channel_id=1, source_target_pairs={{0,4},{1,5},{2,6},{3,7},{4,0},{5,1},{6,2},{7,3},{8,12},{9,13},{10,... | collective-permute-start | bytes 405512 | tf_op jit(solution)/shard_map/ppermute | solution.py:381
  17.9 15.4 %collective-permute-start.3 = (bf16[528,128]{1,0:T(8,128)(2,1)}, bf16[528,128]{1,0:T(8,128)(2,1)S(1)}, u32[]{:S(2)}, u32[]{:S(2)}) collective-permute-start(bf16[528,128]{1,0:T(8,128)(2,1)} %neg_tower.1.refs_4_), channel_id=1, source_target_pairs={{0,1},{1,0},{2,3},{3,2},{4,5},{5,4},{6,7},{7,6},{8,9},{9,8},{10,11... | collective-permute-start | bytes 405512 | tf_op jit(solution)/shard_map/ppermute | solution.py:381
  31.2 18.8 %copy-start.1 = (bf16[528,128]{1,0:T(8,128)(2,1)}, bf16[528,128]{1,0:T(8,128)(2,1)S(1)}, u32[]{:S(2)}) copy-start(bf16[528,128]{1,0:T(8,128)(2,1)S(1)} %collective-permute-done.6.refs_8_) | copy-start | bytes 405508
  31.2 6.5 %collective-permute-start.8 = (bf16[528,128]{1,0:T(8,128)(2,1)S(1)}, bf16[528,128]{1,0:T(8,128)(2,1)S(1)}, u32[]{:S(2)}, u32[]{:S(2)}) collective-permute-start(bf16[528,128]{1,0:T(8,128)(2,1)S(1)} %collective-permute-done.6.refs_8_), channel_id=1, source_target_pairs={{0,2},{1,3},{2,0},{3,1},{4,6},{5,7},{6,4},{7,5},{8,10},{9,11},{10,... | collective-permute-start | bytes 405512 | tf_op jit(solution)/shard_map/ppermute | solution.py:381
  31.2 25.1 %collective-permute-start.4 = (bf16[528,128]{1,0:T(8,128)(2,1)}, bf16[528,128]{1,0:T(8,128)(2,1)S(1)}, u32[]{:S(2)}, u32[]{:S(2)}) collective-permute-start(bf16[528,128]{1,0:T(8,128)(2,1)} %neg_tower.1.refs_4_), channel_id=1, source_target_pairs={{0,2},{1,3},{2,0},{3,1},{4,6},{5,7},{6,4},{7,5},{8,10},{9,11},{10,... | collective-permute-start | bytes 405512 | tf_op jit(solution)/shard_map/ppermute | solution.py:381
  33.3 28.0 %copy-start.2 = (bf16[528,128]{1,0:T(8,128)(2,1)}, bf16[528,128]{1,0:T(8,128)(2,1)S(1)}, u32[]{:S(2)}) copy-start(bf16[528,128]{1,0:T(8,128)(2,1)S(1)} %collective-permute-done.3.refs_5_) | copy-start | bytes 405508
  33.3 24.6 %collective-permute-start.5 = (bf16[528,128]{1,0:T(8,128)(2,1)S(1)}, bf16[528,128]{1,0:T(8,128)(2,1)S(1)}, u32[]{:S(2)}, u32[]{:S(2)}) collective-permute-start(bf16[528,128]{1,0:T(8,128)(2,1)S(1)} %collective-permute-done.3.refs_5_), channel_id=1, source_target_pairs={{0,2},{1,3},{2,0},{3,1},{4,6},{5,7},{6,4},{7,5},{8,10},{9,11},{10,... | collective-permute-start | bytes 405512 | tf_op jit(solution)/shard_map/ppermute | solution.py:381
  33.3 25.9 %collective-permute-start.7 = (bf16[528,128]{1,0:T(8,128)(2,1)S(1)}, bf16[528,128]{1,0:T(8,128)(2,1)S(1)}, u32[]{:S(2)}, u32[]{:S(2)}) collective-permute-start(bf16[528,128]{1,0:T(8,128)(2,1)S(1)} %collective-permute-done.6.refs_8_), channel_id=1, source_target_pairs={{0,1},{1,0},{2,3},{3,2},{4,5},{5,4},{6,7},{7,6},{8,9},{9,8},{10,11... | collective-permute-start | bytes 405512 | tf_op jit(solution)/shard_map/ppermute | solution.py:381
  37.7 23.6 %copy-start.3 = (bf16[528,128]{1,0:T(8,128)(2,1)}, bf16[528,128]{1,0:T(8,128)(2,1)S(1)}, u32[]{:S(2)}) copy-start(bf16[528,128]{1,0:T(8,128)(2,1)S(1)} %collective-permute-done.8.refs_10_) | copy-start | bytes 405508
  37.7 21.6 %collective-permute-start.9 = (bf16[528,128]{1,0:T(8,128)(2,1)S(1)}, bf16[528,128]{1,0:T(8,128)(2,1)S(1)}, u32[]{:S(2)}, u32[]{:S(2)}) collective-permute-start(bf16[528,128]{1,0:T(8,128)(2,1)S(1)} %collective-permute-done.8.refs_10_), channel_id=1, source_target_pairs={{0,1},{1,0},{2,3},{3,2},{4,5},{5,4},{6,7},{7,6},{8,9},{9,8},{10,11... | collective-permute-start | bytes 405512 | tf_op jit(solution)/shard_map/ppermute | solution.py:381
  42.4 0.8 %copy-start = (bf16[32,16,512]{2,1,0:T(8,128)(2,1)}, bf16[32,16,512]{2,1,0:T(8,128)(2,1)S(1)}, u32[]{:S(2)}) copy-start(bf16[32,16,512]{2,1,0:T(8,128)(2,1)S(1)} %all-to-all-done) | copy-start | bytes 1572868
  56.3 3.6 %collective-permute-start = (bf16[32,640]{1,0:T(8,128)(2,1)}, bf16[32,640]{1,0:T(8,128)(2,1)S(1)}, u32[]{:S(2)}, u32[]{:S(2)}) collective-permute-start(bf16[32,640]{1,0:T(8,128)(2,1)} %get-tuple-element.19.refs_0_), channel_id=1, source_target_pairs={{0,8},{8,16},{16,24},{24,0},{1,9},{9,17},{17,25},{25,1},{2,10},{10... | collective-permute-start | bytes 122888 | tf_op jit(solution)/shard_map/ppermute | solution.py:388
  56.3 5.0 %copy-start.4 = (bf16[528,128]{1,0:T(8,128)(2,1)}, bf16[528,128]{1,0:T(8,128)(2,1)S(1)}, u32[]{:S(2)}) copy-start(bf16[528,128]{1,0:T(8,128)(2,1)S(1)} %collective-permute-done.4.refs_6_) | copy-start | bytes 405508
  56.3 4.3 %collective-permute-start.1 = (bf16[32,640]{1,0:T(8,128)(2,1)}, bf16[32,640]{1,0:T(8,128)(2,1)S(1)}, u32[]{:S(2)}, u32[]{:S(2)}) collective-permute-start(bf16[32,640]{1,0:T(8,128)(2,1)} %get-tuple-element.19.refs_0_), channel_id=1, source_target_pairs={{0,16},{8,24},{16,0},{24,8},{1,17},{9,25},{17,1},{25,9},{2,18},{10... | collective-permute-start | bytes 122888 | tf_op jit(solution)/shard_map/ppermute | solution.py:388
  57.9 3.4 %copy-start.5 = (bf16[528,128]{1,0:T(8,128)(2,1)}, bf16[528,128]{1,0:T(8,128)(2,1)S(1)}, u32[]{:S(2)}) copy-start(bf16[528,128]{1,0:T(8,128)(2,1)S(1)} %collective-permute-done.5.refs_7_) | copy-start | bytes 405508
  57.9 3.4 %collective-permute-start.2 = (bf16[32,640]{1,0:T(8,128)(2,1)}, bf16[32,640]{1,0:T(8,128)(2,1)S(1)}, u32[]{:S(2)}, u32[]{:S(2)}) collective-permute-start(bf16[32,640]{1,0:T(8,128)(2,1)} %get-tuple-element.19.refs_0_), channel_id=1, source_target_pairs={{0,24},{8,0},{16,8},{24,16},{1,25},{9,1},{17,9},{25,17},{2,26},{10... | collective-permute-start | bytes 122888 | tf_op jit(solution)/shard_map/ppermute | solution.py:388
  59.3 2.0 %copy-start.6 = (bf16[528,128]{1,0:T(8,128)(2,1)}, bf16[528,128]{1,0:T(8,128)(2,1)S(1)}, u32[]{:S(2)}) copy-start(bf16[528,128]{1,0:T(8,128)(2,1)S(1)} %collective-permute-done.7.refs_9_) | copy-start | bytes 405508
  59.3 2.0 %copy-start.7 = (bf16[528,128]{1,0:T(8,128)(2,1)}, bf16[528,128]{1,0:T(8,128)(2,1)S(1)}, u32[]{:S(2)}) copy-start(bf16[528,128]{1,0:T(8,128)(2,1)S(1)} %collective-permute-done.9.refs_11_) | copy-start | bytes 405508
  60.0 1.4 %copy-start.8 = (bf16[32,640]{1,0:T(8,128)(2,1)}, bf16[32,640]{1,0:T(8,128)(2,1)S(1)}, u32[]{:S(2)}) copy-start(bf16[32,640]{1,0:T(8,128)(2,1)S(1)} %collective-permute-done.refs_1_) | copy-start | bytes 122884
  60.6 0.7 %copy-start.9 = (bf16[32,640]{1,0:T(8,128)(2,1)}, bf16[32,640]{1,0:T(8,128)(2,1)S(1)}, u32[]{:S(2)}) copy-start(bf16[32,640]{1,0:T(8,128)(2,1)S(1)} %collective-permute-done.1.refs_2_) | copy-start | bytes 122884
  61.3 0.6 copy-start.10
  64.4 3.1 %collective-permute-start.12 = (f32[1,32]{1,0:T(1,128)}, f32[1,32]{1,0:T(1,128)S(1)}, u32[]{:S(2)}, u32[]{:S(2)}) collective-permute-start(f32[1,32]{1,0:T(1,128)} %get-tuple-element.23), channel_id=1, source_target_pairs={{0,8},{8,16},{16,24},{24,0},{1,9},{9,17},{17,25},{25,1},{2,10},{10... | collective-permute-start | bytes 392 | tf_op jit(solution)/shard_map/ppermute | solution.py:388
  65.0 3.8 %collective-permute-start.11 = (f32[1,32]{1,0:T(1,128)}, f32[1,32]{1,0:T(1,128)S(1)}, u32[]{:S(2)}, u32[]{:S(2)}) collective-permute-start(f32[1,32]{1,0:T(1,128)} %get-tuple-element.22), channel_id=1, source_target_pairs={{0,16},{8,24},{16,0},{24,8},{1,17},{9,25},{17,1},{25,9},{2,18},{10... | collective-permute-start | bytes 392 | tf_op jit(solution)/shard_map/ppermute | solution.py:388
  66.5 2.4 %collective-permute-start.10 = (f32[1,32]{1,0:T(1,128)}, f32[1,32]{1,0:T(1,128)S(1)}, u32[]{:S(2)}, u32[]{:S(2)}) collective-permute-start(f32[1,32]{1,0:T(1,128)} %get-tuple-element.21), channel_id=1, source_target_pairs={{0,24},{8,0},{16,8},{24,16},{1,25},{9,1},{17,9},{25,17},{2,26},{10... | collective-permute-start | bytes 392 | tf_op jit(solution)/shard_map/ppermute | solution.py:388

commit v3 on v2

--- a/solution.py
+++ b/solution.py
@@ -24,6 +24,19 @@
 i32 = jnp.int32
 
 
+INSIDE = pl.BlockSpec(memory_space=pltpu.VMEM)
+OUTSIDE = pl.BlockSpec(memory_space=pltpu.HBM)
+PARAMS = pltpu.CompilerParams(vmem_limit_bytes=20 << 20)
+
+
+def near(array):
+    return pltpu.with_memory_space_constraint(array, pltpu.VMEM)
+
+
+def far(array):
+    return pltpu.with_memory_space_constraint(array, pltpu.HBM)
+
+
 def mm(a, b):
     return jnp.dot(a, b, preferred_element_type=f32)
 
@@ -63,7 +76,9 @@
     return out
 
 
-def select_kernel(fetch_ref, rows_ref, out_ref):
+def select_kernel(fetch_ref, rows, out_ref, rows_ref, sem):
+    copy = pltpu.make_async_copy(rows, rows_ref, sem)
+    copy.start()
     _, cap, blocks = fetch_ref.shape
     count = blocks * cap
     fetch = fetch_ref[0]
@@ -76,6 +91,7 @@
     column = jnp.sum(jnp.where(place, high * 128.0 + low, 0.0), axis=1, keepdims=True)
     item = iota((count, rows_ref.shape[0]), 1).astype(f32)
     chosen = jnp.where(item == column, 1.0, 0.0).astype(bf16)
+    copy.wait()
     out_ref[...] = mm(chosen, rows_ref[...]).astype(bf16)
 
 
@@ -83,103 +99,83 @@
     blocks, _, cap = fetch.shape
     return pl.pallas_call(
         select_kernel,
+        in_specs=[INSIDE, OUTSIDE],
         out_shape=pltpu.VMEM((blocks * cap, rows.shape[1]), bf16),
+        scratch_shapes=[pltpu.VMEM(rows.shape, bf16), pltpu.SemaphoreType.DMA(())],
+        compiler_params=PARAMS,
         name="select_rows",
-    )(fetch.transpose(1, 2, 0), rows)
-
-
-def tower_step(rows_ref, w_in_ref, bias_ref, w_out_ref, acc_ref):
-    hidden = mm(rows_ref[...], w_in_ref[...]) + bias_ref[...]
-    hidden = jnp.maximum(hidden, 0.0).astype(bf16)
-    part = mm(hidden, w_out_ref[...])
-
-    @pl.when(pl.program_id(0) == 0)
-    def _():
-        acc_ref[...] = part
-
-    @pl.when(pl.program_id(0) > 0)
-    def _():
-        acc_ref[...] += part
-
-
-def unit_of(acc_ref, kind):
-    embedding = acc_ref[...]
+    )(fetch.transpose(1, 2, 0), far(rows))
+
+
+def tower(rows_ref, w_in_ref, bias, w_out, bias_ref, out_ref, sems):
+    small = pltpu.make_async_copy(bias, bias_ref, sems.at[0])
+    small.start()
+    large = pltpu.make_async_copy(w_out, out_ref, sems.at[1])
+    large.start()
+    hidden = mm(rows_ref[...], w_in_ref[...])
+    small.wait()
+    hidden = jnp.maximum(hidden + bias_ref[...], 0.0).astype(bf16)
+    large.wait()
+    embedding = mm(hidden, out_ref[...])
     total = jnp.sum(embedding * embedding, axis=1, keepdims=True)
-    return (embedding * lax.rsqrt(total + norm_epsilon)).astype(kind)
-
-
-def item_kernel(rows_ref, w_in_ref, bias_ref, w_out_ref, bilinear_ref, unit_ref, mapped_ref, acc_ref):
-    tower_step(rows_ref, w_in_ref, bias_ref, w_out_ref, acc_ref)
-
-    @pl.when(pl.program_id(0) == pl.num_programs(0) - 1)
-    def _():
-        unit = unit_of(acc_ref, bf16)
-        unit_ref[...] = unit
-        mapped_ref[...] = mm(unit, bilinear_ref[...]).astype(bf16)
-
-
-def neg_kernel(rows_ref, w_in_ref, bias_ref, w_out_ref, ids_ref, counts_ref, out_ref, acc_ref):
-    tower_step(rows_ref, w_in_ref, bias_ref, w_out_ref, acc_ref)
-
-    @pl.when(pl.program_id(0) == pl.num_programs(0) - 1)
-    def _():
-        count, width = acc_ref.shape
-        out_ref[:width, :] = unit_of(acc_ref, f32).T.astype(bf16)
-        rows = id_digits(ids_ref[...]) + (counts_ref[...].astype(f32),)
-        at = iota((EXTRA, count), 0)
-        extra = jnp.zeros((EXTRA, count), f32)
-        for place, row in enumerate(rows):
-            extra = jnp.where(at == place, row, extra)
-        out_ref[width:, :] = extra.astype(bf16)
-
-
-def chunk_of(hidden_units):
-    return 512 if hidden_units % 512 == 0 else hidden_units
-
-
-def tower_specs(rows, w_in, w_out):
-    chunk = chunk_of(w_in.shape[1])
-    return chunk, [
-        pl.BlockSpec(rows.shape, lambda i: (0, 0)),
-        pl.BlockSpec((w_in.shape[0], chunk), lambda i: (0, i)),
-        pl.BlockSpec((1, chunk), lambda i: (0, i)),
-        pl.BlockSpec((chunk, w_out.shape[1]), lambda i: (i, 0)),
-    ]
-
-
-def whole(shape):
-    return pl.BlockSpec(shape, lambda i: (0,) * len(shape))
-
-
-def item_tower(rows, w_in, bias, w_out, bilinear):
-    chunk, specs = tower_specs(rows, w_in, w_out)
-    shape = (rows.shape[0], w_out.shape[1])
+    return embedding * lax.rsqrt(total + norm_epsilon)
+
+
+def item_kernel(
+    rows_ref, w_in_ref, bias, w_out, bilinear, unit_ref, mapped_ref, bias_ref, out_ref, map_ref, sems
+):
+    fetch = pltpu.make_async_copy(bilinear, map_ref, sems.at[2])
+    fetch.start()
+    unit = tower(rows_ref, w_in_ref, bias, w_out, bias_ref, out_ref, sems).astype(bf16)
+    unit_ref[...] = unit
+    fetch.wait()
+    mapped_ref[...] = mm(unit, map_ref[...]).astype(bf16)
+
+
+def neg_kernel(
+    rows_ref, w_in_ref, bias, w_out, ids_ref, counts_ref, out_ref, bias_ref, w_out_ref, sems
+):
+    unit = tower(rows_ref, w_in_ref, bias, w_out, bias_ref, w_out_ref, sems)
+    count, width = unit.shape
+    out_ref[:width, :] = unit.T.astype(bf16)
+    rows = id_digits(ids_ref[...]) + (counts_ref[...].astype(f32),)
+    at = iota((EXTRA, count), 0)
+    extra = jnp.zeros((EXTRA, count), f32)
+    for place, row in enumerate(rows):
+        extra = jnp.where(at == place, row, extra)
+    out_ref[width:, :] = extra.astype(bf16)
+
+
+def item_tower(rows, weights, bilinear):
+    shape = (rows.shape[0], bilinear.shape[1])
     return pl.pallas_call(
         item_kernel,
-        grid=(w_in.shape[1] // chunk,),
-        in_specs=specs + [whole(bilinear.shape)],
-        out_specs=[whole(shape), whole((shape[0], bilinear.shape[1]))],
-        out_shape=[
-            jax.ShapeDtypeStruct(shape, bf16),
-            jax.ShapeDtypeStruct((shape[0], bilinear.shape[1]), bf16),
+        in_specs=[INSIDE, INSIDE, OUTSIDE, OUTSIDE, OUTSIDE],
+        out_shape=[pltpu.VMEM(rows.shape, bf16), pltpu.VMEM(shape, bf16)],
+        scratch_shapes=[
+            pltpu.VMEM(weights[1].shape, f32),
+            pltpu.VMEM(weights[2].shape, bf16),
+            pltpu.VMEM(bilinear.shape, bf16),
+            pltpu.SemaphoreType.DMA((3,)),
         ],
-        scratch_shapes=[pltpu.VMEM(shape, f32)],
+        compiler_params=PARAMS,
         name="item_tower",
-    )(rows, w_in, bias, w_out, bilinear)
-
-
-def neg_tower(rows, w_in, bias, w_out, ids, counts):
-    chunk, specs = tower_specs(rows, w_in, w_out)
-    shape = (rows.shape[0], w_out.shape[1])
+    )(near(rows), *weights, far(bilinear))
+
+
+def neg_tower(rows, weights, ids, counts):
     return pl.pallas_call(
         neg_kernel,
-        grid=(w_in.shape[1] // chunk,),
-        in_specs=specs + [whole(ids.shape), whole(counts.shape)],
-        out_specs=whole((shape[1] + EXTRA, shape[0])),
-        out_shape=jax.ShapeDtypeStruct((shape[1] + EXTRA, shape[0]), bf16),
-        scratch_shapes=[pltpu.VMEM(shape, f32)],
+        in_specs=[INSIDE, INSIDE, OUTSIDE, OUTSIDE, INSIDE, INSIDE],
+        out_shape=pltpu.VMEM((rows.shape[1] + EXTRA, rows.shape[0]), bf16),
+        scratch_shapes=[
+            pltpu.VMEM(weights[1].shape, f32),
+            pltpu.VMEM(weights[2].shape, bf16),
+            pltpu.SemaphoreType.DMA((2,)),
+        ],
+        compiler_params=PARAMS,
         name="neg_tower",
-    )(rows, w_in, bias, w_out, ids, counts)
+    )(near(rows), *weights, ids, counts)
 
 
 def event_weights(logits, live):
@@ -249,13 +245,12 @@
     return pl.pallas_call(
         prepare_kernel,
         out_shape=[
-            jax.ShapeDtypeStruct(
-                (users // GROUP_USERS, 2 * LANES, GROUP_USERS // 2 * events), bf16
-            ),
-            jax.ShapeDtypeStruct((INTERESTS * users, slots), f32),
+            pltpu.VMEM((users // GROUP_USERS, 2 * LANES, GROUP_USERS // 2 * events), bf16),
+            pltpu.VMEM((INTERESTS * users, slots), f32),
         ],
+        compiler_params=PARAMS,
         name="prepare",
-    )(index, length, init)
+    )(near(index), length, near(init))
 
 
 def route_kernel(
@@ -335,12 +330,24 @@
         route_kernel,
         out_shape=[
             jax.ShapeDtypeStruct((users, INTERESTS * width), f32),
-            jax.ShapeDtypeStruct((users, width + LANES), bf16),
-            jax.ShapeDtypeStruct((1, users), f32),
+            pltpu.VMEM((users, width + LANES), bf16),
+            pltpu.VMEM((1, users), f32),
         ],
         scratch_shapes=[pltpu.VMEM(first.shape, f32)],
+        compiler_params=PARAMS,
         name="route",
-    )(unit, mapped, onehot, first, index, length, init, label, ids, counts)
+    )(
+        near(unit),
+        near(mapped),
+        near(onehot),
+        near(first),
+        near(index),
+        length,
+        near(init),
+        label,
+        ids,
+        counts,
+    )
 
 
 def sums_kernel(parts, pieces, *refs):
@@ -369,9 +376,10 @@
     users = vecs[0].shape[0]
     return pl.pallas_call(
         functools.partial(sums_kernel, len(vecs), len(negs)),
-        out_shape=[jax.ShapeDtypeStruct((1, users), f32) for _ in vecs],
+        out_shape=[pltpu.VMEM((1, users), f32) for _ in vecs],
+        compiler_params=PARAMS,
         name="negative_sums",
-    )(*vecs, *negs)
+    )(*[near(one) for one in [*vecs, *negs]])
 
 
 def gather_pool(own, size):
@@ -407,7 +415,7 @@
     neg_ids,
     neg_counts,
 ):
-    bias = bias_in.reshape(1, -1)
+    weights = (near(w_in), far(bias_in.reshape(1, -1)), far(w_out))
     outgoing = select_rows(fetch_table, item_feats)
     arrived = lax.all_to_all(
         outgoing.reshape(fetch_table.shape[0], fetch_table.shape[2], -1),
@@ -419,13 +427,13 @@
     arrived = arrived.reshape(outgoing.shape)
 
     own_neg = neg_tower(
-        neg_feats, w_in, bias, w_out, neg_ids.reshape(1, -1), neg_counts.reshape(1, -1)
+        neg_feats, weights, neg_ids.reshape(1, -1), neg_counts.reshape(1, -1)
     )
     length = hist_len.reshape(1, -1)
     onehot, first = prepare(hist_index, length, route_init, outgoing.shape[0])
     negs = gather_pool(own_neg, pool_size)
 
-    unit, mapped = item_tower(arrived, w_in, bias, w_out, bilinear)
+    unit, mapped = item_tower(arrived, weights, bilinear)
     interests, vec, positive = route(
         unit,
         mapped,

time: 70.5 us -> 62.3 us (0.88)
  Pallas kernels: 26.1 us -> 15.6 us
  local copies, waits for them, and re-layouts: 1.44 us -> 3.14 us
  waiting for transfers between devices: 18.2 us -> 19.6 us
    pallas_call x4, Pallas kernels: 17.3 us -> 9.77 us  [the longest x1 4.07 us: item_tower(): pl.pallas_call(item_kernel, in_specs=[INSIDE, INSIDE, OUTSIDE, OUTSIDE, O...]
    pallas_call x1, Pallas kernels: 6.29 us -> 4.13 us  [route(): pl.pallas_call(route_kernel, out_shape=[jax.ShapeDtypeStruct((users, INTE...]
    unnamed x22 -> x30, local copies, waits for them, and re-layouts: 1.44 us -> 3.14 us
    ppermute x7, waiting for transfers between devices: 14.8 us -> 16.3 us  [gather_pool(): lax.ppermute(pieces[mask ^ bit], 'pool', [(at, at ^ bit) for at in range(...]
    pallas_call x1, Pallas kernels: 2.48 us -> 1.69 us  [negative_sums(): pl.pallas_call(functools.partial(sums_kernel, len(vecs), len(negs)), out_...]
  transfers between devices with their start and end apart: 14 -> 14, of which waited for: 7 -> 7; matrix products, arithmetic and copies ran while one was open for 0% -> 0% of each run, Pallas kernels for 30% -> 19%
where the time goes in v3:
time: 62.3 us; the launch traced here: 61.8 us
  starting transfers between devices  22.1 us (35%)
  waiting for transfers between devices  19.6 us (31%)
  Pallas kernels  15.6 us (25%)
  local copies, waits for them, and re-layouts  3.14 us (5%)
  between operations  0.82 us (1%)
    ppermute x7, waiting for transfers between devices, gather_pool(): lax.ppermute(pieces[mask ^ bit], 'pool', [(at, at ^ bit) for at in range(...  16.3 us
    ppermute x7, starting transfers between devices, gather_pool(): lax.ppermute(pieces[mask ^ bit], 'pool', [(at, at ^ bit) for at in range(...  9.19 us
    all_to_all x1, starting transfers between devices, on_device(): lax.all_to_all(outgoing.reshape(fetch_table.shape[0], fetch_table.shape[2...  7.33 us
    ppermute x6, starting transfers between devices, rotate(): lax.ppermute(array, axis, [(at, (at + step) % size) for at in range(size)])  5.59 us
    pallas_call x1, Pallas kernels, route(): pl.pallas_call(route_kernel, out_shape=[jax.ShapeDtypeStruct((users, INTE...  4.13 us
    pallas_call x1, Pallas kernels, item_tower(): pl.pallas_call(item_kernel, in_specs=[INSIDE, INSIDE, OUTSIDE, OUTSIDE, O...  4.07 us
    ppermute x6, waiting for transfers between devices, rotate(): lax.ppermute(array, axis, [(at, (at + step) % size) for at in range(size)])  3.27 us
    unnamed x30, local copies, waits for them, and re-layouts  3.14 us
  transfers between devices with their start and end apart: 14, of which 7 were waited for; matrix products, arithmetic and copies ran while one was open for 0% of the time, Pallas kernels for 19%

profile of v3, /device:TPU:0, one launch (start us, length us, event | category | flops | bytes accessed | tf_op | source)
XLA Modules:
  0.0 61.8 jit_solution(3118171694037274239)
XLA Ops:
  0.6 0.0 copy-start
  0.6 0.0 copy-start.7
  0.7 0.8 %copy-done.7 = s32[32,1,16]{0,2,1:T(8,128)S(1)} copy-done((s32[32,1,16]{0,2,1:T(8,128)S(1)}, s32[32,1,16]{0,2,1:T(8,128)}, u32[]{:S(2)}) %copy-start.7) | copy-done | bytes 2072
  1.5 2.3 %select_rows.1 = bf16[512,512]{1,0:T(8,128)(2,1)} custom-call(s32[1,16,32]{2,1,0:T(8,128)S(1)} %bitcast.13, bf16[512,512]{1,0:T(8,128)(2,1)} %rows.1), custom_call_target="tpu_custom_call" | custom-call | tf_op jit(solution)/shard_map/select_rows/pallas_call | solution.py:100
  3.8 7.3 %all-to-all-start = ((bf16[32,16,512]{2,1,0:T(8,128)(2,1)}), bf16[32,16,512]{2,1,0:T(8,128)(2,1)S(1)}, u32[]{:S(2)}, u32[]{:S(2)}) async-start(bf16[32,16,512]{2,1,0:T(8,128)(2,1)} %bitcast.1), calls=%async_computation | async-start | bytes 1048576 | tf_op jit(solution)/shard_map/all_to_all | solution.py:420
  11.2 0.0 copy-done
  11.2 0.0 copy-done.10
  11.2 0.0 copy-done.11
  11.2 0.0 copy-start.6
  11.2 0.9 %copy-done.6 = bf16[128,512]{1,0:T(8,128)(2,1)S(1)} copy-done((bf16[128,512]{1,0:T(8,128)(2,1)S(1)}, bf16[128,512]{1,0:T(8,128)(2,1)}, u32[]{:S(2)}) %copy-start.6) | copy-done | bytes 131096
  12.1 2.3 %neg_tower.1.refs_4_ = bf16[528,128]{1,0:T(8,128)(2,1)S(1)} custom-call(bf16[128,512]{1,0:T(8,128)(2,1)S(1)} %copy-done.6, bf16[512,2048]{1,0:T(8,128)(2,1)S(1)} %copy-done, f32[1,2048]{1,0:T(1,128)} %bitcast.21, bf16[2048,512]{1,0:T(8,128)(2,1)} %w_out.3, s32[1,128]{1,0:T(1,128)S(1)} %bitcast.16, s32[1,128]{1,0:T(1,128)S(1)} %bitcast.17), custom_call_target="tpu_custom_call" | custom-call | tf_op jit(solution)/shard_map/neg_tower/pallas_call | solution.py:167
  14.4 2.7 %collective-permute-start.6 = (bf16[528,128]{1,0:T(8,128)(2,1)S(1)}, bf16[528,128]{1,0:T(8,128)(2,1)S(1)}, u32[]{:S(2)}, u32[]{:S(2)}) collective-permute-start(bf16[528,128]{1,0:T(8,128)(2,1)S(1)} %neg_tower.1.refs_4_), channel_id=1, source_target_pairs={{0,4},{1,5},{2,6},{3,7},{4,0},{5,1},{6,2},{7,3},{8,12},{9,13},{10,... | collective-permute-start | bytes 405512 | tf_op jit(solution)/shard_map/ppermute | solution.py:389
  17.1 1.5 %collective-permute-start.3 = (bf16[528,128]{1,0:T(8,128)(2,1)S(1)}, bf16[528,128]{1,0:T(8,128)(2,1)S(1)}, u32[]{:S(2)}, u32[]{:S(2)}) collective-permute-start(bf16[528,128]{1,0:T(8,128)(2,1)S(1)} %neg_tower.1.refs_4_), channel_id=1, source_target_pairs={{0,1},{1,0},{2,3},{3,2},{4,5},{5,4},{6,7},{7,6},{8,9},{9,8},{10,11... | collective-permute-start | bytes 405512 | tf_op jit(solution)/shard_map/ppermute | solution.py:389
  18.6 13.3 %collective-permute-done.6.refs_8_ = bf16[528,128]{1,0:T(8,128)(2,1)S(1)} collective-permute-done((bf16[528,128]{1,0:T(8,128)(2,1)S(1)}, bf16[528,128]{1,0:T(8,128)(2,1)S(1)}, u32[]{:S(2)}, u32[]{:S(2)}) %collective-permute-start.6) | collective-permute-done | bytes 135200 | tf_op jit(solution)/shard_map/ppermute | solution.py:389
  31.9 0.0 collective-permute-start.8
  31.9 2.0 %collective-permute-start.4 = (bf16[528,128]{1,0:T(8,128)(2,1)S(1)}, bf16[528,128]{1,0:T(8,128)(2,1)}, u32[]{:S(2)}, u32[]{:S(2)}) collective-permute-start(bf16[528,128]{1,0:T(8,128)(2,1)S(1)} %neg_tower.1.refs_4_), channel_id=1, source_target_pairs={{0,2},{1,3},{2,0},{3,1},{4,6},{5,7},{6,4},{7,5},{8,10},{9,11},{10,... | collective-permute-start | bytes 405512 | tf_op jit(solution)/shard_map/ppermute | solution.py:389
  33.9 0.0 collective-permute-done.3.refs_5_
  34.0 0.0 collective-permute-start.5
  34.0 1.5 %collective-permute-start.7 = (bf16[528,128]{1,0:T(8,128)(2,1)S(1)}, bf16[528,128]{1,0:T(8,128)(2,1)}, u32[]{:S(2)}, u32[]{:S(2)}) collective-permute-start(bf16[528,128]{1,0:T(8,128)(2,1)S(1)} %collective-permute-done.6.refs_8_), channel_id=1, source_target_pairs={{0,1},{1,0},{2,3},{3,2},{4,5},{5,4},{6,7},{7,6},{8,9},{9,8},{10,11... | collective-permute-start | bytes 405512 | tf_op jit(solution)/shard_map/ppermute | solution.py:389
  35.4 2.9 %collective-permute-done.8.refs_10_ = bf16[528,128]{1,0:T(8,128)(2,1)S(1)} collective-permute-done((bf16[528,128]{1,0:T(8,128)(2,1)S(1)}, bf16[528,128]{1,0:T(8,128)(2,1)S(1)}, u32[]{:S(2)}, u32[]{:S(2)}) %collective-permute-start.8) | collective-permute-done | bytes 135200 | tf_op jit(solution)/shard_map/ppermute | solution.py:389
  38.4 1.5 %collective-permute-start.9 = (bf16[528,128]{1,0:T(8,128)(2,1)S(1)}, bf16[528,128]{1,0:T(8,128)(2,1)}, u32[]{:S(2)}, u32[]{:S(2)}) collective-permute-start(bf16[528,128]{1,0:T(8,128)(2,1)S(1)} %collective-permute-done.8.refs_10_), channel_id=1, source_target_pairs={{0,1},{1,0},{2,3},{3,2},{4,5},{5,4},{6,7},{7,6},{8,9},{9,8},{10,11... | collective-permute-start | bytes 405512 | tf_op jit(solution)/shard_map/ppermute | solution.py:389
  39.8 0.0 copy-done.3
  39.9 1.1 %prepare.1 = (bf16[4,256,1024]{2,1,0:T(8,128)(2,1)S(1)}, f32[128,512]{1,0:T(8,128)S(1)}) custom-call(s32[32,256]{1,0:T(8,128)S(1)} %copy-done.4, s32[1,32]{1,0:T(1,128)S(1)} %bitcast.14, f32[32,4,256]{2,1,0:T(4,128)S(1)} %copy-done.3), custom_call_target="tpu_custom_call" | custom-call | tf_op jit(solution)/shard_map/prepare/pallas_call | solution.py:245
  41.0 1.3 %copy-done.1 = bf16[4,256,1024]{2,1,0:T(8,128)(2,1)} copy-done((bf16[4,256,1024]{2,1,0:T(8,128)(2,1)}, bf16[4,256,1024]{2,1,0:T(8,128)(2,1)S(1)}, u32[]{:S(2)}) %copy-start.1) | copy-done | bytes 2097176
  42.3 0.0 all-to-all-done
  42.4 0.0 copy-start.12
  42.4 0.0 copy-start.13
  42.4 0.0 copy-start.14
  42.4 4.1 %item_tower.1 = (bf16[512,512]{1,0:T(8,128)(2,1)S(1)}, bf16[512,512]{1,0:T(8,128)(2,1)S(1)}) custom-call(bf16[512,512]{1,0:T(8,128)(2,1)S(1)} %bitcast.12, bf16[512,2048]{1,0:T(8,128)(2,1)S(1)} %copy-done, f32[1,2048]{1,0:T(1,128)} %bitcast.22, bf16[2048,512]{1,0:T(8,128)(2,1)} %w_out.3, bf16[512,512]{1,0:T(8,128)(2,1)} %bilinear.1), custom_call_target="tpu_custom_call" | custom-call | tf_op jit(solution)/shard_map/item_tower/pallas_call | solution.py:151
  46.5 4.1 %route.1 = (f32[32,2048]{1,0:T(8,128)}, bf16[32,640]{1,0:T(8,128)(2,1)S(1)}, f32[1,32]{1,0:T(1,128)S(1)}) custom-call(bf16[512,512]{1,0:T(8,128)(2,1)S(1)} %get-tuple-element.13.unit_ref, bf16[512,512]{1,0:T(8,128)(2,1)S(1)} %get-tuple-element.14.mapped_ref, bf16[4,256,1024]{2,1,0:T(8,128)(2,1)S(1)} %copy-done.2, ...), custom_call_target="tpu_custom_call" | custom-call | tf_op jit(solution)/shard_map/route/pallas_call | solution.py:329
  50.7 0.0 collective-permute-start
  50.7 0.0 collective-permute-done.4.refs_6_
  50.7 1.5 %collective-permute-start.1 = (bf16[32,640]{1,0:T(8,128)(2,1)S(1)}, bf16[32,640]{1,0:T(8,128)(2,1)S(1)}, u32[]{:S(2)}, u32[]{:S(2)}) collective-permute-start(bf16[32,640]{1,0:T(8,128)(2,1)S(1)} %get-tuple-element.19.refs_0_), channel_id=1, source_target_pairs={{0,16},{8,24},{16,0},{24,8},{1,17},{9,25},{17,1},{25,9},{2,18},{10... | collective-permute-start | bytes 122888 | tf_op jit(solution)/shard_map/ppermute | solution.py:396
  52.2 0.0 collective-permute-done.5.refs_7_
  52.2 1.5 %collective-permute-start.2 = (bf16[32,640]{1,0:T(8,128)(2,1)S(1)}, bf16[32,640]{1,0:T(8,128)(2,1)S(1)}, u32[]{:S(2)}, u32[]{:S(2)}) collective-permute-start(bf16[32,640]{1,0:T(8,128)(2,1)S(1)} %get-tuple-element.19.refs_0_), channel_id=1, source_target_pairs={{0,24},{8,0},{16,8},{24,16},{1,25},{9,1},{17,9},{25,17},{2,26},{10... | collective-permute-start | bytes 122888 | tf_op jit(solution)/shard_map/ppermute | solution.py:396
  53.6 0.0 collective-permute-done.7.refs_9_
  53.6 0.0 collective-permute-done.9.refs_11_
  53.6 0.5 collective-permute-done.refs_1_
  54.1 0.6 collective-permute-done.1.refs_2_
  54.7 0.6 %collective-permute-done.2.refs_3_ = bf16[32,640]{1,0:T(8,128)(2,1)S(1)} collective-permute-done((bf16[32,640]{1,0:T(8,128)(2,1)S(1)}, bf16[32,640]{1,0:T(8,128)(2,1)S(1)}, u32[]{:S(2)}, u32[]{:S(2)}) %collective-permute-start.2) | collective-permute-done | bytes 40992 | tf_op jit(solution)/shard_map/ppermute | solution.py:396
  55.3 1.7 %negative_sums.1 = (f32[1,32]{1,0:T(1,128)S(1)}, f32[1,32]{1,0:T(1,128)S(1)}, f32[1,32]{1,0:T(1,128)S(1)}, f32[1,32]{1,0:T(1,128)S(1)}) custom-call(bf16[32,640]{1,0:T(8,128)(2,1)S(1)} %get-tuple-element.19.refs_0_, bf16[32,640]{1,0:T(8,128)(2,1)S(1)} %collective-permute-done.refs_1_, bf16[32,640]{1,0:T(8,128)(2,1)S(1)} %collective-permute-done.1.refs_2_, ...), custom_call_target="tpu_custom_call" | custom-call | tf_op jit(solution)/shard_map/negative_sums/pallas_call | solution.py:377
  57.0 0.7 %collective-permute-start.12 = (f32[1,32]{1,0:T(1,128)S(1)}, f32[1,32]{1,0:T(1,128)S(1)}, u32[]{:S(2)}, u32[]{:S(2)}) collective-permute-start(f32[1,32]{1,0:T(1,128)S(1)} %get-tuple-element.23), channel_id=1, source_target_pairs={{0,8},{8,16},{16,24},{24,0},{1,9},{9,17},{17,25},{25,1},{2,10},{10... | collective-permute-start | bytes 392 | tf_op jit(solution)/shard_map/ppermute | solution.py:396
  57.7 1.5 %collective-permute-start.11 = (f32[1,32]{1,0:T(1,128)S(1)}, f32[1,32]{1,0:T(1,128)S(1)}, u32[]{:S(2)}, u32[]{:S(2)}) collective-permute-start(f32[1,32]{1,0:T(1,128)S(1)} %get-tuple-element.22), channel_id=1, source_target_pairs={{0,16},{8,24},{16,0},{24,8},{1,17},{9,25},{17,1},{25,9},{2,18},{10... | collective-permute-start | bytes 392 | tf_op jit(solution)/shard_map/ppermute | solution.py:396
  59.1 0.5 collective-permute-start.10
  59.6 0.4 collective-permute-done.12
  60.0 1.2 %collective-permute-done.11 = f32[1,32]{1,0:T(1,128)S(1)} collective-permute-done((f32[1,32]{1,0:T(1,128)S(1)}, f32[1,32]{1,0:T(1,128)S(1)}, u32[]{:S(2)}, u32[]{:S(2)}) %collective-permute-start.11) | collective-permute-done | bytes 160 | tf_op jit(solution)/shard_map/ppermute | solution.py:396
  61.2 0.0 collective-permute-done.10
  61.2 0.5 subtract_bitcast_fusion
  (17 shorter events, 0.0 us)
Async XLA Ops:
  0.6 10.5 %copy-start = (bf16[512,2048]{1,0:T(8,128)(2,1)S(1)}, bf16[512,2048]{1,0:T(8,128)(2,1)}, u32[]{:S(2)}) copy-start(bf16[512,2048]{1,0:T(8,128)(2,1)} %w_in_ref.3) | copy-start | bytes 6291460
  0.6 0.8 %copy-start.7 = (s32[32,1,16]{0,2,1:T(8,128)S(1)}, s32[32,1,16]{0,2,1:T(8,128)}, u32[]{:S(2)}) copy-start(s32[32,1,16]{0,2,1:T(8,128)} %param.20) | copy-start | bytes 6148
  1.5 9.7 %copy-start.10 = (s32[128]{0:T(128)S(1)}, s32[128]{0:T(128)}, u32[]{:S(2)}) copy-start(s32[128]{0:T(128)} %param.28) | copy-start | bytes 1540
  1.5 9.7 %copy-start.11 = (s32[128]{0:T(128)S(1)}, s32[128]{0:T(128)}, u32[]{:S(2)}) copy-start(s32[128]{0:T(128)} %param.29) | copy-start | bytes 1540
  3.8 38.5 %all-to-all-start = ((bf16[32,16,512]{2,1,0:T(8,128)(2,1)}), bf16[32,16,512]{2,1,0:T(8,128)(2,1)S(1)}, u32[]{:S(2)}, u32[]{:S(2)}) async-start(bf16[32,16,512]{2,1,0:T(8,128)(2,1)} %bitcast.1), calls=%async_computation | async-start | bytes 1048576 | tf_op jit(solution)/shard_map/all_to_all | solution.py:420
  11.2 0.9 %copy-start.6 = (bf16[128,512]{1,0:T(8,128)(2,1)S(1)}, bf16[128,512]{1,0:T(8,128)(2,1)}, u32[]{:S(2)}) copy-start(bf16[128,512]{1,0:T(8,128)(2,1)} %rows_ref.1) | copy-start | bytes 393220
  12.1 27.7 %copy-start.3 = (f32[32,4,256]{2,1,0:T(4,128)S(1)}, f32[32,4,256]{2,1,0:T(4,128)}, u32[]{:S(2)}) copy-start(f32[32,4,256]{2,1,0:T(4,128)} %init_ref.3) | copy-start | bytes 393220
  12.1 27.8 %copy-start.4 = (s32[32,256]{1,0:T(8,128)S(1)}, s32[32,256]{1,0:T(8,128)}, u32[]{:S(2)}) copy-start(s32[32,256]{1,0:T(8,128)} %index_ref.3) | copy-start | bytes 98308
  12.1 27.8 %copy-start.8 = (s32[32]{0:T(128)S(1)}, s32[32]{0:T(128)}, u32[]{:S(2)}) copy-start(s32[32]{0:T(128)} %param.22) | copy-start | bytes 388
  14.4 17.5 %collective-permute-start.6 = (bf16[528,128]{1,0:T(8,128)(2,1)S(1)}, bf16[528,128]{1,0:T(8,128)(2,1)S(1)}, u32[]{:S(2)}, u32[]{:S(2)}) collective-permute-start(bf16[528,128]{1,0:T(8,128)(2,1)S(1)} %neg_tower.1.refs_4_), channel_id=1, source_target_pairs={{0,4},{1,5},{2,6},{3,7},{4,0},{5,1},{6,2},{7,3},{8,12},{9,13},{10,... | collective-permute-start | bytes 405512 | tf_op jit(solution)/shard_map/ppermute | solution.py:389
  17.1 16.8 %collective-permute-start.3 = (bf16[528,128]{1,0:T(8,128)(2,1)S(1)}, bf16[528,128]{1,0:T(8,128)(2,1)S(1)}, u32[]{:S(2)}, u32[]{:S(2)}) collective-permute-start(bf16[528,128]{1,0:T(8,128)(2,1)S(1)} %neg_tower.1.refs_4_), channel_id=1, source_target_pairs={{0,1},{1,0},{2,3},{3,2},{4,5},{5,4},{6,7},{7,6},{8,9},{9,8},{10,11... | collective-permute-start | bytes 405512 | tf_op jit(solution)/shard_map/ppermute | solution.py:389
  31.9 6.5 %collective-permute-start.8 = (bf16[528,128]{1,0:T(8,128)(2,1)S(1)}, bf16[528,128]{1,0:T(8,128)(2,1)S(1)}, u32[]{:S(2)}, u32[]{:S(2)}) collective-permute-start(bf16[528,128]{1,0:T(8,128)(2,1)S(1)} %collective-permute-done.6.refs_8_), channel_id=1, source_target_pairs={{0,2},{1,3},{2,0},{3,1},{4,6},{5,7},{6,4},{7,5},{8,10},{9,11},{10,... | collective-permute-start | bytes 405512 | tf_op jit(solution)/shard_map/ppermute | solution.py:389
  31.9 18.7 %collective-permute-start.4 = (bf16[528,128]{1,0:T(8,128)(2,1)S(1)}, bf16[528,128]{1,0:T(8,128)(2,1)}, u32[]{:S(2)}, u32[]{:S(2)}) collective-permute-start(bf16[528,128]{1,0:T(8,128)(2,1)S(1)} %neg_tower.1.refs_4_), channel_id=1, source_target_pairs={{0,2},{1,3},{2,0},{3,1},{4,6},{5,7},{6,4},{7,5},{8,10},{9,11},{10,... | collective-permute-start | bytes 405512 | tf_op jit(solution)/shard_map/ppermute | solution.py:389
  34.0 18.2 %collective-permute-start.5 = (bf16[528,128]{1,0:T(8,128)(2,1)S(1)}, bf16[528,128]{1,0:T(8,128)(2,1)}, u32[]{:S(2)}, u32[]{:S(2)}) collective-permute-start(bf16[528,128]{1,0:T(8,128)(2,1)S(1)} %collective-permute-done.3.refs_5_), channel_id=1, source_target_pairs={{0,2},{1,3},{2,0},{3,1},{4,6},{5,7},{6,4},{7,5},{8,10},{9,11},{10,... | collective-permute-start | bytes 405512 | tf_op jit(solution)/shard_map/ppermute | solution.py:389
  34.0 19.6 %collective-permute-start.7 = (bf16[528,128]{1,0:T(8,128)(2,1)S(1)}, bf16[528,128]{1,0:T(8,128)(2,1)}, u32[]{:S(2)}, u32[]{:S(2)}) collective-permute-start(bf16[528,128]{1,0:T(8,128)(2,1)S(1)} %collective-permute-done.6.refs_8_), channel_id=1, source_target_pairs={{0,1},{1,0},{2,3},{3,2},{4,5},{5,4},{6,7},{7,6},{8,9},{9,8},{10,11... | collective-permute-start | bytes 405512 | tf_op jit(solution)/shard_map/ppermute | solution.py:389
  38.4 15.2 %collective-permute-start.9 = (bf16[528,128]{1,0:T(8,128)(2,1)S(1)}, bf16[528,128]{1,0:T(8,128)(2,1)}, u32[]{:S(2)}, u32[]{:S(2)}) collective-permute-start(bf16[528,128]{1,0:T(8,128)(2,1)S(1)} %collective-permute-done.8.refs_10_), channel_id=1, source_target_pairs={{0,1},{1,0},{2,3},{3,2},{4,5},{5,4},{6,7},{7,6},{8,9},{9,8},{10,11... | collective-permute-start | bytes 405512 | tf_op jit(solution)/shard_map/ppermute | solution.py:389
  41.0 1.4 %copy-start.1 = (bf16[4,256,1024]{2,1,0:T(8,128)(2,1)}, bf16[4,256,1024]{2,1,0:T(8,128)(2,1)S(1)}, u32[]{:S(2)}) copy-start(bf16[4,256,1024]{2,1,0:T(8,128)(2,1)S(1)} %get-tuple-element.15.onehot_ref) | copy-start | bytes 6291460
  42.3 4.1 %copy-start.2 = (bf16[4,256,1024]{2,1,0:T(8,128)(2,1)S(1)}, bf16[4,256,1024]{2,1,0:T(8,128)(2,1)}, u32[]{:S(2)}) copy-start(bf16[4,256,1024]{2,1,0:T(8,128)(2,1)} %copy-done.1) | copy-start | bytes 6291460
  42.3 4.1 %copy-start.5 = (s32[32,256]{1,0:T(8,128)S(1)}, s32[32,256]{1,0:T(8,128)}, u32[]{:S(2)}) copy-start(s32[32,256]{1,0:T(8,128)} %index_ref.3) | copy-start | bytes 98308
  42.3 4.1 %copy-start.9 = (s32[32]{0:T(128)S(1)}, s32[32]{0:T(128)}, u32[]{:S(2)}) copy-start(s32[32]{0:T(128)} %param.22) | copy-start | bytes 388
  42.4 4.1 %copy-start.12 = (s32[32]{0:T(128)S(1)}, s32[32]{0:T(128)}, u32[]{:S(2)}) copy-start(s32[32]{0:T(128)} %param.24) | copy-start | bytes 388
  42.4 4.1 %copy-start.13 = (s32[32]{0:T(128)S(1)}, s32[32]{0:T(128)}, u32[]{:S(2)}) copy-start(s32[32]{0:T(128)} %param.25) | copy-start | bytes 388
  42.4 4.1 %copy-start.14 = (s32[32]{0:T(128)S(1)}, s32[32]{0:T(128)}, u32[]{:S(2)}) copy-start(s32[32]{0:T(128)} %param.26) | copy-start | bytes 388
  50.7 3.4 %collective-permute-start = (bf16[32,640]{1,0:T(8,128)(2,1)S(1)}, bf16[32,640]{1,0:T(8,128)(2,1)S(1)}, u32[]{:S(2)}, u32[]{:S(2)}) collective-permute-start(bf16[32,640]{1,0:T(8,128)(2,1)S(1)} %get-tuple-element.19.refs_0_), channel_id=1, source_target_pairs={{0,8},{8,16},{16,24},{24,0},{1,9},{9,17},{17,25},{25,1},{2,10},{10... | collective-permute-start | bytes 122888 | tf_op jit(solution)/shard_map/ppermute | solution.py:396
  50.7 4.0 %collective-permute-start.1 = (bf16[32,640]{1,0:T(8,128)(2,1)S(1)}, bf16[32,640]{1,0:T(8,128)(2,1)S(1)}, u32[]{:S(2)}, u32[]{:S(2)}) collective-permute-start(bf16[32,640]{1,0:T(8,128)(2,1)S(1)} %get-tuple-element.19.refs_0_), channel_id=1, source_target_pairs={{0,16},{8,24},{16,0},{24,8},{1,17},{9,25},{17,1},{25,9},{2,18},{10... | collective-permute-start | bytes 122888 | tf_op jit(solution)/shard_map/ppermute | solution.py:396
  52.2 3.1 %collective-permute-start.2 = (bf16[32,640]{1,0:T(8,128)(2,1)S(1)}, bf16[32,640]{1,0:T(8,128)(2,1)S(1)}, u32[]{:S(2)}, u32[]{:S(2)}) collective-permute-start(bf16[32,640]{1,0:T(8,128)(2,1)S(1)} %get-tuple-element.19.refs_0_), channel_id=1, source_target_pairs={{0,24},{8,0},{16,8},{24,16},{1,25},{9,1},{17,9},{25,17},{2,26},{10... | collective-permute-start | bytes 122888 | tf_op jit(solution)/shard_map/ppermute | solution.py:396
  57.0 3.0 %collective-permute-start.12 = (f32[1,32]{1,0:T(1,128)S(1)}, f32[1,32]{1,0:T(1,128)S(1)}, u32[]{:S(2)}, u32[]{:S(2)}) collective-permute-start(f32[1,32]{1,0:T(1,128)S(1)} %get-tuple-element.23), channel_id=1, source_target_pairs={{0,8},{8,16},{16,24},{24,0},{1,9},{9,17},{17,25},{25,1},{2,10},{10... | collective-permute-start | bytes 392 | tf_op jit(solution)/shard_map/ppermute | solution.py:396
  57.7 3.6 %collective-permute-start.11 = (f32[1,32]{1,0:T(1,128)S(1)}, f32[1,32]{1,0:T(1,128)S(1)}, u32[]{:S(2)}, u32[]{:S(2)}) collective-permute-start(f32[1,32]{1,0:T(1,128)S(1)} %get-tuple-element.22), channel_id=1, source_target_pairs={{0,16},{8,24},{16,0},{24,8},{1,17},{9,25},{17,1},{25,9},{2,18},{10... | collective-permute-start | bytes 392 | tf_op jit(solution)/shard_map/ppermute | solution.py:396
  59.1 2.1 %collective-permute-start.10 = (f32[1,32]{1,0:T(1,128)S(1)}, f32[1,32]{1,0:T(1,128)S(1)}, u32[]{:S(2)}, u32[]{:S(2)}) collective-permute-start(f32[1,32]{1,0:T(1,128)S(1)} %get-tuple-element.21), channel_id=1, source_target_pairs={{0,24},{8,0},{16,8},{24,16},{1,25},{9,1},{17,9},{25,17},{2,26},{10... | collective-permute-start | bytes 392 | tf_op jit(solution)/shard_map/ppermute | solution.py:396

commit v4 on v3

--- a/solution.py
+++ b/solution.py
@@ -76,17 +76,20 @@
     return out
 
 
-def select_kernel(fetch_ref, rows, out_ref, rows_ref, sem):
-    copy = pltpu.make_async_copy(rows, rows_ref, sem)
+def select_kernel(fetch, rows, out_ref, fetch_ref, rows_ref, sems):
+    table = pltpu.make_async_copy(fetch, fetch_ref, sems.at[0])
+    table.start()
+    copy = pltpu.make_async_copy(rows, rows_ref, sems.at[1])
     copy.start()
     _, cap, blocks = fetch_ref.shape
     count = blocks * cap
-    fetch = fetch_ref[0]
     row = iota((count, blocks), 0)
     block = iota((count, blocks), 1)
     pick = jnp.where((row >= block * cap) & (row < block * cap + cap), 1.0, 0.0).astype(bf16)
-    high = mm_nt(pick, (fetch >> 7).astype(f32).astype(bf16))
-    low = mm_nt(pick, (fetch & 127).astype(f32).astype(bf16))
+    table.wait()
+    picked = fetch_ref[0]
+    high = mm_nt(pick, (picked >> 7).astype(f32).astype(bf16))
+    low = mm_nt(pick, (picked & 127).astype(f32).astype(bf16))
     place = iota((count, cap), 1) == lax.rem(iota((count, cap), 0), jnp.int32(cap))
     column = jnp.sum(jnp.where(place, high * 128.0 + low, 0.0), axis=1, keepdims=True)
     item = iota((count, rows_ref.shape[0]), 1).astype(f32)
@@ -99,12 +102,16 @@
     blocks, _, cap = fetch.shape
     return pl.pallas_call(
         select_kernel,
-        in_specs=[INSIDE, OUTSIDE],
+        in_specs=[OUTSIDE, OUTSIDE],
         out_shape=pltpu.VMEM((blocks * cap, rows.shape[1]), bf16),
-        scratch_shapes=[pltpu.VMEM(rows.shape, bf16), pltpu.SemaphoreType.DMA(())],
+        scratch_shapes=[
+            pltpu.VMEM((1, cap, blocks), i32),
+            pltpu.VMEM(rows.shape, bf16),
+            pltpu.SemaphoreType.DMA((2,)),
+        ],
         compiler_params=PARAMS,
         name="select_rows",
-    )(fetch.transpose(1, 2, 0), far(rows))
+    )(far(fetch.transpose(1, 2, 0)), far(rows))
 
 
 def tower(rows_ref, w_in_ref, bias, w_out, bias_ref, out_ref, sems):
@@ -245,7 +252,9 @@
     return pl.pallas_call(
         prepare_kernel,
         out_shape=[
-            pltpu.VMEM((users // GROUP_USERS, 2 * LANES, GROUP_USERS // 2 * events), bf16),
+            jax.ShapeDtypeStruct(
+                (users // GROUP_USERS, 2 * LANES, GROUP_USERS // 2 * events), bf16
+            ),
             pltpu.VMEM((INTERESTS * users, slots), f32),
         ],
         compiler_params=PARAMS,
@@ -256,7 +265,7 @@
 def route_kernel(
     unit_ref,
     mapped_ref,
-    onehot_ref,
+    onehot,
     first_ref,
     index_ref,
     length_ref,
@@ -268,7 +277,11 @@
     vec_ref,
     positive_ref,
     slot_ref,
+    onehot_ref,
+    sem,
 ):
+    fetch = pltpu.make_async_copy(onehot, onehot_ref, sem)
+    fetch.start()
     users, events = index_ref.shape
     slots, width = mapped_ref.shape
     index = index_ref[...]
@@ -279,6 +292,8 @@
     logits = [init_ref[:, k, :] for k in range(INTERESTS)]
     capsules = None
     for iteration in range(ITERS):
+        if iteration == 1:
+            fetch.wait()
         if iteration:
             scatter_weights(event_weights(logits, live), upper, onehot_ref, slot_ref)
         slot_weights = first_ref[...] if iteration == 0 else slot_ref[...]
@@ -333,13 +348,18 @@
             pltpu.VMEM((users, width + LANES), bf16),
             pltpu.VMEM((1, users), f32),
         ],
-        scratch_shapes=[pltpu.VMEM(first.shape, f32)],
+        in_specs=[INSIDE, INSIDE, OUTSIDE] + [INSIDE] * 7,
+        scratch_shapes=[
+            pltpu.VMEM(first.shape, f32),
+            pltpu.VMEM(onehot.shape, bf16),
+            pltpu.SemaphoreType.DMA(()),
+        ],
         compiler_params=PARAMS,
         name="route",
     )(
         near(unit),
         near(mapped),
-        near(onehot),
+        far(onehot),
         near(first),
         near(index),
         length,
@@ -382,18 +402,26 @@
     )(*[near(one) for one in [*vecs, *negs]])
 
 
-def gather_pool(own, size):
-    pieces = {0: own}
-    for mask in range(1, size):
-        bit = 1 << (mask.bit_length() - 1) if mask < 4 else mask & -mask
-        pieces[mask] = lax.ppermute(
-            pieces[mask ^ bit], "pool", [(at, at ^ bit) for at in range(size)]
-        )
-    return list(pieces.values())
-
-
-def rotate(array, axis, size, step):
-    return lax.ppermute(array, axis, [(at, (at + step) % size) for at in range(size)])
+def swap_pool(array, size):
+    return lax.ppermute(array, "pool", [(at, at ^ 1) for at in range(size)])
+
+
+def rotate_user(array, size, step):
+    return lax.ppermute(array, "user", [(at, (at + step) % size) for at in range(size)])
+
+
+def rotate_pool(array, size, step):
+    return lax.ppermute(array, "pool", [(at, (at + 2 * step) % size) for at in range(size)])
+
+
+def gather_negatives(own, user_size, pool_size):
+    pair = swap_pool(own, pool_size)
+    pieces = [own, pair]
+    for step in range(1, user_size):
+        pieces.append(rotate_user(own, user_size, step))
+    for step in range(1, user_size):
+        pieces.append(rotate_user(pair, user_size, step))
+    return pieces
 
 
 def on_device(
@@ -431,7 +459,7 @@
     )
     length = hist_len.reshape(1, -1)
     onehot, first = prepare(hist_index, length, route_init, outgoing.shape[0])
-    negs = gather_pool(own_neg, pool_size)
+    negs = gather_negatives(own_neg, user_size, pool_size)
 
     unit, mapped = item_tower(arrived, weights, bilinear)
     interests, vec, positive = route(
@@ -446,13 +474,12 @@
         label_ids.reshape(1, -1),
         label_counts.reshape(1, -1),
     )
-    vecs = [vec]
-    for step in range(1, user_size):
-        vecs.append(rotate(vec, "user", user_size, step))
+    late = pool_size // 2
+    vecs = [vec] + [rotate_pool(vec, pool_size, step) for step in range(1, late)]
     sums = negative_sums(vecs, negs)
     partition = jnp.exp(positive) + sums[0]
-    for step in range(1, user_size):
-        partition += rotate(sums[step], "user", user_size, user_size - step)
+    for step in range(1, late):
+        partition += rotate_pool(sums[step], pool_size, late - step)
     user_loss = jnp.log(partition) - positive
     return (interests, user_loss.reshape(-1))
 

time: 62.3 us -> 53.6 us (0.86)
  waiting for transfers between devices: 19.6 us -> 9.7 us
  starting transfers between devices: 22.1 us -> 23.3 us
  Pallas kernels: 15.6 us -> 16.6 us
  local copies, waits for them, and re-layouts: 3.14 us -> 2.29 us
    ppermute x13, waiting for transfers between devices: 19.6 us -> 9.7 us  [the longest x6 6.03 us: rotate_pool(): lax.ppermute(array, 'pool', [(at, (at + 2 * step) % size) for at in range...]
    ppermute x13, starting transfers between devices: 14.8 us -> 16 us  [the longest x6 8.22 us: rotate_pool(): lax.ppermute(array, 'pool', [(at, (at + 2 * step) % size) for at in range...]
    pallas_call x1, Pallas kernels: 4.13 us -> 5.09 us  [route(): pl.pallas_call(route_kernel, out_shape=[jax.ShapeDtypeStruct((users, INTE...]
    unnamed x30 -> x26, local copies, waits for them, and re-layouts: 3.14 us -> 2.29 us
  transfers between devices with their start and end apart: 14 -> 14, of which waited for: 7 -> 6; matrix products, arithmetic and copies ran while one was open for 0% -> 0% of each run, Pallas kernels for 19% -> 23%
where the time goes in v4:
time: 53.6 us; the launch traced here: 53.3 us
  starting transfers between devices  23.3 us (43%)
  Pallas kernels  16.6 us (31%)
  waiting for transfers between devices  9.7 us (18%)
  local copies, waits for them, and re-layouts  2.29 us (4%)
  between operations  0.84 us (2%)
    ppermute x6, starting transfers between devices, rotate_pool(): lax.ppermute(array, 'pool', [(at, (at + 2 * step) % size) for at in range...  8.22 us
    all_to_all x1, starting transfers between devices, on_device(): lax.all_to_all(outgoing.reshape(fetch_table.shape[0], fetch_table.shape[2...  7.33 us
    ppermute x6, waiting for transfers between devices, rotate_pool(): lax.ppermute(array, 'pool', [(at, (at + 2 * step) % size) for at in range...  6.03 us
    ppermute x6, starting transfers between devices, rotate_user(): lax.ppermute(array, 'user', [(at, (at + step) % size) for at in range(siz...  5.93 us
    pallas_call x1, Pallas kernels, route(): pl.pallas_call(route_kernel, out_shape=[jax.ShapeDtypeStruct((users, INTE...  5.09 us
    pallas_call x1, Pallas kernels, item_tower(): pl.pallas_call(item_kernel, in_specs=[INSIDE, INSIDE, OUTSIDE, OUTSIDE, O...  3.97 us
    ppermute x1, waiting for transfers between devices, swap_pool(): return lax.ppermute(array, 'pool', [(at, at ^ 1) for at in range(size)])  3.65 us
    pallas_call x1, Pallas kernels, select_rows(): pl.pallas_call(select_kernel, in_specs=[OUTSIDE, OUTSIDE], out_shape=pltp...  2.47 us
  transfers between devices with their start and end apart: 14, of which 6 were waited for; matrix products, arithmetic and copies ran while one was open for 0% of the time, Pallas kernels for 23%

profile of v4, /device:TPU:0, one launch (start us, length us, event | category | flops | bytes accessed | tf_op | source)
XLA Modules:
  0.0 53.3 jit_solution(6031766469719856407)
XLA Ops:
  0.6 0.0 copy-start
  0.6 0.0 copy-start.8
  0.7 0.0 copy-start.9
  0.7 2.5 %select_rows.1 = bf16[512,512]{1,0:T(8,128)(2,1)} custom-call(s32[1,16,32]{2,1,0:T(8,128)} %bitcast.22, bf16[512,512]{1,0:T(8,128)(2,1)} %rows.1), custom_call_target="tpu_custom_call" | custom-call | tf_op jit(solution)/shard_map/select_rows/pallas_call | solution.py:103
  3.1 7.3 %all-to-all-start = ((bf16[32,16,512]{2,1,0:T(8,128)(2,1)}), bf16[32,16,512]{2,1,0:T(8,128)(2,1)S(1)}, u32[]{:S(2)}, u32[]{:S(2)}) async-start(bf16[32,16,512]{2,1,0:T(8,128)(2,1)} %bitcast.1), calls=%async_computation | async-start | bytes 1048576 | tf_op jit(solution)/shard_map/all_to_all | solution.py:448
  10.5 0.0 copy-done
  10.5 0.0 copy-done.8
  10.5 0.0 copy-done.9
  10.5 0.0 copy-start.5
  10.5 0.9 %copy-done.5 = bf16[128,512]{1,0:T(8,128)(2,1)S(1)} copy-done((bf16[128,512]{1,0:T(8,128)(2,1)S(1)}, bf16[128,512]{1,0:T(8,128)(2,1)}, u32[]{:S(2)}) %copy-start.5) | copy-done | bytes 131096
  11.4 2.3 %neg_tower.1.refs_4_ = bf16[528,128]{1,0:T(8,128)(2,1)S(1)} custom-call(bf16[128,512]{1,0:T(8,128)(2,1)S(1)} %copy-done.5, bf16[512,2048]{1,0:T(8,128)(2,1)S(1)} %copy-done, f32[1,2048]{1,0:T(1,128)} %bitcast.20, bf16[2048,512]{1,0:T(8,128)(2,1)} %w_out.3, s32[1,128]{1,0:T(1,128)S(1)} %bitcast.15, s32[1,128]{1,0:T(1,128)S(1)} %bitcast.16), custom_call_target="tpu_custom_call" | custom-call | tf_op jit(solution)/shard_map/neg_tower/pallas_call | solution.py:174
  13.7 1.8 %collective-permute-start.3 = (bf16[528,128]{1,0:T(8,128)(2,1)S(1)}, bf16[528,128]{1,0:T(8,128)(2,1)S(1)}, u32[]{:S(2)}, u32[]{:S(2)}) collective-permute-start(bf16[528,128]{1,0:T(8,128)(2,1)S(1)} %neg_tower.1.refs_4_), channel_id=1, source_target_pairs={{0,1},{1,0},{2,3},{3,2},{4,5},{5,4},{6,7},{7,6},{8,9},{9,8},{10,11... | collective-permute-start | bytes 405512 | tf_op jit(solution)/shard_map/ppermute | solution.py:406
  15.5 0.0 collective-permute-start.4
  15.5 1.5 %collective-permute-start.5 = (bf16[528,128]{1,0:T(8,128)(2,1)S(1)}, bf16[528,128]{1,0:T(8,128)(2,1)S(1)}, u32[]{:S(2)}, u32[]{:S(2)}) collective-permute-start(bf16[528,128]{1,0:T(8,128)(2,1)S(1)} %neg_tower.1.refs_4_), channel_id=1, source_target_pairs={{0,16},{8,24},{16,0},{24,8},{1,17},{9,25},{17,1},{25,9},{2,18},{10... | collective-permute-start | bytes 405512 | tf_op jit(solution)/shard_map/ppermute | solution.py:410
  17.0 1.5 %collective-permute-start.6 = (bf16[528,128]{1,0:T(8,128)(2,1)S(1)}, bf16[528,128]{1,0:T(8,128)(2,1)}, u32[]{:S(2)}, u32[]{:S(2)}) collective-permute-start(bf16[528,128]{1,0:T(8,128)(2,1)S(1)} %neg_tower.1.refs_4_), channel_id=1, source_target_pairs={{0,24},{8,0},{16,8},{24,16},{1,25},{9,1},{17,9},{25,17},{2,26},{10... | collective-permute-start | bytes 405512 | tf_op jit(solution)/shard_map/ppermute | solution.py:410
  18.5 3.6 %collective-permute-done.3.refs_5_ = bf16[528,128]{1,0:T(8,128)(2,1)S(1)} collective-permute-done((bf16[528,128]{1,0:T(8,128)(2,1)S(1)}, bf16[528,128]{1,0:T(8,128)(2,1)S(1)}, u32[]{:S(2)}, u32[]{:S(2)}) %collective-permute-start.3) | collective-permute-done | bytes 135200 | tf_op jit(solution)/shard_map/ppermute | solution.py:406
  22.1 0.0 collective-permute-start.7
  22.1 1.5 %collective-permute-start.8 = (bf16[528,128]{1,0:T(8,128)(2,1)S(1)}, bf16[528,128]{1,0:T(8,128)(2,1)}, u32[]{:S(2)}, u32[]{:S(2)}) collective-permute-start(bf16[528,128]{1,0:T(8,128)(2,1)S(1)} %collective-permute-done.3.refs_5_), channel_id=1, source_target_pairs={{0,16},{8,24},{16,0},{24,8},{1,17},{9,25},{17,1},{25,9},{2,18},{10... | collective-permute-start | bytes 405512 | tf_op jit(solution)/shard_map/ppermute | solution.py:410
  23.6 0.0 collective-permute-done.4.refs_6_
  23.7 1.5 %collective-permute-start.9 = (bf16[528,128]{1,0:T(8,128)(2,1)S(1)}, bf16[528,128]{1,0:T(8,128)(2,1)}, u32[]{:S(2)}, u32[]{:S(2)}) collective-permute-start(bf16[528,128]{1,0:T(8,128)(2,1)S(1)} %collective-permute-done.3.refs_5_), channel_id=1, source_target_pairs={{0,24},{8,0},{16,8},{24,16},{1,25},{9,1},{17,9},{25,17},{2,26},{10... | collective-permute-start | bytes 405512 | tf_op jit(solution)/shard_map/ppermute | solution.py:410
  25.1 0.0 copy-done.2
  25.1 0.0 copy-done.6
  25.1 1.1 %prepare.1 = (bf16[4,256,1024]{2,1,0:T(8,128)(2,1)S(1)}, f32[128,512]{1,0:T(8,128)S(1)}) custom-call(s32[32,256]{1,0:T(8,128)S(1)} %copy-done.3, s32[1,32]{1,0:T(1,128)S(1)} %bitcast.13, f32[32,4,256]{2,1,0:T(4,128)S(1)} %copy-done.2), custom_call_target="tpu_custom_call" | custom-call | tf_op jit(solution)/shard_map/prepare/pallas_call | solution.py:252
  26.3 1.3 %copy-done.1 = bf16[4,256,1024]{2,1,0:T(8,128)(2,1)} copy-done((bf16[4,256,1024]{2,1,0:T(8,128)(2,1)}, bf16[4,256,1024]{2,1,0:T(8,128)(2,1)S(1)}, u32[]{:S(2)}) %copy-start.1) | copy-done | bytes 2097176
  27.6 0.0 all-to-all-done
  27.6 0.0 copy-start.11
  27.6 0.0 copy-start.12
  27.6 4.0 %item_tower.1 = (bf16[512,512]{1,0:T(8,128)(2,1)S(1)}, bf16[512,512]{1,0:T(8,128)(2,1)S(1)}) custom-call(bf16[512,512]{1,0:T(8,128)(2,1)S(1)} %bitcast.12, bf16[512,2048]{1,0:T(8,128)(2,1)S(1)} %copy-done, f32[1,2048]{1,0:T(1,128)} %bitcast.21, bf16[2048,512]{1,0:T(8,128)(2,1)} %w_out.3, bf16[512,512]{1,0:T(8,128)(2,1)} %bilinear.1), custom_call_target="tpu_custom_call" | custom-call | tf_op jit(solution)/shard_map/item_tower/pallas_call | solution.py:158
  31.7 5.1 %route.1 = (f32[32,2048]{1,0:T(8,128)}, bf16[32,640]{1,0:T(8,128)(2,1)S(1)}, f32[1,32]{1,0:T(1,128)S(1)}) custom-call(bf16[512,512]{1,0:T(8,128)(2,1)S(1)} %get-tuple-element.13.unit_ref, bf16[512,512]{1,0:T(8,128)(2,1)S(1)} %get-tuple-element.14.mapped_ref, bf16[4,256,1024]{2,1,0:T(8,128)(2,1)} %copy-done.1, f32[128,512]{1,0:T(8,128)S(1)} %get-tuple-element.16.first_ref, ...), custom_call_target="tpu_custom_call" | custom-call | tf_op jit(solution)/shard_map/route/pallas_call | solution.py:344
  36.8 0.0 collective-permute-done.5.refs_7_
  36.8 0.1 collective-permute-start
  36.8 0.0 collective-permute-done.6.refs_8_
  36.9 2.9 %collective-permute-start.1 = (bf16[32,640]{1,0:T(8,128)(2,1)S(1)}, bf16[32,640]{1,0:T(8,128)(2,1)S(1)}, u32[]{:S(2)}, u32[]{:S(2)}) collective-permute-start(bf16[32,640]{1,0:T(8,128)(2,1)S(1)} %get-tuple-element.19.refs_0_), channel_id=1, source_target_pairs={{0,4},{1,5},{2,6},{3,7},{4,0},{5,1},{6,2},{7,3},{8,12},{9,13},{10,... | collective-permute-start | bytes 122888 | tf_op jit(solution)/shard_map/ppermute | solution.py:414
  39.8 0.0 collective-permute-done.7.refs_9_
  39.8 1.4 %collective-permute-start.2 = (bf16[32,640]{1,0:T(8,128)(2,1)S(1)}, bf16[32,640]{1,0:T(8,128)(2,1)S(1)}, u32[]{:S(2)}, u32[]{:S(2)}) collective-permute-start(bf16[32,640]{1,0:T(8,128)(2,1)S(1)} %get-tuple-element.19.refs_0_), channel_id=1, source_target_pairs={{0,6},{1,7},{2,0},{3,1},{4,2},{5,3},{6,4},{7,5},{8,14},{9,15},{10,... | collective-permute-start | bytes 122888 | tf_op jit(solution)/shard_map/ppermute | solution.py:414
  41.1 0.0 collective-permute-done.8.refs_10_
  41.1 0.0 collective-permute-done.9.refs_11_
  41.1 1.6 %collective-permute-done.refs_1_ = bf16[32,640]{1,0:T(8,128)(2,1)S(1)} collective-permute-done((bf16[32,640]{1,0:T(8,128)(2,1)S(1)}, bf16[32,640]{1,0:T(8,128)(2,1)S(1)}, u32[]{:S(2)}, u32[]{:S(2)}) %collective-permute-start) | collective-permute-done | bytes 40992 | tf_op jit(solution)/shard_map/ppermute | solution.py:414
  42.7 0.0 collective-permute-done.1.refs_2_
  42.7 1.1 %collective-permute-done.2.refs_3_ = bf16[32,640]{1,0:T(8,128)(2,1)S(1)} collective-permute-done((bf16[32,640]{1,0:T(8,128)(2,1)S(1)}, bf16[32,640]{1,0:T(8,128)(2,1)S(1)}, u32[]{:S(2)}, u32[]{:S(2)}) %collective-permute-start.2) | collective-permute-done | bytes 40992 | tf_op jit(solution)/shard_map/ppermute | solution.py:414
  43.8 1.7 %negative_sums.1 = (f32[1,32]{1,0:T(1,128)S(1)}, f32[1,32]{1,0:T(1,128)S(1)}, f32[1,32]{1,0:T(1,128)S(1)}, f32[1,32]{1,0:T(1,128)S(1)}) custom-call(bf16[32,640]{1,0:T(8,128)(2,1)S(1)} %get-tuple-element.19.refs_0_, bf16[32,640]{1,0:T(8,128)(2,1)S(1)} %collective-permute-done.refs_1_, bf16[32,640]{1,0:T(8,128)(2,1)S(1)} %collective-permute-done.1.refs_2_, ...), custom_call_target="tpu_custom_call" | custom-call | tf_op jit(solution)/shard_map/negative_sums/pallas_call | solution.py:397
  45.5 1.5 %collective-permute-start.12 = (f32[1,32]{1,0:T(1,128)S(1)}, f32[1,32]{1,0:T(1,128)S(1)}, u32[]{:S(2)}, u32[]{:S(2)}) collective-permute-start(f32[1,32]{1,0:T(1,128)S(1)} %get-tuple-element.23), channel_id=1, source_target_pairs={{0,2},{1,3},{2,4},{3,5},{4,6},{5,7},{6,0},{7,1},{8,10},{9,11},{10,... | collective-permute-start | bytes 392 | tf_op jit(solution)/shard_map/ppermute | solution.py:414
  46.9 2.3 %collective-permute-start.11 = (f32[1,32]{1,0:T(1,128)S(1)}, f32[1,32]{1,0:T(1,128)S(1)}, u32[]{:S(2)}, u32[]{:S(2)}) collective-permute-start(f32[1,32]{1,0:T(1,128)S(1)} %get-tuple-element.22), channel_id=1, source_target_pairs={{0,4},{1,5},{2,6},{3,7},{4,0},{5,1},{6,2},{7,3},{8,12},{9,13},{10,... | collective-permute-start | bytes 392 | tf_op jit(solution)/shard_map/ppermute | solution.py:414
  49.2 0.2 collective-permute-start.10
  49.4 1.5 %collective-permute-done.12 = f32[1,32]{1,0:T(1,128)S(1)} collective-permute-done((f32[1,32]{1,0:T(1,128)S(1)}, f32[1,32]{1,0:T(1,128)S(1)}, u32[]{:S(2)}, u32[]{:S(2)}) %collective-permute-start.12) | collective-permute-done | bytes 160 | tf_op jit(solution)/shard_map/ppermute | solution.py:414
  50.8 0.6 %collective-permute-done.11 = f32[1,32]{1,0:T(1,128)S(1)} collective-permute-done((f32[1,32]{1,0:T(1,128)S(1)}, f32[1,32]{1,0:T(1,128)S(1)}, u32[]{:S(2)}, u32[]{:S(2)}) %collective-permute-start.11) | collective-permute-done | bytes 160 | tf_op jit(solution)/shard_map/ppermute | solution.py:414
  51.4 1.4 %collective-permute-done.10 = f32[1,32]{1,0:T(1,128)S(1)} collective-permute-done((f32[1,32]{1,0:T(1,128)S(1)}, f32[1,32]{1,0:T(1,128)S(1)}, u32[]{:S(2)}, u32[]{:S(2)}) %collective-permute-start.10) | collective-permute-done | bytes 160 | tf_op jit(solution)/shard_map/ppermute | solution.py:414
  52.8 0.5 subtract_bitcast_fusion
  (13 shorter events, 0.0 us)
Async XLA Ops:
  0.6 9.9 %copy-start = (bf16[512,2048]{1,0:T(8,128)(2,1)S(1)}, bf16[512,2048]{1,0:T(8,128)(2,1)}, u32[]{:S(2)}) copy-start(bf16[512,2048]{1,0:T(8,128)(2,1)} %w_in_ref.3) | copy-start | bytes 6291460
  0.6 9.9 %copy-start.8 = (s32[128]{0:T(128)S(1)}, s32[128]{0:T(128)}, u32[]{:S(2)}) copy-start(s32[128]{0:T(128)} %param.28) | copy-start | bytes 1540
  0.7 9.9 %copy-start.9 = (s32[128]{0:T(128)S(1)}, s32[128]{0:T(128)}, u32[]{:S(2)}) copy-start(s32[128]{0:T(128)} %param.29) | copy-start | bytes 1540
  3.1 24.5 %all-to-all-start = ((bf16[32,16,512]{2,1,0:T(8,128)(2,1)}), bf16[32,16,512]{2,1,0:T(8,128)(2,1)S(1)}, u32[]{:S(2)}, u32[]{:S(2)}) async-start(bf16[32,16,512]{2,1,0:T(8,128)(2,1)} %bitcast.1), calls=%async_computation | async-start | bytes 1048576 | tf_op jit(solution)/shard_map/all_to_all | solution.py:448
  10.5 0.9 %copy-start.5 = (bf16[128,512]{1,0:T(8,128)(2,1)S(1)}, bf16[128,512]{1,0:T(8,128)(2,1)}, u32[]{:S(2)}) copy-start(bf16[128,512]{1,0:T(8,128)(2,1)} %rows_ref.1) | copy-start | bytes 393220
  11.4 13.7 %copy-start.2 = (f32[32,4,256]{2,1,0:T(4,128)S(1)}, f32[32,4,256]{2,1,0:T(4,128)}, u32[]{:S(2)}) copy-start(f32[32,4,256]{2,1,0:T(4,128)} %init_ref.3) | copy-start | bytes 393220
  11.4 13.7 %copy-start.3 = (s32[32,256]{1,0:T(8,128)S(1)}, s32[32,256]{1,0:T(8,128)}, u32[]{:S(2)}) copy-start(s32[32,256]{1,0:T(8,128)} %index_ref.3) | copy-start | bytes 98308
  11.4 13.7 %copy-start.6 = (s32[32]{0:T(128)S(1)}, s32[32]{0:T(128)}, u32[]{:S(2)}) copy-start(s32[32]{0:T(128)} %param.22) | copy-start | bytes 388
  13.7 8.4 %collective-permute-start.3 = (bf16[528,128]{1,0:T(8,128)(2,1)S(1)}, bf16[528,128]{1,0:T(8,128)(2,1)S(1)}, u32[]{:S(2)}, u32[]{:S(2)}) collective-permute-start(bf16[528,128]{1,0:T(8,128)(2,1)S(1)} %neg_tower.1.refs_4_), channel_id=1, source_target_pairs={{0,1},{1,0},{2,3},{3,2},{4,5},{5,4},{6,7},{7,6},{8,9},{9,8},{10,11... | collective-permute-start | bytes 405512 | tf_op jit(solution)/shard_map/ppermute | solution.py:406
  15.5 8.1 %collective-permute-start.4 = (bf16[528,128]{1,0:T(8,128)(2,1)S(1)}, bf16[528,128]{1,0:T(8,128)(2,1)S(1)}, u32[]{:S(2)}, u32[]{:S(2)}) collective-permute-start(bf16[528,128]{1,0:T(8,128)(2,1)S(1)} %neg_tower.1.refs_4_), channel_id=1, source_target_pairs={{0,8},{8,16},{16,24},{24,0},{1,9},{9,17},{17,25},{25,1},{2,10},{10... | collective-permute-start | bytes 405512 | tf_op jit(solution)/shard_map/ppermute | solution.py:410
  15.5 21.2 %collective-permute-start.5 = (bf16[528,128]{1,0:T(8,128)(2,1)S(1)}, bf16[528,128]{1,0:T(8,128)(2,1)S(1)}, u32[]{:S(2)}, u32[]{:S(2)}) collective-permute-start(bf16[528,128]{1,0:T(8,128)(2,1)S(1)} %neg_tower.1.refs_4_), channel_id=1, source_target_pairs={{0,16},{8,24},{16,0},{24,8},{1,17},{9,25},{17,1},{25,9},{2,18},{10... | collective-permute-start | bytes 405512 | tf_op jit(solution)/shard_map/ppermute | solution.py:410
  17.0 19.9 %collective-permute-start.6 = (bf16[528,128]{1,0:T(8,128)(2,1)S(1)}, bf16[528,128]{1,0:T(8,128)(2,1)}, u32[]{:S(2)}, u32[]{:S(2)}) collective-permute-start(bf16[528,128]{1,0:T(8,128)(2,1)S(1)} %neg_tower.1.refs_4_), channel_id=1, source_target_pairs={{0,24},{8,0},{16,8},{24,16},{1,25},{9,1},{17,9},{25,17},{2,26},{10... | collective-permute-start | bytes 405512 | tf_op jit(solution)/shard_map/ppermute | solution.py:410
  22.1 17.6 %collective-permute-start.7 = (bf16[528,128]{1,0:T(8,128)(2,1)S(1)}, bf16[528,128]{1,0:T(8,128)(2,1)}, u32[]{:S(2)}, u32[]{:S(2)}) collective-permute-start(bf16[528,128]{1,0:T(8,128)(2,1)S(1)} %collective-permute-done.3.refs_5_), channel_id=1, source_target_pairs={{0,8},{8,16},{16,24},{24,0},{1,9},{9,17},{17,25},{25,1},{2,10},{10... | collective-permute-start | bytes 405512 | tf_op jit(solution)/shard_map/ppermute | solution.py:410
  22.1 19.0 %collective-permute-start.8 = (bf16[528,128]{1,0:T(8,128)(2,1)S(1)}, bf16[528,128]{1,0:T(8,128)(2,1)}, u32[]{:S(2)}, u32[]{:S(2)}) collective-permute-start(bf16[528,128]{1,0:T(8,128)(2,1)S(1)} %collective-permute-done.3.refs_5_), channel_id=1, source_target_pairs={{0,16},{8,24},{16,0},{24,8},{1,17},{9,25},{17,1},{25,9},{2,18},{10... | collective-permute-start | bytes 405512 | tf_op jit(solution)/shard_map/ppermute | solution.py:410
  23.7 17.5 %collective-permute-start.9 = (bf16[528,128]{1,0:T(8,128)(2,1)S(1)}, bf16[528,128]{1,0:T(8,128)(2,1)}, u32[]{:S(2)}, u32[]{:S(2)}) collective-permute-start(bf16[528,128]{1,0:T(8,128)(2,1)S(1)} %collective-permute-done.3.refs_5_), channel_id=1, source_target_pairs={{0,24},{8,0},{16,8},{24,16},{1,25},{9,1},{17,9},{25,17},{2,26},{10... | collective-permute-start | bytes 405512 | tf_op jit(solution)/shard_map/ppermute | solution.py:410
  26.3 1.3 %copy-start.1 = (bf16[4,256,1024]{2,1,0:T(8,128)(2,1)}, bf16[4,256,1024]{2,1,0:T(8,128)(2,1)S(1)}, u32[]{:S(2)}) copy-start(bf16[4,256,1024]{2,1,0:T(8,128)(2,1)S(1)} %get-tuple-element.15.onehot) | copy-start | bytes 6291460
  27.6 4.0 %copy-start.4 = (s32[32,256]{1,0:T(8,128)S(1)}, s32[32,256]{1,0:T(8,128)}, u32[]{:S(2)}) copy-start(s32[32,256]{1,0:T(8,128)} %index_ref.3) | copy-start | bytes 98308
  27.6 4.0 %copy-start.7 = (s32[32]{0:T(128)S(1)}, s32[32]{0:T(128)}, u32[]{:S(2)}) copy-start(s32[32]{0:T(128)} %param.22) | copy-start | bytes 388
  27.6 4.0 %copy-start.10 = (s32[32]{0:T(128)S(1)}, s32[32]{0:T(128)}, u32[]{:S(2)}) copy-start(s32[32]{0:T(128)} %param.24) | copy-start | bytes 388
  27.6 4.0 %copy-start.11 = (s32[32]{0:T(128)S(1)}, s32[32]{0:T(128)}, u32[]{:S(2)}) copy-start(s32[32]{0:T(128)} %param.25) | copy-start | bytes 388
  27.6 4.0 %copy-start.12 = (s32[32]{0:T(128)S(1)}, s32[32]{0:T(128)}, u32[]{:S(2)}) copy-start(s32[32]{0:T(128)} %param.26) | copy-start | bytes 388
  36.8 5.9 %collective-permute-start = (bf16[32,640]{1,0:T(8,128)(2,1)S(1)}, bf16[32,640]{1,0:T(8,128)(2,1)S(1)}, u32[]{:S(2)}, u32[]{:S(2)}) collective-permute-start(bf16[32,640]{1,0:T(8,128)(2,1)S(1)} %get-tuple-element.19.refs_0_), channel_id=1, source_target_pairs={{0,2},{1,3},{2,4},{3,5},{4,6},{5,7},{6,0},{7,1},{8,10},{9,11},{10,... | collective-permute-start | bytes 122888 | tf_op jit(solution)/shard_map/ppermute | solution.py:414
  36.9 5.8 %collective-permute-start.1 = (bf16[32,640]{1,0:T(8,128)(2,1)S(1)}, bf16[32,640]{1,0:T(8,128)(2,1)S(1)}, u32[]{:S(2)}, u32[]{:S(2)}) collective-permute-start(bf16[32,640]{1,0:T(8,128)(2,1)S(1)} %get-tuple-element.19.refs_0_), channel_id=1, source_target_pairs={{0,4},{1,5},{2,6},{3,7},{4,0},{5,1},{6,2},{7,3},{8,12},{9,13},{10,... | collective-permute-start | bytes 122888 | tf_op jit(solution)/shard_map/ppermute | solution.py:414
  39.8 4.0 %collective-permute-start.2 = (bf16[32,640]{1,0:T(8,128)(2,1)S(1)}, bf16[32,640]{1,0:T(8,128)(2,1)S(1)}, u32[]{:S(2)}, u32[]{:S(2)}) collective-permute-start(bf16[32,640]{1,0:T(8,128)(2,1)S(1)} %get-tuple-element.19.refs_0_), channel_id=1, source_target_pairs={{0,6},{1,7},{2,0},{3,1},{4,2},{5,3},{6,4},{7,5},{8,14},{9,15},{10,... | collective-permute-start | bytes 122888 | tf_op jit(solution)/shard_map/ppermute | solution.py:414
  45.5 5.4 %collective-permute-start.12 = (f32[1,32]{1,0:T(1,128)S(1)}, f32[1,32]{1,0:T(1,128)S(1)}, u32[]{:S(2)}, u32[]{:S(2)}) collective-permute-start(f32[1,32]{1,0:T(1,128)S(1)} %get-tuple-element.23), channel_id=1, source_target_pairs={{0,2},{1,3},{2,4},{3,5},{4,6},{5,7},{6,0},{7,1},{8,10},{9,11},{10,... | collective-permute-start | bytes 392 | tf_op jit(solution)/shard_map/ppermute | solution.py:414
  46.9 4.5 %collective-permute-start.11 = (f32[1,32]{1,0:T(1,128)S(1)}, f32[1,32]{1,0:T(1,128)S(1)}, u32[]{:S(2)}, u32[]{:S(2)}) collective-permute-start(f32[1,32]{1,0:T(1,128)S(1)} %get-tuple-element.22), channel_id=1, source_target_pairs={{0,4},{1,5},{2,6},{3,7},{4,0},{5,1},{6,2},{7,3},{8,12},{9,13},{10,... | collective-permute-start | bytes 392 | tf_op jit(solution)/shard_map/ppermute | solution.py:414
  49.2 3.6 %collective-permute-start.10 = (f32[1,32]{1,0:T(1,128)S(1)}, f32[1,32]{1,0:T(1,128)S(1)}, u32[]{:S(2)}, u32[]{:S(2)}) collective-permute-start(f32[1,32]{1,0:T(1,128)S(1)} %get-tuple-element.21), channel_id=1, source_target_pairs={{0,6},{1,7},{2,0},{3,1},{4,2},{5,3},{6,4},{7,5},{8,14},{9,15},{10,... | collective-permute-start | bytes 392 | tf_op jit(solution)/shard_map/ppermute | solution.py:414

commit v5 on v4

--- a/solution.py
+++ b/solution.py
@@ -13,6 +13,7 @@
 LANES = 128
 SUB = 8
 EXTRA = 16
+SPLIT = 4
 GROUP_USERS = 8
 
 norm_epsilon = 1e-06
@@ -74,6 +75,25 @@
     for at, column in enumerate(columns):
         out = jnp.where(lane == at, column, out)
     return out
+
+
+class Copies:
+    def __init__(self, source, target, sems, first, count):
+        size = source.shape[0] // count
+        self.copies = [
+            pltpu.make_async_copy(
+                source.at[pl.ds(at * size, size)],
+                target.at[pl.ds(at * size, size)],
+                sems.at[first + at],
+            )
+            for at in range(count)
+        ]
+        for copy in self.copies:
+            copy.start()
+
+    def wait(self):
+        for copy in self.copies:
+            copy.wait()
 
 
 def select_kernel(fetch, rows, out_ref, fetch_ref, rows_ref, sems):
@@ -115,10 +135,8 @@
 
 
 def tower(rows_ref, w_in_ref, bias, w_out, bias_ref, out_ref, sems):
-    small = pltpu.make_async_copy(bias, bias_ref, sems.at[0])
-    small.start()
-    large = pltpu.make_async_copy(w_out, out_ref, sems.at[1])
-    large.start()
+    small = Copies(bias, bias_ref, sems, 0, 1)
+    large = Copies(w_out, out_ref, sems, 1, SPLIT)
     hidden = mm(rows_ref[...], w_in_ref[...])
     small.wait()
     hidden = jnp.maximum(hidden + bias_ref[...], 0.0).astype(bf16)
@@ -128,61 +146,50 @@
     return embedding * lax.rsqrt(total + norm_epsilon)
 
 
-def item_kernel(
-    rows_ref, w_in_ref, bias, w_out, bilinear, unit_ref, mapped_ref, bias_ref, out_ref, map_ref, sems
+def neg_kernel(
+    own_ref,
+    apart_ref,
+    w_in_ref,
+    bias,
+    w_out,
+    numbers_ref,
+    numbers_apart_ref,
+    out_ref,
+    rows_ref,
+    bias_ref,
+    w_out_ref,
+    sems,
 ):
-    fetch = pltpu.make_async_copy(bilinear, map_ref, sems.at[2])
-    fetch.start()
-    unit = tower(rows_ref, w_in_ref, bias, w_out, bias_ref, out_ref, sems).astype(bf16)
-    unit_ref[...] = unit
-    fetch.wait()
-    mapped_ref[...] = mm(unit, map_ref[...]).astype(bf16)
-
-
-def neg_kernel(
-    rows_ref, w_in_ref, bias, w_out, ids_ref, counts_ref, out_ref, bias_ref, w_out_ref, sems
-):
+    count = own_ref.shape[0]
+    rows_ref[:count, :] = own_ref[...]
+    rows_ref[count:, :] = apart_ref[...]
     unit = tower(rows_ref, w_in_ref, bias, w_out, bias_ref, w_out_ref, sems)
-    count, width = unit.shape
+    width = unit.shape[1]
     out_ref[:width, :] = unit.T.astype(bf16)
-    rows = id_digits(ids_ref[...]) + (counts_ref[...].astype(f32),)
-    at = iota((EXTRA, count), 0)
-    extra = jnp.zeros((EXTRA, count), f32)
-    for place, row in enumerate(rows):
-        extra = jnp.where(at == place, row, extra)
-    out_ref[width:, :] = extra.astype(bf16)
-
-
-def item_tower(rows, weights, bilinear):
-    shape = (rows.shape[0], bilinear.shape[1])
+    for start, ref in ((0, numbers_ref), (count, numbers_apart_ref)):
+        rows = id_digits(ref[0:1, :]) + (ref[1:2, :].astype(f32),)
+        at = iota((EXTRA, count), 0)
+        extra = jnp.zeros((EXTRA, count), f32)
+        for place, row in enumerate(rows):
+            extra = jnp.where(at == place, row, extra)
+        out_ref[width:, start : start + count] = extra.astype(bf16)
+
+
+def neg_tower(own, apart, weights, numbers, numbers_apart):
+    count, width = own.shape
     return pl.pallas_call(
-        item_kernel,
-        in_specs=[INSIDE, INSIDE, OUTSIDE, OUTSIDE, OUTSIDE],
-        out_shape=[pltpu.VMEM(rows.shape, bf16), pltpu.VMEM(shape, bf16)],
+        neg_kernel,
+        in_specs=[INSIDE, INSIDE, INSIDE, OUTSIDE, OUTSIDE, INSIDE, INSIDE],
+        out_shape=pltpu.VMEM((width + EXTRA, 2 * count), bf16),
         scratch_shapes=[
+            pltpu.VMEM((2 * count, width), bf16),
             pltpu.VMEM(weights[1].shape, f32),
             pltpu.VMEM(weights[2].shape, bf16),
-            pltpu.VMEM(bilinear.shape, bf16),
-            pltpu.SemaphoreType.DMA((3,)),
-        ],
-        compiler_params=PARAMS,
-        name="item_tower",
-    )(near(rows), *weights, far(bilinear))
-
-
-def neg_tower(rows, weights, ids, counts):
-    return pl.pallas_call(
-        neg_kernel,
-        in_specs=[INSIDE, INSIDE, OUTSIDE, OUTSIDE, INSIDE, INSIDE],
-        out_shape=pltpu.VMEM((rows.shape[1] + EXTRA, rows.shape[0]), bf16),
-        scratch_shapes=[
-            pltpu.VMEM(weights[1].shape, f32),
-            pltpu.VMEM(weights[2].shape, bf16),
-            pltpu.SemaphoreType.DMA((2,)),
+            pltpu.SemaphoreType.DMA((1 + SPLIT,)),
         ],
         compiler_params=PARAMS,
         name="neg_tower",
-    )(near(rows), *weights, ids, counts)
+    )(near(own), near(apart), *weights, near(numbers), near(numbers_apart))
 
 
 def event_weights(logits, live):
@@ -263,32 +270,57 @@
 
 
 def route_kernel(
-    unit_ref,
-    mapped_ref,
+    rows_ref,
+    w_in_ref,
+    first_ref,
+    bias,
+    w_out,
+    bilinear,
     onehot,
-    first_ref,
+    index,
+    length,
+    init,
+    label,
+    ids,
+    counts,
+    interests_ref,
+    vec_ref,
+    positive_ref,
+    bias_ref,
+    out_ref,
+    map_ref,
+    onehot_ref,
     index_ref,
     length_ref,
     init_ref,
     label_ref,
     ids_ref,
     counts_ref,
-    interests_ref,
-    vec_ref,
-    positive_ref,
     slot_ref,
-    onehot_ref,
-    sem,
+    sems,
 ):
-    fetch = pltpu.make_async_copy(onehot, onehot_ref, sem)
-    fetch.start()
+    pairs = (
+        (bilinear, map_ref),
+        (index, index_ref),
+        (length, length_ref),
+        (init, init_ref),
+        (label, label_ref),
+        (ids, ids_ref),
+        (counts, counts_ref),
+    )
+    start = 1 + SPLIT
+    others = [Copies(*pair, sems, start + at, 1) for at, pair in enumerate(pairs)]
+    unit = tower(rows_ref, w_in_ref, bias, w_out, bias_ref, out_ref, sems).astype(bf16)
+    fetch = Copies(onehot, onehot_ref, sems, start + len(pairs), onehot.shape[0])
+    for other in others:
+        other.wait()
+    mapped = mm(unit, map_ref[...]).astype(bf16)
     users, events = index_ref.shape
-    slots, width = mapped_ref.shape
+    slots, width = mapped.shape
     index = index_ref[...]
     upper = index >> 7
     lower = index & (LANES - 1)
     live = live_mask(length_ref, index.shape)
-    mapped = mapped_ref[...]
     logits = [init_ref[:, k, :] for k in range(INTERESTS)]
     capsules = None
     for iteration in range(ITERS):
@@ -325,7 +357,7 @@
         interests_ref[:, k * width : (k + 1) * width] = each[k]
     label = to_column(label_ref[...].astype(f32))
     chosen = jnp.where(iota((users, slots), 1).astype(f32) == label, 1.0, 0.0).astype(bf16)
-    label_rows = mm(chosen, unit_ref[...])
+    label_rows = mm(chosen, unit)
     raised = [
         jnp.exp(attend_scale * jnp.sum(one * label_rows, axis=1, keepdims=True)) for one in each
     ]
@@ -338,36 +370,26 @@
     positive_ref[...] = logit_scale * to_row(match) - jnp.log(counts_ref[...].astype(f32))
 
 
-def route(unit, mapped, onehot, first, index, length, init, label, ids, counts):
+def route(rows, w_in, first, *others):
+    _, _, bilinear, onehot, index, _, _, _, _, _ = others
     users = index.shape[0]
-    width = mapped.shape[1]
+    width = bilinear.shape[1]
     return pl.pallas_call(
         route_kernel,
+        in_specs=[INSIDE] * 3 + [OUTSIDE] * len(others),
         out_shape=[
             jax.ShapeDtypeStruct((users, INTERESTS * width), f32),
             pltpu.VMEM((users, width + LANES), bf16),
             pltpu.VMEM((1, users), f32),
         ],
-        in_specs=[INSIDE, INSIDE, OUTSIDE] + [INSIDE] * 7,
-        scratch_shapes=[
+        scratch_shapes=[pltpu.VMEM(one.shape, one.dtype) for one in others]
+        + [
             pltpu.VMEM(first.shape, f32),
-            pltpu.VMEM(onehot.shape, bf16),
-            pltpu.SemaphoreType.DMA(()),
+            pltpu.SemaphoreType.DMA((SPLIT + len(others) - 1 + onehot.shape[0],)),
         ],
         compiler_params=PARAMS,
         name="route",
-    )(
-        near(unit),
-        near(mapped),
-        far(onehot),
-        near(first),
-        near(index),
-        length,
-        near(init),
-        label,
-        ids,
-        counts,
-    )
+    )(near(rows), near(w_in), near(first), *[far(one) for one in others])
 
 
 def sums_kernel(parts, pieces, *refs):
@@ -402,26 +424,20 @@
     )(*[near(one) for one in [*vecs, *negs]])
 
 
-def swap_pool(array, size):
-    return lax.ppermute(array, "pool", [(at, at ^ 1) for at in range(size)])
+def swap_pool(array, size, bit):
+    return lax.ppermute(array, "pool", [(at, at ^ bit) for at in range(size)])
 
 
 def rotate_user(array, size, step):
     return lax.ppermute(array, "user", [(at, (at + step) % size) for at in range(size)])
 
 
-def rotate_pool(array, size, step):
-    return lax.ppermute(array, "pool", [(at, (at + 2 * step) % size) for at in range(size)])
-
-
-def gather_negatives(own, user_size, pool_size):
-    pair = swap_pool(own, pool_size)
-    pieces = [own, pair]
-    for step in range(1, user_size):
-        pieces.append(rotate_user(own, user_size, step))
-    for step in range(1, user_size):
-        pieces.append(rotate_user(pair, user_size, step))
-    return pieces
+def gather_negatives(own, bits, size):
+    pieces = {0: own}
+    for mask in range(1, 1 << len(bits)):
+        last = mask.bit_length() - 1
+        pieces[mask] = swap_pool(pieces[mask ^ (1 << last)], size, bits[last])
+    return list(pieces.values())
 
 
 def on_device(
@@ -444,6 +460,7 @@
     neg_counts,
 ):
     weights = (near(w_in), far(bias_in.reshape(1, -1)), far(w_out))
+    apart = swap_pool(neg_feats, pool_size, pool_size // 2)
     outgoing = select_rows(fetch_table, item_feats)
     arrived = lax.all_to_all(
         outgoing.reshape(fetch_table.shape[0], fetch_table.shape[2], -1),
@@ -454,19 +471,22 @@
     )
     arrived = arrived.reshape(outgoing.shape)
 
-    own_neg = neg_tower(
-        neg_feats, weights, neg_ids.reshape(1, -1), neg_counts.reshape(1, -1)
-    )
+    numbers = jnp.stack([neg_ids, neg_counts])
+    numbers_apart = swap_pool(numbers, pool_size, pool_size // 2)
+    own_neg = neg_tower(neg_feats, apart, weights, numbers, numbers_apart)
     length = hist_len.reshape(1, -1)
     onehot, first = prepare(hist_index, length, route_init, outgoing.shape[0])
-    negs = gather_negatives(own_neg, user_size, pool_size)
-
-    unit, mapped = item_tower(arrived, weights, bilinear)
+    bits = [1 << at for at in range(pool_size.bit_length() - 2)]
+    negs = gather_negatives(own_neg, bits[1:] + bits[:1], pool_size)
+
     interests, vec, positive = route(
-        unit,
-        mapped,
+        arrived,
+        w_in,
+        first,
+        bias_in.reshape(1, -1),
+        w_out,
+        bilinear,
         onehot,
-        first,
         hist_index,
         length,
         route_init,
@@ -474,12 +494,11 @@
         label_ids.reshape(1, -1),
         label_counts.reshape(1, -1),
     )
-    late = pool_size // 2
-    vecs = [vec] + [rotate_pool(vec, pool_size, step) for step in range(1, late)]
+    vecs = [vec] + [rotate_user(vec, user_size, step) for step in range(1, user_size)]
     sums = negative_sums(vecs, negs)
     partition = jnp.exp(positive) + sums[0]
-    for step in range(1, late):
-        partition += rotate_pool(sums[step], pool_size, late - step)
+    for step in range(1, user_size):
+        partition += rotate_user(sums[step], user_size, user_size - step)
     user_loss = jnp.log(partition) - positive
     return (interests, user_loss.reshape(-1))
 

time: 53.6 us -> 66.4 us (1.24)
  waiting for transfers between devices: 9.7 us -> 27.2 us
  starting transfers between devices: 23.3 us -> 19.1 us
    ppermute x7 -> x5, waiting for transfers between devices: 9.68 us -> 23.9 us  [swap_pool(): return lax.ppermute(array, 'pool', [(at, at ^ bit) for at in range(size)])]
    ppermute x7 -> x5, starting transfers between devices: 10 us -> 6.12 us  [swap_pool(): return lax.ppermute(array, 'pool', [(at, at ^ bit) for at in range(size)])]
    ppermute x6, waiting for transfers between devices: 0.02 us -> 3.26 us  [rotate_user(): lax.ppermute(array, 'user', [(at, (at + step) % size) for at in range(siz...]
    pallas_call x3 -> x2, Pallas kernels: 11.3 us -> 11 us  [the longest x1 8.5 us: route(): pl.pallas_call(route_kernel, in_specs=[INSIDE] * 3 + [OUTSIDE] * len(othe...]
    unnamed x26 -> x16, local copies, waits for them, and re-layouts: 2.29 us -> 2.24 us
  transfers between devices with their start and end apart: 14 -> 12, of which waited for: 6 -> 7; matrix products, arithmetic and copies ran while one was open for 0% -> 0% of each run, Pallas kernels for 23% -> 18%
where the time goes in v5:
time: 66.4 us; the launch traced here: 65.9 us
  waiting for transfers between devices  27.2 us (41%)
  starting transfers between devices  19.1 us (29%)
  Pallas kernels  16.1 us (24%)
  local copies, waits for them, and re-layouts  2.24 us (3%)
  between operations  0.74 us (1%)
    ppermute x5, waiting for transfers between devices, swap_pool(): return lax.ppermute(array, 'pool', [(at, at ^ bit) for at in range(size)])  23.9 us
    pallas_call x1, Pallas kernels, route(): pl.pallas_call(route_kernel, in_specs=[INSIDE] * 3 + [OUTSIDE] * len(othe...  8.5 us
    all_to_all x1, starting transfers between devices, on_device(): lax.all_to_all(outgoing.reshape(fetch_table.shape[0], fetch_table.shape[2...  7.33 us
    ppermute x5, starting transfers between devices, swap_pool(): return lax.ppermute(array, 'pool', [(at, at ^ bit) for at in range(size)])  6.12 us
    ppermute x6, starting transfers between devices, rotate_user(): lax.ppermute(array, 'user', [(at, (at + step) % size) for at in range(siz...  5.65 us
    ppermute x6, waiting for transfers between devices, rotate_user(): lax.ppermute(array, 'user', [(at, (at + step) % size) for at in range(siz...  3.26 us
    pallas_call x1, Pallas kernels, neg_tower(): pl.pallas_call(neg_kernel, in_specs=[INSIDE, INSIDE, INSIDE, OUTSIDE, OUT...  2.48 us
    pallas_call x1, Pallas kernels, select_rows(): pl.pallas_call(select_kernel, in_specs=[OUTSIDE, OUTSIDE], out_shape=pltp...  2.45 us
  transfers between devices with their start and end apart: 12, of which 7 were waited for; matrix products, arithmetic and copies ran while one was open for 0% of the time, Pallas kernels for 18%

profile of v5, /device:TPU:0, one launch (start us, length us, event | category | flops | bytes accessed | tf_op | source)
XLA Modules:
  0.0 65.9 jit_solution(4935912066230415886)
XLA Ops:
  0.6 0.0 copy-start.6
  0.6 0.0 copy-start.7
  0.7 0.0 copy-start
  0.7 2.5 %select_rows.1 = bf16[512,512]{1,0:T(8,128)(2,1)} custom-call(s32[1,16,32]{2,1,0:T(8,128)} %bitcast.17, bf16[512,512]{1,0:T(8,128)(2,1)} %rows.1), custom_call_target="tpu_custom_call" | custom-call | tf_op jit(solution)/shard_map/select_rows/pallas_call | solution.py:123
  3.1 7.3 %all-to-all-start = ((bf16[32,16,512]{2,1,0:T(8,128)(2,1)}), bf16[32,16,512]{2,1,0:T(8,128)(2,1)S(1)}, u32[]{:S(2)}, u32[]{:S(2)}) async-start(bf16[32,16,512]{2,1,0:T(8,128)(2,1)} %bitcast.1), calls=%async_computation | async-start | bytes 1048576 | tf_op jit(solution)/shard_map/all_to_all | solution.py:465
  10.5 2.7 %collective-permute-start.3 = (bf16[128,512]{1,0:T(8,128)(2,1)}, bf16[128,512]{1,0:T(8,128)(2,1)S(1)}, u32[]{:S(2)}, u32[]{:S(2)}) collective-permute-start(bf16[128,512]{1,0:T(8,128)(2,1)} %own_ref.1), channel_id=1, source_target_pairs={{0,4},{1,5},{2,6},{3,7},{4,0},{5,1},{6,2},{7,3},{8,12},{9,13},{10,... | collective-permute-start | bytes 393224 | tf_op jit(solution)/shard_map/ppermute | solution.py:428
  13.2 0.0 copy-done.6
  13.2 0.0 copy-done.7
  13.2 0.3 collective-permute-start.4
  13.5 17.6 %collective-permute-done.4.numbers_apart_ref = s32[2,128]{1,0:T(2,128)S(1)} collective-permute-done((s32[2,128]{1,0:T(2,128)S(1)}, s32[2,128]{1,0:T(2,128)S(1)}, u32[]{:S(2)}, u32[]{:S(2)}) %collective-permute-start.4) | collective-permute-done | bytes 1056 | tf_op jit(solution)/shard_map/ppermute | solution.py:428
  31.1 0.0 collective-permute-done.3.apart_ref
  31.1 0.0 copy-done
  31.1 0.0 copy-start.4
  31.1 0.9 %copy-done.4 = bf16[128,512]{1,0:T(8,128)(2,1)S(1)} copy-done((bf16[128,512]{1,0:T(8,128)(2,1)S(1)}, bf16[128,512]{1,0:T(8,128)(2,1)}, u32[]{:S(2)}) %copy-start.4) | copy-done | bytes 131096
  32.0 0.0 copy-start.2
  32.0 0.0 copy-start.3
  32.0 0.0 copy-start.5
  32.0 2.5 %neg_tower.1.refs_4_ = bf16[528,256]{1,0:T(8,128)(2,1)S(1)} custom-call(bf16[128,512]{1,0:T(8,128)(2,1)S(1)} %copy-done.4, bf16[128,512]{1,0:T(8,128)(2,1)S(1)} %collective-permute-done.3.apart_ref, bf16[512,2048]{1,0:T(8,128)(2,1)S(1)} %copy-done, f32[1,2048]{1,0:T(1,128)} %bitcast.15, bf16[2048,512]{1,0:T(8,128)(2,1)} %w_out.3, ...), custom_call_target="tpu_custom_call" | custom-call | tf_op jit(solution)/shard_map/neg_tower/pallas_call | solution.py:180
  34.5 0.1 collective-permute-start.5
  34.6 1.5 %collective-permute-start.6 = (bf16[528,256]{1,0:T(8,128)(2,1)S(1)}, bf16[528,256]{1,0:T(8,128)(2,1)}, u32[]{:S(2)}, u32[]{:S(2)}) collective-permute-start(bf16[528,256]{1,0:T(8,128)(2,1)S(1)} %neg_tower.1.refs_4_), channel_id=1, source_target_pairs={{0,1},{1,0},{2,3},{3,2},{4,5},{5,4},{6,7},{7,6},{8,9},{9,8},{10,11... | collective-permute-start | bytes 811016 | tf_op jit(solution)/shard_map/ppermute | solution.py:428
  36.2 6.3 %collective-permute-done.5.refs_5_ = bf16[528,256]{1,0:T(8,128)(2,1)S(1)} collective-permute-done((bf16[528,256]{1,0:T(8,128)(2,1)S(1)}, bf16[528,256]{1,0:T(8,128)(2,1)S(1)}, u32[]{:S(2)}, u32[]{:S(2)}) %collective-permute-start.5) | collective-permute-done | bytes 270368 | tf_op jit(solution)/shard_map/ppermute | solution.py:428
  42.5 1.5 %collective-permute-start.7 = (bf16[528,256]{1,0:T(8,128)(2,1)S(1)}, bf16[528,256]{1,0:T(8,128)(2,1)}, u32[]{:S(2)}, u32[]{:S(2)}) collective-permute-start(bf16[528,256]{1,0:T(8,128)(2,1)S(1)} %collective-permute-done.5.refs_5_), channel_id=1, source_target_pairs={{0,1},{1,0},{2,3},{3,2},{4,5},{5,4},{6,7},{7,6},{8,9},{9,8},{10,11... | collective-permute-start | bytes 811016 | tf_op jit(solution)/shard_map/ppermute | solution.py:428
  44.0 0.0 copy-done.2
  44.0 0.0 copy-done.3
  44.0 0.0 copy-done.5
  44.0 1.1 %prepare.1 = (bf16[4,256,1024]{2,1,0:T(8,128)(2,1)S(1)}, f32[128,512]{1,0:T(8,128)S(1)}) custom-call(s32[32,256]{1,0:T(8,128)S(1)} %copy-done.3, s32[1,32]{1,0:T(1,128)S(1)} %bitcast.14, f32[32,4,256]{2,1,0:T(4,128)S(1)} %copy-done.2), custom_call_target="tpu_custom_call" | custom-call | tf_op jit(solution)/shard_map/prepare/pallas_call | solution.py:259
  45.1 0.0 copy-start.1
  45.1 1.3 %copy-done.1 = bf16[4,256,1024]{2,1,0:T(8,128)(2,1)} copy-done((bf16[4,256,1024]{2,1,0:T(8,128)(2,1)}, bf16[4,256,1024]{2,1,0:T(8,128)(2,1)S(1)}, u32[]{:S(2)}) %copy-start.1) | copy-done | bytes 2097176
  46.4 0.0 all-to-all-done
  46.4 8.5 %route.1 = (f32[32,2048]{1,0:T(8,128)}, bf16[32,640]{1,0:T(8,128)(2,1)S(1)}, f32[1,32]{1,0:T(1,128)S(1)}) custom-call(bf16[512,512]{1,0:T(8,128)(2,1)S(1)} %bitcast.12, bf16[512,2048]{1,0:T(8,128)(2,1)S(1)} %copy-done, f32[128,512]{1,0:T(8,128)S(1)} %get-tuple-element.11.first_ref, f32[1,2048]{1,0:T(1,128)} %bitcast.16, bf16[2048,512]{1,0:T(8,128)(2,1)} %w_out.3, ...), custom_call_target="tpu_custom_call" | custom-call | tf_op jit(solution)/shard_map/route/pallas_call | solution.py:377
  54.9 0.1 collective-permute-start
  55.0 1.6 %collective-permute-start.1 = (bf16[32,640]{1,0:T(8,128)(2,1)S(1)}, bf16[32,640]{1,0:T(8,128)(2,1)S(1)}, u32[]{:S(2)}, u32[]{:S(2)}) collective-permute-start(bf16[32,640]{1,0:T(8,128)(2,1)S(1)} %get-tuple-element.15.refs_0_), channel_id=1, source_target_pairs={{0,16},{8,24},{16,0},{24,8},{1,17},{9,25},{17,1},{25,9},{2,18},{10... | collective-permute-start | bytes 122888 | tf_op jit(solution)/shard_map/ppermute | solution.py:432
  56.6 1.4 %collective-permute-start.2 = (bf16[32,640]{1,0:T(8,128)(2,1)S(1)}, bf16[32,640]{1,0:T(8,128)(2,1)S(1)}, u32[]{:S(2)}, u32[]{:S(2)}) collective-permute-start(bf16[32,640]{1,0:T(8,128)(2,1)S(1)} %get-tuple-element.15.refs_0_), channel_id=1, source_target_pairs={{0,24},{8,0},{16,8},{24,16},{1,25},{9,1},{17,9},{25,17},{2,26},{10... | collective-permute-start | bytes 122888 | tf_op jit(solution)/shard_map/ppermute | solution.py:432
  57.9 0.0 collective-permute-done.6.refs_6_
  58.0 0.0 collective-permute-done.7.refs_7_
  58.0 0.5 collective-permute-done.refs_1_
  58.4 0.7 collective-permute-done.1.refs_2_
  59.1 0.6 collective-permute-done.2.refs_3_
  59.6 1.5 %negative_sums.1 = (f32[1,32]{1,0:T(1,128)S(1)}, f32[1,32]{1,0:T(1,128)S(1)}, f32[1,32]{1,0:T(1,128)S(1)}, f32[1,32]{1,0:T(1,128)S(1)}) custom-call(bf16[32,640]{1,0:T(8,128)(2,1)S(1)} %get-tuple-element.15.refs_0_, bf16[32,640]{1,0:T(8,128)(2,1)S(1)} %collective-permute-done.refs_1_, bf16[32,640]{1,0:T(8,128)(2,1)S(1)} %collective-permute-done.1.refs_2_, ...), custom_call_target="tpu_custom_call" | custom-call | tf_op jit(solution)/shard_map/negative_sums/pallas_call | solution.py:419
  61.2 0.7 collective-permute-start.10
  61.8 1.5 %collective-permute-start.9 = (f32[1,32]{1,0:T(1,128)S(1)}, f32[1,32]{1,0:T(1,128)S(1)}, u32[]{:S(2)}, u32[]{:S(2)}) collective-permute-start(f32[1,32]{1,0:T(1,128)S(1)} %get-tuple-element.18), channel_id=1, source_target_pairs={{0,16},{8,24},{16,0},{24,8},{1,17},{9,25},{17,1},{25,9},{2,18},{10... | collective-permute-start | bytes 392 | tf_op jit(solution)/shard_map/ppermute | solution.py:432
  63.3 0.5 collective-permute-start.8
  63.8 0.4 collective-permute-done.10
  64.2 1.2 %collective-permute-done.9 = f32[1,32]{1,0:T(1,128)S(1)} collective-permute-done((f32[1,32]{1,0:T(1,128)S(1)}, f32[1,32]{1,0:T(1,128)S(1)}, u32[]{:S(2)}, u32[]{:S(2)}) %collective-permute-start.9) | collective-permute-done | bytes 160 | tf_op jit(solution)/shard_map/ppermute | solution.py:432
  65.4 0.0 collective-permute-done.8
  65.4 0.5 subtract_bitcast_fusion
  (1 shorter events, 0.0 us)
Async XLA Ops:
  0.6 12.6 %copy-start.6 = (s32[128]{0:T(128)S(1)}, s32[128]{0:T(128)}, u32[]{:S(2)}) copy-start(s32[128]{0:T(128)} %param.29) | copy-start | bytes 1540
  0.6 12.6 %copy-start.7 = (s32[128]{0:T(128)S(1)}, s32[128]{0:T(128)}, u32[]{:S(2)}) copy-start(s32[128]{0:T(128)} %param.28) | copy-start | bytes 1540
  0.7 30.5 %copy-start = (bf16[512,2048]{1,0:T(8,128)(2,1)S(1)}, bf16[512,2048]{1,0:T(8,128)(2,1)}, u32[]{:S(2)}) copy-start(bf16[512,2048]{1,0:T(8,128)(2,1)} %w_in_ref.3) | copy-start | bytes 6291460
  3.1 43.3 %all-to-all-start = ((bf16[32,16,512]{2,1,0:T(8,128)(2,1)}), bf16[32,16,512]{2,1,0:T(8,128)(2,1)S(1)}, u32[]{:S(2)}, u32[]{:S(2)}) async-start(bf16[32,16,512]{2,1,0:T(8,128)(2,1)} %bitcast.1), calls=%async_computation | async-start | bytes 1048576 | tf_op jit(solution)/shard_map/all_to_all | solution.py:465
  10.5 20.7 %collective-permute-start.3 = (bf16[128,512]{1,0:T(8,128)(2,1)}, bf16[128,512]{1,0:T(8,128)(2,1)S(1)}, u32[]{:S(2)}, u32[]{:S(2)}) collective-permute-start(bf16[128,512]{1,0:T(8,128)(2,1)} %own_ref.1), channel_id=1, source_target_pairs={{0,4},{1,5},{2,6},{3,7},{4,0},{5,1},{6,2},{7,3},{8,12},{9,13},{10,... | collective-permute-start | bytes 393224 | tf_op jit(solution)/shard_map/ppermute | solution.py:428
  13.2 17.9 %collective-permute-start.4 = (s32[2,128]{1,0:T(2,128)S(1)}, s32[2,128]{1,0:T(2,128)S(1)}, u32[]{:S(2)}, u32[]{:S(2)}) collective-permute-start(s32[2,128]{1,0:T(2,128)S(1)} %pad_add_fusion.numbers_ref), channel_id=1, source_target_pairs={{0,4},{1,5},{2,6},{3,7},{4,0},{5,1},{6,2},{7,3},{8,12},{9,13},{10,... | collective-permute-start | bytes 3080 | tf_op jit(solution)/shard_map/ppermute | solution.py:428
  31.1 0.9 %copy-start.4 = (bf16[128,512]{1,0:T(8,128)(2,1)S(1)}, bf16[128,512]{1,0:T(8,128)(2,1)}, u32[]{:S(2)}) copy-start(bf16[128,512]{1,0:T(8,128)(2,1)} %own_ref.1) | copy-start | bytes 393220
  32.0 11.9 %copy-start.2 = (f32[32,4,256]{2,1,0:T(4,128)S(1)}, f32[32,4,256]{2,1,0:T(4,128)}, u32[]{:S(2)}) copy-start(f32[32,4,256]{2,1,0:T(4,128)} %init.1) | copy-start | bytes 393220
  32.0 11.9 %copy-start.3 = (s32[32,256]{1,0:T(8,128)S(1)}, s32[32,256]{1,0:T(8,128)}, u32[]{:S(2)}) copy-start(s32[32,256]{1,0:T(8,128)} %index.1) | copy-start | bytes 98308
  32.0 11.9 %copy-start.5 = (s32[32]{0:T(128)S(1)}, s32[32]{0:T(128)}, u32[]{:S(2)}) copy-start(s32[32]{0:T(128)} %param.22) | copy-start | bytes 388
  34.5 7.9 %collective-permute-start.5 = (bf16[528,256]{1,0:T(8,128)(2,1)S(1)}, bf16[528,256]{1,0:T(8,128)(2,1)S(1)}, u32[]{:S(2)}, u32[]{:S(2)}) collective-permute-start(bf16[528,256]{1,0:T(8,128)(2,1)S(1)} %neg_tower.1.refs_4_), channel_id=1, source_target_pairs={{0,2},{1,3},{2,0},{3,1},{4,6},{5,7},{6,4},{7,5},{8,10},{9,11},{10,... | collective-permute-start | bytes 811016 | tf_op jit(solution)/shard_map/ppermute | solution.py:428
  34.6 23.3 %collective-permute-start.6 = (bf16[528,256]{1,0:T(8,128)(2,1)S(1)}, bf16[528,256]{1,0:T(8,128)(2,1)}, u32[]{:S(2)}, u32[]{:S(2)}) collective-permute-start(bf16[528,256]{1,0:T(8,128)(2,1)S(1)} %neg_tower.1.refs_4_), channel_id=1, source_target_pairs={{0,1},{1,0},{2,3},{3,2},{4,5},{5,4},{6,7},{7,6},{8,9},{9,8},{10,11... | collective-permute-start | bytes 811016 | tf_op jit(solution)/shard_map/ppermute | solution.py:428
  42.5 15.5 %collective-permute-start.7 = (bf16[528,256]{1,0:T(8,128)(2,1)S(1)}, bf16[528,256]{1,0:T(8,128)(2,1)}, u32[]{:S(2)}, u32[]{:S(2)}) collective-permute-start(bf16[528,256]{1,0:T(8,128)(2,1)S(1)} %collective-permute-done.5.refs_5_), channel_id=1, source_target_pairs={{0,1},{1,0},{2,3},{3,2},{4,5},{5,4},{6,7},{7,6},{8,9},{9,8},{10,11... | collective-permute-start | bytes 811016 | tf_op jit(solution)/shard_map/ppermute | solution.py:428
  45.1 1.3 %copy-start.1 = (bf16[4,256,1024]{2,1,0:T(8,128)(2,1)}, bf16[4,256,1024]{2,1,0:T(8,128)(2,1)S(1)}, u32[]{:S(2)}) copy-start(bf16[4,256,1024]{2,1,0:T(8,128)(2,1)S(1)} %get-tuple-element.12.onehot) | copy-start | bytes 6291460
  54.9 3.5 %collective-permute-start = (bf16[32,640]{1,0:T(8,128)(2,1)S(1)}, bf16[32,640]{1,0:T(8,128)(2,1)S(1)}, u32[]{:S(2)}, u32[]{:S(2)}) collective-permute-start(bf16[32,640]{1,0:T(8,128)(2,1)S(1)} %get-tuple-element.15.refs_0_), channel_id=1, source_target_pairs={{0,8},{8,16},{16,24},{24,0},{1,9},{9,17},{17,25},{25,1},{2,10},{10... | collective-permute-start | bytes 122888 | tf_op jit(solution)/shard_map/ppermute | solution.py:432
  55.0 4.1 %collective-permute-start.1 = (bf16[32,640]{1,0:T(8,128)(2,1)S(1)}, bf16[32,640]{1,0:T(8,128)(2,1)S(1)}, u32[]{:S(2)}, u32[]{:S(2)}) collective-permute-start(bf16[32,640]{1,0:T(8,128)(2,1)S(1)} %get-tuple-element.15.refs_0_), channel_id=1, source_target_pairs={{0,16},{8,24},{16,0},{24,8},{1,17},{9,25},{17,1},{25,9},{2,18},{10... | collective-permute-start | bytes 122888 | tf_op jit(solution)/shard_map/ppermute | solution.py:432
  56.6 3.1 %collective-permute-start.2 = (bf16[32,640]{1,0:T(8,128)(2,1)S(1)}, bf16[32,640]{1,0:T(8,128)(2,1)S(1)}, u32[]{:S(2)}, u32[]{:S(2)}) collective-permute-start(bf16[32,640]{1,0:T(8,128)(2,1)S(1)} %get-tuple-element.15.refs_0_), channel_id=1, source_target_pairs={{0,24},{8,0},{16,8},{24,16},{1,25},{9,1},{17,9},{25,17},{2,26},{10... | collective-permute-start | bytes 122888 | tf_op jit(solution)/shard_map/ppermute | solution.py:432
  61.2 3.0 %collective-permute-start.10 = (f32[1,32]{1,0:T(1,128)S(1)}, f32[1,32]{1,0:T(1,128)S(1)}, u32[]{:S(2)}, u32[]{:S(2)}) collective-permute-start(f32[1,32]{1,0:T(1,128)S(1)} %get-tuple-element.19), channel_id=1, source_target_pairs={{0,8},{8,16},{16,24},{24,0},{1,9},{9,17},{17,25},{25,1},{2,10},{10... | collective-permute-start | bytes 392 | tf_op jit(solution)/shard_map/ppermute | solution.py:432
  61.8 3.6 %collective-permute-start.9 = (f32[1,32]{1,0:T(1,128)S(1)}, f32[1,32]{1,0:T(1,128)S(1)}, u32[]{:S(2)}, u32[]{:S(2)}) collective-permute-start(f32[1,32]{1,0:T(1,128)S(1)} %get-tuple-element.18), channel_id=1, source_target_pairs={{0,16},{8,24},{16,0},{24,8},{1,17},{9,25},{17,1},{25,9},{2,18},{10... | collective-permute-start | bytes 392 | tf_op jit(solution)/shard_map/ppermute | solution.py:432
  63.3 2.1 %collective-permute-start.8 = (f32[1,32]{1,0:T(1,128)S(1)}, f32[1,32]{1,0:T(1,128)S(1)}, u32[]{:S(2)}, u32[]{:S(2)}) collective-permute-start(f32[1,32]{1,0:T(1,128)S(1)} %get-tuple-element.17), channel_id=1, source_target_pairs={{0,24},{8,0},{16,8},{24,16},{1,25},{9,1},{17,9},{25,17},{2,26},{10... | collective-permute-start | bytes 392 | tf_op jit(solution)/shard_map/ppermute | solution.py:432

commit v6 on v5

--- a/solution.py
+++ b/solution.py
@@ -96,7 +96,28 @@
             copy.wait()
 
 
-def select_kernel(fetch, rows, out_ref, fetch_ref, rows_ref, sems):
+def select_kernel(
+    fetch,
+    rows,
+    negs,
+    ids,
+    counts,
+    out_ref,
+    packed,
+    fetch_ref,
+    rows_ref,
+    extra_ref,
+    ids_ref,
+    counts_ref,
+    sems,
+):
+    small = [
+        Copies(ids, ids_ref, sems, 4, 1),
+        Copies(counts, counts_ref, sems, 5, 1),
+    ]
+    kept = negs.shape[0]
+    body = pltpu.make_async_copy(negs, packed.at[pl.ds(0, kept)], sems.at[2])
+    body.start()
     table = pltpu.make_async_copy(fetch, fetch_ref, sems.at[0])
     table.start()
     copy = pltpu.make_async_copy(rows, rows_ref, sems.at[1])
@@ -106,6 +127,17 @@
     row = iota((count, blocks), 0)
     block = iota((count, blocks), 1)
     pick = jnp.where((row >= block * cap) & (row < block * cap + cap), 1.0, 0.0).astype(bf16)
+    for one in small:
+        one.wait()
+    numbers = id_digits(ids_ref[...]) + (counts_ref[...].astype(f32),)
+    at = iota((EXTRA, kept), 0)
+    extra = jnp.zeros((EXTRA, kept), f32)
+    for place, one in enumerate(numbers):
+        extra = jnp.where(at == place, one, extra)
+    extra_ref[...] = jnp.zeros(extra_ref.shape, bf16)
+    extra_ref[:, :kept] = extra.astype(bf16)
+    tail = pltpu.make_async_copy(extra_ref, packed.at[pl.ds(kept, EXTRA)], sems.at[3])
+    tail.start()
     table.wait()
     picked = fetch_ref[0]
     high = mm_nt(pick, (picked >> 7).astype(f32).astype(bf16))
@@ -116,22 +148,32 @@
     chosen = jnp.where(item == column, 1.0, 0.0).astype(bf16)
     copy.wait()
     out_ref[...] = mm(chosen, rows_ref[...]).astype(bf16)
-
-
-def select_rows(fetch, rows):
+    body.wait()
+    tail.wait()
+
+
+def select_rows(fetch, rows, negs, ids, counts):
     blocks, _, cap = fetch.shape
+    packed = (negs.shape[0] + EXTRA, negs.shape[1])
     return pl.pallas_call(
         select_kernel,
-        in_specs=[OUTSIDE, OUTSIDE],
-        out_shape=pltpu.VMEM((blocks * cap, rows.shape[1]), bf16),
+        in_specs=[OUTSIDE] * 5,
+        out_specs=[INSIDE, OUTSIDE],
+        out_shape=[
+            pltpu.VMEM((blocks * cap, rows.shape[1]), bf16),
+            jax.ShapeDtypeStruct(packed, bf16),
+        ],
         scratch_shapes=[
             pltpu.VMEM((1, cap, blocks), i32),
             pltpu.VMEM(rows.shape, bf16),
-            pltpu.SemaphoreType.DMA((2,)),
+            pltpu.VMEM((EXTRA, negs.shape[1]), bf16),
+            pltpu.VMEM(ids.shape, i32),
+            pltpu.VMEM(counts.shape, i32),
+            pltpu.SemaphoreType.DMA((6,)),
         ],
         compiler_params=PARAMS,
         name="select_rows",
-    )(far(fetch.transpose(1, 2, 0)), far(rows))
+    )(*[far(one) for one in (fetch.transpose(1, 2, 0), rows, negs, ids, counts)])
 
 
 def tower(rows_ref, w_in_ref, bias, w_out, bias_ref, out_ref, sems):
@@ -147,39 +189,24 @@
 
 
 def neg_kernel(
-    own_ref,
-    apart_ref,
-    w_in_ref,
-    bias,
-    w_out,
-    numbers_ref,
-    numbers_apart_ref,
-    out_ref,
-    rows_ref,
-    bias_ref,
-    w_out_ref,
-    sems,
+    own_ref, apart_ref, w_in_ref, bias, w_out, out_ref, rows_ref, bias_ref, w_out_ref, sems
 ):
-    count = own_ref.shape[0]
-    rows_ref[:count, :] = own_ref[...]
-    rows_ref[count:, :] = apart_ref[...]
+    count = rows_ref.shape[0] // 2
+    rows_ref[:count, :] = own_ref[:count, :]
+    rows_ref[count:, :] = apart_ref[:count, :]
     unit = tower(rows_ref, w_in_ref, bias, w_out, bias_ref, w_out_ref, sems)
     width = unit.shape[1]
     out_ref[:width, :] = unit.T.astype(bf16)
-    for start, ref in ((0, numbers_ref), (count, numbers_apart_ref)):
-        rows = id_digits(ref[0:1, :]) + (ref[1:2, :].astype(f32),)
-        at = iota((EXTRA, count), 0)
-        extra = jnp.zeros((EXTRA, count), f32)
-        for place, row in enumerate(rows):
-            extra = jnp.where(at == place, row, extra)
-        out_ref[width:, start : start + count] = extra.astype(bf16)
-
-
-def neg_tower(own, apart, weights, numbers, numbers_apart):
-    count, width = own.shape
+    out_ref[width:, :count] = own_ref[count:, :count]
+    out_ref[width:, count:] = apart_ref[count:, :count]
+
+
+def neg_tower(own, apart, weights):
+    count = own.shape[0] - EXTRA
+    width = own.shape[1]
     return pl.pallas_call(
         neg_kernel,
-        in_specs=[INSIDE, INSIDE, INSIDE, OUTSIDE, OUTSIDE, INSIDE, INSIDE],
+        in_specs=[INSIDE, INSIDE, INSIDE, OUTSIDE, OUTSIDE],
         out_shape=pltpu.VMEM((width + EXTRA, 2 * count), bf16),
         scratch_shapes=[
             pltpu.VMEM((2 * count, width), bf16),
@@ -189,7 +216,7 @@
         ],
         compiler_params=PARAMS,
         name="neg_tower",
-    )(near(own), near(apart), *weights, near(numbers), near(numbers_apart))
+    )(near(own), near(apart), *weights)
 
 
 def event_weights(logits, live):
@@ -460,8 +487,10 @@
     neg_counts,
 ):
     weights = (near(w_in), far(bias_in.reshape(1, -1)), far(w_out))
-    apart = swap_pool(neg_feats, pool_size, pool_size // 2)
-    outgoing = select_rows(fetch_table, item_feats)
+    outgoing, packed = select_rows(
+        fetch_table, item_feats, neg_feats, neg_ids.reshape(1, -1), neg_counts.reshape(1, -1)
+    )
+    apart = swap_pool(packed, pool_size, pool_size // 2)
     arrived = lax.all_to_all(
         outgoing.reshape(fetch_table.shape[0], fetch_table.shape[2], -1),
         ("user", "pool"),
@@ -471,9 +500,7 @@
     )
     arrived = arrived.reshape(outgoing.shape)
 
-    numbers = jnp.stack([neg_ids, neg_counts])
-    numbers_apart = swap_pool(numbers, pool_size, pool_size // 2)
-    own_neg = neg_tower(neg_feats, apart, weights, numbers, numbers_apart)
+    own_neg = neg_tower(packed, apart, weights)
     length = hist_len.reshape(1, -1)
     onehot, first = prepare(hist_index, length, route_init, outgoing.shape[0])
     bits = [1 << at for at in range(pool_size.bit_length() - 2)]

time: 66.4 us -> 67.9 us (1.023)
  waiting for transfers between devices: 27.2 us -> 28.2 us
  local copies, waits for them, and re-layouts: 2.24 us -> 2.93 us
    ppermute x5 -> x4, waiting for transfers between devices: 23.9 us -> 24.9 us  [swap_pool(): return lax.ppermute(array, 'pool', [(at, at ^ bit) for at in range(size)])]
    unnamed x16 -> x12, local copies, waits for them, and re-layouts: 2.24 us -> 2.93 us
    ppermute x5 -> x4, starting transfers between devices: 6.12 us -> 5.81 us  [swap_pool(): return lax.ppermute(array, 'pool', [(at, at ^ bit) for at in range(size)])]
  transfers between devices with their start and end apart: 12 -> 11, of which waited for: 7 -> 7; matrix products, arithmetic and copies ran while one was open for 0% -> 0% of each run, Pallas kernels for 18% -> 18%
where the time goes in v6:
time: 67.9 us; the launch traced here: 67.4 us
  waiting for transfers between devices  28.2 us (42%)
  starting transfers between devices  18.8 us (28%)
  Pallas kernels  16.2 us (24%)
  local copies, waits for them, and re-layouts  2.93 us (4%)
  between operations  0.71 us (1%)
    ppermute x4, waiting for transfers between devices, swap_pool(): return lax.ppermute(array, 'pool', [(at, at ^ bit) for at in range(size)])  24.9 us
    pallas_call x1, Pallas kernels, route(): pl.pallas_call(route_kernel, in_specs=[INSIDE] * 3 + [OUTSIDE] * len(othe...  8.5 us
    all_to_all x1, starting transfers between devices, on_device(): lax.all_to_all(outgoing.reshape(fetch_table.shape[0], fetch_table.shape[2...  7.33 us
    ppermute x4, starting transfers between devices, swap_pool(): return lax.ppermute(array, 'pool', [(at, at ^ bit) for at in range(size)])  5.81 us
    ppermute x6, starting transfers between devices, rotate_user(): lax.ppermute(array, 'user', [(at, (at + step) % size) for at in range(siz...  5.66 us
    ppermute x6, waiting for transfers between devices, rotate_user(): lax.ppermute(array, 'user', [(at, (at + step) % size) for at in range(siz...  3.25 us
    unnamed x12, local copies, waits for them, and re-layouts  2.93 us
    pallas_call x1, Pallas kernels, neg_tower(): pl.pallas_call(neg_kernel, in_specs=[INSIDE, INSIDE, INSIDE, OUTSIDE, OUT...  2.6 us
  transfers between devices with their start and end apart: 11, of which 7 were waited for; matrix products, arithmetic and copies ran while one was open for 0% of the time, Pallas kernels for 18%

profile of v6, /device:TPU:0, one launch (start us, length us, event | category | flops | bytes accessed | tf_op | source)
XLA Modules:
  0.0 67.4 jit_solution(2385551623913906913)
XLA Ops:
  0.6 2.4 %select_rows.1 = (bf16[512,512]{1,0:T(8,128)(2,1)}, bf16[144,512]{1,0:T(8,128)(2,1)S(1)}) custom-call(s32[1,16,32]{2,1,0:T(8,128)} %bitcast.17, bf16[512,512]{1,0:T(8,128)(2,1)} %rows.1, bf16[128,512]{1,0:T(8,128)(2,1)} %negs.1, s32[1,128]{1,0:T(1,128)} %bitcast.21, s32[1,128]{1,0:T(1,128)} %bitcast.22), custom_call_target="tpu_custom_call" | custom-call | tf_op jit(solution)/shard_map/select_rows/pallas_call | solution.py:158
  3.1 7.3 %all-to-all-start = ((bf16[32,16,512]{2,1,0:T(8,128)(2,1)}), bf16[32,16,512]{2,1,0:T(8,128)(2,1)S(1)}, u32[]{:S(2)}, u32[]{:S(2)}) async-start(bf16[32,16,512]{2,1,0:T(8,128)(2,1)} %bitcast.3), calls=%async_computation | async-start | bytes 1048576 | tf_op jit(solution)/shard_map/all_to_all | solution.py:494
  10.4 2.7 %collective-permute-start.3 = (bf16[144,512]{1,0:T(8,128)(2,1)S(1)}, bf16[144,512]{1,0:T(8,128)(2,1)S(1)}, u32[]{:S(2)}, u32[]{:S(2)}) collective-permute-start(bf16[144,512]{1,0:T(8,128)(2,1)S(1)} %get-tuple-element.19.own_ref), channel_id=1, source_target_pairs={{0,4},{1,5},{2,6},{3,7},{4,0},{5,1},{6,2},{7,3},{8,12},{9,13},{10,... | collective-permute-start | bytes 442376 | tf_op jit(solution)/shard_map/ppermute | solution.py:455
  13.2 18.5 %collective-permute-done.3.apart_ref = bf16[144,512]{1,0:T(8,128)(2,1)S(1)} collective-permute-done((bf16[144,512]{1,0:T(8,128)(2,1)S(1)}, bf16[144,512]{1,0:T(8,128)(2,1)S(1)}, u32[]{:S(2)}, u32[]{:S(2)}) %collective-permute-start.3) | collective-permute-done | bytes 147488 | tf_op jit(solution)/shard_map/ppermute | solution.py:455
  31.7 0.0 copy-start
  31.7 1.6 %copy-done = bf16[512,2048]{1,0:T(8,128)(2,1)S(1)} copy-done((bf16[512,2048]{1,0:T(8,128)(2,1)S(1)}, bf16[512,2048]{1,0:T(8,128)(2,1)}, u32[]{:S(2)}) %copy-start) | copy-done | bytes 2097176
  33.3 0.0 copy-start.3
  33.3 0.0 copy-start.4
  33.3 0.0 copy-start.5
  33.3 0.0 copy-start.1
  33.3 2.6 %neg_tower.1.refs_4_ = bf16[528,256]{1,0:T(8,128)(2,1)S(1)} custom-call(bf16[144,512]{1,0:T(8,128)(2,1)S(1)} %get-tuple-element.19.own_ref, bf16[144,512]{1,0:T(8,128)(2,1)S(1)} %collective-permute-done.3.apart_ref, bf16[512,2048]{1,0:T(8,128)(2,1)S(1)} %copy-done, f32[1,2048]{1,0:T(1,128)} %bitcast.15, bf16[2048,512]{1,0:T(8,128)(2,1)} %w_out.3), custom_call_target="tpu_custom_call" | custom-call | tf_op jit(solution)/shard_map/neg_tower/pallas_call | solution.py:207
  35.9 0.1 collective-permute-start.4
  36.0 1.5 %collective-permute-start.5 = (bf16[528,256]{1,0:T(8,128)(2,1)S(1)}, bf16[528,256]{1,0:T(8,128)(2,1)}, u32[]{:S(2)}, u32[]{:S(2)}) collective-permute-start(bf16[528,256]{1,0:T(8,128)(2,1)S(1)} %neg_tower.1.refs_4_), channel_id=1, source_target_pairs={{0,1},{1,0},{2,3},{3,2},{4,5},{5,4},{6,7},{7,6},{8,9},{9,8},{10,11... | collective-permute-start | bytes 811016 | tf_op jit(solution)/shard_map/ppermute | solution.py:455
  37.5 6.4 %collective-permute-done.4.refs_5_ = bf16[528,256]{1,0:T(8,128)(2,1)S(1)} collective-permute-done((bf16[528,256]{1,0:T(8,128)(2,1)S(1)}, bf16[528,256]{1,0:T(8,128)(2,1)S(1)}, u32[]{:S(2)}, u32[]{:S(2)}) %collective-permute-start.4) | collective-permute-done | bytes 270368 | tf_op jit(solution)/shard_map/ppermute | solution.py:455
  43.9 1.5 %collective-permute-start.6 = (bf16[528,256]{1,0:T(8,128)(2,1)S(1)}, bf16[528,256]{1,0:T(8,128)(2,1)}, u32[]{:S(2)}, u32[]{:S(2)}) collective-permute-start(bf16[528,256]{1,0:T(8,128)(2,1)S(1)} %collective-permute-done.4.refs_5_), channel_id=1, source_target_pairs={{0,1},{1,0},{2,3},{3,2},{4,5},{5,4},{6,7},{7,6},{8,9},{9,8},{10,11... | collective-permute-start | bytes 811016 | tf_op jit(solution)/shard_map/ppermute | solution.py:455
  45.4 0.0 copy-done.3
  45.4 0.0 copy-done.4
  45.4 0.0 copy-done.5
  45.4 1.1 %prepare.1 = (bf16[4,256,1024]{2,1,0:T(8,128)(2,1)S(1)}, f32[128,512]{1,0:T(8,128)S(1)}) custom-call(s32[32,256]{1,0:T(8,128)S(1)} %copy-done.4, s32[1,32]{1,0:T(1,128)S(1)} %bitcast.14, f32[32,4,256]{2,1,0:T(4,128)S(1)} %copy-done.3), custom_call_target="tpu_custom_call" | custom-call | tf_op jit(solution)/shard_map/prepare/pallas_call | solution.py:286
  46.5 0.0 copy-start.2
  46.5 1.3 %copy-done.2 = bf16[4,256,1024]{2,1,0:T(8,128)(2,1)} copy-done((bf16[4,256,1024]{2,1,0:T(8,128)(2,1)}, bf16[4,256,1024]{2,1,0:T(8,128)(2,1)S(1)}, u32[]{:S(2)}) %copy-start.2) | copy-done | bytes 2097176
  47.8 0.0 all-to-all-done
  47.9 0.0 copy-done.1
  47.9 8.5 %route.1 = (f32[32,2048]{1,0:T(8,128)}, bf16[32,640]{1,0:T(8,128)(2,1)S(1)}, f32[1,32]{1,0:T(1,128)S(1)}) custom-call(bf16[512,512]{1,0:T(8,128)(2,1)S(1)} %bitcast.12, bf16[512,2048]{1,0:T(8,128)(2,1)S(1)} %copy-done.1, f32[128,512]{1,0:T(8,128)S(1)} %get-tuple-element.14.first_ref, f32[1,2048]{1,0:T(1,128)} %bitcast.16, bf16[2048,512]{1,0:T(8,128)(2,1)} %w_out.3, ...), custom_call_target="tpu_custom_call" | custom-call | tf_op jit(solution)/shard_map/route/pallas_call | solution.py:404
  56.4 0.1 collective-permute-start
  56.4 1.6 %collective-permute-start.1 = (bf16[32,640]{1,0:T(8,128)(2,1)S(1)}, bf16[32,640]{1,0:T(8,128)(2,1)S(1)}, u32[]{:S(2)}, u32[]{:S(2)}) collective-permute-start(bf16[32,640]{1,0:T(8,128)(2,1)S(1)} %get-tuple-element.18.refs_0_), channel_id=1, source_target_pairs={{0,16},{8,24},{16,0},{24,8},{1,17},{9,25},{17,1},{25,9},{2,18},{10... | collective-permute-start | bytes 122888 | tf_op jit(solution)/shard_map/ppermute | solution.py:459
  58.0 1.4 %collective-permute-start.2 = (bf16[32,640]{1,0:T(8,128)(2,1)S(1)}, bf16[32,640]{1,0:T(8,128)(2,1)S(1)}, u32[]{:S(2)}, u32[]{:S(2)}) collective-permute-start(bf16[32,640]{1,0:T(8,128)(2,1)S(1)} %get-tuple-element.18.refs_0_), channel_id=1, source_target_pairs={{0,24},{8,0},{16,8},{24,16},{1,25},{9,1},{17,9},{25,17},{2,26},{10... | collective-permute-start | bytes 122888 | tf_op jit(solution)/shard_map/ppermute | solution.py:459
  59.4 0.0 collective-permute-done.5.refs_6_
  59.4 0.0 collective-permute-done.6.refs_7_
  59.4 0.4 collective-permute-done.refs_1_
  59.8 0.7 collective-permute-done.1.refs_2_
  60.5 0.6 collective-permute-done.2.refs_3_
  61.1 1.5 %negative_sums.1 = (f32[1,32]{1,0:T(1,128)S(1)}, f32[1,32]{1,0:T(1,128)S(1)}, f32[1,32]{1,0:T(1,128)S(1)}, f32[1,32]{1,0:T(1,128)S(1)}) custom-call(bf16[32,640]{1,0:T(8,128)(2,1)S(1)} %get-tuple-element.18.refs_0_, bf16[32,640]{1,0:T(8,128)(2,1)S(1)} %collective-permute-done.refs_1_, bf16[32,640]{1,0:T(8,128)(2,1)S(1)} %collective-permute-done.1.refs_2_, ...), custom_call_target="tpu_custom_call" | custom-call | tf_op jit(solution)/shard_map/negative_sums/pallas_call | solution.py:446
  62.6 0.6 collective-permute-start.9
  63.3 1.5 %collective-permute-start.8 = (f32[1,32]{1,0:T(1,128)S(1)}, f32[1,32]{1,0:T(1,128)S(1)}, u32[]{:S(2)}, u32[]{:S(2)}) collective-permute-start(f32[1,32]{1,0:T(1,128)S(1)} %get-tuple-element.22), channel_id=1, source_target_pairs={{0,16},{8,24},{16,0},{24,8},{1,17},{9,25},{17,1},{25,9},{2,18},{10... | collective-permute-start | bytes 392 | tf_op jit(solution)/shard_map/ppermute | solution.py:459
  64.8 0.5 collective-permute-start.7
  65.2 0.4 collective-permute-done.9
  65.6 1.2 %collective-permute-done.8 = f32[1,32]{1,0:T(1,128)S(1)} collective-permute-done((f32[1,32]{1,0:T(1,128)S(1)}, f32[1,32]{1,0:T(1,128)S(1)}, u32[]{:S(2)}, u32[]{:S(2)}) %collective-permute-start.8) | collective-permute-done | bytes 160 | tf_op jit(solution)/shard_map/ppermute | solution.py:459
  66.8 0.0 collective-permute-done.7
  66.8 0.5 subtract_bitcast_fusion
Async XLA Ops:
  3.1 44.8 %all-to-all-start = ((bf16[32,16,512]{2,1,0:T(8,128)(2,1)}), bf16[32,16,512]{2,1,0:T(8,128)(2,1)S(1)}, u32[]{:S(2)}, u32[]{:S(2)}) async-start(bf16[32,16,512]{2,1,0:T(8,128)(2,1)} %bitcast.3), calls=%async_computation | async-start | bytes 1048576 | tf_op jit(solution)/shard_map/all_to_all | solution.py:494
  10.4 21.3 %collective-permute-start.3 = (bf16[144,512]{1,0:T(8,128)(2,1)S(1)}, bf16[144,512]{1,0:T(8,128)(2,1)S(1)}, u32[]{:S(2)}, u32[]{:S(2)}) collective-permute-start(bf16[144,512]{1,0:T(8,128)(2,1)S(1)} %get-tuple-element.19.own_ref), channel_id=1, source_target_pairs={{0,4},{1,5},{2,6},{3,7},{4,0},{5,1},{6,2},{7,3},{8,12},{9,13},{10,... | collective-permute-start | bytes 442376 | tf_op jit(solution)/shard_map/ppermute | solution.py:455
  31.7 1.6 %copy-start = (bf16[512,2048]{1,0:T(8,128)(2,1)S(1)}, bf16[512,2048]{1,0:T(8,128)(2,1)}, u32[]{:S(2)}) copy-start(bf16[512,2048]{1,0:T(8,128)(2,1)} %w_in_ref.3) | copy-start | bytes 6291460
  33.3 12.1 %copy-start.3 = (f32[32,4,256]{2,1,0:T(4,128)S(1)}, f32[32,4,256]{2,1,0:T(4,128)}, u32[]{:S(2)}) copy-start(f32[32,4,256]{2,1,0:T(4,128)} %init.1) | copy-start | bytes 393220
  33.3 12.1 %copy-start.4 = (s32[32,256]{1,0:T(8,128)S(1)}, s32[32,256]{1,0:T(8,128)}, u32[]{:S(2)}) copy-start(s32[32,256]{1,0:T(8,128)} %index.1) | copy-start | bytes 98308
  33.3 12.1 %copy-start.5 = (s32[32]{0:T(128)S(1)}, s32[32]{0:T(128)}, u32[]{:S(2)}) copy-start(s32[32]{0:T(128)} %param.22) | copy-start | bytes 388
  33.3 14.5 %copy-start.1 = (bf16[512,2048]{1,0:T(8,128)(2,1)S(1)}, bf16[512,2048]{1,0:T(8,128)(2,1)}, u32[]{:S(2)}) copy-start(bf16[512,2048]{1,0:T(8,128)(2,1)} %w_in_ref.3) | copy-start | bytes 6291460
  35.9 8.0 %collective-permute-start.4 = (bf16[528,256]{1,0:T(8,128)(2,1)S(1)}, bf16[528,256]{1,0:T(8,128)(2,1)S(1)}, u32[]{:S(2)}, u32[]{:S(2)}) collective-permute-start(bf16[528,256]{1,0:T(8,128)(2,1)S(1)} %neg_tower.1.refs_4_), channel_id=1, source_target_pairs={{0,2},{1,3},{2,0},{3,1},{4,6},{5,7},{6,4},{7,5},{8,10},{9,11},{10,... | collective-permute-start | bytes 811016 | tf_op jit(solution)/shard_map/ppermute | solution.py:455
  36.0 23.4 %collective-permute-start.5 = (bf16[528,256]{1,0:T(8,128)(2,1)S(1)}, bf16[528,256]{1,0:T(8,128)(2,1)}, u32[]{:S(2)}, u32[]{:S(2)}) collective-permute-start(bf16[528,256]{1,0:T(8,128)(2,1)S(1)} %neg_tower.1.refs_4_), channel_id=1, source_target_pairs={{0,1},{1,0},{2,3},{3,2},{4,5},{5,4},{6,7},{7,6},{8,9},{9,8},{10,11... | collective-permute-start | bytes 811016 | tf_op jit(solution)/shard_map/ppermute | solution.py:455
  43.9 15.5 %collective-permute-start.6 = (bf16[528,256]{1,0:T(8,128)(2,1)S(1)}, bf16[528,256]{1,0:T(8,128)(2,1)}, u32[]{:S(2)}, u32[]{:S(2)}) collective-permute-start(bf16[528,256]{1,0:T(8,128)(2,1)S(1)} %collective-permute-done.4.refs_5_), channel_id=1, source_target_pairs={{0,1},{1,0},{2,3},{3,2},{4,5},{5,4},{6,7},{7,6},{8,9},{9,8},{10,11... | collective-permute-start | bytes 811016 | tf_op jit(solution)/shard_map/ppermute | solution.py:455
  46.5 1.3 %copy-start.2 = (bf16[4,256,1024]{2,1,0:T(8,128)(2,1)}, bf16[4,256,1024]{2,1,0:T(8,128)(2,1)S(1)}, u32[]{:S(2)}) copy-start(bf16[4,256,1024]{2,1,0:T(8,128)(2,1)S(1)} %get-tuple-element.15.onehot) | copy-start | bytes 6291460
  56.4 3.5 %collective-permute-start = (bf16[32,640]{1,0:T(8,128)(2,1)S(1)}, bf16[32,640]{1,0:T(8,128)(2,1)S(1)}, u32[]{:S(2)}, u32[]{:S(2)}) collective-permute-start(bf16[32,640]{1,0:T(8,128)(2,1)S(1)} %get-tuple-element.18.refs_0_), channel_id=1, source_target_pairs={{0,8},{8,16},{16,24},{24,0},{1,9},{9,17},{17,25},{25,1},{2,10},{10... | collective-permute-start | bytes 122888 | tf_op jit(solution)/shard_map/ppermute | solution.py:459
  56.4 4.1 %collective-permute-start.1 = (bf16[32,640]{1,0:T(8,128)(2,1)S(1)}, bf16[32,640]{1,0:T(8,128)(2,1)S(1)}, u32[]{:S(2)}, u32[]{:S(2)}) collective-permute-start(bf16[32,640]{1,0:T(8,128)(2,1)S(1)} %get-tuple-element.18.refs_0_), channel_id=1, source_target_pairs={{0,16},{8,24},{16,0},{24,8},{1,17},{9,25},{17,1},{25,9},{2,18},{10... | collective-permute-start | bytes 122888 | tf_op jit(solution)/shard_map/ppermute | solution.py:459
  58.0 3.1 %collective-permute-start.2 = (bf16[32,640]{1,0:T(8,128)(2,1)S(1)}, bf16[32,640]{1,0:T(8,128)(2,1)S(1)}, u32[]{:S(2)}, u32[]{:S(2)}) collective-permute-start(bf16[32,640]{1,0:T(8,128)(2,1)S(1)} %get-tuple-element.18.refs_0_), channel_id=1, source_target_pairs={{0,24},{8,0},{16,8},{24,16},{1,25},{9,1},{17,9},{25,17},{2,26},{10... | collective-permute-start | bytes 122888 | tf_op jit(solution)/shard_map/ppermute | solution.py:459
  62.6 3.0 %collective-permute-start.9 = (f32[1,32]{1,0:T(1,128)S(1)}, f32[1,32]{1,0:T(1,128)S(1)}, u32[]{:S(2)}, u32[]{:S(2)}) collective-permute-start(f32[1,32]{1,0:T(1,128)S(1)} %get-tuple-element.23), channel_id=1, source_target_pairs={{0,8},{8,16},{16,24},{24,0},{1,9},{9,17},{17,25},{25,1},{2,10},{10... | collective-permute-start | bytes 392 | tf_op jit(solution)/shard_map/ppermute | solution.py:459
  63.3 3.6 %collective-permute-start.8 = (f32[1,32]{1,0:T(1,128)S(1)}, f32[1,32]{1,0:T(1,128)S(1)}, u32[]{:S(2)}, u32[]{:S(2)}) collective-permute-start(f32[1,32]{1,0:T(1,128)S(1)} %get-tuple-element.22), channel_id=1, source_target_pairs={{0,16},{8,24},{16,0},{24,8},{1,17},{9,25},{17,1},{25,9},{2,18},{10... | collective-permute-start | bytes 392 | tf_op jit(solution)/shard_map/ppermute | solution.py:459
  64.8 2.1 %collective-permute-start.7 = (f32[1,32]{1,0:T(1,128)S(1)}, f32[1,32]{1,0:T(1,128)S(1)}, u32[]{:S(2)}, u32[]{:S(2)}) collective-permute-start(f32[1,32]{1,0:T(1,128)S(1)} %get-tuple-element.21), channel_id=1, source_target_pairs={{0,24},{8,0},{16,8},{24,16},{1,25},{9,1},{17,9},{25,17},{2,26},{10... | collective-permute-start | bytes 392 | tf_op jit(solution)/shard_map/ppermute | solution.py:459

commit v7 on v6

--- a/solution.py
+++ b/solution.py
@@ -176,12 +176,23 @@
     )(*[far(one) for one in (fetch.transpose(1, 2, 0), rows, negs, ids, counts)])
 
 
-def tower(rows_ref, w_in_ref, bias, w_out, bias_ref, out_ref, sems):
+def tower(rows_ref, w_in_ref, bias, w_out, bias_ref, out_ref, sems, parts=None):
     small = Copies(bias, bias_ref, sems, 0, 1)
     large = Copies(w_out, out_ref, sems, 1, SPLIT)
-    hidden = mm(rows_ref[...], w_in_ref[...])
-    small.wait()
-    hidden = jnp.maximum(hidden + bias_ref[...], 0.0).astype(bf16)
+    if parts is None:
+        hidden = mm(rows_ref[...], w_in_ref[...])
+        small.wait()
+        hidden = jnp.maximum(hidden + bias_ref[...], 0.0).astype(bf16)
+    else:
+        small.wait()
+        pieces = []
+        for at, part in enumerate(parts):
+            part.wait()
+            size = w_in_ref.shape[1] // len(parts)
+            cut = slice(at * size, (at + 1) * size)
+            piece = mm(rows_ref[...], w_in_ref[:, cut]) + bias_ref[:, cut]
+            pieces.append(jnp.maximum(piece, 0.0).astype(bf16))
+        hidden = jnp.concatenate(pieces, axis=1)
     large.wait()
     embedding = mm(hidden, out_ref[...])
     total = jnp.sum(embedding * embedding, axis=1, keepdims=True)
@@ -189,12 +200,23 @@
 
 
 def neg_kernel(
-    own_ref, apart_ref, w_in_ref, bias, w_out, out_ref, rows_ref, bias_ref, w_out_ref, sems
+    own_ref, apart_ref, w_in, bias, w_out, out_ref, rows_ref, w_in_ref, bias_ref, w_out_ref, sems
 ):
+    size = w_in.shape[1] // SPLIT
+    parts = [
+        pltpu.make_async_copy(
+            w_in.at[:, pl.ds(at * size, size)],
+            w_in_ref.at[:, pl.ds(at * size, size)],
+            sems.at[1 + SPLIT + at],
+        )
+        for at in range(SPLIT)
+    ]
+    for part in parts:
+        part.start()
     count = rows_ref.shape[0] // 2
     rows_ref[:count, :] = own_ref[:count, :]
     rows_ref[count:, :] = apart_ref[:count, :]
-    unit = tower(rows_ref, w_in_ref, bias, w_out, bias_ref, w_out_ref, sems)
+    unit = tower(rows_ref, w_in_ref, bias, w_out, bias_ref, w_out_ref, sems, parts)
     width = unit.shape[1]
     out_ref[:width, :] = unit.T.astype(bf16)
     out_ref[width:, :count] = own_ref[count:, :count]
@@ -206,17 +228,14 @@
     width = own.shape[1]
     return pl.pallas_call(
         neg_kernel,
-        in_specs=[INSIDE, INSIDE, INSIDE, OUTSIDE, OUTSIDE],
+        in_specs=[INSIDE, INSIDE, OUTSIDE, OUTSIDE, OUTSIDE],
         out_shape=pltpu.VMEM((width + EXTRA, 2 * count), bf16),
-        scratch_shapes=[
-            pltpu.VMEM((2 * count, width), bf16),
-            pltpu.VMEM(weights[1].shape, f32),
-            pltpu.VMEM(weights[2].shape, bf16),
-            pltpu.SemaphoreType.DMA((1 + SPLIT,)),
-        ],
+        scratch_shapes=[pltpu.VMEM((2 * count, width), bf16)]
+        + [pltpu.VMEM(one.shape, one.dtype) for one in weights]
+        + [pltpu.SemaphoreType.DMA((1 + 2 * SPLIT,))],
         compiler_params=PARAMS,
         name="neg_tower",
-    )(near(own), near(apart), *weights)
+    )(near(own), near(apart), *[far(one) for one in weights])
 
 
 def event_weights(logits, live):
@@ -289,7 +308,7 @@
             jax.ShapeDtypeStruct(
                 (users // GROUP_USERS, 2 * LANES, GROUP_USERS // 2 * events), bf16
             ),
-            pltpu.VMEM((INTERESTS * users, slots), f32),
+            jax.ShapeDtypeStruct((INTERESTS * users, slots), f32),
         ],
         compiler_params=PARAMS,
         name="prepare",
@@ -299,11 +318,11 @@
 def route_kernel(
     rows_ref,
     w_in_ref,
-    first_ref,
     bias,
     w_out,
     bilinear,
     onehot,
+    first,
     index,
     length,
     init,
@@ -317,6 +336,7 @@
     out_ref,
     map_ref,
     onehot_ref,
+    first_ref,
     index_ref,
     length_ref,
     init_ref,
@@ -328,6 +348,7 @@
 ):
     pairs = (
         (bilinear, map_ref),
+        (first, first_ref),
         (index, index_ref),
         (length, length_ref),
         (init, init_ref),
@@ -397,13 +418,13 @@
     positive_ref[...] = logit_scale * to_row(match) - jnp.log(counts_ref[...].astype(f32))
 
 
-def route(rows, w_in, first, *others):
-    _, _, bilinear, onehot, index, _, _, _, _, _ = others
+def route(rows, w_in, *others):
+    _, _, bilinear, onehot, first, index, _, _, _, _, _ = others
     users = index.shape[0]
     width = bilinear.shape[1]
     return pl.pallas_call(
         route_kernel,
-        in_specs=[INSIDE] * 3 + [OUTSIDE] * len(others),
+        in_specs=[INSIDE] * 2 + [OUTSIDE] * len(others),
         out_shape=[
             jax.ShapeDtypeStruct((users, INTERESTS * width), f32),
             pltpu.VMEM((users, width + LANES), bf16),
@@ -416,7 +437,7 @@
         ],
         compiler_params=PARAMS,
         name="route",
-    )(near(rows), near(w_in), near(first), *[far(one) for one in others])
+    )(near(rows), near(w_in), *[far(one) for one in others])
 
 
 def sums_kernel(parts, pieces, *refs):
@@ -459,12 +480,11 @@
     return lax.ppermute(array, "user", [(at, (at + step) % size) for at in range(size)])
 
 
-def gather_negatives(own, bits, size):
-    pieces = {0: own}
-    for mask in range(1, 1 << len(bits)):
-        last = mask.bit_length() - 1
-        pieces[mask] = swap_pool(pieces[mask ^ (1 << last)], size, bits[last])
-    return list(pieces.values())
+def gather_negatives(own, size):
+    pieces = [own]
+    for mask in range(1, size // 2):
+        pieces.append(swap_pool(own, size, mask))
+    return pieces
 
 
 def on_device(
@@ -486,7 +506,7 @@
     neg_ids,
     neg_counts,
 ):
-    weights = (near(w_in), far(bias_in.reshape(1, -1)), far(w_out))
+    weights = (w_in, bias_in.reshape(1, -1), w_out)
     outgoing, packed = select_rows(
         fetch_table, item_feats, neg_feats, neg_ids.reshape(1, -1), neg_counts.reshape(1, -1)
     )
@@ -503,17 +523,16 @@
     own_neg = neg_tower(packed, apart, weights)
     length = hist_len.reshape(1, -1)
     onehot, first = prepare(hist_index, length, route_init, outgoing.shape[0])
-    bits = [1 << at for at in range(pool_size.bit_length() - 2)]
-    negs = gather_negatives(own_neg, bits[1:] + bits[:1], pool_size)
+    negs = gather_negatives(own_neg, pool_size)
 
     interests, vec, positive = route(
         arrived,
         w_in,
-        first,
         bias_in.reshape(1, -1),
         w_out,
         bilinear,
         onehot,
+        first,
         hist_index,
         length,
         route_init,

time: 67.9 us -> 62.2 us (0.916)
  waiting for transfers between devices: 28.2 us -> 21.8 us
  Pallas kernels: 16.2 us -> 17.4 us
  local copies, waits for them, and re-layouts: 2.93 us -> 2.02 us
    ppermute x4, waiting for transfers between devices: 24.9 us -> 18.6 us  [swap_pool(): return lax.ppermute(array, 'pool', [(at, at ^ bit) for at in range(size)])]
    pallas_call x2, Pallas kernels: 11.1 us -> 12.3 us  [the longest x1 8.61 us: route(): pl.pallas_call(route_kernel, in_specs=[INSIDE] * 2 + [OUTSIDE] * len(othe...]
    unnamed x12, local copies, waits for them, and re-layouts: 2.93 us -> 2.02 us
  transfers between devices with their start and end apart: 11 -> 11, of which waited for: 7 -> 6; matrix products, arithmetic and copies ran while one was open for 0% -> 0% of each run, Pallas kernels for 18% -> 22%
where the time goes in v7:
time: 62.2 us; the launch traced here: 61.7 us
  waiting for transfers between devices  21.8 us (35%)
  starting transfers between devices  19.2 us (31%)
  Pallas kernels  17.4 us (28%)
  local copies, waits for them, and re-layouts  2.02 us (3%)
  between operations  0.71 us (1%)
    ppermute x4, waiting for transfers between devices, swap_pool(): return lax.ppermute(array, 'pool', [(at, at ^ bit) for at in range(size)])  18.6 us
    pallas_call x1, Pallas kernels, route(): pl.pallas_call(route_kernel, in_specs=[INSIDE] * 2 + [OUTSIDE] * len(othe...  8.61 us
    all_to_all x1, starting transfers between devices, on_device(): lax.all_to_all(outgoing.reshape(fetch_table.shape[0], fetch_table.shape[2...  7.33 us
    ppermute x4, starting transfers between devices, swap_pool(): return lax.ppermute(array, 'pool', [(at, at ^ bit) for at in range(size)])  6.29 us
    ppermute x6, starting transfers between devices, rotate_user(): lax.ppermute(array, 'user', [(at, (at + step) % size) for at in range(siz...  5.62 us
    pallas_call x1, Pallas kernels, neg_tower(): pl.pallas_call(neg_kernel, in_specs=[INSIDE, INSIDE, OUTSIDE, OUTSIDE, OU...  3.69 us
    ppermute x6, waiting for transfers between devices, rotate_user(): lax.ppermute(array, 'user', [(at, (at + step) % size) for at in range(siz...  3.29 us
    pallas_call x1, Pallas kernels, select_rows(): pl.pallas_call(select_kernel, in_specs=[OUTSIDE] * 5, out_specs=[INSIDE,...  2.44 us
  transfers between devices with their start and end apart: 11, of which 6 were waited for; matrix products, arithmetic and copies ran while one was open for 0% of the time, Pallas kernels for 22%

profile of v7, /device:TPU:0, one launch (start us, length us, event | category | flops | bytes accessed | tf_op | source)
XLA Modules:
  0.0 61.7 jit_solution(8472504188509620581)
XLA Ops:
  0.6 2.4 %select_rows.1 = (bf16[512,512]{1,0:T(8,128)(2,1)}, bf16[144,512]{1,0:T(8,128)(2,1)S(1)}) custom-call(s32[1,16,32]{2,1,0:T(8,128)} %bitcast.17, bf16[512,512]{1,0:T(8,128)(2,1)} %rows.1, bf16[128,512]{1,0:T(8,128)(2,1)} %negs.1, s32[1,128]{1,0:T(1,128)} %bitcast.21, s32[1,128]{1,0:T(1,128)} %bitcast.22), custom_call_target="tpu_custom_call" | custom-call | tf_op jit(solution)/shard_map/select_rows/pallas_call | solution.py:158
  3.1 7.3 %all-to-all-start = ((bf16[32,16,512]{2,1,0:T(8,128)(2,1)}), bf16[32,16,512]{2,1,0:T(8,128)(2,1)S(1)}, u32[]{:S(2)}, u32[]{:S(2)}) async-start(bf16[32,16,512]{2,1,0:T(8,128)(2,1)} %bitcast.3), calls=%async_computation | async-start | bytes 1048576 | tf_op jit(solution)/shard_map/all_to_all | solution.py:514
  10.4 2.7 %collective-permute-start.3 = (bf16[144,512]{1,0:T(8,128)(2,1)S(1)}, bf16[144,512]{1,0:T(8,128)(2,1)S(1)}, u32[]{:S(2)}, u32[]{:S(2)}) collective-permute-start(bf16[144,512]{1,0:T(8,128)(2,1)S(1)} %get-tuple-element.19.own_ref), channel_id=1, source_target_pairs={{0,4},{1,5},{2,6},{3,7},{4,0},{5,1},{6,2},{7,3},{8,12},{9,13},{10,... | collective-permute-start | bytes 442376 | tf_op jit(solution)/shard_map/ppermute | solution.py:476
  13.2 18.5 %collective-permute-done.3.apart_ref = bf16[144,512]{1,0:T(8,128)(2,1)S(1)} collective-permute-done((bf16[144,512]{1,0:T(8,128)(2,1)S(1)}, bf16[144,512]{1,0:T(8,128)(2,1)S(1)}, u32[]{:S(2)}, u32[]{:S(2)}) %collective-permute-start.3) | collective-permute-done | bytes 147488 | tf_op jit(solution)/shard_map/ppermute | solution.py:476
  31.7 0.0 copy-start.2
  31.7 0.0 copy-start.4
  31.7 0.0 copy-start.5
  31.7 0.0 copy-start
  31.7 3.7 %neg_tower.1.refs_4_ = bf16[528,256]{1,0:T(8,128)(2,1)S(1)} custom-call(bf16[144,512]{1,0:T(8,128)(2,1)S(1)} %get-tuple-element.19.own_ref, bf16[144,512]{1,0:T(8,128)(2,1)S(1)} %collective-permute-done.3.apart_ref, bf16[512,2048]{1,0:T(8,128)(2,1)} %w_in.1, f32[1,2048]{1,0:T(1,128)} %bitcast.15, bf16[2048,512]{1,0:T(8,128)(2,1)} %w_out.3), custom_call_target="tpu_custom_call" | custom-call | tf_op jit(solution)/shard_map/neg_tower/pallas_call | solution.py:229
  35.4 1.5 %collective-permute-start.4 = (bf16[528,256]{1,0:T(8,128)(2,1)S(1)}, bf16[528,256]{1,0:T(8,128)(2,1)S(1)}, u32[]{:S(2)}, u32[]{:S(2)}) collective-permute-start(bf16[528,256]{1,0:T(8,128)(2,1)S(1)} %neg_tower.1.refs_4_), channel_id=1, source_target_pairs={{0,1},{1,0},{2,3},{3,2},{4,5},{5,4},{6,7},{7,6},{8,9},{9,8},{10,11... | collective-permute-start | bytes 811016 | tf_op jit(solution)/shard_map/ppermute | solution.py:476
  36.9 0.0 collective-permute-start.5
  37.0 2.0 %collective-permute-start.6 = (bf16[528,256]{1,0:T(8,128)(2,1)S(1)}, bf16[528,256]{1,0:T(8,128)(2,1)}, u32[]{:S(2)}, u32[]{:S(2)}) collective-permute-start(bf16[528,256]{1,0:T(8,128)(2,1)S(1)} %neg_tower.1.refs_4_), channel_id=1, source_target_pairs={{0,3},{1,2},{2,1},{3,0},{4,7},{5,6},{6,5},{7,4},{8,11},{9,10},{10,... | collective-permute-start | bytes 811016 | tf_op jit(solution)/shard_map/ppermute | solution.py:476
  39.0 0.0 copy-done.2
  39.0 0.0 copy-done.4
  39.0 0.0 copy-done.5
  39.0 1.1 %prepare.1 = (bf16[4,256,1024]{2,1,0:T(8,128)(2,1)S(1)}, f32[128,512]{1,0:T(8,128)S(1)}) custom-call(s32[32,256]{1,0:T(8,128)S(1)} %copy-done.4, s32[1,32]{1,0:T(1,128)S(1)} %bitcast.14, f32[32,4,256]{2,1,0:T(4,128)S(1)} %copy-done.2), custom_call_target="tpu_custom_call" | custom-call | tf_op jit(solution)/shard_map/prepare/pallas_call | solution.py:305
  40.1 0.0 copy-start.1
  40.1 1.3 %copy-done.1 = bf16[4,256,1024]{2,1,0:T(8,128)(2,1)} copy-done((bf16[4,256,1024]{2,1,0:T(8,128)(2,1)}, bf16[4,256,1024]{2,1,0:T(8,128)(2,1)S(1)}, u32[]{:S(2)}) %copy-start.1) | copy-done | bytes 2097176
  41.4 0.0 copy-start.3
  41.4 0.7 %copy-done.3 = f32[128,512]{1,0:T(8,128)} copy-done((f32[128,512]{1,0:T(8,128)}, f32[128,512]{1,0:T(8,128)S(1)}, u32[]{:S(2)}) %copy-start.3) | copy-done | bytes 262168
  42.1 0.0 all-to-all-done
  42.1 0.0 copy-done
  42.1 8.6 %route.1 = (f32[32,2048]{1,0:T(8,128)}, bf16[32,640]{1,0:T(8,128)(2,1)S(1)}, f32[1,32]{1,0:T(1,128)S(1)}) custom-call(bf16[512,512]{1,0:T(8,128)(2,1)S(1)} %bitcast.12, bf16[512,2048]{1,0:T(8,128)(2,1)S(1)} %copy-done, f32[1,2048]{1,0:T(1,128)} %bitcast.16, bf16[2048,512]{1,0:T(8,128)(2,1)} %w_out.3, bf16[512,512]{1,0:T(8,128)(2,1)} %bilinear.1, ...), custom_call_target="tpu_custom_call" | custom-call | tf_op jit(solution)/shard_map/route/pallas_call | solution.py:425
  50.7 0.1 collective-permute-start
  50.8 1.5 %collective-permute-start.1 = (bf16[32,640]{1,0:T(8,128)(2,1)S(1)}, bf16[32,640]{1,0:T(8,128)(2,1)S(1)}, u32[]{:S(2)}, u32[]{:S(2)}) collective-permute-start(bf16[32,640]{1,0:T(8,128)(2,1)S(1)} %get-tuple-element.18.refs_0_), channel_id=1, source_target_pairs={{0,16},{8,24},{16,0},{24,8},{1,17},{9,25},{17,1},{25,9},{2,18},{10... | collective-permute-start | bytes 122888 | tf_op jit(solution)/shard_map/ppermute | solution.py:480
  52.3 0.0 collective-permute-done.4.refs_5_
  52.3 1.4 %collective-permute-start.2 = (bf16[32,640]{1,0:T(8,128)(2,1)S(1)}, bf16[32,640]{1,0:T(8,128)(2,1)S(1)}, u32[]{:S(2)}, u32[]{:S(2)}) collective-permute-start(bf16[32,640]{1,0:T(8,128)(2,1)S(1)} %get-tuple-element.18.refs_0_), channel_id=1, source_target_pairs={{0,24},{8,0},{16,8},{24,16},{1,25},{9,1},{17,9},{25,17},{2,26},{10... | collective-permute-start | bytes 122888 | tf_op jit(solution)/shard_map/ppermute | solution.py:480
  53.7 0.0 collective-permute-done.5.refs_6_
  53.7 0.0 collective-permute-done.6.refs_7_
  53.7 0.5 collective-permute-done.refs_1_
  54.2 0.7 %collective-permute-done.1.refs_2_ = bf16[32,640]{1,0:T(8,128)(2,1)S(1)} collective-permute-done((bf16[32,640]{1,0:T(8,128)(2,1)S(1)}, bf16[32,640]{1,0:T(8,128)(2,1)S(1)}, u32[]{:S(2)}, u32[]{:S(2)}) %collective-permute-start.1) | collective-permute-done | bytes 40992 | tf_op jit(solution)/shard_map/ppermute | solution.py:480
  54.9 0.5 collective-permute-done.2.refs_3_
  55.4 1.5 %negative_sums.1 = (f32[1,32]{1,0:T(1,128)S(1)}, f32[1,32]{1,0:T(1,128)S(1)}, f32[1,32]{1,0:T(1,128)S(1)}, f32[1,32]{1,0:T(1,128)S(1)}) custom-call(bf16[32,640]{1,0:T(8,128)(2,1)S(1)} %get-tuple-element.18.refs_0_, bf16[32,640]{1,0:T(8,128)(2,1)S(1)} %collective-permute-done.refs_1_, bf16[32,640]{1,0:T(8,128)(2,1)S(1)} %collective-permute-done.1.refs_2_, ...), custom_call_target="tpu_custom_call" | custom-call | tf_op jit(solution)/shard_map/negative_sums/pallas_call | solution.py:467
  56.9 0.7 %collective-permute-start.9 = (f32[1,32]{1,0:T(1,128)S(1)}, f32[1,32]{1,0:T(1,128)S(1)}, u32[]{:S(2)}, u32[]{:S(2)}) collective-permute-start(f32[1,32]{1,0:T(1,128)S(1)} %get-tuple-element.23), channel_id=1, source_target_pairs={{0,8},{8,16},{16,24},{24,0},{1,9},{9,17},{17,25},{25,1},{2,10},{10... | collective-permute-start | bytes 392 | tf_op jit(solution)/shard_map/ppermute | solution.py:480
  57.6 1.5 %collective-permute-start.8 = (f32[1,32]{1,0:T(1,128)S(1)}, f32[1,32]{1,0:T(1,128)S(1)}, u32[]{:S(2)}, u32[]{:S(2)}) collective-permute-start(f32[1,32]{1,0:T(1,128)S(1)} %get-tuple-element.22), channel_id=1, source_target_pairs={{0,16},{8,24},{16,0},{24,8},{1,17},{9,25},{17,1},{25,9},{2,18},{10... | collective-permute-start | bytes 392 | tf_op jit(solution)/shard_map/ppermute | solution.py:480
  59.1 0.5 collective-permute-start.7
  59.6 0.4 collective-permute-done.9
  60.0 1.2 %collective-permute-done.8 = f32[1,32]{1,0:T(1,128)S(1)} collective-permute-done((f32[1,32]{1,0:T(1,128)S(1)}, f32[1,32]{1,0:T(1,128)S(1)}, u32[]{:S(2)}, u32[]{:S(2)}) %collective-permute-start.8) | collective-permute-done | bytes 160 | tf_op jit(solution)/shard_map/ppermute | solution.py:480
  61.2 0.0 collective-permute-done.7
  61.2 0.5 subtract_bitcast_fusion
Async XLA Ops:
  3.1 39.0 %all-to-all-start = ((bf16[32,16,512]{2,1,0:T(8,128)(2,1)}), bf16[32,16,512]{2,1,0:T(8,128)(2,1)S(1)}, u32[]{:S(2)}, u32[]{:S(2)}) async-start(bf16[32,16,512]{2,1,0:T(8,128)(2,1)} %bitcast.3), calls=%async_computation | async-start | bytes 1048576 | tf_op jit(solution)/shard_map/all_to_all | solution.py:514
  10.4 21.3 %collective-permute-start.3 = (bf16[144,512]{1,0:T(8,128)(2,1)S(1)}, bf16[144,512]{1,0:T(8,128)(2,1)S(1)}, u32[]{:S(2)}, u32[]{:S(2)}) collective-permute-start(bf16[144,512]{1,0:T(8,128)(2,1)S(1)} %get-tuple-element.19.own_ref), channel_id=1, source_target_pairs={{0,4},{1,5},{2,6},{3,7},{4,0},{5,1},{6,2},{7,3},{8,12},{9,13},{10,... | collective-permute-start | bytes 442376 | tf_op jit(solution)/shard_map/ppermute | solution.py:476
  31.7 7.3 %copy-start.2 = (f32[32,4,256]{2,1,0:T(4,128)S(1)}, f32[32,4,256]{2,1,0:T(4,128)}, u32[]{:S(2)}) copy-start(f32[32,4,256]{2,1,0:T(4,128)} %init.1) | copy-start | bytes 393220
  31.7 7.3 %copy-start.4 = (s32[32,256]{1,0:T(8,128)S(1)}, s32[32,256]{1,0:T(8,128)}, u32[]{:S(2)}) copy-start(s32[32,256]{1,0:T(8,128)} %index.1) | copy-start | bytes 98308
  31.7 7.3 %copy-start.5 = (s32[32]{0:T(128)S(1)}, s32[32]{0:T(128)}, u32[]{:S(2)}) copy-start(s32[32]{0:T(128)} %param.22) | copy-start | bytes 388
  31.7 10.4 %copy-start = (bf16[512,2048]{1,0:T(8,128)(2,1)S(1)}, bf16[512,2048]{1,0:T(8,128)(2,1)}, u32[]{:S(2)}) copy-start(bf16[512,2048]{1,0:T(8,128)(2,1)} %w_in.1) | copy-start | bytes 6291460
  35.4 16.9 %collective-permute-start.4 = (bf16[528,256]{1,0:T(8,128)(2,1)S(1)}, bf16[528,256]{1,0:T(8,128)(2,1)S(1)}, u32[]{:S(2)}, u32[]{:S(2)}) collective-permute-start(bf16[528,256]{1,0:T(8,128)(2,1)S(1)} %neg_tower.1.refs_4_), channel_id=1, source_target_pairs={{0,1},{1,0},{2,3},{3,2},{4,5},{5,4},{6,7},{7,6},{8,9},{9,8},{10,11... | collective-permute-start | bytes 811016 | tf_op jit(solution)/shard_map/ppermute | solution.py:476
  36.9 16.8 %collective-permute-start.5 = (bf16[528,256]{1,0:T(8,128)(2,1)S(1)}, bf16[528,256]{1,0:T(8,128)(2,1)}, u32[]{:S(2)}, u32[]{:S(2)}) collective-permute-start(bf16[528,256]{1,0:T(8,128)(2,1)S(1)} %neg_tower.1.refs_4_), channel_id=1, source_target_pairs={{0,2},{1,3},{2,0},{3,1},{4,6},{5,7},{6,4},{7,5},{8,10},{9,11},{10,... | collective-permute-start | bytes 811016 | tf_op jit(solution)/shard_map/ppermute | solution.py:476
  37.0 16.8 %collective-permute-start.6 = (bf16[528,256]{1,0:T(8,128)(2,1)S(1)}, bf16[528,256]{1,0:T(8,128)(2,1)}, u32[]{:S(2)}, u32[]{:S(2)}) collective-permute-start(bf16[528,256]{1,0:T(8,128)(2,1)S(1)} %neg_tower.1.refs_4_), channel_id=1, source_target_pairs={{0,3},{1,2},{2,1},{3,0},{4,7},{5,6},{6,5},{7,4},{8,11},{9,10},{10,... | collective-permute-start | bytes 811016 | tf_op jit(solution)/shard_map/ppermute | solution.py:476
  40.1 1.3 %copy-start.1 = (bf16[4,256,1024]{2,1,0:T(8,128)(2,1)}, bf16[4,256,1024]{2,1,0:T(8,128)(2,1)S(1)}, u32[]{:S(2)}) copy-start(bf16[4,256,1024]{2,1,0:T(8,128)(2,1)S(1)} %get-tuple-element.14.onehot) | copy-start | bytes 6291460
  41.4 0.7 %copy-start.3 = (f32[128,512]{1,0:T(8,128)}, f32[128,512]{1,0:T(8,128)S(1)}, u32[]{:S(2)}) copy-start(f32[128,512]{1,0:T(8,128)S(1)} %get-tuple-element.15.first) | copy-start | bytes 786436
  50.7 3.5 %collective-permute-start = (bf16[32,640]{1,0:T(8,128)(2,1)S(1)}, bf16[32,640]{1,0:T(8,128)(2,1)S(1)}, u32[]{:S(2)}, u32[]{:S(2)}) collective-permute-start(bf16[32,640]{1,0:T(8,128)(2,1)S(1)} %get-tuple-element.18.refs_0_), channel_id=1, source_target_pairs={{0,8},{8,16},{16,24},{24,0},{1,9},{9,17},{17,25},{25,1},{2,10},{10... | collective-permute-start | bytes 122888 | tf_op jit(solution)/shard_map/ppermute | solution.py:480
  50.8 4.1 %collective-permute-start.1 = (bf16[32,640]{1,0:T(8,128)(2,1)S(1)}, bf16[32,640]{1,0:T(8,128)(2,1)S(1)}, u32[]{:S(2)}, u32[]{:S(2)}) collective-permute-start(bf16[32,640]{1,0:T(8,128)(2,1)S(1)} %get-tuple-element.18.refs_0_), channel_id=1, source_target_pairs={{0,16},{8,24},{16,0},{24,8},{1,17},{9,25},{17,1},{25,9},{2,18},{10... | collective-permute-start | bytes 122888 | tf_op jit(solution)/shard_map/ppermute | solution.py:480
  52.3 3.1 %collective-permute-start.2 = (bf16[32,640]{1,0:T(8,128)(2,1)S(1)}, bf16[32,640]{1,0:T(8,128)(2,1)S(1)}, u32[]{:S(2)}, u32[]{:S(2)}) collective-permute-start(bf16[32,640]{1,0:T(8,128)(2,1)S(1)} %get-tuple-element.18.refs_0_), channel_id=1, source_target_pairs={{0,24},{8,0},{16,8},{24,16},{1,25},{9,1},{17,9},{25,17},{2,26},{10... | collective-permute-start | bytes 122888 | tf_op jit(solution)/shard_map/ppermute | solution.py:480
  56.9 3.0 %collective-permute-start.9 = (f32[1,32]{1,0:T(1,128)S(1)}, f32[1,32]{1,0:T(1,128)S(1)}, u32[]{:S(2)}, u32[]{:S(2)}) collective-permute-start(f32[1,32]{1,0:T(1,128)S(1)} %get-tuple-element.23), channel_id=1, source_target_pairs={{0,8},{8,16},{16,24},{24,0},{1,9},{9,17},{17,25},{25,1},{2,10},{10... | collective-permute-start | bytes 392 | tf_op jit(solution)/shard_map/ppermute | solution.py:480
  57.6 3.6 %collective-permute-start.8 = (f32[1,32]{1,0:T(1,128)S(1)}, f32[1,32]{1,0:T(1,128)S(1)}, u32[]{:S(2)}, u32[]{:S(2)}) collective-permute-start(f32[1,32]{1,0:T(1,128)S(1)} %get-tuple-element.22), channel_id=1, source_target_pairs={{0,16},{8,24},{16,0},{24,8},{1,17},{9,25},{17,1},{25,9},{2,18},{10... | collective-permute-start | bytes 392 | tf_op jit(solution)/shard_map/ppermute | solution.py:480
  59.1 2.1 %collective-permute-start.7 = (f32[1,32]{1,0:T(1,128)S(1)}, f32[1,32]{1,0:T(1,128)S(1)}, u32[]{:S(2)}, u32[]{:S(2)}) collective-permute-start(f32[1,32]{1,0:T(1,128)S(1)} %get-tuple-element.21), channel_id=1, source_target_pairs={{0,24},{8,0},{16,8},{24,16},{1,25},{9,1},{17,9},{25,17},{2,26},{10... | collective-permute-start | bytes 392 | tf_op jit(solution)/shard_map/ppermute | solution.py:480

commit v8 on v7

--- a/solution.py
+++ b/solution.py
@@ -75,6 +75,17 @@
     for at, column in enumerate(columns):
         out = jnp.where(lane == at, column, out)
     return out
+
+
+def shift_of(size):
+    assert size & (size - 1) == 0
+    return size.bit_length() - 1
+
+
+def renumber(slot, cap, user_size, pool_size):
+    block = slot >> shift_of(cap)
+    place = ((block & (pool_size - 1)) << shift_of(user_size)) + (block >> shift_of(pool_size))
+    return (place << shift_of(cap)) + (slot & (cap - 1))
 
 
 class Copies:
@@ -97,79 +108,83 @@
 
 
 def select_kernel(
+    user_size,
+    pool_size,
     fetch,
     rows,
     negs,
     ids,
     counts,
-    out_ref,
+    out,
     packed,
     fetch_ref,
     rows_ref,
+    out_ref,
     extra_ref,
     ids_ref,
     counts_ref,
     sems,
 ):
-    small = [
-        Copies(ids, ids_ref, sems, 4, 1),
-        Copies(counts, counts_ref, sems, 5, 1),
-    ]
+    table = Copies(fetch, fetch_ref, sems, 0, 1)
+    small = [Copies(ids, ids_ref, sems, 1, 1), Copies(counts, counts_ref, sems, 2, 1)]
+    copy = Copies(rows, rows_ref, sems, 5, SPLIT)
     kept = negs.shape[0]
-    body = pltpu.make_async_copy(negs, packed.at[pl.ds(0, kept)], sems.at[2])
+    body = pltpu.make_async_copy(negs, packed.at[pl.ds(0, kept)], sems.at[3])
     body.start()
-    table = pltpu.make_async_copy(fetch, fetch_ref, sems.at[0])
-    table.start()
-    copy = pltpu.make_async_copy(rows, rows_ref, sems.at[1])
-    copy.start()
     _, cap, blocks = fetch_ref.shape
     count = blocks * cap
     row = iota((count, blocks), 0)
-    block = iota((count, blocks), 1)
-    pick = jnp.where((row >= block * cap) & (row < block * cap + cap), 1.0, 0.0).astype(bf16)
+    start = renumber(iota((1, blocks), 1) * cap, cap, user_size, pool_size)
+    pick = jnp.where((row >= start) & (row < start + cap), 1.0, 0.0).astype(bf16)
+    place = iota((count, cap), 1) == (iota((count, cap), 0) & (cap - 1))
+    table.wait()
+    picked = fetch_ref[0]
+    high = mm_nt(pick, (picked >> 7).astype(f32).astype(bf16))
+    low = mm_nt(pick, (picked & 127).astype(f32).astype(bf16))
+    column = jnp.sum(jnp.where(place, high * 128.0 + low, 0.0), axis=1, keepdims=True)
+    item = iota((count, rows_ref.shape[0]), 1).astype(f32)
+    chosen = jnp.where(item == column, 1.0, 0.0).astype(bf16)
     for one in small:
         one.wait()
     numbers = id_digits(ids_ref[...]) + (counts_ref[...].astype(f32),)
     at = iota((EXTRA, kept), 0)
     extra = jnp.zeros((EXTRA, kept), f32)
-    for place, one in enumerate(numbers):
-        extra = jnp.where(at == place, one, extra)
+    for line, one in enumerate(numbers):
+        extra = jnp.where(at == line, one, extra)
     extra_ref[...] = jnp.zeros(extra_ref.shape, bf16)
     extra_ref[:, :kept] = extra.astype(bf16)
-    tail = pltpu.make_async_copy(extra_ref, packed.at[pl.ds(kept, EXTRA)], sems.at[3])
+    tail = pltpu.make_async_copy(extra_ref, packed.at[pl.ds(kept, EXTRA)], sems.at[4])
     tail.start()
-    table.wait()
-    picked = fetch_ref[0]
-    high = mm_nt(pick, (picked >> 7).astype(f32).astype(bf16))
-    low = mm_nt(pick, (picked & 127).astype(f32).astype(bf16))
-    place = iota((count, cap), 1) == lax.rem(iota((count, cap), 0), jnp.int32(cap))
-    column = jnp.sum(jnp.where(place, high * 128.0 + low, 0.0), axis=1, keepdims=True)
-    item = iota((count, rows_ref.shape[0]), 1).astype(f32)
-    chosen = jnp.where(item == column, 1.0, 0.0).astype(bf16)
     copy.wait()
-    out_ref[...] = mm(chosen, rows_ref[...]).astype(bf16)
+    size = count // SPLIT
+    for part in range(SPLIT):
+        cut = slice(part * size, (part + 1) * size)
+        out_ref[cut, :] = mm(chosen[cut], rows_ref[...]).astype(bf16)
+        Copies(out_ref.at[pl.ds(part * size, size)], out.at[pl.ds(part * size, size)], sems, 5 + SPLIT + part, 1)
     body.wait()
     tail.wait()
-
-
-def select_rows(fetch, rows, negs, ids, counts):
+    for part in range(SPLIT):
+        there = pl.ds(part * size, size)
+        pltpu.make_async_copy(out_ref.at[there], out.at[there], sems.at[5 + SPLIT + part]).wait()
+
+
+def select_rows(user_size, pool_size, fetch, rows, negs, ids, counts):
     blocks, _, cap = fetch.shape
     packed = (negs.shape[0] + EXTRA, negs.shape[1])
+    chosen = (blocks * cap, rows.shape[1])
     return pl.pallas_call(
-        select_kernel,
+        functools.partial(select_kernel, user_size, pool_size),
         in_specs=[OUTSIDE] * 5,
-        out_specs=[INSIDE, OUTSIDE],
-        out_shape=[
-            pltpu.VMEM((blocks * cap, rows.shape[1]), bf16),
-            jax.ShapeDtypeStruct(packed, bf16),
-        ],
+        out_specs=[OUTSIDE, OUTSIDE],
+        out_shape=[jax.ShapeDtypeStruct(chosen, bf16), jax.ShapeDtypeStruct(packed, bf16)],
         scratch_shapes=[
             pltpu.VMEM((1, cap, blocks), i32),
             pltpu.VMEM(rows.shape, bf16),
+            pltpu.VMEM(chosen, bf16),
             pltpu.VMEM((EXTRA, negs.shape[1]), bf16),
             pltpu.VMEM(ids.shape, i32),
             pltpu.VMEM(counts.shape, i32),
-            pltpu.SemaphoreType.DMA((6,)),
+            pltpu.SemaphoreType.DMA((5 + 2 * SPLIT,)),
         ],
         compiler_params=PARAMS,
         name="select_rows",
@@ -266,7 +281,7 @@
             ],
             axis=1,
         )
-        both = mm_nt(left, onehot_ref[group])
+        both = mm(left, onehot_ref[group])
         own = jnp.where((user & 1) == 0, both[:, :LANES], both[:, LANES:])
         for page in range(pages):
             for k in range(INTERESTS):
@@ -282,40 +297,83 @@
     return jnp.where(iota(shape, 1).astype(f32) < length, 1.0, 0.0)
 
 
-def prepare_kernel(index_ref, length_ref, init_ref, onehot_ref, slot_ref):
+def prepare_kernel(
+    renumbered,
+    index,
+    length,
+    init,
+    onehot,
+    slots,
+    moved,
+    index_ref,
+    length_ref,
+    init_ref,
+    onehot_ref,
+    slot_ref,
+    moved_ref,
+    sems,
+):
+    pairs = ((index, index_ref), (length, length_ref), (init, init_ref))
+    copies = [Copies(*pair, sems, at, 1) for at, pair in enumerate(pairs)]
     users, events = index_ref.shape
-    index = index_ref[...]
+    groups = users // GROUP_USERS
+    copies[0].wait()
+    index = renumbered(index_ref[...])
+    moved_ref[...] = index
+    back = [Copies(moved_ref, moved, sems, 3, 1)]
     upper = index >> 7
-    lower = index & (LANES - 1)
-    lane_id = iota((LANES, events), 0)
-    for user in range(users):
-        group, within = divmod(user, GROUP_USERS)
-        pair, side = divmod(within, 2)
-        hit = jnp.where(lane_id == lower[user : user + 1], 1.0, 0.0).astype(bf16)
-        onehot_ref[
-            group, side * LANES : (side + 1) * LANES, pair * events : (pair + 1) * events
-        ] = hit
+    lower = (index & (LANES - 1)).astype(f32).T
+    lane_id = iota((events, LANES), 1).astype(f32)
+    for group in range(groups):
+        for within in range(GROUP_USERS):
+            user = group * GROUP_USERS + within
+            pair, side = divmod(within, 2)
+            hit = jnp.where(lane_id == lower[:, user : user + 1], 1.0, 0.0).astype(bf16)
+            onehot_ref[
+                group, pair * events : (pair + 1) * events, side * LANES : (side + 1) * LANES
+            ] = hit
+        there = pl.ds(group, 1)
+        back.append(Copies(onehot_ref.at[there], onehot.at[there], sems, 5 + group, 1))
+    for one in copies[1:]:
+        one.wait()
     live = live_mask(length_ref, index.shape)
     weights = event_weights([init_ref[:, k, :] for k in range(INTERESTS)], live)
     scatter_weights(weights, upper, onehot_ref, slot_ref)
-
-
-def prepare(index, length, init, slots):
+    back.append(Copies(slot_ref, slots, sems, 4, 1))
+    for one in back:
+        one.wait()
+
+
+def prepare(renumbered, index, length, init, slots):
     users, events = index.shape
+    groups = users // GROUP_USERS
+    onehot = (groups, GROUP_USERS // 2 * events, 2 * LANES)
+    first = (INTERESTS * users, slots)
     return pl.pallas_call(
-        prepare_kernel,
+        functools.partial(prepare_kernel, renumbered),
+        in_specs=[OUTSIDE] * 3,
+        out_specs=[OUTSIDE] * 3,
         out_shape=[
-            jax.ShapeDtypeStruct(
-                (users // GROUP_USERS, 2 * LANES, GROUP_USERS // 2 * events), bf16
-            ),
-            jax.ShapeDtypeStruct((INTERESTS * users, slots), f32),
+            pltpu.HBM(onehot, bf16),
+            pltpu.HBM(first, f32),
+            pltpu.HBM(index.shape, i32),
+        ],
+        scratch_shapes=[
+            pltpu.VMEM(index.shape, i32),
+            pltpu.VMEM(length.shape, i32),
+            pltpu.VMEM(init.shape, f32),
+            pltpu.VMEM(onehot, bf16),
+            pltpu.VMEM(first, f32),
+            pltpu.VMEM(index.shape, i32),
+            pltpu.SemaphoreType.DMA((5 + groups,)),
         ],
         compiler_params=PARAMS,
         name="prepare",
-    )(near(index), length, near(init))
+    )(far(index), far(length), far(init))
 
 
 def route_kernel(
+    renumbered,
     rows_ref,
     w_in_ref,
     bias,
@@ -403,7 +461,7 @@
     each = [capsules[k * users : (k + 1) * users] for k in range(INTERESTS)]
     for k in range(INTERESTS):
         interests_ref[:, k * width : (k + 1) * width] = each[k]
-    label = to_column(label_ref[...].astype(f32))
+    label = to_column(renumbered(label_ref[...]).astype(f32))
     chosen = jnp.where(iota((users, slots), 1).astype(f32) == label, 1.0, 0.0).astype(bf16)
     label_rows = mm(chosen, unit)
     raised = [
@@ -418,12 +476,12 @@
     positive_ref[...] = logit_scale * to_row(match) - jnp.log(counts_ref[...].astype(f32))
 
 
-def route(rows, w_in, *others):
+def route(renumbered, rows, w_in, *others):
     _, _, bilinear, onehot, first, index, _, _, _, _, _ = others
     users = index.shape[0]
     width = bilinear.shape[1]
     return pl.pallas_call(
-        route_kernel,
+        functools.partial(route_kernel, renumbered),
         in_specs=[INSIDE] * 2 + [OUTSIDE] * len(others),
         out_shape=[
             jax.ShapeDtypeStruct((users, INTERESTS * width), f32),
@@ -508,12 +566,12 @@
 ):
     weights = (w_in, bias_in.reshape(1, -1), w_out)
     outgoing, packed = select_rows(
-        fetch_table, item_feats, neg_feats, neg_ids.reshape(1, -1), neg_counts.reshape(1, -1)
+        user_size, pool_size, fetch_table, item_feats, neg_feats, neg_ids.reshape(1, -1), neg_counts.reshape(1, -1)
     )
     apart = swap_pool(packed, pool_size, pool_size // 2)
     arrived = lax.all_to_all(
         outgoing.reshape(fetch_table.shape[0], fetch_table.shape[2], -1),
-        ("user", "pool"),
+        ("pool", "user"),
         split_axis=0,
         concat_axis=0,
         tiled=True,
@@ -522,10 +580,14 @@
 
     own_neg = neg_tower(packed, apart, weights)
     length = hist_len.reshape(1, -1)
-    onehot, first = prepare(hist_index, length, route_init, outgoing.shape[0])
+    renumbered = functools.partial(
+        renumber, cap=fetch_table.shape[2], user_size=user_size, pool_size=pool_size
+    )
+    onehot, first, moved = prepare(renumbered, hist_index, length, route_init, outgoing.shape[0])
     negs = gather_negatives(own_neg, pool_size)
 
     interests, vec, positive = route(
+        renumbered,
         arrived,
         w_in,
         bias_in.reshape(1, -1),
@@ -533,7 +595,7 @@
         bilinear,
         onehot,
         first,
-        hist_index,
+        moved,
         length,
         route_init,
         label_index.reshape(1, -1),

time: 62.2 us -> 61.6 us (level)
  local copies, waits for them, and re-layouts: 2.02 us -> 0.01 us
  Pallas kernels: 17.4 us -> 18.7 us
    unnamed x12 -> x2, local copies, waits for them, and re-layouts: 2.02 us -> 0.01 us
    pallas_call x3, Pallas kernels: 12.2 us -> 13.6 us  [the longest x1 7.93 us: route(): pl.pallas_call(functools.partial(route_kernel, renumbered), in_specs=[INS...]
  transfers between devices with their start and end apart: 11 -> 11, of which waited for: 6 -> 6; matrix products, arithmetic and copies ran while one was open for 0% -> 0% of each run, Pallas kernels for 22% -> 24%
where the time goes in v8:
time: 61.6 us; the launch traced here: 61.1 us
  waiting for transfers between devices  21.8 us (35%)
  starting transfers between devices  19.3 us (31%)
  Pallas kernels  18.7 us (30%)
  between operations  0.71 us (1%)
    ppermute x4, waiting for transfers between devices, swap_pool(): return lax.ppermute(array, 'pool', [(at, at ^ bit) for at in range(size)])  18.6 us
    pallas_call x1, Pallas kernels, route(): pl.pallas_call(functools.partial(route_kernel, renumbered), in_specs=[INS...  7.93 us
    all_to_all x1, starting transfers between devices, on_device(): lax.all_to_all(outgoing.reshape(fetch_table.shape[0], fetch_table.shape[2...  7.33 us
    ppermute x4, starting transfers between devices, swap_pool(): return lax.ppermute(array, 'pool', [(at, at ^ bit) for at in range(size)])  6.29 us
    ppermute x6, starting transfers between devices, rotate_user(): lax.ppermute(array, 'user', [(at, (at + step) % size) for at in range(siz...  5.63 us
    pallas_call x1, Pallas kernels, neg_tower(): pl.pallas_call(neg_kernel, in_specs=[INSIDE, INSIDE, OUTSIDE, OUTSIDE, OU...  3.68 us
    pallas_call x1, Pallas kernels, prepare(): pl.pallas_call(functools.partial(prepare_kernel, renumbered), in_specs=[O...  3.33 us
    ppermute x6, waiting for transfers between devices, rotate_user(): lax.ppermute(array, 'user', [(at, (at + step) % size) for at in range(siz...  3.27 us
  transfers between devices with their start and end apart: 11, of which 6 were waited for; matrix products, arithmetic and copies ran while one was open for 0% of the time, Pallas kernels for 24%

profile of v8, /device:TPU:0, one launch (start us, length us, event | category | flops | bytes accessed | tf_op | source)
XLA Modules:
  0.0 61.1 jit_solution(3693685465508755291)
XLA Ops:
  0.6 2.3 %select_rows.1 = (bf16[512,512]{1,0:T(8,128)(2,1)}, bf16[144,512]{1,0:T(8,128)(2,1)S(1)}) custom-call(s32[1,16,32]{2,1,0:T(8,128)} %bitcast.15, bf16[512,512]{1,0:T(8,128)(2,1)} %rows.1, bf16[128,512]{1,0:T(8,128)(2,1)} %negs.1, s32[1,128]{1,0:T(1,128)} %bitcast.21, s32[1,128]{1,0:T(1,128)} %bitcast.22), custom_call_target="tpu_custom_call" | custom-call | tf_op jit(solution)/shard_map/select_rows/pallas_call | solution.py:175
  3.0 7.3 %all-to-all-start = ((bf16[32,16,512]{2,1,0:T(8,128)(2,1)}), bf16[32,16,512]{2,1,0:T(8,128)(2,1)S(1)}, u32[]{:S(2)}, u32[]{:S(2)}) async-start(bf16[32,16,512]{2,1,0:T(8,128)(2,1)} %bitcast.3), calls=%async_computation | async-start | bytes 1048576 | tf_op jit(solution)/shard_map/all_to_all | solution.py:572
  10.3 2.7 %collective-permute-start.3 = (bf16[144,512]{1,0:T(8,128)(2,1)S(1)}, bf16[144,512]{1,0:T(8,128)(2,1)S(1)}, u32[]{:S(2)}, u32[]{:S(2)}) collective-permute-start(bf16[144,512]{1,0:T(8,128)(2,1)S(1)} %get-tuple-element.21.own_ref), channel_id=1, source_target_pairs={{0,4},{1,5},{2,6},{3,7},{4,0},{5,1},{6,2},{7,3},{8,12},{9,13},{10,... | collective-permute-start | bytes 442376 | tf_op jit(solution)/shard_map/ppermute | solution.py:534
  13.1 18.5 %collective-permute-done.3.apart_ref = bf16[144,512]{1,0:T(8,128)(2,1)S(1)} collective-permute-done((bf16[144,512]{1,0:T(8,128)(2,1)S(1)}, bf16[144,512]{1,0:T(8,128)(2,1)S(1)}, u32[]{:S(2)}, u32[]{:S(2)}) %collective-permute-start.3) | collective-permute-done | bytes 147488 | tf_op jit(solution)/shard_map/ppermute | solution.py:534
  31.6 0.0 copy-start
  31.6 3.7 %neg_tower.1.refs_4_ = bf16[528,256]{1,0:T(8,128)(2,1)S(1)} custom-call(bf16[144,512]{1,0:T(8,128)(2,1)S(1)} %get-tuple-element.21.own_ref, bf16[144,512]{1,0:T(8,128)(2,1)S(1)} %collective-permute-done.3.apart_ref, bf16[512,2048]{1,0:T(8,128)(2,1)} %w_in.1, f32[1,2048]{1,0:T(1,128)} %bitcast.13, bf16[2048,512]{1,0:T(8,128)(2,1)} %w_out.3), custom_call_target="tpu_custom_call" | custom-call | tf_op jit(solution)/shard_map/neg_tower/pallas_call | solution.py:244
  35.3 1.5 %collective-permute-start.4 = (bf16[528,256]{1,0:T(8,128)(2,1)S(1)}, bf16[528,256]{1,0:T(8,128)(2,1)S(1)}, u32[]{:S(2)}, u32[]{:S(2)}) collective-permute-start(bf16[528,256]{1,0:T(8,128)(2,1)S(1)} %neg_tower.1.refs_4_), channel_id=1, source_target_pairs={{0,1},{1,0},{2,3},{3,2},{4,5},{5,4},{6,7},{7,6},{8,9},{9,8},{10,11... | collective-permute-start | bytes 811016 | tf_op jit(solution)/shard_map/ppermute | solution.py:534
  36.8 0.0 collective-permute-start.5
  36.8 2.0 %collective-permute-start.6 = (bf16[528,256]{1,0:T(8,128)(2,1)S(1)}, bf16[528,256]{1,0:T(8,128)(2,1)}, u32[]{:S(2)}, u32[]{:S(2)}) collective-permute-start(bf16[528,256]{1,0:T(8,128)(2,1)S(1)} %neg_tower.1.refs_4_), channel_id=1, source_target_pairs={{0,3},{1,2},{2,1},{3,0},{4,7},{5,6},{6,5},{7,4},{8,11},{9,10},{10,... | collective-permute-start | bytes 811016 | tf_op jit(solution)/shard_map/ppermute | solution.py:534
  38.9 3.3 %prepare.1 = (bf16[4,1024,256]{2,1,0:T(8,128)(2,1)}, f32[128,512]{1,0:T(8,128)}, s32[32,256]{1,0:T(8,128)}) custom-call(s32[32,256]{1,0:T(8,128)} %index.1, s32[1,32]{1,0:T(1,128)} %bitcast.16, f32[32,4,256]{2,1,0:T(4,128)} %init.3), custom_call_target="tpu_custom_call" | custom-call | tf_op jit(solution)/shard_map/prepare/pallas_call | solution.py:352
  42.2 0.0 all-to-all-done
  42.2 0.0 copy-done
  42.2 7.9 %route.1 = (f32[32,2048]{1,0:T(8,128)}, bf16[32,640]{1,0:T(8,128)(2,1)S(1)}, f32[1,32]{1,0:T(1,128)S(1)}) custom-call(bf16[512,512]{1,0:T(8,128)(2,1)S(1)} %bitcast.12, bf16[512,2048]{1,0:T(8,128)(2,1)S(1)} %copy-done, f32[1,2048]{1,0:T(1,128)} %bitcast.14, bf16[2048,512]{1,0:T(8,128)(2,1)} %w_out.3, bf16[512,512]{1,0:T(8,128)(2,1)} %bilinear.1, ...), custom_call_target="tpu_custom_call" | custom-call | tf_op jit(solution)/shard_map/route/pallas_call | solution.py:483
  50.2 0.1 collective-permute-start
  50.2 1.6 %collective-permute-start.1 = (bf16[32,640]{1,0:T(8,128)(2,1)S(1)}, bf16[32,640]{1,0:T(8,128)(2,1)S(1)}, u32[]{:S(2)}, u32[]{:S(2)}) collective-permute-start(bf16[32,640]{1,0:T(8,128)(2,1)S(1)} %get-tuple-element.20.refs_0_), channel_id=1, source_target_pairs={{0,16},{8,24},{16,0},{24,8},{1,17},{9,25},{17,1},{25,9},{2,18},{10... | collective-permute-start | bytes 122888 | tf_op jit(solution)/shard_map/ppermute | solution.py:538
  51.8 0.0 collective-permute-done.4.refs_5_
  51.8 1.4 %collective-permute-start.2 = (bf16[32,640]{1,0:T(8,128)(2,1)S(1)}, bf16[32,640]{1,0:T(8,128)(2,1)S(1)}, u32[]{:S(2)}, u32[]{:S(2)}) collective-permute-start(bf16[32,640]{1,0:T(8,128)(2,1)S(1)} %get-tuple-element.20.refs_0_), channel_id=1, source_target_pairs={{0,24},{8,0},{16,8},{24,16},{1,25},{9,1},{17,9},{25,17},{2,26},{10... | collective-permute-start | bytes 122888 | tf_op jit(solution)/shard_map/ppermute | solution.py:538
  53.2 0.0 collective-permute-done.5.refs_6_
  53.2 0.0 collective-permute-done.6.refs_7_
  53.2 0.5 collective-permute-done.refs_1_
  53.6 0.7 %collective-permute-done.1.refs_2_ = bf16[32,640]{1,0:T(8,128)(2,1)S(1)} collective-permute-done((bf16[32,640]{1,0:T(8,128)(2,1)S(1)}, bf16[32,640]{1,0:T(8,128)(2,1)S(1)}, u32[]{:S(2)}, u32[]{:S(2)}) %collective-permute-start.1) | collective-permute-done | bytes 40992 | tf_op jit(solution)/shard_map/ppermute | solution.py:538
  54.3 0.5 collective-permute-done.2.refs_3_
  54.8 1.5 %negative_sums.1 = (f32[1,32]{1,0:T(1,128)S(1)}, f32[1,32]{1,0:T(1,128)S(1)}, f32[1,32]{1,0:T(1,128)S(1)}, f32[1,32]{1,0:T(1,128)S(1)}) custom-call(bf16[32,640]{1,0:T(8,128)(2,1)S(1)} %get-tuple-element.20.refs_0_, bf16[32,640]{1,0:T(8,128)(2,1)S(1)} %collective-permute-done.refs_1_, bf16[32,640]{1,0:T(8,128)(2,1)S(1)} %collective-permute-done.1.refs_2_, ...), custom_call_target="tpu_custom_call" | custom-call | tf_op jit(solution)/shard_map/negative_sums/pallas_call | solution.py:525
  56.3 0.7 %collective-permute-start.9 = (f32[1,32]{1,0:T(1,128)S(1)}, f32[1,32]{1,0:T(1,128)S(1)}, u32[]{:S(2)}, u32[]{:S(2)}) collective-permute-start(f32[1,32]{1,0:T(1,128)S(1)} %get-tuple-element.25), channel_id=1, source_target_pairs={{0,8},{8,16},{16,24},{24,0},{1,9},{9,17},{17,25},{25,1},{2,10},{10... | collective-permute-start | bytes 392 | tf_op jit(solution)/shard_map/ppermute | solution.py:538
  57.0 1.5 %collective-permute-start.8 = (f32[1,32]{1,0:T(1,128)S(1)}, f32[1,32]{1,0:T(1,128)S(1)}, u32[]{:S(2)}, u32[]{:S(2)}) collective-permute-start(f32[1,32]{1,0:T(1,128)S(1)} %get-tuple-element.24), channel_id=1, source_target_pairs={{0,16},{8,24},{16,0},{24,8},{1,17},{9,25},{17,1},{25,9},{2,18},{10... | collective-permute-start | bytes 392 | tf_op jit(solution)/shard_map/ppermute | solution.py:538
  58.4 0.5 collective-permute-start.7
  58.9 0.4 collective-permute-done.9
  59.3 1.2 %collective-permute-done.8 = f32[1,32]{1,0:T(1,128)S(1)} collective-permute-done((f32[1,32]{1,0:T(1,128)S(1)}, f32[1,32]{1,0:T(1,128)S(1)}, u32[]{:S(2)}, u32[]{:S(2)}) %collective-permute-start.8) | collective-permute-done | bytes 160 | tf_op jit(solution)/shard_map/ppermute | solution.py:538
  60.5 0.0 collective-permute-done.7
  60.5 0.5 subtract_bitcast_fusion
Async XLA Ops:
  3.0 39.2 %all-to-all-start = ((bf16[32,16,512]{2,1,0:T(8,128)(2,1)}), bf16[32,16,512]{2,1,0:T(8,128)(2,1)S(1)}, u32[]{:S(2)}, u32[]{:S(2)}) async-start(bf16[32,16,512]{2,1,0:T(8,128)(2,1)} %bitcast.3), calls=%async_computation | async-start | bytes 1048576 | tf_op jit(solution)/shard_map/all_to_all | solution.py:572
  10.3 21.3 %collective-permute-start.3 = (bf16[144,512]{1,0:T(8,128)(2,1)S(1)}, bf16[144,512]{1,0:T(8,128)(2,1)S(1)}, u32[]{:S(2)}, u32[]{:S(2)}) collective-permute-start(bf16[144,512]{1,0:T(8,128)(2,1)S(1)} %get-tuple-element.21.own_ref), channel_id=1, source_target_pairs={{0,4},{1,5},{2,6},{3,7},{4,0},{5,1},{6,2},{7,3},{8,12},{9,13},{10,... | collective-permute-start | bytes 442376 | tf_op jit(solution)/shard_map/ppermute | solution.py:534
  31.6 10.6 %copy-start = (bf16[512,2048]{1,0:T(8,128)(2,1)S(1)}, bf16[512,2048]{1,0:T(8,128)(2,1)}, u32[]{:S(2)}) copy-start(bf16[512,2048]{1,0:T(8,128)(2,1)} %w_in.1) | copy-start | bytes 6291460
  35.3 16.5 %collective-permute-start.4 = (bf16[528,256]{1,0:T(8,128)(2,1)S(1)}, bf16[528,256]{1,0:T(8,128)(2,1)S(1)}, u32[]{:S(2)}, u32[]{:S(2)}) collective-permute-start(bf16[528,256]{1,0:T(8,128)(2,1)S(1)} %neg_tower.1.refs_4_), channel_id=1, source_target_pairs={{0,1},{1,0},{2,3},{3,2},{4,5},{5,4},{6,7},{7,6},{8,9},{9,8},{10,11... | collective-permute-start | bytes 811016 | tf_op jit(solution)/shard_map/ppermute | solution.py:534
  36.8 16.3 %collective-permute-start.5 = (bf16[528,256]{1,0:T(8,128)(2,1)S(1)}, bf16[528,256]{1,0:T(8,128)(2,1)S(1)}, u32[]{:S(2)}, u32[]{:S(2)}) collective-permute-start(bf16[528,256]{1,0:T(8,128)(2,1)S(1)} %neg_tower.1.refs_4_), channel_id=1, source_target_pairs={{0,2},{1,3},{2,0},{3,1},{4,6},{5,7},{6,4},{7,5},{8,10},{9,11},{10,... | collective-permute-start | bytes 811016 | tf_op jit(solution)/shard_map/ppermute | solution.py:534
  36.8 16.3 %collective-permute-start.6 = (bf16[528,256]{1,0:T(8,128)(2,1)S(1)}, bf16[528,256]{1,0:T(8,128)(2,1)}, u32[]{:S(2)}, u32[]{:S(2)}) collective-permute-start(bf16[528,256]{1,0:T(8,128)(2,1)S(1)} %neg_tower.1.refs_4_), channel_id=1, source_target_pairs={{0,3},{1,2},{2,1},{3,0},{4,7},{5,6},{6,5},{7,4},{8,11},{9,10},{10,... | collective-permute-start | bytes 811016 | tf_op jit(solution)/shard_map/ppermute | solution.py:534
  50.2 3.5 %collective-permute-start = (bf16[32,640]{1,0:T(8,128)(2,1)S(1)}, bf16[32,640]{1,0:T(8,128)(2,1)S(1)}, u32[]{:S(2)}, u32[]{:S(2)}) collective-permute-start(bf16[32,640]{1,0:T(8,128)(2,1)S(1)} %get-tuple-element.20.refs_0_), channel_id=1, source_target_pairs={{0,8},{8,16},{16,24},{24,0},{1,9},{9,17},{17,25},{25,1},{2,10},{10... | collective-permute-start | bytes 122888 | tf_op jit(solution)/shard_map/ppermute | solution.py:538
  50.2 4.1 %collective-permute-start.1 = (bf16[32,640]{1,0:T(8,128)(2,1)S(1)}, bf16[32,640]{1,0:T(8,128)(2,1)S(1)}, u32[]{:S(2)}, u32[]{:S(2)}) collective-permute-start(bf16[32,640]{1,0:T(8,128)(2,1)S(1)} %get-tuple-element.20.refs_0_), channel_id=1, source_target_pairs={{0,16},{8,24},{16,0},{24,8},{1,17},{9,25},{17,1},{25,9},{2,18},{10... | collective-permute-start | bytes 122888 | tf_op jit(solution)/shard_map/ppermute | solution.py:538
  51.8 3.1 %collective-permute-start.2 = (bf16[32,640]{1,0:T(8,128)(2,1)S(1)}, bf16[32,640]{1,0:T(8,128)(2,1)S(1)}, u32[]{:S(2)}, u32[]{:S(2)}) collective-permute-start(bf16[32,640]{1,0:T(8,128)(2,1)S(1)} %get-tuple-element.20.refs_0_), channel_id=1, source_target_pairs={{0,24},{8,0},{16,8},{24,16},{1,25},{9,1},{17,9},{25,17},{2,26},{10... | collective-permute-start | bytes 122888 | tf_op jit(solution)/shard_map/ppermute | solution.py:538
  56.3 3.0 %collective-permute-start.9 = (f32[1,32]{1,0:T(1,128)S(1)}, f32[1,32]{1,0:T(1,128)S(1)}, u32[]{:S(2)}, u32[]{:S(2)}) collective-permute-start(f32[1,32]{1,0:T(1,128)S(1)} %get-tuple-element.25), channel_id=1, source_target_pairs={{0,8},{8,16},{16,24},{24,0},{1,9},{9,17},{17,25},{25,1},{2,10},{10... | collective-permute-start | bytes 392 | tf_op jit(solution)/shard_map/ppermute | solution.py:538
  57.0 3.6 %collective-permute-start.8 = (f32[1,32]{1,0:T(1,128)S(1)}, f32[1,32]{1,0:T(1,128)S(1)}, u32[]{:S(2)}, u32[]{:S(2)}) collective-permute-start(f32[1,32]{1,0:T(1,128)S(1)} %get-tuple-element.24), channel_id=1, source_target_pairs={{0,16},{8,24},{16,0},{24,8},{1,17},{9,25},{17,1},{25,9},{2,18},{10... | collective-permute-start | bytes 392 | tf_op jit(solution)/shard_map/ppermute | solution.py:538
  58.4 2.1 %collective-permute-start.7 = (f32[1,32]{1,0:T(1,128)S(1)}, f32[1,32]{1,0:T(1,128)S(1)}, u32[]{:S(2)}, u32[]{:S(2)}) collective-permute-start(f32[1,32]{1,0:T(1,128)S(1)} %get-tuple-element.23), channel_id=1, source_target_pairs={{0,24},{8,0},{16,8},{24,16},{1,25},{9,1},{17,9},{25,17},{2,26},{10... | collective-permute-start | bytes 392 | tf_op jit(solution)/shard_map/ppermute | solution.py:538

commit v9 on v8

--- a/solution.py
+++ b/solution.py
@@ -534,15 +534,18 @@
     return lax.ppermute(array, "pool", [(at, at ^ bit) for at in range(size)])
 
 
-def rotate_user(array, size, step):
-    return lax.ppermute(array, "user", [(at, (at + step) % size) for at in range(size)])
-
-
-def gather_negatives(own, size):
+def swap_user(array, size, mask):
+    return lax.ppermute(array, "user", [(at, at ^ mask) for at in range(size)])
+
+
+def gather_negatives(own, user_size, pool_size):
     pieces = [own]
-    for mask in range(1, size // 2):
-        pieces.append(swap_pool(own, size, mask))
-    return pieces
+    for mask in range(1, pool_size // 2):
+        pieces.append(swap_pool(own, pool_size, mask))
+    others = []
+    for piece in pieces:
+        others.append(swap_user(piece, user_size, 1))
+    return pieces + others
 
 
 def on_device(
@@ -584,7 +587,7 @@
         renumber, cap=fetch_table.shape[2], user_size=user_size, pool_size=pool_size
     )
     onehot, first, moved = prepare(renumbered, hist_index, length, route_init, outgoing.shape[0])
-    negs = gather_negatives(own_neg, pool_size)
+    negs = gather_negatives(own_neg, user_size, pool_size)
 
     interests, vec, positive = route(
         renumbered,
@@ -602,11 +605,14 @@
         label_ids.reshape(1, -1),
         label_counts.reshape(1, -1),
     )
-    vecs = [vec] + [rotate_user(vec, user_size, step) for step in range(1, user_size)]
+    away = range(2, user_size, 2)
+    vecs = [vec]
+    for mask in away:
+        vecs.append(swap_user(vec, user_size, mask))
     sums = negative_sums(vecs, negs)
     partition = jnp.exp(positive) + sums[0]
-    for step in range(1, user_size):
-        partition += rotate_user(sums[step], user_size, user_size - step)
+    for mask, one in zip(away, sums[1:]):
+        partition += swap_user(one, user_size, mask)
     user_loss = jnp.log(partition) - positive
     return (interests, user_loss.reshape(-1))
 

time: 61.6 us -> 72.1 us (1.17)
  waiting for transfers between devices: 21.8 us -> 34.6 us
  starting transfers between devices: 19.3 us -> 16.7 us
    ppermute x4, waiting for transfers between devices: 18.6 us -> 30.1 us  [swap_pool(): return lax.ppermute(array, 'pool', [(at, at ^ bit) for at in range(size)])]
    ppermute x6, starting transfers between devices: 5.63 us -> 3.05 us  [swap_user(): return lax.ppermute(array, 'user', [(at, at ^ mask) for at in range(size)])]
    ppermute x6, waiting for transfers between devices: 3.27 us -> 4.59 us  [swap_user(): return lax.ppermute(array, 'user', [(at, at ^ mask) for at in range(size)])]
  transfers between devices with their start and end apart: 11 -> 11, of which waited for: 6 -> 6; matrix products, arithmetic and copies ran while one was open for 0% -> 0% of each run, Pallas kernels for 24% -> 21%
where the time goes in v9:
time: 72.1 us; the launch traced here: 71.8 us
  waiting for transfers between devices  34.6 us (48%)
  Pallas kernels  19.2 us (27%)
  starting transfers between devices  16.7 us (23%)
    ppermute x4, waiting for transfers between devices, swap_pool(): return lax.ppermute(array, 'pool', [(at, at ^ bit) for at in range(size)])  30.1 us
    pallas_call x1, Pallas kernels, route(): pl.pallas_call(functools.partial(route_kernel, renumbered), in_specs=[INS...  7.94 us
    all_to_all x1, starting transfers between devices, on_device(): lax.all_to_all(outgoing.reshape(fetch_table.shape[0], fetch_table.shape[2...  7.33 us
    ppermute x4, starting transfers between devices, swap_pool(): return lax.ppermute(array, 'pool', [(at, at ^ bit) for at in range(size)])  6.29 us
    ppermute x6, waiting for transfers between devices, swap_user(): return lax.ppermute(array, 'user', [(at, at ^ mask) for at in range(size)])  4.59 us
    pallas_call x1, Pallas kernels, neg_tower(): pl.pallas_call(neg_kernel, in_specs=[INSIDE, INSIDE, OUTSIDE, OUTSIDE, OU...  3.68 us
    pallas_call x1, Pallas kernels, prepare(): pl.pallas_call(functools.partial(prepare_kernel, renumbered), in_specs=[O...  3.33 us
    ppermute x6, starting transfers between devices, swap_user(): return lax.ppermute(array, 'user', [(at, at ^ mask) for at in range(size)])  3.05 us
  transfers between devices with their start and end apart: 11, of which 6 were waited for; matrix products, arithmetic and copies ran while one was open for 0% of the time, Pallas kernels for 21%

profile of v9, /device:TPU:0, one launch (start us, length us, event | category | flops | bytes accessed | tf_op | source)
XLA Modules:
  0.0 71.8 jit_solution(17492926917523446138)
XLA Ops:
  0.6 2.3 %select_rows.1 = (bf16[512,512]{1,0:T(8,128)(2,1)}, bf16[144,512]{1,0:T(8,128)(2,1)S(1)}) custom-call(s32[1,16,32]{2,1,0:T(8,128)} %bitcast.15, bf16[512,512]{1,0:T(8,128)(2,1)} %rows.1, bf16[128,512]{1,0:T(8,128)(2,1)} %negs.1, s32[1,128]{1,0:T(1,128)} %bitcast.21, s32[1,128]{1,0:T(1,128)} %bitcast.22), custom_call_target="tpu_custom_call" | custom-call | tf_op jit(solution)/shard_map/select_rows/pallas_call | solution.py:175
  3.0 7.3 %all-to-all-start = ((bf16[32,16,512]{2,1,0:T(8,128)(2,1)}), bf16[32,16,512]{2,1,0:T(8,128)(2,1)S(1)}, u32[]{:S(2)}, u32[]{:S(2)}) async-start(bf16[32,16,512]{2,1,0:T(8,128)(2,1)} %bitcast.3), calls=%async_computation | async-start | bytes 1048576 | tf_op jit(solution)/shard_map/all_to_all | solution.py:575
  10.3 2.7 %collective-permute-start.1 = (bf16[144,512]{1,0:T(8,128)(2,1)S(1)}, bf16[144,512]{1,0:T(8,128)(2,1)S(1)}, u32[]{:S(2)}, u32[]{:S(2)}) collective-permute-start(bf16[144,512]{1,0:T(8,128)(2,1)S(1)} %get-tuple-element.19.own_ref), channel_id=1, source_target_pairs={{0,4},{1,5},{2,6},{3,7},{4,0},{5,1},{6,2},{7,3},{8,12},{9,13},{10,... | collective-permute-start | bytes 442376 | tf_op jit(solution)/shard_map/ppermute | solution.py:534
  13.1 18.5 %collective-permute-done.1.apart_ref = bf16[144,512]{1,0:T(8,128)(2,1)S(1)} collective-permute-done((bf16[144,512]{1,0:T(8,128)(2,1)S(1)}, bf16[144,512]{1,0:T(8,128)(2,1)S(1)}, u32[]{:S(2)}, u32[]{:S(2)}) %collective-permute-start.1) | collective-permute-done | bytes 147488 | tf_op jit(solution)/shard_map/ppermute | solution.py:534
  31.6 0.0 copy-start
  31.6 3.7 %neg_tower.1.refs_2_ = bf16[528,256]{1,0:T(8,128)(2,1)S(1)} custom-call(bf16[144,512]{1,0:T(8,128)(2,1)S(1)} %get-tuple-element.19.own_ref, bf16[144,512]{1,0:T(8,128)(2,1)S(1)} %collective-permute-done.1.apart_ref, bf16[512,2048]{1,0:T(8,128)(2,1)} %w_in.1, f32[1,2048]{1,0:T(1,128)} %bitcast.13, bf16[2048,512]{1,0:T(8,128)(2,1)} %w_out.3), custom_call_target="tpu_custom_call" | custom-call | tf_op jit(solution)/shard_map/neg_tower/pallas_call | solution.py:244
  35.3 1.5 %collective-permute-start.2 = (bf16[528,256]{1,0:T(8,128)(2,1)S(1)}, bf16[528,256]{1,0:T(8,128)(2,1)S(1)}, u32[]{:S(2)}, u32[]{:S(2)}) collective-permute-start(bf16[528,256]{1,0:T(8,128)(2,1)S(1)} %neg_tower.1.refs_2_), channel_id=1, source_target_pairs={{0,1},{1,0},{2,3},{3,2},{4,5},{5,4},{6,7},{7,6},{8,9},{9,8},{10,11... | collective-permute-start | bytes 811016 | tf_op jit(solution)/shard_map/ppermute | solution.py:534
  36.8 0.0 collective-permute-start.3
  36.8 2.0 %collective-permute-start.4 = (bf16[528,256]{1,0:T(8,128)(2,1)S(1)}, bf16[528,256]{1,0:T(8,128)(2,1)}, u32[]{:S(2)}, u32[]{:S(2)}) collective-permute-start(bf16[528,256]{1,0:T(8,128)(2,1)S(1)} %neg_tower.1.refs_2_), channel_id=1, source_target_pairs={{0,3},{1,2},{2,1},{3,0},{4,7},{5,6},{6,5},{7,4},{8,11},{9,10},{10,... | collective-permute-start | bytes 811016 | tf_op jit(solution)/shard_map/ppermute | solution.py:534
  38.9 0.0 collective-permute-start.5
  38.9 5.0 %collective-permute-done.2.refs_3_ = bf16[528,256]{1,0:T(8,128)(2,1)S(1)} collective-permute-done((bf16[528,256]{1,0:T(8,128)(2,1)S(1)}, bf16[528,256]{1,0:T(8,128)(2,1)S(1)}, u32[]{:S(2)}, u32[]{:S(2)}) %collective-permute-start.2) | collective-permute-done | bytes 270368 | tf_op jit(solution)/shard_map/ppermute | solution.py:534
  43.8 0.0 collective-permute-start.6
  43.8 2.4 %collective-permute-done.3.refs_4_ = bf16[528,256]{1,0:T(8,128)(2,1)S(1)} collective-permute-done((bf16[528,256]{1,0:T(8,128)(2,1)S(1)}, bf16[528,256]{1,0:T(8,128)(2,1)S(1)}, u32[]{:S(2)}, u32[]{:S(2)}) %collective-permute-start.3) | collective-permute-done | bytes 270368 | tf_op jit(solution)/shard_map/ppermute | solution.py:534
  46.2 0.0 collective-permute-start.7
  46.2 4.2 %collective-permute-done.4.refs_5_ = bf16[528,256]{1,0:T(8,128)(2,1)} collective-permute-done((bf16[528,256]{1,0:T(8,128)(2,1)S(1)}, bf16[528,256]{1,0:T(8,128)(2,1)}, u32[]{:S(2)}, u32[]{:S(2)}) %collective-permute-start.4) | collective-permute-done | bytes 270368 | tf_op jit(solution)/shard_map/ppermute | solution.py:534
  50.4 0.0 collective-permute-start.8
  50.4 3.3 %prepare.1 = (bf16[4,1024,256]{2,1,0:T(8,128)(2,1)}, f32[128,512]{1,0:T(8,128)}, s32[32,256]{1,0:T(8,128)}) custom-call(s32[32,256]{1,0:T(8,128)} %index.1, s32[1,32]{1,0:T(1,128)} %bitcast.16, f32[32,4,256]{2,1,0:T(4,128)} %init.3), custom_call_target="tpu_custom_call" | custom-call | tf_op jit(solution)/shard_map/prepare/pallas_call | solution.py:352
  53.7 0.0 all-to-all-done
  53.7 0.0 copy-done
  53.7 7.9 %route.1 = (f32[32,2048]{1,0:T(8,128)}, bf16[32,640]{1,0:T(8,128)(2,1)S(1)}, f32[1,32]{1,0:T(1,128)S(1)}) custom-call(bf16[512,512]{1,0:T(8,128)(2,1)S(1)} %bitcast.12, bf16[512,2048]{1,0:T(8,128)(2,1)S(1)} %copy-done, f32[1,2048]{1,0:T(1,128)} %bitcast.14, bf16[2048,512]{1,0:T(8,128)(2,1)} %w_out.3, bf16[512,512]{1,0:T(8,128)(2,1)} %bilinear.1, ...), custom_call_target="tpu_custom_call" | custom-call | tf_op jit(solution)/shard_map/route/pallas_call | solution.py:483
  61.7 1.6 %collective-permute-start = (bf16[32,640]{1,0:T(8,128)(2,1)S(1)}, bf16[32,640]{1,0:T(8,128)(2,1)S(1)}, u32[]{:S(2)}, u32[]{:S(2)}) collective-permute-start(bf16[32,640]{1,0:T(8,128)(2,1)S(1)} %get-tuple-element.18.refs_0_), channel_id=1, source_target_pairs={{0,16},{8,24},{16,0},{24,8},{1,17},{9,25},{17,1},{25,9},{2,18},{10... | collective-permute-start | bytes 122888 | tf_op jit(solution)/shard_map/ppermute | solution.py:538
  63.2 0.0 collective-permute-done.5.refs_6_
  63.2 0.0 collective-permute-done.6.refs_7_
  63.2 0.0 collective-permute-done.7.refs_8_
  63.3 0.0 collective-permute-done.8.refs_9_
  63.3 2.5 %collective-permute-done.refs_1_ = bf16[32,640]{1,0:T(8,128)(2,1)S(1)} collective-permute-done((bf16[32,640]{1,0:T(8,128)(2,1)S(1)}, bf16[32,640]{1,0:T(8,128)(2,1)S(1)}, u32[]{:S(2)}, u32[]{:S(2)}) %collective-permute-start) | collective-permute-done | bytes 40992 | tf_op jit(solution)/shard_map/ppermute | solution.py:538
  65.8 1.9 %negative_sums.1 = (f32[1,32]{1,0:T(1,128)S(1)}, f32[1,32]{1,0:T(1,128)S(1)}) custom-call(bf16[32,640]{1,0:T(8,128)(2,1)S(1)} %get-tuple-element.18.refs_0_, bf16[32,640]{1,0:T(8,128)(2,1)S(1)} %collective-permute-done.refs_1_, bf16[528,256]{1,0:T(8,128)(2,1)S(1)} %neg_tower.1.refs_2_, bf16[528,256]{1,0:T(8,128)(2,1)S(1)} %collective-permute-done.2.refs_3_, ...), custom_call_target="tpu_custom_call" | custom-call | tf_op jit(solution)/shard_map/negative_sums/pallas_call | solution.py:525
  67.7 1.5 %collective-permute-start.9 = (f32[1,32]{1,0:T(1,128)S(1)}, f32[1,32]{1,0:T(1,128)S(1)}, u32[]{:S(2)}, u32[]{:S(2)}) collective-permute-start(f32[1,32]{1,0:T(1,128)S(1)} %get-tuple-element.21), channel_id=1, source_target_pairs={{0,16},{8,24},{16,0},{24,8},{1,17},{9,25},{17,1},{25,9},{2,18},{10... | collective-permute-start | bytes 392 | tf_op jit(solution)/shard_map/ppermute | solution.py:538
  69.2 2.1 %collective-permute-done.9 = f32[1,32]{1,0:T(1,128)S(1)} collective-permute-done((f32[1,32]{1,0:T(1,128)S(1)}, f32[1,32]{1,0:T(1,128)S(1)}, u32[]{:S(2)}, u32[]{:S(2)}) %collective-permute-start.9) | collective-permute-done | bytes 160 | tf_op jit(solution)/shard_map/ppermute | solution.py:538
  71.3 0.5 subtract_bitcast_fusion
Async XLA Ops:
  3.0 50.7 %all-to-all-start = ((bf16[32,16,512]{2,1,0:T(8,128)(2,1)}), bf16[32,16,512]{2,1,0:T(8,128)(2,1)S(1)}, u32[]{:S(2)}, u32[]{:S(2)}) async-start(bf16[32,16,512]{2,1,0:T(8,128)(2,1)} %bitcast.3), calls=%async_computation | async-start | bytes 1048576 | tf_op jit(solution)/shard_map/all_to_all | solution.py:575
  10.3 21.3 %collective-permute-start.1 = (bf16[144,512]{1,0:T(8,128)(2,1)S(1)}, bf16[144,512]{1,0:T(8,128)(2,1)S(1)}, u32[]{:S(2)}, u32[]{:S(2)}) collective-permute-start(bf16[144,512]{1,0:T(8,128)(2,1)S(1)} %get-tuple-element.19.own_ref), channel_id=1, source_target_pairs={{0,4},{1,5},{2,6},{3,7},{4,0},{5,1},{6,2},{7,3},{8,12},{9,13},{10,... | collective-permute-start | bytes 442376 | tf_op jit(solution)/shard_map/ppermute | solution.py:534
  31.6 22.1 %copy-start = (bf16[512,2048]{1,0:T(8,128)(2,1)S(1)}, bf16[512,2048]{1,0:T(8,128)(2,1)}, u32[]{:S(2)}) copy-start(bf16[512,2048]{1,0:T(8,128)(2,1)} %w_in.1) | copy-start | bytes 6291460
  35.3 8.5 %collective-permute-start.2 = (bf16[528,256]{1,0:T(8,128)(2,1)S(1)}, bf16[528,256]{1,0:T(8,128)(2,1)S(1)}, u32[]{:S(2)}, u32[]{:S(2)}) collective-permute-start(bf16[528,256]{1,0:T(8,128)(2,1)S(1)} %neg_tower.1.refs_2_), channel_id=1, source_target_pairs={{0,1},{1,0},{2,3},{3,2},{4,5},{5,4},{6,7},{7,6},{8,9},{9,8},{10,11... | collective-permute-start | bytes 811016 | tf_op jit(solution)/shard_map/ppermute | solution.py:534
  36.8 9.4 %collective-permute-start.3 = (bf16[528,256]{1,0:T(8,128)(2,1)S(1)}, bf16[528,256]{1,0:T(8,128)(2,1)S(1)}, u32[]{:S(2)}, u32[]{:S(2)}) collective-permute-start(bf16[528,256]{1,0:T(8,128)(2,1)S(1)} %neg_tower.1.refs_2_), channel_id=1, source_target_pairs={{0,2},{1,3},{2,0},{3,1},{4,6},{5,7},{6,4},{7,5},{8,10},{9,11},{10,... | collective-permute-start | bytes 811016 | tf_op jit(solution)/shard_map/ppermute | solution.py:534
  36.8 13.5 %collective-permute-start.4 = (bf16[528,256]{1,0:T(8,128)(2,1)S(1)}, bf16[528,256]{1,0:T(8,128)(2,1)}, u32[]{:S(2)}, u32[]{:S(2)}) collective-permute-start(bf16[528,256]{1,0:T(8,128)(2,1)S(1)} %neg_tower.1.refs_2_), channel_id=1, source_target_pairs={{0,3},{1,2},{2,1},{3,0},{4,7},{5,6},{6,5},{7,4},{8,11},{9,10},{10,... | collective-permute-start | bytes 811016 | tf_op jit(solution)/shard_map/ppermute | solution.py:534
  38.9 24.4 %collective-permute-start.5 = (bf16[528,256]{1,0:T(8,128)(2,1)S(1)}, bf16[528,256]{1,0:T(8,128)(2,1)}, u32[]{:S(2)}, u32[]{:S(2)}) collective-permute-start(bf16[528,256]{1,0:T(8,128)(2,1)S(1)} %neg_tower.1.refs_2_), channel_id=1, source_target_pairs={{0,8},{8,0},{16,24},{24,16},{1,9},{9,1},{17,25},{25,17},{2,10},{10... | collective-permute-start | bytes 811016 | tf_op jit(solution)/shard_map/ppermute | solution.py:538
  43.8 19.4 %collective-permute-start.6 = (bf16[528,256]{1,0:T(8,128)(2,1)S(1)}, bf16[528,256]{1,0:T(8,128)(2,1)}, u32[]{:S(2)}, u32[]{:S(2)}) collective-permute-start(bf16[528,256]{1,0:T(8,128)(2,1)S(1)} %collective-permute-done.2.refs_3_), channel_id=1, source_target_pairs={{0,8},{8,0},{16,24},{24,16},{1,9},{9,1},{17,25},{25,17},{2,10},{10... | collective-permute-start | bytes 811016 | tf_op jit(solution)/shard_map/ppermute | solution.py:538
  46.2 17.1 %collective-permute-start.7 = (bf16[528,256]{1,0:T(8,128)(2,1)S(1)}, bf16[528,256]{1,0:T(8,128)(2,1)}, u32[]{:S(2)}, u32[]{:S(2)}) collective-permute-start(bf16[528,256]{1,0:T(8,128)(2,1)S(1)} %collective-permute-done.3.refs_4_), channel_id=1, source_target_pairs={{0,8},{8,0},{16,24},{24,16},{1,9},{9,1},{17,25},{25,17},{2,10},{10... | collective-permute-start | bytes 811016 | tf_op jit(solution)/shard_map/ppermute | solution.py:538
  50.4 12.9 %collective-permute-start.8 = (bf16[528,256]{1,0:T(8,128)(2,1)}, bf16[528,256]{1,0:T(8,128)(2,1)}, u32[]{:S(2)}, u32[]{:S(2)}) collective-permute-start(bf16[528,256]{1,0:T(8,128)(2,1)} %collective-permute-done.4.refs_5_), channel_id=1, source_target_pairs={{0,8},{8,0},{16,24},{24,16},{1,9},{9,1},{17,25},{25,17},{2,10},{10... | collective-permute-start | bytes 811016 | tf_op jit(solution)/shard_map/ppermute | solution.py:538
  61.7 4.1 %collective-permute-start = (bf16[32,640]{1,0:T(8,128)(2,1)S(1)}, bf16[32,640]{1,0:T(8,128)(2,1)S(1)}, u32[]{:S(2)}, u32[]{:S(2)}) collective-permute-start(bf16[32,640]{1,0:T(8,128)(2,1)S(1)} %get-tuple-element.18.refs_0_), channel_id=1, source_target_pairs={{0,16},{8,24},{16,0},{24,8},{1,17},{9,25},{17,1},{25,9},{2,18},{10... | collective-permute-start | bytes 122888 | tf_op jit(solution)/shard_map/ppermute | solution.py:538
  67.7 3.6 %collective-permute-start.9 = (f32[1,32]{1,0:T(1,128)S(1)}, f32[1,32]{1,0:T(1,128)S(1)}, u32[]{:S(2)}, u32[]{:S(2)}) collective-permute-start(f32[1,32]{1,0:T(1,128)S(1)} %get-tuple-element.21), channel_id=1, source_target_pairs={{0,16},{8,24},{16,0},{24,8},{1,17},{9,25},{17,1},{25,9},{2,18},{10... | collective-permute-start | bytes 392 | tf_op jit(solution)/shard_map/ppermute | solution.py:538

commit v10 on v9

--- a/solution.py
+++ b/solution.py
@@ -191,23 +191,12 @@
     )(*[far(one) for one in (fetch.transpose(1, 2, 0), rows, negs, ids, counts)])
 
 
-def tower(rows_ref, w_in_ref, bias, w_out, bias_ref, out_ref, sems, parts=None):
+def tower(rows_ref, w_in_ref, bias, w_out, bias_ref, out_ref, sems):
     small = Copies(bias, bias_ref, sems, 0, 1)
     large = Copies(w_out, out_ref, sems, 1, SPLIT)
-    if parts is None:
-        hidden = mm(rows_ref[...], w_in_ref[...])
-        small.wait()
-        hidden = jnp.maximum(hidden + bias_ref[...], 0.0).astype(bf16)
-    else:
-        small.wait()
-        pieces = []
-        for at, part in enumerate(parts):
-            part.wait()
-            size = w_in_ref.shape[1] // len(parts)
-            cut = slice(at * size, (at + 1) * size)
-            piece = mm(rows_ref[...], w_in_ref[:, cut]) + bias_ref[:, cut]
-            pieces.append(jnp.maximum(piece, 0.0).astype(bf16))
-        hidden = jnp.concatenate(pieces, axis=1)
+    hidden = mm(rows_ref[...], w_in_ref[...])
+    small.wait()
+    hidden = jnp.maximum(hidden + bias_ref[...], 0.0).astype(bf16)
     large.wait()
     embedding = mm(hidden, out_ref[...])
     total = jnp.sum(embedding * embedding, axis=1, keepdims=True)
@@ -215,42 +204,34 @@
 
 
 def neg_kernel(
-    own_ref, apart_ref, w_in, bias, w_out, out_ref, rows_ref, w_in_ref, bias_ref, w_out_ref, sems
+    own_ref, apart_ref, w_in_ref, bias, w_out, out_ref, rows_ref, bias_ref, w_out_ref, sems
 ):
-    size = w_in.shape[1] // SPLIT
-    parts = [
-        pltpu.make_async_copy(
-            w_in.at[:, pl.ds(at * size, size)],
-            w_in_ref.at[:, pl.ds(at * size, size)],
-            sems.at[1 + SPLIT + at],
-        )
-        for at in range(SPLIT)
-    ]
-    for part in parts:
-        part.start()
     count = rows_ref.shape[0] // 2
     rows_ref[:count, :] = own_ref[:count, :]
     rows_ref[count:, :] = apart_ref[:count, :]
-    unit = tower(rows_ref, w_in_ref, bias, w_out, bias_ref, w_out_ref, sems, parts)
+    unit = tower(rows_ref, w_in_ref, bias, w_out, bias_ref, w_out_ref, sems)
     width = unit.shape[1]
     out_ref[:width, :] = unit.T.astype(bf16)
     out_ref[width:, :count] = own_ref[count:, :count]
     out_ref[width:, count:] = apart_ref[count:, :count]
 
 
-def neg_tower(own, apart, weights):
+def neg_tower(own, apart, w_in, bias, w_out):
     count = own.shape[0] - EXTRA
     width = own.shape[1]
     return pl.pallas_call(
         neg_kernel,
-        in_specs=[INSIDE, INSIDE, OUTSIDE, OUTSIDE, OUTSIDE],
+        in_specs=[INSIDE, INSIDE, INSIDE, OUTSIDE, OUTSIDE],
         out_shape=pltpu.VMEM((width + EXTRA, 2 * count), bf16),
-        scratch_shapes=[pltpu.VMEM((2 * count, width), bf16)]
-        + [pltpu.VMEM(one.shape, one.dtype) for one in weights]
-        + [pltpu.SemaphoreType.DMA((1 + 2 * SPLIT,))],
+        scratch_shapes=[
+            pltpu.VMEM((2 * count, width), bf16),
+            pltpu.VMEM(bias.shape, f32),
+            pltpu.VMEM(w_out.shape, bf16),
+            pltpu.SemaphoreType.DMA((1 + SPLIT,)),
+        ],
         compiler_params=PARAMS,
         name="neg_tower",
-    )(near(own), near(apart), *[far(one) for one in weights])
+    )(near(own), near(apart), near(w_in), far(bias), far(w_out))
 
 
 def event_weights(logits, live):
@@ -302,9 +283,11 @@
     index,
     length,
     init,
+    w_in,
     onehot,
     slots,
     moved,
+    w_in_ref,
     index_ref,
     length_ref,
     init_ref,
@@ -317,6 +300,7 @@
     copies = [Copies(*pair, sems, at, 1) for at, pair in enumerate(pairs)]
     users, events = index_ref.shape
     groups = users // GROUP_USERS
+    weight = Copies(w_in, w_in_ref, sems, 5 + groups, SPLIT)
     copies[0].wait()
     index = renumbered(index_ref[...])
     moved_ref[...] = index
@@ -340,23 +324,25 @@
     weights = event_weights([init_ref[:, k, :] for k in range(INTERESTS)], live)
     scatter_weights(weights, upper, onehot_ref, slot_ref)
     back.append(Copies(slot_ref, slots, sems, 4, 1))
+    back.append(weight)
     for one in back:
         one.wait()
 
 
-def prepare(renumbered, index, length, init, slots):
+def prepare(renumbered, index, length, init, w_in, slots):
     users, events = index.shape
     groups = users // GROUP_USERS
     onehot = (groups, GROUP_USERS // 2 * events, 2 * LANES)
     first = (INTERESTS * users, slots)
     return pl.pallas_call(
         functools.partial(prepare_kernel, renumbered),
-        in_specs=[OUTSIDE] * 3,
-        out_specs=[OUTSIDE] * 3,
+        in_specs=[OUTSIDE] * 4,
+        out_specs=[OUTSIDE] * 3 + [INSIDE],
         out_shape=[
             pltpu.HBM(onehot, bf16),
             pltpu.HBM(first, f32),
             pltpu.HBM(index.shape, i32),
+            pltpu.VMEM(w_in.shape, bf16),
         ],
         scratch_shapes=[
             pltpu.VMEM(index.shape, i32),
@@ -365,11 +351,11 @@
             pltpu.VMEM(onehot, bf16),
             pltpu.VMEM(first, f32),
             pltpu.VMEM(index.shape, i32),
-            pltpu.SemaphoreType.DMA((5 + groups,)),
+            pltpu.SemaphoreType.DMA((5 + groups + SPLIT,)),
         ],
         compiler_params=PARAMS,
         name="prepare",
-    )(far(index), far(length), far(init))
+    )(far(index), far(length), far(init), far(w_in))
 
 
 def route_kernel(
@@ -534,14 +520,32 @@
     return lax.ppermute(array, "pool", [(at, at ^ bit) for at in range(size)])
 
 
+def late_masks(pool_size):
+    return range(2, pool_size // 2, 2)
+
+
 def swap_user(array, size, mask):
     return lax.ppermute(array, "user", [(at, at ^ mask) for at in range(size)])
 
 
+def swap_both(array, user_size, pool_size, user_mask, pool_mask):
+    perm = [
+        (user * pool_size + pool, (user ^ user_mask) * pool_size + (pool ^ pool_mask))
+        for user in range(user_size)
+        for pool in range(pool_size)
+    ]
+    return lax.ppermute(array, ("user", "pool"), perm)
+
+
+def piece_masks(user_size):
+    masks = [(user, pool) for user in range(0, user_size, 2) for pool in (0, 1)]
+    return masks[:0:-1]
+
+
 def gather_negatives(own, user_size, pool_size):
     pieces = [own]
-    for mask in range(1, pool_size // 2):
-        pieces.append(swap_pool(own, pool_size, mask))
+    for user, pool in piece_masks(user_size):
+        pieces.append(swap_both(own, user_size, pool_size, user, pool))
     others = []
     for piece in pieces:
         others.append(swap_user(piece, user_size, 1))
@@ -567,7 +571,6 @@
     neg_ids,
     neg_counts,
 ):
-    weights = (w_in, bias_in.reshape(1, -1), w_out)
     outgoing, packed = select_rows(
         user_size, pool_size, fetch_table, item_feats, neg_feats, neg_ids.reshape(1, -1), neg_counts.reshape(1, -1)
     )
@@ -581,12 +584,14 @@
     )
     arrived = arrived.reshape(outgoing.shape)
 
-    own_neg = neg_tower(packed, apart, weights)
     length = hist_len.reshape(1, -1)
     renumbered = functools.partial(
         renumber, cap=fetch_table.shape[2], user_size=user_size, pool_size=pool_size
     )
-    onehot, first, moved = prepare(renumbered, hist_index, length, route_init, outgoing.shape[0])
+    onehot, first, moved, w_in = prepare(
+        renumbered, hist_index, length, route_init, w_in, outgoing.shape[0]
+    )
+    own_neg = neg_tower(packed, apart, w_in, bias_in.reshape(1, -1), w_out)
     negs = gather_negatives(own_neg, user_size, pool_size)
 
     interests, vec, positive = route(
@@ -605,14 +610,14 @@
         label_ids.reshape(1, -1),
         label_counts.reshape(1, -1),
     )
-    away = range(2, user_size, 2)
+    away = late_masks(pool_size)
     vecs = [vec]
     for mask in away:
-        vecs.append(swap_user(vec, user_size, mask))
+        vecs.append(swap_pool(vec, pool_size, mask))
     sums = negative_sums(vecs, negs)
     partition = jnp.exp(positive) + sums[0]
     for mask, one in zip(away, sums[1:]):
-        partition += swap_user(one, user_size, mask)
+        partition += swap_pool(one, pool_size, mask)
     user_loss = jnp.log(partition) - positive
     return (interests, user_loss.reshape(-1))
 

time: 72.1 us -> 67.7 us (0.939)
  starting transfers between devices: 16.7 us -> 14.2 us
  Pallas kernels: 19.2 us -> 18 us
    ppermute x0 -> x3, waiting for transfers between devices: none -> 11.2 us  [swap_both(): return lax.ppermute(array, ('user', 'pool'), perm)]
    ppermute x4 -> x3, waiting for transfers between devices: 30.1 us -> 22.7 us  [swap_pool(): return lax.ppermute(array, 'pool', [(at, at ^ bit) for at in range(size)])]
    ppermute x6 -> x4, waiting for transfers between devices: 4.59 us -> 0.01 us  [swap_user(): return lax.ppermute(array, 'user', [(at, at ^ mask) for at in range(size)])]
    ppermute x0 -> x3, starting transfers between devices: none -> 3.55 us  [swap_both(): return lax.ppermute(array, ('user', 'pool'), perm)]
    ppermute x4 -> x3, starting transfers between devices: 6.29 us -> 2.82 us  [swap_pool(): return lax.ppermute(array, 'pool', [(at, at ^ bit) for at in range(size)])]
    ppermute x6 -> x4, starting transfers between devices: 3.05 us -> 0.46 us  [swap_user(): return lax.ppermute(array, 'user', [(at, at ^ mask) for at in range(size)])]
    pallas_call x1, Pallas kernels: 3.68 us -> 2.45 us  [neg_tower(): pl.pallas_call(neg_kernel, in_specs=[INSIDE, INSIDE, INSIDE, OUTSIDE, OUT...]
  transfers between devices with their start and end apart: 11 -> 11, of which waited for: 6 -> 6; matrix products, arithmetic and copies ran while one was open for 0% -> 0% of each run, Pallas kernels for 21% -> 20%
where the time goes in v10:
time: 67.7 us; the launch traced here: 67.3 us
  waiting for transfers between devices  33.9 us (50%)
  Pallas kernels  18 us (27%)
  starting transfers between devices  14.2 us (21%)
  between operations  0.73 us (1%)
    ppermute x3, waiting for transfers between devices, swap_pool(): return lax.ppermute(array, 'pool', [(at, at ^ bit) for at in range(size)])  22.7 us
    ppermute x3, waiting for transfers between devices, swap_both(): return lax.ppermute(array, ('user', 'pool'), perm)  11.2 us
    pallas_call x1, Pallas kernels, route(): pl.pallas_call(functools.partial(route_kernel, renumbered), in_specs=[INS...  7.91 us
    all_to_all x1, starting transfers between devices, on_device(): lax.all_to_all(outgoing.reshape(fetch_table.shape[0], fetch_table.shape[2...  7.33 us
    ppermute x3, starting transfers between devices, swap_both(): return lax.ppermute(array, ('user', 'pool'), perm)  3.55 us
    pallas_call x1, Pallas kernels, prepare(): pl.pallas_call(functools.partial(prepare_kernel, renumbered), in_specs=[O...  3.37 us
    ppermute x3, starting transfers between devices, swap_pool(): return lax.ppermute(array, 'pool', [(at, at ^ bit) for at in range(size)])  2.82 us
    pallas_call x1, Pallas kernels, neg_tower(): pl.pallas_call(neg_kernel, in_specs=[INSIDE, INSIDE, INSIDE, OUTSIDE, OUT...  2.45 us
  transfers between devices with their start and end apart: 11, of which 6 were waited for; matrix products, arithmetic and copies ran while one was open for 0% of the time, Pallas kernels for 20%

profile of v10, /device:TPU:0, one launch (start us, length us, event | category | flops | bytes accessed | tf_op | source)
XLA Modules:
  0.0 67.3 jit_solution(13740014993446134979)
XLA Ops:
  0.6 2.4 %select_rows.1 = (bf16[512,512]{1,0:T(8,128)(2,1)}, bf16[144,512]{1,0:T(8,128)(2,1)S(1)}) custom-call(s32[1,16,32]{2,1,0:T(8,128)} %bitcast.15, bf16[512,512]{1,0:T(8,128)(2,1)} %rows.1, bf16[128,512]{1,0:T(8,128)(2,1)} %negs.1, s32[1,128]{1,0:T(1,128)} %bitcast.21, s32[1,128]{1,0:T(1,128)} %bitcast.22), custom_call_target="tpu_custom_call" | custom-call | tf_op jit(solution)/shard_map/select_rows/pallas_call | solution.py:175
  3.0 7.3 %all-to-all-start = ((bf16[32,16,512]{2,1,0:T(8,128)(2,1)}), bf16[32,16,512]{2,1,0:T(8,128)(2,1)S(1)}, u32[]{:S(2)}, u32[]{:S(2)}) async-start(bf16[32,16,512]{2,1,0:T(8,128)(2,1)} %bitcast.3), calls=%async_computation | async-start | bytes 1048576 | tf_op jit(solution)/shard_map/all_to_all | solution.py:578
  10.3 2.7 %collective-permute-start.1 = (bf16[144,512]{1,0:T(8,128)(2,1)S(1)}, bf16[144,512]{1,0:T(8,128)(2,1)S(1)}, u32[]{:S(2)}, u32[]{:S(2)}) collective-permute-start(bf16[144,512]{1,0:T(8,128)(2,1)S(1)} %get-tuple-element.21.own_ref), channel_id=1, source_target_pairs={{0,4},{1,5},{2,6},{3,7},{4,0},{5,1},{6,2},{7,3},{8,12},{9,13},{10,... | collective-permute-start | bytes 442376 | tf_op jit(solution)/shard_map/ppermute | solution.py:520
  13.1 3.4 %prepare.1 = (bf16[4,1024,256]{2,1,0:T(8,128)(2,1)}, f32[128,512]{1,0:T(8,128)}, s32[32,256]{1,0:T(8,128)}, bf16[512,2048]{1,0:T(8,128)(2,1)S(1)}) custom-call(s32[32,256]{1,0:T(8,128)} %index.1, s32[1,32]{1,0:T(1,128)} %bitcast.16, f32[32,4,256]{2,1,0:T(4,128)} %init.3, bf16[512,2048]{1,0:T(8,128)(2,1)} %w_in.1), custom_call_target="tpu_custom_call" | custom-call | tf_op jit(solution)/shard_map/prepare/pallas_call | solution.py:337
  16.5 15.2 %collective-permute-done.1.apart_ref = bf16[144,512]{1,0:T(8,128)(2,1)S(1)} collective-permute-done((bf16[144,512]{1,0:T(8,128)(2,1)S(1)}, bf16[144,512]{1,0:T(8,128)(2,1)S(1)}, u32[]{:S(2)}, u32[]{:S(2)}) %collective-permute-start.1) | collective-permute-done | bytes 147488 | tf_op jit(solution)/shard_map/ppermute | solution.py:520
  31.6 2.4 %neg_tower.1.refs_2_ = bf16[528,256]{1,0:T(8,128)(2,1)S(1)} custom-call(bf16[144,512]{1,0:T(8,128)(2,1)S(1)} %get-tuple-element.21.own_ref, bf16[144,512]{1,0:T(8,128)(2,1)S(1)} %collective-permute-done.1.apart_ref, bf16[512,2048]{1,0:T(8,128)(2,1)S(1)} %get-tuple-element.14.w_in_ref, f32[1,2048]{1,0:T(1,128)} %bitcast.13, bf16[2048,512]{1,0:T(8,128)(2,1)} %w_out.3), custom_call_target="tpu_custom_call" | custom-call | tf_op jit(solution)/shard_map/neg_tower/pallas_call | solution.py:222
  34.1 2.5 %collective-permute-start.2 = (bf16[528,256]{1,0:T(8,128)(2,1)S(1)}, bf16[528,256]{1,0:T(8,128)(2,1)S(1)}, u32[]{:S(2)}, u32[]{:S(2)}) collective-permute-start(bf16[528,256]{1,0:T(8,128)(2,1)S(1)} %neg_tower.1.refs_2_), channel_id=1, source_target_pairs={{0,17},{1,16},{2,19},{3,18},{4,21},{5,20},{6,23},{7,22},{8,25},{9,... | collective-permute-start | bytes 811016 | tf_op jit(solution)/shard_map/ppermute | solution.py:537
  36.5 0.5 collective-permute-start.3
  37.1 0.6 collective-permute-start.4
  37.6 0.0 collective-permute-start.5
  37.6 6.8 %collective-permute-done.2.refs_3_ = bf16[528,256]{1,0:T(8,128)(2,1)S(1)} collective-permute-done((bf16[528,256]{1,0:T(8,128)(2,1)S(1)}, bf16[528,256]{1,0:T(8,128)(2,1)S(1)}, u32[]{:S(2)}, u32[]{:S(2)}) %collective-permute-start.2) | collective-permute-done | bytes 270368 | tf_op jit(solution)/shard_map/ppermute | solution.py:537
  44.4 0.0 collective-permute-start.6
  44.4 4.3 %collective-permute-done.3.refs_4_ = bf16[528,256]{1,0:T(8,128)(2,1)S(1)} collective-permute-done((bf16[528,256]{1,0:T(8,128)(2,1)S(1)}, bf16[528,256]{1,0:T(8,128)(2,1)S(1)}, u32[]{:S(2)}, u32[]{:S(2)}) %collective-permute-start.3) | collective-permute-done | bytes 270368 | tf_op jit(solution)/shard_map/ppermute | solution.py:537
  48.8 0.1 collective-permute-start.7
  48.9 0.1 collective-permute-done.4.refs_5_
  48.9 0.3 collective-permute-start.8
  49.3 0.0 all-to-all-done
  49.3 7.9 %route.1 = (f32[32,2048]{1,0:T(8,128)}, bf16[32,640]{1,0:T(8,128)(2,1)S(1)}, f32[1,32]{1,0:T(1,128)S(1)}) custom-call(bf16[512,512]{1,0:T(8,128)(2,1)S(1)} %bitcast.12, bf16[512,2048]{1,0:T(8,128)(2,1)S(1)} %get-tuple-element.14.w_in_ref, f32[1,2048]{1,0:T(1,128)} %bitcast.14, bf16[2048,512]{1,0:T(8,128)(2,1)} %w_out.3, bf16[512,512]{1,0:T(8,128)(2,1)} %bilinear.1, ...), custom_call_target="tpu_custom_call" | custom-call | tf_op jit(solution)/shard_map/route/pallas_call | solution.py:469
  57.2 0.1 collective-permute-start
  57.3 0.0 collective-permute-done.5.refs_6_
  57.3 0.0 collective-permute-done.6.refs_7_
  57.3 0.0 collective-permute-done.7.refs_8_
  57.3 0.0 collective-permute-done.8.refs_9_
  57.3 3.9 %collective-permute-done.refs_1_ = bf16[32,640]{1,0:T(8,128)(2,1)S(1)} collective-permute-done((bf16[32,640]{1,0:T(8,128)(2,1)S(1)}, bf16[32,640]{1,0:T(8,128)(2,1)S(1)}, u32[]{:S(2)}, u32[]{:S(2)}) %collective-permute-start) | collective-permute-done | bytes 40992 | tf_op jit(solution)/shard_map/ppermute | solution.py:520
  61.3 1.9 %negative_sums.1 = (f32[1,32]{1,0:T(1,128)S(1)}, f32[1,32]{1,0:T(1,128)S(1)}) custom-call(bf16[32,640]{1,0:T(8,128)(2,1)S(1)} %get-tuple-element.20.refs_0_, bf16[32,640]{1,0:T(8,128)(2,1)S(1)} %collective-permute-done.refs_1_, bf16[528,256]{1,0:T(8,128)(2,1)S(1)} %neg_tower.1.refs_2_, bf16[528,256]{1,0:T(8,128)(2,1)S(1)} %collective-permute-done.2.refs_3_, ...), custom_call_target="tpu_custom_call" | custom-call | tf_op jit(solution)/shard_map/negative_sums/pallas_call | solution.py:511
  63.2 0.0 collective-permute-start.9
  63.2 3.6 %collective-permute-done.9 = f32[1,32]{1,0:T(1,128)S(1)} collective-permute-done((f32[1,32]{1,0:T(1,128)S(1)}, f32[1,32]{1,0:T(1,128)S(1)}, u32[]{:S(2)}, u32[]{:S(2)}) %collective-permute-start.9) | collective-permute-done | bytes 160 | tf_op jit(solution)/shard_map/ppermute | solution.py:520
  66.8 0.5 subtract_bitcast_fusion
Async XLA Ops:
  3.0 46.3 %all-to-all-start = ((bf16[32,16,512]{2,1,0:T(8,128)(2,1)}), bf16[32,16,512]{2,1,0:T(8,128)(2,1)S(1)}, u32[]{:S(2)}, u32[]{:S(2)}) async-start(bf16[32,16,512]{2,1,0:T(8,128)(2,1)} %bitcast.3), calls=%async_computation | async-start | bytes 1048576 | tf_op jit(solution)/shard_map/all_to_all | solution.py:578
  10.3 21.3 %collective-permute-start.1 = (bf16[144,512]{1,0:T(8,128)(2,1)S(1)}, bf16[144,512]{1,0:T(8,128)(2,1)S(1)}, u32[]{:S(2)}, u32[]{:S(2)}) collective-permute-start(bf16[144,512]{1,0:T(8,128)(2,1)S(1)} %get-tuple-element.21.own_ref), channel_id=1, source_target_pairs={{0,4},{1,5},{2,6},{3,7},{4,0},{5,1},{6,2},{7,3},{8,12},{9,13},{10,... | collective-permute-start | bytes 442376 | tf_op jit(solution)/shard_map/ppermute | solution.py:520
  34.1 10.4 %collective-permute-start.2 = (bf16[528,256]{1,0:T(8,128)(2,1)S(1)}, bf16[528,256]{1,0:T(8,128)(2,1)S(1)}, u32[]{:S(2)}, u32[]{:S(2)}) collective-permute-start(bf16[528,256]{1,0:T(8,128)(2,1)S(1)} %neg_tower.1.refs_2_), channel_id=1, source_target_pairs={{0,17},{1,16},{2,19},{3,18},{4,21},{5,20},{6,23},{7,22},{8,25},{9,... | collective-permute-start | bytes 811016 | tf_op jit(solution)/shard_map/ppermute | solution.py:537
  36.5 12.2 %collective-permute-start.3 = (bf16[528,256]{1,0:T(8,128)(2,1)S(1)}, bf16[528,256]{1,0:T(8,128)(2,1)S(1)}, u32[]{:S(2)}, u32[]{:S(2)}) collective-permute-start(bf16[528,256]{1,0:T(8,128)(2,1)S(1)} %neg_tower.1.refs_2_), channel_id=1, source_target_pairs={{0,16},{1,17},{2,18},{3,19},{4,20},{5,21},{6,22},{7,23},{8,24},{9,... | collective-permute-start | bytes 811016 | tf_op jit(solution)/shard_map/ppermute | solution.py:537
  37.1 11.9 %collective-permute-start.4 = (bf16[528,256]{1,0:T(8,128)(2,1)S(1)}, bf16[528,256]{1,0:T(8,128)(2,1)}, u32[]{:S(2)}, u32[]{:S(2)}) collective-permute-start(bf16[528,256]{1,0:T(8,128)(2,1)S(1)} %neg_tower.1.refs_2_), channel_id=1, source_target_pairs={{0,1},{1,0},{2,3},{3,2},{4,5},{5,4},{6,7},{7,6},{8,9},{9,8},{10,11... | collective-permute-start | bytes 811016 | tf_op jit(solution)/shard_map/ppermute | solution.py:537
  37.6 19.6 %collective-permute-start.5 = (bf16[528,256]{1,0:T(8,128)(2,1)S(1)}, bf16[528,256]{1,0:T(8,128)(2,1)}, u32[]{:S(2)}, u32[]{:S(2)}) collective-permute-start(bf16[528,256]{1,0:T(8,128)(2,1)S(1)} %neg_tower.1.refs_2_), channel_id=1, source_target_pairs={{0,8},{8,0},{16,24},{24,16},{1,9},{9,1},{17,25},{25,17},{2,10},{10... | collective-permute-start | bytes 811016 | tf_op jit(solution)/shard_map/ppermute | solution.py:528
  44.4 12.9 %collective-permute-start.6 = (bf16[528,256]{1,0:T(8,128)(2,1)S(1)}, bf16[528,256]{1,0:T(8,128)(2,1)}, u32[]{:S(2)}, u32[]{:S(2)}) collective-permute-start(bf16[528,256]{1,0:T(8,128)(2,1)S(1)} %collective-permute-done.2.refs_3_), channel_id=1, source_target_pairs={{0,8},{8,0},{16,24},{24,16},{1,9},{9,1},{17,25},{25,17},{2,10},{10... | collective-permute-start | bytes 811016 | tf_op jit(solution)/shard_map/ppermute | solution.py:528
  48.8 8.5 %collective-permute-start.7 = (bf16[528,256]{1,0:T(8,128)(2,1)S(1)}, bf16[528,256]{1,0:T(8,128)(2,1)}, u32[]{:S(2)}, u32[]{:S(2)}) collective-permute-start(bf16[528,256]{1,0:T(8,128)(2,1)S(1)} %collective-permute-done.3.refs_4_), channel_id=1, source_target_pairs={{0,8},{8,0},{16,24},{24,16},{1,9},{9,1},{17,25},{25,17},{2,10},{10... | collective-permute-start | bytes 811016 | tf_op jit(solution)/shard_map/ppermute | solution.py:528
  48.9 8.4 %collective-permute-start.8 = (bf16[528,256]{1,0:T(8,128)(2,1)}, bf16[528,256]{1,0:T(8,128)(2,1)}, u32[]{:S(2)}, u32[]{:S(2)}) collective-permute-start(bf16[528,256]{1,0:T(8,128)(2,1)} %collective-permute-done.4.refs_5_), channel_id=1, source_target_pairs={{0,8},{8,0},{16,24},{24,16},{1,9},{9,1},{17,25},{25,17},{2,10},{10... | collective-permute-start | bytes 811016 | tf_op jit(solution)/shard_map/ppermute | solution.py:528
  57.2 4.1 %collective-permute-start = (bf16[32,640]{1,0:T(8,128)(2,1)S(1)}, bf16[32,640]{1,0:T(8,128)(2,1)S(1)}, u32[]{:S(2)}, u32[]{:S(2)}) collective-permute-start(bf16[32,640]{1,0:T(8,128)(2,1)S(1)} %get-tuple-element.20.refs_0_), channel_id=1, source_target_pairs={{0,2},{1,3},{2,0},{3,1},{4,6},{5,7},{6,4},{7,5},{8,10},{9,11},{10,... | collective-permute-start | bytes 122888 | tf_op jit(solution)/shard_map/ppermute | solution.py:520
  63.2 3.6 %collective-permute-start.9 = (f32[1,32]{1,0:T(1,128)S(1)}, f32[1,32]{1,0:T(1,128)S(1)}, u32[]{:S(2)}, u32[]{:S(2)}) collective-permute-start(f32[1,32]{1,0:T(1,128)S(1)} %get-tuple-element.23), channel_id=1, source_target_pairs={{0,2},{1,3},{2,0},{3,1},{4,6},{5,7},{6,4},{7,5},{8,10},{9,11},{10,... | collective-permute-start | bytes 392 | tf_op jit(solution)/shard_map/ppermute | solution.py:520

commit v11 on v10

--- a/solution.py
+++ b/solution.py
@@ -14,6 +14,7 @@
 SUB = 8
 EXTRA = 16
 SPLIT = 4
+HALVES = 2
 GROUP_USERS = 8
 
 norm_epsilon = 1e-06
@@ -156,14 +157,14 @@
     tail = pltpu.make_async_copy(extra_ref, packed.at[pl.ds(kept, EXTRA)], sems.at[4])
     tail.start()
     copy.wait()
-    size = count // SPLIT
-    for part in range(SPLIT):
+    size = count // HALVES
+    for part in range(HALVES):
         cut = slice(part * size, (part + 1) * size)
         out_ref[cut, :] = mm(chosen[cut], rows_ref[...]).astype(bf16)
         Copies(out_ref.at[pl.ds(part * size, size)], out.at[pl.ds(part * size, size)], sems, 5 + SPLIT + part, 1)
     body.wait()
     tail.wait()
-    for part in range(SPLIT):
+    for part in range(HALVES):
         there = pl.ds(part * size, size)
         pltpu.make_async_copy(out_ref.at[there], out.at[there], sems.at[5 + SPLIT + part]).wait()
 
@@ -222,7 +223,7 @@
     return pl.pallas_call(
         neg_kernel,
         in_specs=[INSIDE, INSIDE, INSIDE, OUTSIDE, OUTSIDE],
-        out_shape=pltpu.VMEM((width + EXTRA, 2 * count), bf16),
+        out_shape=pltpu.HBM((width + EXTRA, 2 * count), bf16),
         scratch_shapes=[
             pltpu.VMEM((2 * count, width), bf16),
             pltpu.VMEM(bias.shape, f32),
@@ -428,22 +429,28 @@
         capsules = sums * (jnp.sqrt(norm_sq) / (1.0 + norm_sq))
         if iteration + 1 < ITERS:
             scores = mm_nt(capsules.astype(bf16), mapped)
+            found = [[None] * (events // LANES) for _ in range(INTERESTS)]
+            for part in range(events // LANES):
+                rows = [[] for _ in range(INTERESTS)]
+                for user in range(0, users, SUB):
+                    low = lower[user : user + SUB, part * LANES : (part + 1) * LANES]
+                    high = upper[user : user + SUB, part * LANES : (part + 1) * LANES]
+                    for k in range(INTERESTS):
+                        one = None
+                        for page in range(slots // LANES):
+                            piece = scores[
+                                k * users + user : k * users + user + SUB,
+                                page * LANES : (page + 1) * LANES,
+                            ]
+                            taken = jnp.take_along_axis(
+                                piece, low, axis=1, mode="promise_in_bounds"
+                            )
+                            one = taken if one is None else jnp.where(high == page, taken, one)
+                        rows[k].append(one)
+                for k in range(INTERESTS):
+                    found[k][part] = jnp.concatenate(rows[k], axis=0)
             for k in range(INTERESTS):
-                chunks = []
-                for at in range(0, events, LANES):
-                    low = lower[:, at : at + LANES]
-                    high = upper[:, at : at + LANES]
-                    found = jnp.zeros((users, LANES), f32)
-                    for page in range(slots // LANES):
-                        piece = scores[
-                            k * users : (k + 1) * users, page * LANES : (page + 1) * LANES
-                        ]
-                        taken = jnp.take_along_axis(
-                            piece, low, axis=1, mode="promise_in_bounds"
-                        )
-                        found = jnp.where(high == page, taken, found)
-                    chunks.append(found)
-                logits[k] = logits[k] + jnp.concatenate(chunks, axis=1)
+                logits[k] = logits[k] + jnp.concatenate(found[k], axis=1)
     each = [capsules[k * users : (k + 1) * users] for k in range(INTERESTS)]
     for k in range(INTERESTS):
         interests_ref[:, k * width : (k + 1) * width] = each[k]
@@ -486,8 +493,10 @@
 
 def sums_kernel(parts, pieces, *refs):
     vec_refs = refs[:parts]
-    neg_refs = refs[parts : parts + pieces]
-    out_refs = refs[parts + pieces :]
+    own, *neg_refs = refs[parts : parts + pieces]
+    out_refs = refs[parts + pieces : -2]
+    own_ref, sems = refs[-2:]
+    fetch = Copies(own, own_ref, sems, 0, 1)
     vec = jnp.concatenate([ref[...] for ref in vec_refs], axis=0)
     users = vec_refs[0].shape[0]
     width = vec.shape[1] - LANES
@@ -495,7 +504,9 @@
     label_ids = digits[:, 0:1] + 256.0 * digits[:, 1:2] + 65536.0 * digits[:, 2:3]
     vec = vec[:, :width]
     total = None
-    for ref in neg_refs:
+    for ref in [*neg_refs, own_ref]:
+        if ref is own_ref:
+            fetch.wait()
         extra = ref[width:, :].astype(f32)
         ids = extra[0:1] + 256.0 * extra[1:2] + 65536.0 * extra[2:3]
         terms = jnp.exp(logit_scale * mm(vec, ref[:width, :])) * (1.0 / extra[3:4])
@@ -510,10 +521,12 @@
     users = vecs[0].shape[0]
     return pl.pallas_call(
         functools.partial(sums_kernel, len(vecs), len(negs)),
+        in_specs=[INSIDE] * len(vecs) + [OUTSIDE] + [INSIDE] * (len(negs) - 1),
+        scratch_shapes=[pltpu.VMEM(negs[0].shape, bf16), pltpu.SemaphoreType.DMA((1,))],
         out_shape=[pltpu.VMEM((1, users), f32) for _ in vecs],
         compiler_params=PARAMS,
         name="negative_sums",
-    )(*[near(one) for one in [*vecs, *negs]])
+    )(*[near(one) for one in vecs], far(negs[0]), *[near(one) for one in negs[1:]])
 
 
 def swap_pool(array, size, bit):

time: 67.7 us -> 69.6 us (1.028)
  Pallas kernels: 18 us -> 19.6 us
    pallas_call x1, Pallas kernels: 1.94 us -> 2.88 us  [negative_sums(): pl.pallas_call(functools.partial(sums_kernel, len(vecs), len(negs)), in_s...]
    pallas_call x1, Pallas kernels: 2.45 us -> 3.18 us  [neg_tower(): pl.pallas_call(neg_kernel, in_specs=[INSIDE, INSIDE, INSIDE, OUTSIDE, OUT...]
  transfers between devices with their start and end apart: 11 -> 11, of which waited for: 6 -> 6; matrix products, arithmetic and copies ran while one was open for 0% -> 0% of each run, Pallas kernels for 20% -> 21%
where the time goes in v11:
time: 69.6 us; the launch traced here: 69.2 us
  waiting for transfers between devices  34.1 us (49%)
  Pallas kernels  19.6 us (28%)
  starting transfers between devices  14.2 us (20%)
  between operations  0.73 us (1%)
    ppermute x3, waiting for transfers between devices, swap_pool(): return lax.ppermute(array, 'pool', [(at, at ^ bit) for at in range(size)])  22.7 us
    ppermute x3, waiting for transfers between devices, swap_both(): return lax.ppermute(array, ('user', 'pool'), perm)  11.4 us
    pallas_call x1, Pallas kernels, route(): pl.pallas_call(functools.partial(route_kernel, renumbered), in_specs=[INS...  7.82 us
    all_to_all x1, starting transfers between devices, on_device(): lax.all_to_all(outgoing.reshape(fetch_table.shape[0], fetch_table.shape[2...  7.33 us
    ppermute x3, starting transfers between devices, swap_both(): return lax.ppermute(array, ('user', 'pool'), perm)  3.55 us
    pallas_call x1, Pallas kernels, prepare(): pl.pallas_call(functools.partial(prepare_kernel, renumbered), in_specs=[O...  3.37 us
    pallas_call x1, Pallas kernels, neg_tower(): pl.pallas_call(neg_kernel, in_specs=[INSIDE, INSIDE, INSIDE, OUTSIDE, OUT...  3.18 us
    ppermute x3, starting transfers between devices, swap_pool(): return lax.ppermute(array, 'pool', [(at, at ^ bit) for at in range(size)])  2.88 us
  transfers between devices with their start and end apart: 11, of which 6 were waited for; matrix products, arithmetic and copies ran while one was open for 0% of the time, Pallas kernels for 21%

profile of v11, /device:TPU:0, one launch (start us, length us, event | category | flops | bytes accessed | tf_op | source)
XLA Modules:
  0.0 69.2 jit_solution(5435940714075691593)
XLA Ops:
  0.6 2.4 %select_rows.1 = (bf16[512,512]{1,0:T(8,128)(2,1)}, bf16[144,512]{1,0:T(8,128)(2,1)S(1)}) custom-call(s32[1,16,32]{2,1,0:T(8,128)} %bitcast.15, bf16[512,512]{1,0:T(8,128)(2,1)} %rows.1, bf16[128,512]{1,0:T(8,128)(2,1)} %negs.1, s32[1,128]{1,0:T(1,128)} %bitcast.21, s32[1,128]{1,0:T(1,128)} %bitcast.22), custom_call_target="tpu_custom_call" | custom-call | tf_op jit(solution)/shard_map/select_rows/pallas_call | solution.py:176
  3.0 7.3 %all-to-all-start = ((bf16[32,16,512]{2,1,0:T(8,128)(2,1)}), bf16[32,16,512]{2,1,0:T(8,128)(2,1)S(1)}, u32[]{:S(2)}, u32[]{:S(2)}) async-start(bf16[32,16,512]{2,1,0:T(8,128)(2,1)} %bitcast.3), calls=%async_computation | async-start | bytes 1048576 | tf_op jit(solution)/shard_map/all_to_all | solution.py:591
  10.4 2.7 %collective-permute-start.1 = (bf16[144,512]{1,0:T(8,128)(2,1)S(1)}, bf16[144,512]{1,0:T(8,128)(2,1)S(1)}, u32[]{:S(2)}, u32[]{:S(2)}) collective-permute-start(bf16[144,512]{1,0:T(8,128)(2,1)S(1)} %get-tuple-element.21.own_ref), channel_id=1, source_target_pairs={{0,4},{1,5},{2,6},{3,7},{4,0},{5,1},{6,2},{7,3},{8,12},{9,13},{10,... | collective-permute-start | bytes 442376 | tf_op jit(solution)/shard_map/ppermute | solution.py:533
  13.1 3.4 %prepare.1 = (bf16[4,1024,256]{2,1,0:T(8,128)(2,1)}, f32[128,512]{1,0:T(8,128)}, s32[32,256]{1,0:T(8,128)}, bf16[512,2048]{1,0:T(8,128)(2,1)S(1)}) custom-call(s32[32,256]{1,0:T(8,128)} %index.1, s32[1,32]{1,0:T(1,128)} %bitcast.16, f32[32,4,256]{2,1,0:T(4,128)} %init.3, bf16[512,2048]{1,0:T(8,128)(2,1)} %w_in.1), custom_call_target="tpu_custom_call" | custom-call | tf_op jit(solution)/shard_map/prepare/pallas_call | solution.py:338
  16.5 15.2 %collective-permute-done.1.apart_ref = bf16[144,512]{1,0:T(8,128)(2,1)S(1)} collective-permute-done((bf16[144,512]{1,0:T(8,128)(2,1)S(1)}, bf16[144,512]{1,0:T(8,128)(2,1)S(1)}, u32[]{:S(2)}, u32[]{:S(2)}) %collective-permute-start.1) | collective-permute-done | bytes 147488 | tf_op jit(solution)/shard_map/ppermute | solution.py:533
  31.7 3.2 %neg_tower.1.refs_2_ = bf16[528,256]{1,0:T(8,128)(2,1)} custom-call(bf16[144,512]{1,0:T(8,128)(2,1)S(1)} %get-tuple-element.21.own_ref, bf16[144,512]{1,0:T(8,128)(2,1)S(1)} %collective-permute-done.1.apart_ref, bf16[512,2048]{1,0:T(8,128)(2,1)S(1)} %get-tuple-element.14.w_in_ref, f32[1,2048]{1,0:T(1,128)} %bitcast.13, bf16[2048,512]{1,0:T(8,128)(2,1)} %w_out.3), custom_call_target="tpu_custom_call" | custom-call | tf_op jit(solution)/shard_map/neg_tower/pallas_call | solution.py:223
  34.9 2.5 %collective-permute-start.2 = (bf16[528,256]{1,0:T(8,128)(2,1)}, bf16[528,256]{1,0:T(8,128)(2,1)S(1)}, u32[]{:S(2)}, u32[]{:S(2)}) collective-permute-start(bf16[528,256]{1,0:T(8,128)(2,1)} %neg_tower.1.refs_2_), channel_id=1, source_target_pairs={{0,17},{1,16},{2,19},{3,18},{4,21},{5,20},{6,23},{7,22},{8,25},{9,... | collective-permute-start | bytes 811016 | tf_op jit(solution)/shard_map/ppermute | solution.py:550
  37.3 0.5 collective-permute-start.3
  37.8 0.6 collective-permute-start.4
  38.4 0.0 collective-permute-start.5
  38.4 7.0 %collective-permute-done.2.refs_3_ = bf16[528,256]{1,0:T(8,128)(2,1)S(1)} collective-permute-done((bf16[528,256]{1,0:T(8,128)(2,1)}, bf16[528,256]{1,0:T(8,128)(2,1)S(1)}, u32[]{:S(2)}, u32[]{:S(2)}) %collective-permute-start.2) | collective-permute-done | bytes 270368 | tf_op jit(solution)/shard_map/ppermute | solution.py:550
  45.4 0.0 collective-permute-start.6
  45.4 4.3 %collective-permute-done.3.refs_4_ = bf16[528,256]{1,0:T(8,128)(2,1)S(1)} collective-permute-done((bf16[528,256]{1,0:T(8,128)(2,1)}, bf16[528,256]{1,0:T(8,128)(2,1)S(1)}, u32[]{:S(2)}, u32[]{:S(2)}) %collective-permute-start.3) | collective-permute-done | bytes 270368 | tf_op jit(solution)/shard_map/ppermute | solution.py:550
  49.7 0.0 collective-permute-start.7
  49.8 0.1 collective-permute-done.4.refs_5_
  49.8 0.4 collective-permute-start.8
  50.3 0.0 all-to-all-done
  50.3 7.8 %route.1 = (f32[32,2048]{1,0:T(8,128)}, bf16[32,640]{1,0:T(8,128)(2,1)S(1)}, f32[1,32]{1,0:T(1,128)S(1)}) custom-call(bf16[512,512]{1,0:T(8,128)(2,1)S(1)} %bitcast.12, bf16[512,2048]{1,0:T(8,128)(2,1)S(1)} %get-tuple-element.14.w_in_ref, f32[1,2048]{1,0:T(1,128)} %bitcast.14, bf16[2048,512]{1,0:T(8,128)(2,1)} %w_out.3, bf16[512,512]{1,0:T(8,128)(2,1)} %bilinear.1, ...), custom_call_target="tpu_custom_call" | custom-call | tf_op jit(solution)/shard_map/route/pallas_call | solution.py:476
  58.1 0.1 collective-permute-start
  58.2 0.0 collective-permute-done.5.refs_6_
  58.2 0.0 collective-permute-done.6.refs_7_
  58.2 0.0 collective-permute-done.7.refs_8_
  58.2 0.0 collective-permute-done.8.refs_9_
  58.2 3.9 %collective-permute-done.refs_1_ = bf16[32,640]{1,0:T(8,128)(2,1)S(1)} collective-permute-done((bf16[32,640]{1,0:T(8,128)(2,1)S(1)}, bf16[32,640]{1,0:T(8,128)(2,1)S(1)}, u32[]{:S(2)}, u32[]{:S(2)}) %collective-permute-start) | collective-permute-done | bytes 40992 | tf_op jit(solution)/shard_map/ppermute | solution.py:533
  62.2 2.9 %negative_sums.1 = (f32[1,32]{1,0:T(1,128)S(1)}, f32[1,32]{1,0:T(1,128)S(1)}) custom-call(bf16[32,640]{1,0:T(8,128)(2,1)S(1)} %get-tuple-element.20.refs_0_, bf16[32,640]{1,0:T(8,128)(2,1)S(1)} %collective-permute-done.refs_1_, bf16[528,256]{1,0:T(8,128)(2,1)} %neg_tower.1.refs_2_, bf16[528,256]{1,0:T(8,128)(2,1)S(1)} %collective-permute-done.2.refs_3_, ...), custom_call_target="tpu_custom_call" | custom-call | tf_op jit(solution)/shard_map/negative_sums/pallas_call | solution.py:522
  65.0 0.1 collective-permute-start.9
  65.1 3.6 %collective-permute-done.9 = f32[1,32]{1,0:T(1,128)S(1)} collective-permute-done((f32[1,32]{1,0:T(1,128)S(1)}, f32[1,32]{1,0:T(1,128)S(1)}, u32[]{:S(2)}, u32[]{:S(2)}) %collective-permute-start.9) | collective-permute-done | bytes 160 | tf_op jit(solution)/shard_map/ppermute | solution.py:533
  68.7 0.5 subtract_bitcast_fusion
Async XLA Ops:
  3.0 47.2 %all-to-all-start = ((bf16[32,16,512]{2,1,0:T(8,128)(2,1)}), bf16[32,16,512]{2,1,0:T(8,128)(2,1)S(1)}, u32[]{:S(2)}, u32[]{:S(2)}) async-start(bf16[32,16,512]{2,1,0:T(8,128)(2,1)} %bitcast.3), calls=%async_computation | async-start | bytes 1048576 | tf_op jit(solution)/shard_map/all_to_all | solution.py:591
  10.4 21.3 %collective-permute-start.1 = (bf16[144,512]{1,0:T(8,128)(2,1)S(1)}, bf16[144,512]{1,0:T(8,128)(2,1)S(1)}, u32[]{:S(2)}, u32[]{:S(2)}) collective-permute-start(bf16[144,512]{1,0:T(8,128)(2,1)S(1)} %get-tuple-element.21.own_ref), channel_id=1, source_target_pairs={{0,4},{1,5},{2,6},{3,7},{4,0},{5,1},{6,2},{7,3},{8,12},{9,13},{10,... | collective-permute-start | bytes 442376 | tf_op jit(solution)/shard_map/ppermute | solution.py:533
  34.9 10.6 %collective-permute-start.2 = (bf16[528,256]{1,0:T(8,128)(2,1)}, bf16[528,256]{1,0:T(8,128)(2,1)S(1)}, u32[]{:S(2)}, u32[]{:S(2)}) collective-permute-start(bf16[528,256]{1,0:T(8,128)(2,1)} %neg_tower.1.refs_2_), channel_id=1, source_target_pairs={{0,17},{1,16},{2,19},{3,18},{4,21},{5,20},{6,23},{7,22},{8,25},{9,... | collective-permute-start | bytes 811016 | tf_op jit(solution)/shard_map/ppermute | solution.py:550
  37.3 12.4 %collective-permute-start.3 = (bf16[528,256]{1,0:T(8,128)(2,1)}, bf16[528,256]{1,0:T(8,128)(2,1)S(1)}, u32[]{:S(2)}, u32[]{:S(2)}) collective-permute-start(bf16[528,256]{1,0:T(8,128)(2,1)} %neg_tower.1.refs_2_), channel_id=1, source_target_pairs={{0,16},{1,17},{2,18},{3,19},{4,20},{5,21},{6,22},{7,23},{8,24},{9,... | collective-permute-start | bytes 811016 | tf_op jit(solution)/shard_map/ppermute | solution.py:550
  37.8 12.0 %collective-permute-start.4 = (bf16[528,256]{1,0:T(8,128)(2,1)}, bf16[528,256]{1,0:T(8,128)(2,1)S(1)}, u32[]{:S(2)}, u32[]{:S(2)}) collective-permute-start(bf16[528,256]{1,0:T(8,128)(2,1)} %neg_tower.1.refs_2_), channel_id=1, source_target_pairs={{0,1},{1,0},{2,3},{3,2},{4,5},{5,4},{6,7},{7,6},{8,9},{9,8},{10,11... | collective-permute-start | bytes 811016 | tf_op jit(solution)/shard_map/ppermute | solution.py:550
  38.4 19.8 %collective-permute-start.5 = (bf16[528,256]{1,0:T(8,128)(2,1)}, bf16[528,256]{1,0:T(8,128)(2,1)}, u32[]{:S(2)}, u32[]{:S(2)}) collective-permute-start(bf16[528,256]{1,0:T(8,128)(2,1)} %neg_tower.1.refs_2_), channel_id=1, source_target_pairs={{0,8},{8,0},{16,24},{24,16},{1,9},{9,1},{17,25},{25,17},{2,10},{10... | collective-permute-start | bytes 811016 | tf_op jit(solution)/shard_map/ppermute | solution.py:541
  45.4 12.8 %collective-permute-start.6 = (bf16[528,256]{1,0:T(8,128)(2,1)S(1)}, bf16[528,256]{1,0:T(8,128)(2,1)}, u32[]{:S(2)}, u32[]{:S(2)}) collective-permute-start(bf16[528,256]{1,0:T(8,128)(2,1)S(1)} %collective-permute-done.2.refs_3_), channel_id=1, source_target_pairs={{0,8},{8,0},{16,24},{24,16},{1,9},{9,1},{17,25},{25,17},{2,10},{10... | collective-permute-start | bytes 811016 | tf_op jit(solution)/shard_map/ppermute | solution.py:541
  49.7 8.4 %collective-permute-start.7 = (bf16[528,256]{1,0:T(8,128)(2,1)S(1)}, bf16[528,256]{1,0:T(8,128)(2,1)}, u32[]{:S(2)}, u32[]{:S(2)}) collective-permute-start(bf16[528,256]{1,0:T(8,128)(2,1)S(1)} %collective-permute-done.3.refs_4_), channel_id=1, source_target_pairs={{0,8},{8,0},{16,24},{24,16},{1,9},{9,1},{17,25},{25,17},{2,10},{10... | collective-permute-start | bytes 811016 | tf_op jit(solution)/shard_map/ppermute | solution.py:541
  49.8 8.4 %collective-permute-start.8 = (bf16[528,256]{1,0:T(8,128)(2,1)S(1)}, bf16[528,256]{1,0:T(8,128)(2,1)}, u32[]{:S(2)}, u32[]{:S(2)}) collective-permute-start(bf16[528,256]{1,0:T(8,128)(2,1)S(1)} %collective-permute-done.4.refs_5_), channel_id=1, source_target_pairs={{0,8},{8,0},{16,24},{24,16},{1,9},{9,1},{17,25},{25,17},{2,10},{10... | collective-permute-start | bytes 811016 | tf_op jit(solution)/shard_map/ppermute | solution.py:541
  58.1 4.1 %collective-permute-start = (bf16[32,640]{1,0:T(8,128)(2,1)S(1)}, bf16[32,640]{1,0:T(8,128)(2,1)S(1)}, u32[]{:S(2)}, u32[]{:S(2)}) collective-permute-start(bf16[32,640]{1,0:T(8,128)(2,1)S(1)} %get-tuple-element.20.refs_0_), channel_id=1, source_target_pairs={{0,2},{1,3},{2,0},{3,1},{4,6},{5,7},{6,4},{7,5},{8,10},{9,11},{10,... | collective-permute-start | bytes 122888 | tf_op jit(solution)/shard_map/ppermute | solution.py:533
  65.0 3.6 %collective-permute-start.9 = (f32[1,32]{1,0:T(1,128)S(1)}, f32[1,32]{1,0:T(1,128)S(1)}, u32[]{:S(2)}, u32[]{:S(2)}) collective-permute-start(f32[1,32]{1,0:T(1,128)S(1)} %get-tuple-element.23), channel_id=1, source_target_pairs={{0,2},{1,3},{2,0},{3,1},{4,6},{5,7},{6,4},{7,5},{8,10},{9,11},{10,... | collective-permute-start | bytes 392 | tf_op jit(solution)/shard_map/ppermute | solution.py:533

commit v12 on v11

--- a/solution.py
+++ b/solution.py
@@ -14,7 +14,6 @@
 SUB = 8
 EXTRA = 16
 SPLIT = 4
-HALVES = 2
 GROUP_USERS = 8
 
 norm_epsilon = 1e-06
@@ -157,14 +156,14 @@
     tail = pltpu.make_async_copy(extra_ref, packed.at[pl.ds(kept, EXTRA)], sems.at[4])
     tail.start()
     copy.wait()
-    size = count // HALVES
-    for part in range(HALVES):
+    size = count // SPLIT
+    for part in range(SPLIT):
         cut = slice(part * size, (part + 1) * size)
         out_ref[cut, :] = mm(chosen[cut], rows_ref[...]).astype(bf16)
         Copies(out_ref.at[pl.ds(part * size, size)], out.at[pl.ds(part * size, size)], sems, 5 + SPLIT + part, 1)
     body.wait()
     tail.wait()
-    for part in range(HALVES):
+    for part in range(SPLIT):
         there = pl.ds(part * size, size)
         pltpu.make_async_copy(out_ref.at[there], out.at[there], sems.at[5 + SPLIT + part]).wait()
 
@@ -477,7 +476,7 @@
         functools.partial(route_kernel, renumbered),
         in_specs=[INSIDE] * 2 + [OUTSIDE] * len(others),
         out_shape=[
-            jax.ShapeDtypeStruct((users, INTERESTS * width), f32),
+            pltpu.VMEM((users, INTERESTS * width), f32),
             pltpu.VMEM((users, width + LANES), bf16),
             pltpu.VMEM((1, users), f32),
         ],
@@ -493,10 +492,8 @@
 
 def sums_kernel(parts, pieces, *refs):
     vec_refs = refs[:parts]
-    own, *neg_refs = refs[parts : parts + pieces]
-    out_refs = refs[parts + pieces : -2]
-    own_ref, sems = refs[-2:]
-    fetch = Copies(own, own_ref, sems, 0, 1)
+    neg_refs = refs[parts : parts + pieces]
+    out_refs = refs[parts + pieces :]
     vec = jnp.concatenate([ref[...] for ref in vec_refs], axis=0)
     users = vec_refs[0].shape[0]
     width = vec.shape[1] - LANES
@@ -504,9 +501,7 @@
     label_ids = digits[:, 0:1] + 256.0 * digits[:, 1:2] + 65536.0 * digits[:, 2:3]
     vec = vec[:, :width]
     total = None
-    for ref in [*neg_refs, own_ref]:
-        if ref is own_ref:
-            fetch.wait()
+    for ref in neg_refs:
         extra = ref[width:, :].astype(f32)
         ids = extra[0:1] + 256.0 * extra[1:2] + 65536.0 * extra[2:3]
         terms = jnp.exp(logit_scale * mm(vec, ref[:width, :])) * (1.0 / extra[3:4])
@@ -521,12 +516,10 @@
     users = vecs[0].shape[0]
     return pl.pallas_call(
         functools.partial(sums_kernel, len(vecs), len(negs)),
-        in_specs=[INSIDE] * len(vecs) + [OUTSIDE] + [INSIDE] * (len(negs) - 1),
-        scratch_shapes=[pltpu.VMEM(negs[0].shape, bf16), pltpu.SemaphoreType.DMA((1,))],
         out_shape=[pltpu.VMEM((1, users), f32) for _ in vecs],
         compiler_params=PARAMS,
         name="negative_sums",
-    )(*[near(one) for one in vecs], far(negs[0]), *[near(one) for one in negs[1:]])
+    )(*[near(one) for one in [*vecs, *negs]])
 
 
 def swap_pool(array, size, bit):

time: 69.6 us -> 68 us (0.977)
  Pallas kernels: 19.6 us -> 18.1 us
  local copies, waits for them, and re-layouts: 0 us -> 0.71 us
  waiting for transfers between devices: 34.1 us -> 33.4 us
    pallas_call x1, Pallas kernels: 2.88 us -> 1.86 us  [negative_sums(): pl.pallas_call(functools.partial(sums_kernel, len(vecs), len(negs)), out_...]
    unnamed x0 -> x3, local copies, waits for them, and re-layouts: none -> 0.71 us
    ppermute x3, waiting for transfers between devices: 22.7 us -> 22 us  [swap_pool(): return lax.ppermute(array, 'pool', [(at, at ^ bit) for at in range(size)])]
  transfers between devices with their start and end apart: 11 -> 11, of which waited for: 6 -> 6; matrix products, arithmetic and copies ran while one was open for 0% -> 1% of each run, Pallas kernels for 21% -> 21%
where the time goes in v12:
time: 68 us; the launch traced here: 67.6 us
  waiting for transfers between devices  33.4 us (49%)
  Pallas kernels  18.1 us (27%)
  starting transfers between devices  14.2 us (21%)
  between operations  0.72 us (1%)
  local copies, waits for them, and re-layouts  0.71 us (1%)
    ppermute x3, waiting for transfers between devices, swap_pool(): return lax.ppermute(array, 'pool', [(at, at ^ bit) for at in range(size)])  22 us
    ppermute x3, waiting for transfers between devices, swap_both(): return lax.ppermute(array, ('user', 'pool'), perm)  11.4 us
    pallas_call x1, Pallas kernels, route(): pl.pallas_call(functools.partial(route_kernel, renumbered), in_specs=[INS...  7.36 us
    all_to_all x1, starting transfers between devices, on_device(): lax.all_to_all(outgoing.reshape(fetch_table.shape[0], fetch_table.shape[2...  7.33 us
    ppermute x3, starting transfers between devices, swap_both(): return lax.ppermute(array, ('user', 'pool'), perm)  3.55 us
    pallas_call x1, Pallas kernels, prepare(): pl.pallas_call(functools.partial(prepare_kernel, renumbered), in_specs=[O...  3.37 us
    pallas_call x1, Pallas kernels, neg_tower(): pl.pallas_call(neg_kernel, in_specs=[INSIDE, INSIDE, INSIDE, OUTSIDE, OUT...  3.17 us
    ppermute x3, starting transfers between devices, swap_pool(): return lax.ppermute(array, 'pool', [(at, at ^ bit) for at in range(size)])  2.82 us
  transfers between devices with their start and end apart: 11, of which 6 were waited for; matrix products, arithmetic and copies ran while one was open for 1% of the time, Pallas kernels for 21%

profile of v12, /device:TPU:0, one launch (start us, length us, event | category | flops | bytes accessed | tf_op | source)
XLA Modules:
  0.0 67.6 jit_solution(13107458534899516305)
XLA Ops:
  0.6 2.3 %select_rows.1 = (bf16[512,512]{1,0:T(8,128)(2,1)}, bf16[144,512]{1,0:T(8,128)(2,1)S(1)}) custom-call(s32[1,16,32]{2,1,0:T(8,128)} %bitcast.15, bf16[512,512]{1,0:T(8,128)(2,1)} %rows.1, bf16[128,512]{1,0:T(8,128)(2,1)} %negs.1, s32[1,128]{1,0:T(1,128)} %bitcast.21, s32[1,128]{1,0:T(1,128)} %bitcast.22), custom_call_target="tpu_custom_call" | custom-call | tf_op jit(solution)/shard_map/select_rows/pallas_call | solution.py:175
  3.0 7.3 %all-to-all-start = ((bf16[32,16,512]{2,1,0:T(8,128)(2,1)}), bf16[32,16,512]{2,1,0:T(8,128)(2,1)S(1)}, u32[]{:S(2)}, u32[]{:S(2)}) async-start(bf16[32,16,512]{2,1,0:T(8,128)(2,1)} %bitcast.3), calls=%async_computation | async-start | bytes 1048576 | tf_op jit(solution)/shard_map/all_to_all | solution.py:584
  10.3 2.7 %collective-permute-start.1 = (bf16[144,512]{1,0:T(8,128)(2,1)S(1)}, bf16[144,512]{1,0:T(8,128)(2,1)S(1)}, u32[]{:S(2)}, u32[]{:S(2)}) collective-permute-start(bf16[144,512]{1,0:T(8,128)(2,1)S(1)} %get-tuple-element.21.own_ref), channel_id=1, source_target_pairs={{0,4},{1,5},{2,6},{3,7},{4,0},{5,1},{6,2},{7,3},{8,12},{9,13},{10,... | collective-permute-start | bytes 442376 | tf_op jit(solution)/shard_map/ppermute | solution.py:526
  13.1 3.4 %prepare.1 = (bf16[4,1024,256]{2,1,0:T(8,128)(2,1)}, f32[128,512]{1,0:T(8,128)}, s32[32,256]{1,0:T(8,128)}, bf16[512,2048]{1,0:T(8,128)(2,1)S(1)}) custom-call(s32[32,256]{1,0:T(8,128)} %index.1, s32[1,32]{1,0:T(1,128)} %bitcast.16, f32[32,4,256]{2,1,0:T(4,128)} %init.3, bf16[512,2048]{1,0:T(8,128)(2,1)} %w_in.1), custom_call_target="tpu_custom_call" | custom-call | tf_op jit(solution)/shard_map/prepare/pallas_call | solution.py:337
  16.4 15.2 %collective-permute-done.1.apart_ref = bf16[144,512]{1,0:T(8,128)(2,1)S(1)} collective-permute-done((bf16[144,512]{1,0:T(8,128)(2,1)S(1)}, bf16[144,512]{1,0:T(8,128)(2,1)S(1)}, u32[]{:S(2)}, u32[]{:S(2)}) %collective-permute-start.1) | collective-permute-done | bytes 147488 | tf_op jit(solution)/shard_map/ppermute | solution.py:526
  31.6 3.2 %neg_tower.1.refs_2_ = bf16[528,256]{1,0:T(8,128)(2,1)} custom-call(bf16[144,512]{1,0:T(8,128)(2,1)S(1)} %get-tuple-element.21.own_ref, bf16[144,512]{1,0:T(8,128)(2,1)S(1)} %collective-permute-done.1.apart_ref, bf16[512,2048]{1,0:T(8,128)(2,1)S(1)} %get-tuple-element.14.w_in_ref, f32[1,2048]{1,0:T(1,128)} %bitcast.13, bf16[2048,512]{1,0:T(8,128)(2,1)} %w_out.3), custom_call_target="tpu_custom_call" | custom-call | tf_op jit(solution)/shard_map/neg_tower/pallas_call | solution.py:222
  34.8 2.5 %collective-permute-start.2 = (bf16[528,256]{1,0:T(8,128)(2,1)}, bf16[528,256]{1,0:T(8,128)(2,1)S(1)}, u32[]{:S(2)}, u32[]{:S(2)}) collective-permute-start(bf16[528,256]{1,0:T(8,128)(2,1)} %neg_tower.1.refs_2_), channel_id=1, source_target_pairs={{0,17},{1,16},{2,19},{3,18},{4,21},{5,20},{6,23},{7,22},{8,25},{9,... | collective-permute-start | bytes 811016 | tf_op jit(solution)/shard_map/ppermute | solution.py:543
  37.3 0.5 collective-permute-start.3
  37.8 0.6 collective-permute-start.4
  38.4 0.0 collective-permute-start.5
  38.4 7.0 %collective-permute-done.2.refs_3_ = bf16[528,256]{1,0:T(8,128)(2,1)S(1)} collective-permute-done((bf16[528,256]{1,0:T(8,128)(2,1)}, bf16[528,256]{1,0:T(8,128)(2,1)S(1)}, u32[]{:S(2)}, u32[]{:S(2)}) %collective-permute-start.2) | collective-permute-done | bytes 270368 | tf_op jit(solution)/shard_map/ppermute | solution.py:543
  45.4 0.0 collective-permute-start.6
  45.4 4.3 %collective-permute-done.3.refs_4_ = bf16[528,256]{1,0:T(8,128)(2,1)S(1)} collective-permute-done((bf16[528,256]{1,0:T(8,128)(2,1)}, bf16[528,256]{1,0:T(8,128)(2,1)S(1)}, u32[]{:S(2)}, u32[]{:S(2)}) %collective-permute-start.3) | collective-permute-done | bytes 270368 | tf_op jit(solution)/shard_map/ppermute | solution.py:543
  49.7 0.0 collective-permute-start.7
  49.7 0.1 collective-permute-done.4.refs_5_
  49.8 0.4 collective-permute-start.8
  50.2 0.0 all-to-all-done
  50.2 0.0 copy-start
  50.2 7.4 %route.1 = (f32[32,2048]{1,0:T(8,128)S(1)}, bf16[32,640]{1,0:T(8,128)(2,1)S(1)}, f32[1,32]{1,0:T(1,128)S(1)}) custom-call(bf16[512,512]{1,0:T(8,128)(2,1)S(1)} %bitcast.12, bf16[512,2048]{1,0:T(8,128)(2,1)S(1)} %get-tuple-element.14.w_in_ref, f32[1,2048]{1,0:T(1,128)} %bitcast.14, bf16[2048,512]{1,0:T(8,128)(2,1)} %w_out.3, bf16[512,512]{1,0:T(8,128)(2,1)} %bilinear.1, ...), custom_call_target="tpu_custom_call" | custom-call | tf_op jit(solution)/shard_map/route/pallas_call | solution.py:475
  57.6 0.1 collective-permute-start
  57.7 0.0 collective-permute-done.5.refs_6_
  57.7 0.0 collective-permute-done.6.refs_7_
  57.7 0.0 collective-permute-done.7.refs_8_
  57.7 0.0 collective-permute-done.8.refs_9_
  57.7 3.9 %collective-permute-done.refs_1_ = bf16[32,640]{1,0:T(8,128)(2,1)S(1)} collective-permute-done((bf16[32,640]{1,0:T(8,128)(2,1)S(1)}, bf16[32,640]{1,0:T(8,128)(2,1)S(1)}, u32[]{:S(2)}, u32[]{:S(2)}) %collective-permute-start) | collective-permute-done | bytes 40992 | tf_op jit(solution)/shard_map/ppermute | solution.py:526
  61.6 0.0 copy-done
  61.6 1.9 %negative_sums.1 = (f32[1,32]{1,0:T(1,128)S(1)}, f32[1,32]{1,0:T(1,128)S(1)}) custom-call(bf16[32,640]{1,0:T(8,128)(2,1)S(1)} %get-tuple-element.20.refs_0_, bf16[32,640]{1,0:T(8,128)(2,1)S(1)} %collective-permute-done.refs_1_, bf16[528,256]{1,0:T(8,128)(2,1)S(1)} %copy-done, bf16[528,256]{1,0:T(8,128)(2,1)S(1)} %collective-permute-done.2.refs_3_, ...), custom_call_target="tpu_custom_call" | custom-call | tf_op jit(solution)/shard_map/negative_sums/pallas_call | solution.py:517
  63.5 0.0 collective-permute-start.9
  63.5 0.7 %copy.17 = f32[32,2048]{1,0:T(8,128)} copy(f32[32,2048]{1,0:T(8,128)S(1)} %get-tuple-element.24) | data formatting | bytes 524288
  64.2 2.9 %collective-permute-done.9 = f32[1,32]{1,0:T(1,128)S(1)} collective-permute-done((f32[1,32]{1,0:T(1,128)S(1)}, f32[1,32]{1,0:T(1,128)S(1)}, u32[]{:S(2)}, u32[]{:S(2)}) %collective-permute-start.9) | collective-permute-done | bytes 160 | tf_op jit(solution)/shard_map/ppermute | solution.py:526
  67.1 0.5 subtract_bitcast_fusion
Async XLA Ops:
  3.0 47.2 %all-to-all-start = ((bf16[32,16,512]{2,1,0:T(8,128)(2,1)}), bf16[32,16,512]{2,1,0:T(8,128)(2,1)S(1)}, u32[]{:S(2)}, u32[]{:S(2)}) async-start(bf16[32,16,512]{2,1,0:T(8,128)(2,1)} %bitcast.3), calls=%async_computation | async-start | bytes 1048576 | tf_op jit(solution)/shard_map/all_to_all | solution.py:584
  10.3 21.3 %collective-permute-start.1 = (bf16[144,512]{1,0:T(8,128)(2,1)S(1)}, bf16[144,512]{1,0:T(8,128)(2,1)S(1)}, u32[]{:S(2)}, u32[]{:S(2)}) collective-permute-start(bf16[144,512]{1,0:T(8,128)(2,1)S(1)} %get-tuple-element.21.own_ref), channel_id=1, source_target_pairs={{0,4},{1,5},{2,6},{3,7},{4,0},{5,1},{6,2},{7,3},{8,12},{9,13},{10,... | collective-permute-start | bytes 442376 | tf_op jit(solution)/shard_map/ppermute | solution.py:526
  34.8 10.6 %collective-permute-start.2 = (bf16[528,256]{1,0:T(8,128)(2,1)}, bf16[528,256]{1,0:T(8,128)(2,1)S(1)}, u32[]{:S(2)}, u32[]{:S(2)}) collective-permute-start(bf16[528,256]{1,0:T(8,128)(2,1)} %neg_tower.1.refs_2_), channel_id=1, source_target_pairs={{0,17},{1,16},{2,19},{3,18},{4,21},{5,20},{6,23},{7,22},{8,25},{9,... | collective-permute-start | bytes 811016 | tf_op jit(solution)/shard_map/ppermute | solution.py:543
  37.3 12.4 %collective-permute-start.3 = (bf16[528,256]{1,0:T(8,128)(2,1)}, bf16[528,256]{1,0:T(8,128)(2,1)S(1)}, u32[]{:S(2)}, u32[]{:S(2)}) collective-permute-start(bf16[528,256]{1,0:T(8,128)(2,1)} %neg_tower.1.refs_2_), channel_id=1, source_target_pairs={{0,16},{1,17},{2,18},{3,19},{4,20},{5,21},{6,22},{7,23},{8,24},{9,... | collective-permute-start | bytes 811016 | tf_op jit(solution)/shard_map/ppermute | solution.py:543
  37.8 12.0 %collective-permute-start.4 = (bf16[528,256]{1,0:T(8,128)(2,1)}, bf16[528,256]{1,0:T(8,128)(2,1)S(1)}, u32[]{:S(2)}, u32[]{:S(2)}) collective-permute-start(bf16[528,256]{1,0:T(8,128)(2,1)} %neg_tower.1.refs_2_), channel_id=1, source_target_pairs={{0,1},{1,0},{2,3},{3,2},{4,5},{5,4},{6,7},{7,6},{8,9},{9,8},{10,11... | collective-permute-start | bytes 811016 | tf_op jit(solution)/shard_map/ppermute | solution.py:543
  38.4 19.3 %collective-permute-start.5 = (bf16[528,256]{1,0:T(8,128)(2,1)}, bf16[528,256]{1,0:T(8,128)(2,1)}, u32[]{:S(2)}, u32[]{:S(2)}) collective-permute-start(bf16[528,256]{1,0:T(8,128)(2,1)} %neg_tower.1.refs_2_), channel_id=1, source_target_pairs={{0,8},{8,0},{16,24},{24,16},{1,9},{9,1},{17,25},{25,17},{2,10},{10... | collective-permute-start | bytes 811016 | tf_op jit(solution)/shard_map/ppermute | solution.py:534
  45.4 12.3 %collective-permute-start.6 = (bf16[528,256]{1,0:T(8,128)(2,1)S(1)}, bf16[528,256]{1,0:T(8,128)(2,1)}, u32[]{:S(2)}, u32[]{:S(2)}) collective-permute-start(bf16[528,256]{1,0:T(8,128)(2,1)S(1)} %collective-permute-done.2.refs_3_), channel_id=1, source_target_pairs={{0,8},{8,0},{16,24},{24,16},{1,9},{9,1},{17,25},{25,17},{2,10},{10... | collective-permute-start | bytes 811016 | tf_op jit(solution)/shard_map/ppermute | solution.py:534
  49.7 8.0 %collective-permute-start.7 = (bf16[528,256]{1,0:T(8,128)(2,1)S(1)}, bf16[528,256]{1,0:T(8,128)(2,1)}, u32[]{:S(2)}, u32[]{:S(2)}) collective-permute-start(bf16[528,256]{1,0:T(8,128)(2,1)S(1)} %collective-permute-done.3.refs_4_), channel_id=1, source_target_pairs={{0,8},{8,0},{16,24},{24,16},{1,9},{9,1},{17,25},{25,17},{2,10},{10... | collective-permute-start | bytes 811016 | tf_op jit(solution)/shard_map/ppermute | solution.py:534
  49.8 7.9 %collective-permute-start.8 = (bf16[528,256]{1,0:T(8,128)(2,1)S(1)}, bf16[528,256]{1,0:T(8,128)(2,1)}, u32[]{:S(2)}, u32[]{:S(2)}) collective-permute-start(bf16[528,256]{1,0:T(8,128)(2,1)S(1)} %collective-permute-done.4.refs_5_), channel_id=1, source_target_pairs={{0,8},{8,0},{16,24},{24,16},{1,9},{9,1},{17,25},{25,17},{2,10},{10... | collective-permute-start | bytes 811016 | tf_op jit(solution)/shard_map/ppermute | solution.py:534
  50.2 11.4 %copy-start = (bf16[528,256]{1,0:T(8,128)(2,1)S(1)}, bf16[528,256]{1,0:T(8,128)(2,1)}, u32[]{:S(2)}) copy-start(bf16[528,256]{1,0:T(8,128)(2,1)} %neg_tower.1.refs_2_) | copy-start | bytes 811012
  57.6 4.1 %collective-permute-start = (bf16[32,640]{1,0:T(8,128)(2,1)S(1)}, bf16[32,640]{1,0:T(8,128)(2,1)S(1)}, u32[]{:S(2)}, u32[]{:S(2)}) collective-permute-start(bf16[32,640]{1,0:T(8,128)(2,1)S(1)} %get-tuple-element.20.refs_0_), channel_id=1, source_target_pairs={{0,2},{1,3},{2,0},{3,1},{4,6},{5,7},{6,4},{7,5},{8,10},{9,11},{10,... | collective-permute-start | bytes 122888 | tf_op jit(solution)/shard_map/ppermute | solution.py:526
  63.5 3.6 %collective-permute-start.9 = (f32[1,32]{1,0:T(1,128)S(1)}, f32[1,32]{1,0:T(1,128)S(1)}, u32[]{:S(2)}, u32[]{:S(2)}) collective-permute-start(f32[1,32]{1,0:T(1,128)S(1)} %get-tuple-element.23), channel_id=1, source_target_pairs={{0,2},{1,3},{2,0},{3,1},{4,6},{5,7},{6,4},{7,5},{8,10},{9,11},{10,... | collective-permute-start | bytes 392 | tf_op jit(solution)/shard_map/ppermute | solution.py:526

commit v13 on v12

--- a/solution.py
+++ b/solution.py
@@ -373,9 +373,11 @@
     label,
     ids,
     counts,
+    held,
     interests_ref,
     vec_ref,
     positive_ref,
+    held_ref,
     bias_ref,
     out_ref,
     map_ref,
@@ -404,6 +406,7 @@
     others = [Copies(*pair, sems, start + at, 1) for at, pair in enumerate(pairs)]
     unit = tower(rows_ref, w_in_ref, bias, w_out, bias_ref, out_ref, sems).astype(bf16)
     fetch = Copies(onehot, onehot_ref, sems, start + len(pairs), onehot.shape[0])
+    keep = Copies(held, held_ref, sems, start + len(pairs) + onehot.shape[0], 1)
     for other in others:
         other.wait()
     mapped = mm(unit, map_ref[...]).astype(bf16)
@@ -414,7 +417,7 @@
     lower = index & (LANES - 1)
     live = live_mask(length_ref, index.shape)
     logits = [init_ref[:, k, :] for k in range(INTERESTS)]
-    capsules = None
+    capsules = label_rows = None
     for iteration in range(ITERS):
         if iteration == 1:
             fetch.wait()
@@ -428,6 +431,10 @@
         capsules = sums * (jnp.sqrt(norm_sq) / (1.0 + norm_sq))
         if iteration + 1 < ITERS:
             scores = mm_nt(capsules.astype(bf16), mapped)
+            if iteration == 0:
+                label = to_column(renumbered(label_ref[...]).astype(f32))
+                chosen = jnp.where(iota((users, slots), 1).astype(f32) == label, 1.0, 0.0)
+                label_rows = mm(chosen.astype(bf16), unit)
             found = [[None] * (events // LANES) for _ in range(INTERESTS)]
             for part in range(events // LANES):
                 rows = [[] for _ in range(INTERESTS)]
@@ -453,9 +460,6 @@
     each = [capsules[k * users : (k + 1) * users] for k in range(INTERESTS)]
     for k in range(INTERESTS):
         interests_ref[:, k * width : (k + 1) * width] = each[k]
-    label = to_column(renumbered(label_ref[...]).astype(f32))
-    chosen = jnp.where(iota((users, slots), 1).astype(f32) == label, 1.0, 0.0).astype(bf16)
-    label_rows = mm(chosen, unit)
     raised = [
         jnp.exp(attend_scale * jnp.sum(one * label_rows, axis=1, keepdims=True)) for one in each
     ]
@@ -466,10 +470,11 @@
     vec_ref[:, width:] = lane_columns([to_column(one) for one in id_digits(ids_ref[...])], users).astype(bf16)
     match = jnp.sum(user_vec.astype(f32) * label_rows, axis=1, keepdims=True)
     positive_ref[...] = logit_scale * to_row(match) - jnp.log(counts_ref[...].astype(f32))
+    keep.wait()
 
 
 def route(renumbered, rows, w_in, *others):
-    _, _, bilinear, onehot, first, index, _, _, _, _, _ = others
+    bias, w_out, bilinear, onehot, first, index, *_, held = others
     users = index.shape[0]
     width = bilinear.shape[1]
     return pl.pallas_call(
@@ -479,8 +484,9 @@
             pltpu.VMEM((users, INTERESTS * width), f32),
             pltpu.VMEM((users, width + LANES), bf16),
             pltpu.VMEM((1, users), f32),
+            pltpu.VMEM(held.shape, held.dtype),
         ],
-        scratch_shapes=[pltpu.VMEM(one.shape, one.dtype) for one in others]
+        scratch_shapes=[pltpu.VMEM(one.shape, one.dtype) for one in others[:-1]]
         + [
             pltpu.VMEM(first.shape, f32),
             pltpu.SemaphoreType.DMA((SPLIT + len(others) - 1 + onehot.shape[0],)),
@@ -600,7 +606,7 @@
     own_neg = neg_tower(packed, apart, w_in, bias_in.reshape(1, -1), w_out)
     negs = gather_negatives(own_neg, user_size, pool_size)
 
-    interests, vec, positive = route(
+    interests, vec, positive, negs[len(negs) // 2] = route(
         renumbered,
         arrived,
         w_in,
@@ -615,6 +621,7 @@
         label_index.reshape(1, -1),
         label_ids.reshape(1, -1),
         label_counts.reshape(1, -1),
+        negs[len(negs) // 2],
     )
     away = late_masks(pool_size)
     vecs = [vec]

time: 68 us -> 67.9 us (level)
  no operation moved by 1% of the time
where the time goes in v13:
time: 67.9 us; the launch traced here: 67.5 us
  waiting for transfers between devices  33.4 us (49%)
  Pallas kernels  18 us (27%)
  starting transfers between devices  14.2 us (21%)
  between operations  0.72 us (1%)
  local copies, waits for them, and re-layouts  0.71 us (1%)
    ppermute x3, waiting for transfers between devices, swap_pool(): return lax.ppermute(array, 'pool', [(at, at ^ bit) for at in range(size)])  22 us
    ppermute x3, waiting for transfers between devices, swap_both(): return lax.ppermute(array, ('user', 'pool'), perm)  11.4 us
    pallas_call x1, Pallas kernels, route(): pl.pallas_call(functools.partial(route_kernel, renumbered), in_specs=[INS...  7.39 us
    all_to_all x1, starting transfers between devices, on_device(): lax.all_to_all(outgoing.reshape(fetch_table.shape[0], fetch_table.shape[2...  7.33 us
    ppermute x3, starting transfers between devices, swap_both(): return lax.ppermute(array, ('user', 'pool'), perm)  3.55 us
    pallas_call x1, Pallas kernels, prepare(): pl.pallas_call(functools.partial(prepare_kernel, renumbered), in_specs=[O...  3.37 us
    pallas_call x1, Pallas kernels, neg_tower(): pl.pallas_call(neg_kernel, in_specs=[INSIDE, INSIDE, INSIDE, OUTSIDE, OUT...  3.14 us
    ppermute x3, starting transfers between devices, swap_pool(): return lax.ppermute(array, 'pool', [(at, at ^ bit) for at in range(size)])  2.82 us
  transfers between devices with their start and end apart: 11, of which 6 were waited for; matrix products, arithmetic and copies ran while one was open for 1% of the time, Pallas kernels for 21%

profile of v13, /device:TPU:0, one launch (start us, length us, event | category | flops | bytes accessed | tf_op | source)
XLA Modules:
  0.0 67.5 jit_solution(597812996470114036)
XLA Ops:
  0.6 2.4 %select_rows.1 = (bf16[512,512]{1,0:T(8,128)(2,1)}, bf16[144,512]{1,0:T(8,128)(2,1)S(1)}) custom-call(s32[1,16,32]{2,1,0:T(8,128)} %bitcast.15, bf16[512,512]{1,0:T(8,128)(2,1)} %rows.1, bf16[128,512]{1,0:T(8,128)(2,1)} %negs.1, s32[1,128]{1,0:T(1,128)} %bitcast.21, s32[1,128]{1,0:T(1,128)} %bitcast.22), custom_call_target="tpu_custom_call" | custom-call | tf_op jit(solution)/shard_map/select_rows/pallas_call | solution.py:175
  3.0 7.3 %all-to-all-start = ((bf16[32,16,512]{2,1,0:T(8,128)(2,1)}), bf16[32,16,512]{2,1,0:T(8,128)(2,1)S(1)}, u32[]{:S(2)}, u32[]{:S(2)}) async-start(bf16[32,16,512]{2,1,0:T(8,128)(2,1)} %bitcast.3), calls=%async_computation | async-start | bytes 1048576 | tf_op jit(solution)/shard_map/all_to_all | solution.py:590
  10.3 2.7 %collective-permute-start = (bf16[144,512]{1,0:T(8,128)(2,1)S(1)}, bf16[144,512]{1,0:T(8,128)(2,1)S(1)}, u32[]{:S(2)}, u32[]{:S(2)}) collective-permute-start(bf16[144,512]{1,0:T(8,128)(2,1)S(1)} %get-tuple-element.19.own_ref), channel_id=1, source_target_pairs={{0,4},{1,5},{2,6},{3,7},{4,0},{5,1},{6,2},{7,3},{8,12},{9,13},{10,... | collective-permute-start | bytes 442376 | tf_op jit(solution)/shard_map/ppermute | solution.py:532
  13.1 3.4 %prepare.1 = (bf16[4,1024,256]{2,1,0:T(8,128)(2,1)}, f32[128,512]{1,0:T(8,128)}, s32[32,256]{1,0:T(8,128)}, bf16[512,2048]{1,0:T(8,128)(2,1)S(1)}) custom-call(s32[32,256]{1,0:T(8,128)} %index.1, s32[1,32]{1,0:T(1,128)} %bitcast.16, f32[32,4,256]{2,1,0:T(4,128)} %init.3, bf16[512,2048]{1,0:T(8,128)(2,1)} %w_in.1), custom_call_target="tpu_custom_call" | custom-call | tf_op jit(solution)/shard_map/prepare/pallas_call | solution.py:337
  16.5 15.2 %collective-permute-done.apart_ref = bf16[144,512]{1,0:T(8,128)(2,1)S(1)} collective-permute-done((bf16[144,512]{1,0:T(8,128)(2,1)S(1)}, bf16[144,512]{1,0:T(8,128)(2,1)S(1)}, u32[]{:S(2)}, u32[]{:S(2)}) %collective-permute-start) | collective-permute-done | bytes 147488 | tf_op jit(solution)/shard_map/ppermute | solution.py:532
  31.6 3.1 %neg_tower.1.refs_2_ = bf16[528,256]{1,0:T(8,128)(2,1)} custom-call(bf16[144,512]{1,0:T(8,128)(2,1)S(1)} %get-tuple-element.19.own_ref, bf16[144,512]{1,0:T(8,128)(2,1)S(1)} %collective-permute-done.apart_ref, bf16[512,2048]{1,0:T(8,128)(2,1)S(1)} %get-tuple-element.15.w_in_ref, f32[1,2048]{1,0:T(1,128)} %bitcast.13, bf16[2048,512]{1,0:T(8,128)(2,1)} %w_out.3), custom_call_target="tpu_custom_call" | custom-call | tf_op jit(solution)/shard_map/neg_tower/pallas_call | solution.py:222
  34.8 2.5 %collective-permute-start.3 = (bf16[528,256]{1,0:T(8,128)(2,1)}, bf16[528,256]{1,0:T(8,128)(2,1)S(1)}, u32[]{:S(2)}, u32[]{:S(2)}) collective-permute-start(bf16[528,256]{1,0:T(8,128)(2,1)} %neg_tower.1.refs_2_), channel_id=1, source_target_pairs={{0,17},{1,16},{2,19},{3,18},{4,21},{5,20},{6,23},{7,22},{8,25},{9,... | collective-permute-start | bytes 811016 | tf_op jit(solution)/shard_map/ppermute | solution.py:549
  37.2 0.5 collective-permute-start.4
  37.8 0.6 collective-permute-start.5
  38.3 0.0 collective-permute-start.1
  38.3 7.0 %collective-permute-done.3.refs_3_ = bf16[528,256]{1,0:T(8,128)(2,1)S(1)} collective-permute-done((bf16[528,256]{1,0:T(8,128)(2,1)}, bf16[528,256]{1,0:T(8,128)(2,1)S(1)}, u32[]{:S(2)}, u32[]{:S(2)}) %collective-permute-start.3) | collective-permute-done | bytes 270368 | tf_op jit(solution)/shard_map/ppermute | solution.py:549
  45.3 0.0 collective-permute-start.6
  45.3 4.3 %collective-permute-done.4.refs_4_ = bf16[528,256]{1,0:T(8,128)(2,1)S(1)} collective-permute-done((bf16[528,256]{1,0:T(8,128)(2,1)}, bf16[528,256]{1,0:T(8,128)(2,1)S(1)}, u32[]{:S(2)}, u32[]{:S(2)}) %collective-permute-start.4) | collective-permute-done | bytes 270368 | tf_op jit(solution)/shard_map/ppermute | solution.py:549
  49.7 0.0 collective-permute-start.7
  49.7 0.1 collective-permute-done.5.refs_5_
  49.7 0.4 collective-permute-start.8
  50.2 0.0 collective-permute-done.1.held
  50.2 0.0 all-to-all-done
  50.2 0.0 copy-start
  50.2 7.4 %route.1 = (f32[32,2048]{1,0:T(8,128)S(1)}, bf16[32,640]{1,0:T(8,128)(2,1)S(1)}, f32[1,32]{1,0:T(1,128)S(1)}, bf16[528,256]{1,0:T(8,128)(2,1)S(1)}) custom-call(bf16[512,512]{1,0:T(8,128)(2,1)S(1)} %bitcast.12, bf16[512,2048]{1,0:T(8,128)(2,1)S(1)} %get-tuple-element.15.w_in_ref, f32[1,2048]{1,0:T(1,128)} %bitcast.14, bf16[2048,512]{1,0:T(8,128)(2,1)} %w_out.3, ...), custom_call_target="tpu_custom_call" | custom-call | tf_op jit(solution)/shard_map/route/pallas_call | solution.py:480
  57.6 0.1 collective-permute-start.2
  57.7 0.0 collective-permute-done.6.refs_7_
  57.7 0.0 collective-permute-done.7.refs_8_
  57.7 0.0 collective-permute-done.8.refs_9_
  57.7 4.0 %collective-permute-done.2.refs_1_ = bf16[32,640]{1,0:T(8,128)(2,1)S(1)} collective-permute-done((bf16[32,640]{1,0:T(8,128)(2,1)S(1)}, bf16[32,640]{1,0:T(8,128)(2,1)S(1)}, u32[]{:S(2)}, u32[]{:S(2)}) %collective-permute-start.2) | collective-permute-done | bytes 40992 | tf_op jit(solution)/shard_map/ppermute | solution.py:532
  61.7 0.0 copy-done
  61.7 1.8 %negative_sums.1 = (f32[1,32]{1,0:T(1,128)S(1)}, f32[1,32]{1,0:T(1,128)S(1)}) custom-call(bf16[32,640]{1,0:T(8,128)(2,1)S(1)} %get-tuple-element.22.refs_0_, bf16[32,640]{1,0:T(8,128)(2,1)S(1)} %collective-permute-done.2.refs_1_, bf16[528,256]{1,0:T(8,128)(2,1)S(1)} %copy-done, bf16[528,256]{1,0:T(8,128)(2,1)S(1)} %collective-permute-done.3.refs_3_, ...), custom_call_target="tpu_custom_call" | custom-call | tf_op jit(solution)/shard_map/negative_sums/pallas_call | solution.py:523
  63.4 0.0 collective-permute-start.9
  63.5 0.7 %copy.17 = f32[32,2048]{1,0:T(8,128)} copy(f32[32,2048]{1,0:T(8,128)S(1)} %get-tuple-element.26) | data formatting | bytes 524288
  64.2 2.9 %collective-permute-done.9 = f32[1,32]{1,0:T(1,128)S(1)} collective-permute-done((f32[1,32]{1,0:T(1,128)S(1)}, f32[1,32]{1,0:T(1,128)S(1)}, u32[]{:S(2)}, u32[]{:S(2)}) %collective-permute-start.9) | collective-permute-done | bytes 160 | tf_op jit(solution)/shard_map/ppermute | solution.py:532
  67.0 0.5 subtract_bitcast_fusion
Async XLA Ops:
  3.0 47.2 %all-to-all-start = ((bf16[32,16,512]{2,1,0:T(8,128)(2,1)}), bf16[32,16,512]{2,1,0:T(8,128)(2,1)S(1)}, u32[]{:S(2)}, u32[]{:S(2)}) async-start(bf16[32,16,512]{2,1,0:T(8,128)(2,1)} %bitcast.3), calls=%async_computation | async-start | bytes 1048576 | tf_op jit(solution)/shard_map/all_to_all | solution.py:590
  10.3 21.3 %collective-permute-start = (bf16[144,512]{1,0:T(8,128)(2,1)S(1)}, bf16[144,512]{1,0:T(8,128)(2,1)S(1)}, u32[]{:S(2)}, u32[]{:S(2)}) collective-permute-start(bf16[144,512]{1,0:T(8,128)(2,1)S(1)} %get-tuple-element.19.own_ref), channel_id=1, source_target_pairs={{0,4},{1,5},{2,6},{3,7},{4,0},{5,1},{6,2},{7,3},{8,12},{9,13},{10,... | collective-permute-start | bytes 442376 | tf_op jit(solution)/shard_map/ppermute | solution.py:532
  34.8 10.6 %collective-permute-start.3 = (bf16[528,256]{1,0:T(8,128)(2,1)}, bf16[528,256]{1,0:T(8,128)(2,1)S(1)}, u32[]{:S(2)}, u32[]{:S(2)}) collective-permute-start(bf16[528,256]{1,0:T(8,128)(2,1)} %neg_tower.1.refs_2_), channel_id=1, source_target_pairs={{0,17},{1,16},{2,19},{3,18},{4,21},{5,20},{6,23},{7,22},{8,25},{9,... | collective-permute-start | bytes 811016 | tf_op jit(solution)/shard_map/ppermute | solution.py:549
  37.2 12.4 %collective-permute-start.4 = (bf16[528,256]{1,0:T(8,128)(2,1)}, bf16[528,256]{1,0:T(8,128)(2,1)S(1)}, u32[]{:S(2)}, u32[]{:S(2)}) collective-permute-start(bf16[528,256]{1,0:T(8,128)(2,1)} %neg_tower.1.refs_2_), channel_id=1, source_target_pairs={{0,16},{1,17},{2,18},{3,19},{4,20},{5,21},{6,22},{7,23},{8,24},{9,... | collective-permute-start | bytes 811016 | tf_op jit(solution)/shard_map/ppermute | solution.py:549
  37.8 12.0 %collective-permute-start.5 = (bf16[528,256]{1,0:T(8,128)(2,1)}, bf16[528,256]{1,0:T(8,128)(2,1)S(1)}, u32[]{:S(2)}, u32[]{:S(2)}) collective-permute-start(bf16[528,256]{1,0:T(8,128)(2,1)} %neg_tower.1.refs_2_), channel_id=1, source_target_pairs={{0,1},{1,0},{2,3},{3,2},{4,5},{5,4},{6,7},{7,6},{8,9},{9,8},{10,11... | collective-permute-start | bytes 811016 | tf_op jit(solution)/shard_map/ppermute | solution.py:549
  38.3 11.9 %collective-permute-start.1 = (bf16[528,256]{1,0:T(8,128)(2,1)}, bf16[528,256]{1,0:T(8,128)(2,1)}, u32[]{:S(2)}, u32[]{:S(2)}) collective-permute-start(bf16[528,256]{1,0:T(8,128)(2,1)} %neg_tower.1.refs_2_), channel_id=1, source_target_pairs={{0,8},{8,0},{16,24},{24,16},{1,9},{9,1},{17,25},{25,17},{2,10},{10... | collective-permute-start | bytes 811016 | tf_op jit(solution)/shard_map/ppermute | solution.py:540
  45.3 12.3 %collective-permute-start.6 = (bf16[528,256]{1,0:T(8,128)(2,1)S(1)}, bf16[528,256]{1,0:T(8,128)(2,1)}, u32[]{:S(2)}, u32[]{:S(2)}) collective-permute-start(bf16[528,256]{1,0:T(8,128)(2,1)S(1)} %collective-permute-done.3.refs_3_), channel_id=1, source_target_pairs={{0,8},{8,0},{16,24},{24,16},{1,9},{9,1},{17,25},{25,17},{2,10},{10... | collective-permute-start | bytes 811016 | tf_op jit(solution)/shard_map/ppermute | solution.py:540
  49.7 8.0 %collective-permute-start.7 = (bf16[528,256]{1,0:T(8,128)(2,1)S(1)}, bf16[528,256]{1,0:T(8,128)(2,1)}, u32[]{:S(2)}, u32[]{:S(2)}) collective-permute-start(bf16[528,256]{1,0:T(8,128)(2,1)S(1)} %collective-permute-done.4.refs_4_), channel_id=1, source_target_pairs={{0,8},{8,0},{16,24},{24,16},{1,9},{9,1},{17,25},{25,17},{2,10},{10... | collective-permute-start | bytes 811016 | tf_op jit(solution)/shard_map/ppermute | solution.py:540
  49.7 8.0 %collective-permute-start.8 = (bf16[528,256]{1,0:T(8,128)(2,1)S(1)}, bf16[528,256]{1,0:T(8,128)(2,1)}, u32[]{:S(2)}, u32[]{:S(2)}) collective-permute-start(bf16[528,256]{1,0:T(8,128)(2,1)S(1)} %collective-permute-done.5.refs_5_), channel_id=1, source_target_pairs={{0,8},{8,0},{16,24},{24,16},{1,9},{9,1},{17,25},{25,17},{2,10},{10... | collective-permute-start | bytes 811016 | tf_op jit(solution)/shard_map/ppermute | solution.py:540
  50.2 11.5 %copy-start = (bf16[528,256]{1,0:T(8,128)(2,1)S(1)}, bf16[528,256]{1,0:T(8,128)(2,1)}, u32[]{:S(2)}) copy-start(bf16[528,256]{1,0:T(8,128)(2,1)} %neg_tower.1.refs_2_) | copy-start | bytes 811012
  57.6 4.1 %collective-permute-start.2 = (bf16[32,640]{1,0:T(8,128)(2,1)S(1)}, bf16[32,640]{1,0:T(8,128)(2,1)S(1)}, u32[]{:S(2)}, u32[]{:S(2)}) collective-permute-start(bf16[32,640]{1,0:T(8,128)(2,1)S(1)} %get-tuple-element.22.refs_0_), channel_id=1, source_target_pairs={{0,2},{1,3},{2,0},{3,1},{4,6},{5,7},{6,4},{7,5},{8,10},{9,11},{10,... | collective-permute-start | bytes 122888 | tf_op jit(solution)/shard_map/ppermute | solution.py:532
  63.4 3.6 %collective-permute-start.9 = (f32[1,32]{1,0:T(1,128)S(1)}, f32[1,32]{1,0:T(1,128)S(1)}, u32[]{:S(2)}, u32[]{:S(2)}) collective-permute-start(f32[1,32]{1,0:T(1,128)S(1)} %get-tuple-element.25), channel_id=1, source_target_pairs={{0,2},{1,3},{2,0},{3,1},{4,6},{5,7},{6,4},{7,5},{8,10},{9,11},{10,... | collective-permute-start | bytes 392 | tf_op jit(solution)/shard_map/ppermute | solution.py:532

commit v14 on v13

--- a/solution.py
+++ b/solution.py
@@ -417,7 +417,7 @@
     lower = index & (LANES - 1)
     live = live_mask(length_ref, index.shape)
     logits = [init_ref[:, k, :] for k in range(INTERESTS)]
-    capsules = label_rows = None
+    capsules = None
     for iteration in range(ITERS):
         if iteration == 1:
             fetch.wait()
@@ -431,10 +431,6 @@
         capsules = sums * (jnp.sqrt(norm_sq) / (1.0 + norm_sq))
         if iteration + 1 < ITERS:
             scores = mm_nt(capsules.astype(bf16), mapped)
-            if iteration == 0:
-                label = to_column(renumbered(label_ref[...]).astype(f32))
-                chosen = jnp.where(iota((users, slots), 1).astype(f32) == label, 1.0, 0.0)
-                label_rows = mm(chosen.astype(bf16), unit)
             found = [[None] * (events // LANES) for _ in range(INTERESTS)]
             for part in range(events // LANES):
                 rows = [[] for _ in range(INTERESTS)]
@@ -460,6 +456,9 @@
     each = [capsules[k * users : (k + 1) * users] for k in range(INTERESTS)]
     for k in range(INTERESTS):
         interests_ref[:, k * width : (k + 1) * width] = each[k]
+    label = to_column(renumbered(label_ref[...]).astype(f32))
+    chosen = jnp.where(iota((users, slots), 1).astype(f32) == label, 1.0, 0.0).astype(bf16)
+    label_rows = mm(chosen, unit)
     raised = [
         jnp.exp(attend_scale * jnp.sum(one * label_rows, axis=1, keepdims=True)) for one in each
     ]

time: 67.9 us -> 67.9 us (level)
  no operation moved by 1% of the time
where the time goes in v14:
time: 67.9 us; the launch traced here: 67.5 us
  waiting for transfers between devices  33.4 us (49%)
  Pallas kernels  18 us (27%)
  starting transfers between devices  14.2 us (21%)
  between operations  0.72 us (1%)
  local copies, waits for them, and re-layouts  0.71 us (1%)
    ppermute x3, waiting for transfers between devices, swap_pool(): return lax.ppermute(array, 'pool', [(at, at ^ bit) for at in range(size)])  22 us
    ppermute x3, waiting for transfers between devices, swap_both(): return lax.ppermute(array, ('user', 'pool'), perm)  11.4 us
    pallas_call x1, Pallas kernels, route(): pl.pallas_call(functools.partial(route_kernel, renumbered), in_specs=[INS...  7.36 us
    all_to_all x1, starting transfers between devices, on_device(): lax.all_to_all(outgoing.reshape(fetch_table.shape[0], fetch_table.shape[2...  7.33 us
    ppermute x3, starting transfers between devices, swap_both(): return lax.ppermute(array, ('user', 'pool'), perm)  3.55 us
    pallas_call x1, Pallas kernels, prepare(): pl.pallas_call(functools.partial(prepare_kernel, renumbered), in_specs=[O...  3.37 us
    pallas_call x1, Pallas kernels, neg_tower(): pl.pallas_call(neg_kernel, in_specs=[INSIDE, INSIDE, INSIDE, OUTSIDE, OUT...  3.14 us
    ppermute x3, starting transfers between devices, swap_pool(): return lax.ppermute(array, 'pool', [(at, at ^ bit) for at in range(size)])  2.82 us
  transfers between devices with their start and end apart: 11, of which 6 were waited for; matrix products, arithmetic and copies ran while one was open for 1% of the time, Pallas kernels for 21%

profile of v14, /device:TPU:0, one launch (start us, length us, event | category | flops | bytes accessed | tf_op | source)
XLA Modules:
  0.0 67.5 jit_solution(1480518092933715000)
XLA Ops:
  0.6 2.4 %select_rows.1 = (bf16[512,512]{1,0:T(8,128)(2,1)}, bf16[144,512]{1,0:T(8,128)(2,1)S(1)}) custom-call(s32[1,16,32]{2,1,0:T(8,128)} %bitcast.15, bf16[512,512]{1,0:T(8,128)(2,1)} %rows.1, bf16[128,512]{1,0:T(8,128)(2,1)} %negs.1, s32[1,128]{1,0:T(1,128)} %bitcast.21, s32[1,128]{1,0:T(1,128)} %bitcast.22), custom_call_target="tpu_custom_call" | custom-call | tf_op jit(solution)/shard_map/select_rows/pallas_call | solution.py:175
  3.0 7.3 %all-to-all-start = ((bf16[32,16,512]{2,1,0:T(8,128)(2,1)}), bf16[32,16,512]{2,1,0:T(8,128)(2,1)S(1)}, u32[]{:S(2)}, u32[]{:S(2)}) async-start(bf16[32,16,512]{2,1,0:T(8,128)(2,1)} %bitcast.3), calls=%async_computation | async-start | bytes 1048576 | tf_op jit(solution)/shard_map/all_to_all | solution.py:589
  10.3 2.7 %collective-permute-start = (bf16[144,512]{1,0:T(8,128)(2,1)S(1)}, bf16[144,512]{1,0:T(8,128)(2,1)S(1)}, u32[]{:S(2)}, u32[]{:S(2)}) collective-permute-start(bf16[144,512]{1,0:T(8,128)(2,1)S(1)} %get-tuple-element.19.own_ref), channel_id=1, source_target_pairs={{0,4},{1,5},{2,6},{3,7},{4,0},{5,1},{6,2},{7,3},{8,12},{9,13},{10,... | collective-permute-start | bytes 442376 | tf_op jit(solution)/shard_map/ppermute | solution.py:531
  13.1 3.4 %prepare.1 = (bf16[4,1024,256]{2,1,0:T(8,128)(2,1)}, f32[128,512]{1,0:T(8,128)}, s32[32,256]{1,0:T(8,128)}, bf16[512,2048]{1,0:T(8,128)(2,1)S(1)}) custom-call(s32[32,256]{1,0:T(8,128)} %index.1, s32[1,32]{1,0:T(1,128)} %bitcast.16, f32[32,4,256]{2,1,0:T(4,128)} %init.3, bf16[512,2048]{1,0:T(8,128)(2,1)} %w_in.1), custom_call_target="tpu_custom_call" | custom-call | tf_op jit(solution)/shard_map/prepare/pallas_call | solution.py:337
  16.5 15.2 %collective-permute-done.apart_ref = bf16[144,512]{1,0:T(8,128)(2,1)S(1)} collective-permute-done((bf16[144,512]{1,0:T(8,128)(2,1)S(1)}, bf16[144,512]{1,0:T(8,128)(2,1)S(1)}, u32[]{:S(2)}, u32[]{:S(2)}) %collective-permute-start) | collective-permute-done | bytes 147488 | tf_op jit(solution)/shard_map/ppermute | solution.py:531
  31.6 3.1 %neg_tower.1.refs_2_ = bf16[528,256]{1,0:T(8,128)(2,1)} custom-call(bf16[144,512]{1,0:T(8,128)(2,1)S(1)} %get-tuple-element.19.own_ref, bf16[144,512]{1,0:T(8,128)(2,1)S(1)} %collective-permute-done.apart_ref, bf16[512,2048]{1,0:T(8,128)(2,1)S(1)} %get-tuple-element.15.w_in_ref, f32[1,2048]{1,0:T(1,128)} %bitcast.13, bf16[2048,512]{1,0:T(8,128)(2,1)} %w_out.3), custom_call_target="tpu_custom_call" | custom-call | tf_op jit(solution)/shard_map/neg_tower/pallas_call | solution.py:222
  34.8 2.5 %collective-permute-start.3 = (bf16[528,256]{1,0:T(8,128)(2,1)}, bf16[528,256]{1,0:T(8,128)(2,1)S(1)}, u32[]{:S(2)}, u32[]{:S(2)}) collective-permute-start(bf16[528,256]{1,0:T(8,128)(2,1)} %neg_tower.1.refs_2_), channel_id=1, source_target_pairs={{0,17},{1,16},{2,19},{3,18},{4,21},{5,20},{6,23},{7,22},{8,25},{9,... | collective-permute-start | bytes 811016 | tf_op jit(solution)/shard_map/ppermute | solution.py:548
  37.2 0.5 collective-permute-start.4
  37.8 0.6 collective-permute-start.5
  38.3 0.0 collective-permute-start.1
  38.3 7.0 %collective-permute-done.3.refs_3_ = bf16[528,256]{1,0:T(8,128)(2,1)S(1)} collective-permute-done((bf16[528,256]{1,0:T(8,128)(2,1)}, bf16[528,256]{1,0:T(8,128)(2,1)S(1)}, u32[]{:S(2)}, u32[]{:S(2)}) %collective-permute-start.3) | collective-permute-done | bytes 270368 | tf_op jit(solution)/shard_map/ppermute | solution.py:548
  45.3 0.0 collective-permute-start.6
  45.3 4.3 %collective-permute-done.4.refs_4_ = bf16[528,256]{1,0:T(8,128)(2,1)S(1)} collective-permute-done((bf16[528,256]{1,0:T(8,128)(2,1)}, bf16[528,256]{1,0:T(8,128)(2,1)S(1)}, u32[]{:S(2)}, u32[]{:S(2)}) %collective-permute-start.4) | collective-permute-done | bytes 270368 | tf_op jit(solution)/shard_map/ppermute | solution.py:548
  49.7 0.0 collective-permute-start.7
  49.7 0.1 collective-permute-done.5.refs_5_
  49.7 0.4 collective-permute-start.8
  50.2 0.0 collective-permute-done.1.held
  50.2 0.0 all-to-all-done
  50.2 0.0 copy-start
  50.2 7.4 %route.1 = (f32[32,2048]{1,0:T(8,128)S(1)}, bf16[32,640]{1,0:T(8,128)(2,1)S(1)}, f32[1,32]{1,0:T(1,128)S(1)}, bf16[528,256]{1,0:T(8,128)(2,1)S(1)}) custom-call(bf16[512,512]{1,0:T(8,128)(2,1)S(1)} %bitcast.12, bf16[512,2048]{1,0:T(8,128)(2,1)S(1)} %get-tuple-element.15.w_in_ref, f32[1,2048]{1,0:T(1,128)} %bitcast.14, bf16[2048,512]{1,0:T(8,128)(2,1)} %w_out.3, ...), custom_call_target="tpu_custom_call" | custom-call | tf_op jit(solution)/shard_map/route/pallas_call | solution.py:479
  57.6 0.1 collective-permute-start.2
  57.6 0.0 collective-permute-done.6.refs_7_
  57.7 0.0 collective-permute-done.7.refs_8_
  57.7 0.0 collective-permute-done.8.refs_9_
  57.7 4.0 %collective-permute-done.2.refs_1_ = bf16[32,640]{1,0:T(8,128)(2,1)S(1)} collective-permute-done((bf16[32,640]{1,0:T(8,128)(2,1)S(1)}, bf16[32,640]{1,0:T(8,128)(2,1)S(1)}, u32[]{:S(2)}, u32[]{:S(2)}) %collective-permute-start.2) | collective-permute-done | bytes 40992 | tf_op jit(solution)/shard_map/ppermute | solution.py:531
  61.6 0.0 copy-done
  61.6 1.8 %negative_sums.1 = (f32[1,32]{1,0:T(1,128)S(1)}, f32[1,32]{1,0:T(1,128)S(1)}) custom-call(bf16[32,640]{1,0:T(8,128)(2,1)S(1)} %get-tuple-element.22.refs_0_, bf16[32,640]{1,0:T(8,128)(2,1)S(1)} %collective-permute-done.2.refs_1_, bf16[528,256]{1,0:T(8,128)(2,1)S(1)} %copy-done, bf16[528,256]{1,0:T(8,128)(2,1)S(1)} %collective-permute-done.3.refs_3_, ...), custom_call_target="tpu_custom_call" | custom-call | tf_op jit(solution)/shard_map/negative_sums/pallas_call | solution.py:522
  63.4 0.0 collective-permute-start.9
  63.4 0.7 %copy.17 = f32[32,2048]{1,0:T(8,128)} copy(f32[32,2048]{1,0:T(8,128)S(1)} %get-tuple-element.26) | data formatting | bytes 524288
  64.1 2.9 %collective-permute-done.9 = f32[1,32]{1,0:T(1,128)S(1)} collective-permute-done((f32[1,32]{1,0:T(1,128)S(1)}, f32[1,32]{1,0:T(1,128)S(1)}, u32[]{:S(2)}, u32[]{:S(2)}) %collective-permute-start.9) | collective-permute-done | bytes 160 | tf_op jit(solution)/shard_map/ppermute | solution.py:531
  67.0 0.5 subtract_bitcast_fusion
Async XLA Ops:
  3.0 47.2 %all-to-all-start = ((bf16[32,16,512]{2,1,0:T(8,128)(2,1)}), bf16[32,16,512]{2,1,0:T(8,128)(2,1)S(1)}, u32[]{:S(2)}, u32[]{:S(2)}) async-start(bf16[32,16,512]{2,1,0:T(8,128)(2,1)} %bitcast.3), calls=%async_computation | async-start | bytes 1048576 | tf_op jit(solution)/shard_map/all_to_all | solution.py:589
  10.3 21.3 %collective-permute-start = (bf16[144,512]{1,0:T(8,128)(2,1)S(1)}, bf16[144,512]{1,0:T(8,128)(2,1)S(1)}, u32[]{:S(2)}, u32[]{:S(2)}) collective-permute-start(bf16[144,512]{1,0:T(8,128)(2,1)S(1)} %get-tuple-element.19.own_ref), channel_id=1, source_target_pairs={{0,4},{1,5},{2,6},{3,7},{4,0},{5,1},{6,2},{7,3},{8,12},{9,13},{10,... | collective-permute-start | bytes 442376 | tf_op jit(solution)/shard_map/ppermute | solution.py:531
  34.8 10.6 %collective-permute-start.3 = (bf16[528,256]{1,0:T(8,128)(2,1)}, bf16[528,256]{1,0:T(8,128)(2,1)S(1)}, u32[]{:S(2)}, u32[]{:S(2)}) collective-permute-start(bf16[528,256]{1,0:T(8,128)(2,1)} %neg_tower.1.refs_2_), channel_id=1, source_target_pairs={{0,17},{1,16},{2,19},{3,18},{4,21},{5,20},{6,23},{7,22},{8,25},{9,... | collective-permute-start | bytes 811016 | tf_op jit(solution)/shard_map/ppermute | solution.py:548
  37.2 12.4 %collective-permute-start.4 = (bf16[528,256]{1,0:T(8,128)(2,1)}, bf16[528,256]{1,0:T(8,128)(2,1)S(1)}, u32[]{:S(2)}, u32[]{:S(2)}) collective-permute-start(bf16[528,256]{1,0:T(8,128)(2,1)} %neg_tower.1.refs_2_), channel_id=1, source_target_pairs={{0,16},{1,17},{2,18},{3,19},{4,20},{5,21},{6,22},{7,23},{8,24},{9,... | collective-permute-start | bytes 811016 | tf_op jit(solution)/shard_map/ppermute | solution.py:548
  37.8 12.0 %collective-permute-start.5 = (bf16[528,256]{1,0:T(8,128)(2,1)}, bf16[528,256]{1,0:T(8,128)(2,1)S(1)}, u32[]{:S(2)}, u32[]{:S(2)}) collective-permute-start(bf16[528,256]{1,0:T(8,128)(2,1)} %neg_tower.1.refs_2_), channel_id=1, source_target_pairs={{0,1},{1,0},{2,3},{3,2},{4,5},{5,4},{6,7},{7,6},{8,9},{9,8},{10,11... | collective-permute-start | bytes 811016 | tf_op jit(solution)/shard_map/ppermute | solution.py:548
  38.3 11.9 %collective-permute-start.1 = (bf16[528,256]{1,0:T(8,128)(2,1)}, bf16[528,256]{1,0:T(8,128)(2,1)}, u32[]{:S(2)}, u32[]{:S(2)}) collective-permute-start(bf16[528,256]{1,0:T(8,128)(2,1)} %neg_tower.1.refs_2_), channel_id=1, source_target_pairs={{0,8},{8,0},{16,24},{24,16},{1,9},{9,1},{17,25},{25,17},{2,10},{10... | collective-permute-start | bytes 811016 | tf_op jit(solution)/shard_map/ppermute | solution.py:539
  45.3 12.3 %collective-permute-start.6 = (bf16[528,256]{1,0:T(8,128)(2,1)S(1)}, bf16[528,256]{1,0:T(8,128)(2,1)}, u32[]{:S(2)}, u32[]{:S(2)}) collective-permute-start(bf16[528,256]{1,0:T(8,128)(2,1)S(1)} %collective-permute-done.3.refs_3_), channel_id=1, source_target_pairs={{0,8},{8,0},{16,24},{24,16},{1,9},{9,1},{17,25},{25,17},{2,10},{10... | collective-permute-start | bytes 811016 | tf_op jit(solution)/shard_map/ppermute | solution.py:539
  49.7 8.0 %collective-permute-start.7 = (bf16[528,256]{1,0:T(8,128)(2,1)S(1)}, bf16[528,256]{1,0:T(8,128)(2,1)}, u32[]{:S(2)}, u32[]{:S(2)}) collective-permute-start(bf16[528,256]{1,0:T(8,128)(2,1)S(1)} %collective-permute-done.4.refs_4_), channel_id=1, source_target_pairs={{0,8},{8,0},{16,24},{24,16},{1,9},{9,1},{17,25},{25,17},{2,10},{10... | collective-permute-start | bytes 811016 | tf_op jit(solution)/shard_map/ppermute | solution.py:539
  49.7 7.9 %collective-permute-start.8 = (bf16[528,256]{1,0:T(8,128)(2,1)S(1)}, bf16[528,256]{1,0:T(8,128)(2,1)}, u32[]{:S(2)}, u32[]{:S(2)}) collective-permute-start(bf16[528,256]{1,0:T(8,128)(2,1)S(1)} %collective-permute-done.5.refs_5_), channel_id=1, source_target_pairs={{0,8},{8,0},{16,24},{24,16},{1,9},{9,1},{17,25},{25,17},{2,10},{10... | collective-permute-start | bytes 811016 | tf_op jit(solution)/shard_map/ppermute | solution.py:539
  50.2 11.4 %copy-start = (bf16[528,256]{1,0:T(8,128)(2,1)S(1)}, bf16[528,256]{1,0:T(8,128)(2,1)}, u32[]{:S(2)}) copy-start(bf16[528,256]{1,0:T(8,128)(2,1)} %neg_tower.1.refs_2_) | copy-start | bytes 811012
  57.6 4.1 %collective-permute-start.2 = (bf16[32,640]{1,0:T(8,128)(2,1)S(1)}, bf16[32,640]{1,0:T(8,128)(2,1)S(1)}, u32[]{:S(2)}, u32[]{:S(2)}) collective-permute-start(bf16[32,640]{1,0:T(8,128)(2,1)S(1)} %get-tuple-element.22.refs_0_), channel_id=1, source_target_pairs={{0,2},{1,3},{2,0},{3,1},{4,6},{5,7},{6,4},{7,5},{8,10},{9,11},{10,... | collective-permute-start | bytes 122888 | tf_op jit(solution)/shard_map/ppermute | solution.py:531
  63.4 3.6 %collective-permute-start.9 = (f32[1,32]{1,0:T(1,128)S(1)}, f32[1,32]{1,0:T(1,128)S(1)}, u32[]{:S(2)}, u32[]{:S(2)}) collective-permute-start(f32[1,32]{1,0:T(1,128)S(1)} %get-tuple-element.25), channel_id=1, source_target_pairs={{0,2},{1,3},{2,0},{3,1},{4,6},{5,7},{6,4},{7,5},{8,10},{9,11},{10,... | collective-permute-start | bytes 392 | tf_op jit(solution)/shard_map/ppermute | solution.py:531

commit v15 on v12

--- a/solution.py
+++ b/solution.py
@@ -194,9 +194,14 @@
 def tower(rows_ref, w_in_ref, bias, w_out, bias_ref, out_ref, sems):
     small = Copies(bias, bias_ref, sems, 0, 1)
     large = Copies(w_out, out_ref, sems, 1, SPLIT)
-    hidden = mm(rows_ref[...], w_in_ref[...])
     small.wait()
-    hidden = jnp.maximum(hidden + bias_ref[...], 0.0).astype(bf16)
+    total_units = w_in_ref.shape[1]
+    chunk = total_units // SPLIT
+    hidden = []
+    for at in range(0, total_units, chunk):
+        piece = mm(rows_ref[...], w_in_ref[:, at : at + chunk]) + bias_ref[:, at : at + chunk]
+        hidden.append(jnp.maximum(piece, 0.0).astype(bf16))
+    hidden = jnp.concatenate(hidden, axis=1)
     large.wait()
     embedding = mm(hidden, out_ref[...])
     total = jnp.sum(embedding * embedding, axis=1, keepdims=True)

time: 68 us -> 68 us (level)
  no operation moved by 1% of the time
where the time goes in v15:
time: 68 us; the launch traced here: 67.6 us
  waiting for transfers between devices  33.4 us (49%)
  Pallas kernels  18.1 us (27%)
  starting transfers between devices  14.2 us (21%)
  between operations  0.73 us (1%)
  local copies, waits for them, and re-layouts  0.71 us (1%)
    ppermute x3, waiting for transfers between devices, swap_pool(): return lax.ppermute(array, 'pool', [(at, at ^ bit) for at in range(size)])  22 us
    ppermute x3, waiting for transfers between devices, swap_both(): return lax.ppermute(array, ('user', 'pool'), perm)  11.4 us
    pallas_call x1, Pallas kernels, route(): pl.pallas_call(functools.partial(route_kernel, renumbered), in_specs=[INS...  7.34 us
    all_to_all x1, starting transfers between devices, on_device(): lax.all_to_all(outgoing.reshape(fetch_table.shape[0], fetch_table.shape[2...  7.33 us
    ppermute x3, starting transfers between devices, swap_both(): return lax.ppermute(array, ('user', 'pool'), perm)  3.55 us
    pallas_call x1, Pallas kernels, prepare(): pl.pallas_call(functools.partial(prepare_kernel, renumbered), in_specs=[O...  3.37 us
    pallas_call x1, Pallas kernels, neg_tower(): pl.pallas_call(neg_kernel, in_specs=[INSIDE, INSIDE, INSIDE, OUTSIDE, OUT...  3.17 us
    ppermute x3, starting transfers between devices, swap_pool(): return lax.ppermute(array, 'pool', [(at, at ^ bit) for at in range(size)])  2.82 us
  transfers between devices with their start and end apart: 11, of which 6 were waited for; matrix products, arithmetic and copies ran while one was open for 1% of the time, Pallas kernels for 21%

profile of v15, /device:TPU:0, one launch (start us, length us, event | category | flops | bytes accessed | tf_op | source)
XLA Modules:
  0.0 67.6 jit_solution(10555431278508034966)
XLA Ops:
  0.6 2.3 %select_rows.1 = (bf16[512,512]{1,0:T(8,128)(2,1)}, bf16[144,512]{1,0:T(8,128)(2,1)S(1)}) custom-call(s32[1,16,32]{2,1,0:T(8,128)} %bitcast.15, bf16[512,512]{1,0:T(8,128)(2,1)} %rows.1, bf16[128,512]{1,0:T(8,128)(2,1)} %negs.1, s32[1,128]{1,0:T(1,128)} %bitcast.21, s32[1,128]{1,0:T(1,128)} %bitcast.22), custom_call_target="tpu_custom_call" | custom-call | tf_op jit(solution)/shard_map/select_rows/pallas_call | solution.py:175
  3.0 7.3 %all-to-all-start = ((bf16[32,16,512]{2,1,0:T(8,128)(2,1)}), bf16[32,16,512]{2,1,0:T(8,128)(2,1)S(1)}, u32[]{:S(2)}, u32[]{:S(2)}) async-start(bf16[32,16,512]{2,1,0:T(8,128)(2,1)} %bitcast.3), calls=%async_computation | async-start | bytes 1048576 | tf_op jit(solution)/shard_map/all_to_all | solution.py:589
  10.3 2.7 %collective-permute-start.1 = (bf16[144,512]{1,0:T(8,128)(2,1)S(1)}, bf16[144,512]{1,0:T(8,128)(2,1)S(1)}, u32[]{:S(2)}, u32[]{:S(2)}) collective-permute-start(bf16[144,512]{1,0:T(8,128)(2,1)S(1)} %get-tuple-element.21.own_ref), channel_id=1, source_target_pairs={{0,4},{1,5},{2,6},{3,7},{4,0},{5,1},{6,2},{7,3},{8,12},{9,13},{10,... | collective-permute-start | bytes 442376 | tf_op jit(solution)/shard_map/ppermute | solution.py:531
  13.1 3.4 %prepare.1 = (bf16[4,1024,256]{2,1,0:T(8,128)(2,1)}, f32[128,512]{1,0:T(8,128)}, s32[32,256]{1,0:T(8,128)}, bf16[512,2048]{1,0:T(8,128)(2,1)S(1)}) custom-call(s32[32,256]{1,0:T(8,128)} %index.1, s32[1,32]{1,0:T(1,128)} %bitcast.16, f32[32,4,256]{2,1,0:T(4,128)} %init.3, bf16[512,2048]{1,0:T(8,128)(2,1)} %w_in.1), custom_call_target="tpu_custom_call" | custom-call | tf_op jit(solution)/shard_map/prepare/pallas_call | solution.py:342
  16.4 15.2 %collective-permute-done.1.apart_ref = bf16[144,512]{1,0:T(8,128)(2,1)S(1)} collective-permute-done((bf16[144,512]{1,0:T(8,128)(2,1)S(1)}, bf16[144,512]{1,0:T(8,128)(2,1)S(1)}, u32[]{:S(2)}, u32[]{:S(2)}) %collective-permute-start.1) | collective-permute-done | bytes 147488 | tf_op jit(solution)/shard_map/ppermute | solution.py:531
  31.6 3.2 %neg_tower.1.refs_2_ = bf16[528,256]{1,0:T(8,128)(2,1)} custom-call(bf16[144,512]{1,0:T(8,128)(2,1)S(1)} %get-tuple-element.21.own_ref, bf16[144,512]{1,0:T(8,128)(2,1)S(1)} %collective-permute-done.1.apart_ref, bf16[512,2048]{1,0:T(8,128)(2,1)S(1)} %get-tuple-element.14.w_in_ref, f32[1,2048]{1,0:T(1,128)} %bitcast.13, bf16[2048,512]{1,0:T(8,128)(2,1)} %w_out.3), custom_call_target="tpu_custom_call" | custom-call | tf_op jit(solution)/shard_map/neg_tower/pallas_call | solution.py:227
  34.8 2.5 %collective-permute-start.2 = (bf16[528,256]{1,0:T(8,128)(2,1)}, bf16[528,256]{1,0:T(8,128)(2,1)S(1)}, u32[]{:S(2)}, u32[]{:S(2)}) collective-permute-start(bf16[528,256]{1,0:T(8,128)(2,1)} %neg_tower.1.refs_2_), channel_id=1, source_target_pairs={{0,17},{1,16},{2,19},{3,18},{4,21},{5,20},{6,23},{7,22},{8,25},{9,... | collective-permute-start | bytes 811016 | tf_op jit(solution)/shard_map/ppermute | solution.py:548
  37.3 0.5 collective-permute-start.3
  37.8 0.6 collective-permute-start.4
  38.4 0.0 collective-permute-start.5
  38.4 7.0 %collective-permute-done.2.refs_3_ = bf16[528,256]{1,0:T(8,128)(2,1)S(1)} collective-permute-done((bf16[528,256]{1,0:T(8,128)(2,1)}, bf16[528,256]{1,0:T(8,128)(2,1)S(1)}, u32[]{:S(2)}, u32[]{:S(2)}) %collective-permute-start.2) | collective-permute-done | bytes 270368 | tf_op jit(solution)/shard_map/ppermute | solution.py:548
  45.4 0.0 collective-permute-start.6
  45.4 4.3 %collective-permute-done.3.refs_4_ = bf16[528,256]{1,0:T(8,128)(2,1)S(1)} collective-permute-done((bf16[528,256]{1,0:T(8,128)(2,1)}, bf16[528,256]{1,0:T(8,128)(2,1)S(1)}, u32[]{:S(2)}, u32[]{:S(2)}) %collective-permute-start.3) | collective-permute-done | bytes 270368 | tf_op jit(solution)/shard_map/ppermute | solution.py:548
  49.7 0.0 collective-permute-start.7
  49.7 0.1 collective-permute-done.4.refs_5_
  49.8 0.4 collective-permute-start.8
  50.2 0.0 all-to-all-done
  50.2 0.0 copy-start
  50.2 7.3 %route.1 = (f32[32,2048]{1,0:T(8,128)S(1)}, bf16[32,640]{1,0:T(8,128)(2,1)S(1)}, f32[1,32]{1,0:T(1,128)S(1)}) custom-call(bf16[512,512]{1,0:T(8,128)(2,1)S(1)} %bitcast.12, bf16[512,2048]{1,0:T(8,128)(2,1)S(1)} %get-tuple-element.14.w_in_ref, f32[1,2048]{1,0:T(1,128)} %bitcast.14, bf16[2048,512]{1,0:T(8,128)(2,1)} %w_out.3, bf16[512,512]{1,0:T(8,128)(2,1)} %bilinear.1, ...), custom_call_target="tpu_custom_call" | custom-call | tf_op jit(solution)/shard_map/route/pallas_call | solution.py:480
  57.6 0.1 collective-permute-start
  57.6 0.0 collective-permute-done.5.refs_6_
  57.7 0.0 collective-permute-done.6.refs_7_
  57.7 0.0 collective-permute-done.7.refs_8_
  57.7 0.0 collective-permute-done.8.refs_9_
  57.7 3.9 %collective-permute-done.refs_1_ = bf16[32,640]{1,0:T(8,128)(2,1)S(1)} collective-permute-done((bf16[32,640]{1,0:T(8,128)(2,1)S(1)}, bf16[32,640]{1,0:T(8,128)(2,1)S(1)}, u32[]{:S(2)}, u32[]{:S(2)}) %collective-permute-start) | collective-permute-done | bytes 40992 | tf_op jit(solution)/shard_map/ppermute | solution.py:531
  61.6 0.0 copy-done
  61.6 1.9 %negative_sums.1 = (f32[1,32]{1,0:T(1,128)S(1)}, f32[1,32]{1,0:T(1,128)S(1)}) custom-call(bf16[32,640]{1,0:T(8,128)(2,1)S(1)} %get-tuple-element.20.refs_0_, bf16[32,640]{1,0:T(8,128)(2,1)S(1)} %collective-permute-done.refs_1_, bf16[528,256]{1,0:T(8,128)(2,1)S(1)} %copy-done, bf16[528,256]{1,0:T(8,128)(2,1)S(1)} %collective-permute-done.2.refs_3_, ...), custom_call_target="tpu_custom_call" | custom-call | tf_op jit(solution)/shard_map/negative_sums/pallas_call | solution.py:522
  63.5 0.0 collective-permute-start.9
  63.5 0.7 %copy.17 = f32[32,2048]{1,0:T(8,128)} copy(f32[32,2048]{1,0:T(8,128)S(1)} %get-tuple-element.24) | data formatting | bytes 524288
  64.2 2.9 %collective-permute-done.9 = f32[1,32]{1,0:T(1,128)S(1)} collective-permute-done((f32[1,32]{1,0:T(1,128)S(1)}, f32[1,32]{1,0:T(1,128)S(1)}, u32[]{:S(2)}, u32[]{:S(2)}) %collective-permute-start.9) | collective-permute-done | bytes 160 | tf_op jit(solution)/shard_map/ppermute | solution.py:531
  67.1 0.5 subtract_bitcast_fusion
Async XLA Ops:
  3.0 47.2 %all-to-all-start = ((bf16[32,16,512]{2,1,0:T(8,128)(2,1)}), bf16[32,16,512]{2,1,0:T(8,128)(2,1)S(1)}, u32[]{:S(2)}, u32[]{:S(2)}) async-start(bf16[32,16,512]{2,1,0:T(8,128)(2,1)} %bitcast.3), calls=%async_computation | async-start | bytes 1048576 | tf_op jit(solution)/shard_map/all_to_all | solution.py:589
  10.3 21.3 %collective-permute-start.1 = (bf16[144,512]{1,0:T(8,128)(2,1)S(1)}, bf16[144,512]{1,0:T(8,128)(2,1)S(1)}, u32[]{:S(2)}, u32[]{:S(2)}) collective-permute-start(bf16[144,512]{1,0:T(8,128)(2,1)S(1)} %get-tuple-element.21.own_ref), channel_id=1, source_target_pairs={{0,4},{1,5},{2,6},{3,7},{4,0},{5,1},{6,2},{7,3},{8,12},{9,13},{10,... | collective-permute-start | bytes 442376 | tf_op jit(solution)/shard_map/ppermute | solution.py:531
  34.8 10.6 %collective-permute-start.2 = (bf16[528,256]{1,0:T(8,128)(2,1)}, bf16[528,256]{1,0:T(8,128)(2,1)S(1)}, u32[]{:S(2)}, u32[]{:S(2)}) collective-permute-start(bf16[528,256]{1,0:T(8,128)(2,1)} %neg_tower.1.refs_2_), channel_id=1, source_target_pairs={{0,17},{1,16},{2,19},{3,18},{4,21},{5,20},{6,23},{7,22},{8,25},{9,... | collective-permute-start | bytes 811016 | tf_op jit(solution)/shard_map/ppermute | solution.py:548
  37.3 12.4 %collective-permute-start.3 = (bf16[528,256]{1,0:T(8,128)(2,1)}, bf16[528,256]{1,0:T(8,128)(2,1)S(1)}, u32[]{:S(2)}, u32[]{:S(2)}) collective-permute-start(bf16[528,256]{1,0:T(8,128)(2,1)} %neg_tower.1.refs_2_), channel_id=1, source_target_pairs={{0,16},{1,17},{2,18},{3,19},{4,20},{5,21},{6,22},{7,23},{8,24},{9,... | collective-permute-start | bytes 811016 | tf_op jit(solution)/shard_map/ppermute | solution.py:548
  37.8 12.0 %collective-permute-start.4 = (bf16[528,256]{1,0:T(8,128)(2,1)}, bf16[528,256]{1,0:T(8,128)(2,1)S(1)}, u32[]{:S(2)}, u32[]{:S(2)}) collective-permute-start(bf16[528,256]{1,0:T(8,128)(2,1)} %neg_tower.1.refs_2_), channel_id=1, source_target_pairs={{0,1},{1,0},{2,3},{3,2},{4,5},{5,4},{6,7},{7,6},{8,9},{9,8},{10,11... | collective-permute-start | bytes 811016 | tf_op jit(solution)/shard_map/ppermute | solution.py:548
  38.4 19.3 %collective-permute-start.5 = (bf16[528,256]{1,0:T(8,128)(2,1)}, bf16[528,256]{1,0:T(8,128)(2,1)}, u32[]{:S(2)}, u32[]{:S(2)}) collective-permute-start(bf16[528,256]{1,0:T(8,128)(2,1)} %neg_tower.1.refs_2_), channel_id=1, source_target_pairs={{0,8},{8,0},{16,24},{24,16},{1,9},{9,1},{17,25},{25,17},{2,10},{10... | collective-permute-start | bytes 811016 | tf_op jit(solution)/shard_map/ppermute | solution.py:539
  45.4 12.3 %collective-permute-start.6 = (bf16[528,256]{1,0:T(8,128)(2,1)S(1)}, bf16[528,256]{1,0:T(8,128)(2,1)}, u32[]{:S(2)}, u32[]{:S(2)}) collective-permute-start(bf16[528,256]{1,0:T(8,128)(2,1)S(1)} %collective-permute-done.2.refs_3_), channel_id=1, source_target_pairs={{0,8},{8,0},{16,24},{24,16},{1,9},{9,1},{17,25},{25,17},{2,10},{10... | collective-permute-start | bytes 811016 | tf_op jit(solution)/shard_map/ppermute | solution.py:539
  49.7 8.0 %collective-permute-start.7 = (bf16[528,256]{1,0:T(8,128)(2,1)S(1)}, bf16[528,256]{1,0:T(8,128)(2,1)}, u32[]{:S(2)}, u32[]{:S(2)}) collective-permute-start(bf16[528,256]{1,0:T(8,128)(2,1)S(1)} %collective-permute-done.3.refs_4_), channel_id=1, source_target_pairs={{0,8},{8,0},{16,24},{24,16},{1,9},{9,1},{17,25},{25,17},{2,10},{10... | collective-permute-start | bytes 811016 | tf_op jit(solution)/shard_map/ppermute | solution.py:539
  49.8 7.9 %collective-permute-start.8 = (bf16[528,256]{1,0:T(8,128)(2,1)S(1)}, bf16[528,256]{1,0:T(8,128)(2,1)}, u32[]{:S(2)}, u32[]{:S(2)}) collective-permute-start(bf16[528,256]{1,0:T(8,128)(2,1)S(1)} %collective-permute-done.4.refs_5_), channel_id=1, source_target_pairs={{0,8},{8,0},{16,24},{24,16},{1,9},{9,1},{17,25},{25,17},{2,10},{10... | collective-permute-start | bytes 811016 | tf_op jit(solution)/shard_map/ppermute | solution.py:539
  50.2 11.4 %copy-start = (bf16[528,256]{1,0:T(8,128)(2,1)S(1)}, bf16[528,256]{1,0:T(8,128)(2,1)}, u32[]{:S(2)}) copy-start(bf16[528,256]{1,0:T(8,128)(2,1)} %neg_tower.1.refs_2_) | copy-start | bytes 811012
  57.6 4.1 %collective-permute-start = (bf16[32,640]{1,0:T(8,128)(2,1)S(1)}, bf16[32,640]{1,0:T(8,128)(2,1)S(1)}, u32[]{:S(2)}, u32[]{:S(2)}) collective-permute-start(bf16[32,640]{1,0:T(8,128)(2,1)S(1)} %get-tuple-element.20.refs_0_), channel_id=1, source_target_pairs={{0,2},{1,3},{2,0},{3,1},{4,6},{5,7},{6,4},{7,5},{8,10},{9,11},{10,... | collective-permute-start | bytes 122888 | tf_op jit(solution)/shard_map/ppermute | solution.py:531
  63.5 3.6 %collective-permute-start.9 = (f32[1,32]{1,0:T(1,128)S(1)}, f32[1,32]{1,0:T(1,128)S(1)}, u32[]{:S(2)}, u32[]{:S(2)}) collective-permute-start(f32[1,32]{1,0:T(1,128)S(1)} %get-tuple-element.23), channel_id=1, source_target_pairs={{0,2},{1,3},{2,0},{3,1},{4,6},{5,7},{6,4},{7,5},{8,10},{9,11},{10,... | collective-permute-start | bytes 392 | tf_op jit(solution)/shard_map/ppermute | solution.py:531

commit v16 on v14

--- a/solution.py
+++ b/solution.py
@@ -194,9 +194,14 @@
 def tower(rows_ref, w_in_ref, bias, w_out, bias_ref, out_ref, sems):
     small = Copies(bias, bias_ref, sems, 0, 1)
     large = Copies(w_out, out_ref, sems, 1, SPLIT)
-    hidden = mm(rows_ref[...], w_in_ref[...])
     small.wait()
-    hidden = jnp.maximum(hidden + bias_ref[...], 0.0).astype(bf16)
+    total_units = w_in_ref.shape[1]
+    chunk = total_units // SPLIT
+    hidden = []
+    for at in range(0, total_units, chunk):
+        piece = mm(rows_ref[...], w_in_ref[:, at : at + chunk]) + bias_ref[:, at : at + chunk]
+        hidden.append(jnp.maximum(piece, 0.0).astype(bf16))
+    hidden = jnp.concatenate(hidden, axis=1)
     large.wait()
     embedding = mm(hidden, out_ref[...])
     total = jnp.sum(embedding * embedding, axis=1, keepdims=True)

time: 67.9 us -> 67.9 us (level)
  no operation moved by 1% of the time
where the time goes in v16:
time: 67.9 us; the launch traced here: 67.5 us
  waiting for transfers between devices  33.4 us (49%)
  Pallas kernels  18 us (27%)
  starting transfers between devices  14.2 us (21%)
  between operations  0.72 us (1%)
  local copies, waits for them, and re-layouts  0.71 us (1%)
    ppermute x3, waiting for transfers between devices, swap_pool(): return lax.ppermute(array, 'pool', [(at, at ^ bit) for at in range(size)])  22 us
    ppermute x3, waiting for transfers between devices, swap_both(): return lax.ppermute(array, ('user', 'pool'), perm)  11.4 us
    pallas_call x1, Pallas kernels, route(): pl.pallas_call(functools.partial(route_kernel, renumbered), in_specs=[INS...  7.36 us
    all_to_all x1, starting transfers between devices, on_device(): lax.all_to_all(outgoing.reshape(fetch_table.shape[0], fetch_table.shape[2...  7.33 us
    ppermute x3, starting transfers between devices, swap_both(): return lax.ppermute(array, ('user', 'pool'), perm)  3.55 us
    pallas_call x1, Pallas kernels, prepare(): pl.pallas_call(functools.partial(prepare_kernel, renumbered), in_specs=[O...  3.37 us
    pallas_call x1, Pallas kernels, neg_tower(): pl.pallas_call(neg_kernel, in_specs=[INSIDE, INSIDE, INSIDE, OUTSIDE, OUT...  3.14 us
    ppermute x3, starting transfers between devices, swap_pool(): return lax.ppermute(array, 'pool', [(at, at ^ bit) for at in range(size)])  2.82 us
  transfers between devices with their start and end apart: 11, of which 6 were waited for; matrix products, arithmetic and copies ran while one was open for 1% of the time, Pallas kernels for 21%

profile of v16, /device:TPU:0, one launch (start us, length us, event | category | flops | bytes accessed | tf_op | source)
XLA Modules:
  0.0 67.5 jit_solution(2604031474617363528)
XLA Ops:
  0.6 2.4 %select_rows.1 = (bf16[512,512]{1,0:T(8,128)(2,1)}, bf16[144,512]{1,0:T(8,128)(2,1)S(1)}) custom-call(s32[1,16,32]{2,1,0:T(8,128)} %bitcast.15, bf16[512,512]{1,0:T(8,128)(2,1)} %rows.1, bf16[128,512]{1,0:T(8,128)(2,1)} %negs.1, s32[1,128]{1,0:T(1,128)} %bitcast.21, s32[1,128]{1,0:T(1,128)} %bitcast.22), custom_call_target="tpu_custom_call" | custom-call | tf_op jit(solution)/shard_map/select_rows/pallas_call | solution.py:175
  3.0 7.3 %all-to-all-start = ((bf16[32,16,512]{2,1,0:T(8,128)(2,1)}), bf16[32,16,512]{2,1,0:T(8,128)(2,1)S(1)}, u32[]{:S(2)}, u32[]{:S(2)}) async-start(bf16[32,16,512]{2,1,0:T(8,128)(2,1)} %bitcast.3), calls=%async_computation | async-start | bytes 1048576 | tf_op jit(solution)/shard_map/all_to_all | solution.py:594
  10.3 2.7 %collective-permute-start = (bf16[144,512]{1,0:T(8,128)(2,1)S(1)}, bf16[144,512]{1,0:T(8,128)(2,1)S(1)}, u32[]{:S(2)}, u32[]{:S(2)}) collective-permute-start(bf16[144,512]{1,0:T(8,128)(2,1)S(1)} %get-tuple-element.19.own_ref), channel_id=1, source_target_pairs={{0,4},{1,5},{2,6},{3,7},{4,0},{5,1},{6,2},{7,3},{8,12},{9,13},{10,... | collective-permute-start | bytes 442376 | tf_op jit(solution)/shard_map/ppermute | solution.py:536
  13.1 3.4 %prepare.1 = (bf16[4,1024,256]{2,1,0:T(8,128)(2,1)}, f32[128,512]{1,0:T(8,128)}, s32[32,256]{1,0:T(8,128)}, bf16[512,2048]{1,0:T(8,128)(2,1)S(1)}) custom-call(s32[32,256]{1,0:T(8,128)} %index.1, s32[1,32]{1,0:T(1,128)} %bitcast.16, f32[32,4,256]{2,1,0:T(4,128)} %init.3, bf16[512,2048]{1,0:T(8,128)(2,1)} %w_in.1), custom_call_target="tpu_custom_call" | custom-call | tf_op jit(solution)/shard_map/prepare/pallas_call | solution.py:342
  16.5 15.2 %collective-permute-done.apart_ref = bf16[144,512]{1,0:T(8,128)(2,1)S(1)} collective-permute-done((bf16[144,512]{1,0:T(8,128)(2,1)S(1)}, bf16[144,512]{1,0:T(8,128)(2,1)S(1)}, u32[]{:S(2)}, u32[]{:S(2)}) %collective-permute-start) | collective-permute-done | bytes 147488 | tf_op jit(solution)/shard_map/ppermute | solution.py:536
  31.6 3.1 %neg_tower.1.refs_2_ = bf16[528,256]{1,0:T(8,128)(2,1)} custom-call(bf16[144,512]{1,0:T(8,128)(2,1)S(1)} %get-tuple-element.19.own_ref, bf16[144,512]{1,0:T(8,128)(2,1)S(1)} %collective-permute-done.apart_ref, bf16[512,2048]{1,0:T(8,128)(2,1)S(1)} %get-tuple-element.15.w_in_ref, f32[1,2048]{1,0:T(1,128)} %bitcast.13, bf16[2048,512]{1,0:T(8,128)(2,1)} %w_out.3), custom_call_target="tpu_custom_call" | custom-call | tf_op jit(solution)/shard_map/neg_tower/pallas_call | solution.py:227
  34.8 2.5 %collective-permute-start.3 = (bf16[528,256]{1,0:T(8,128)(2,1)}, bf16[528,256]{1,0:T(8,128)(2,1)S(1)}, u32[]{:S(2)}, u32[]{:S(2)}) collective-permute-start(bf16[528,256]{1,0:T(8,128)(2,1)} %neg_tower.1.refs_2_), channel_id=1, source_target_pairs={{0,17},{1,16},{2,19},{3,18},{4,21},{5,20},{6,23},{7,22},{8,25},{9,... | collective-permute-start | bytes 811016 | tf_op jit(solution)/shard_map/ppermute | solution.py:553
  37.2 0.5 collective-permute-start.4
  37.8 0.6 collective-permute-start.5
  38.3 0.0 collective-permute-start.1
  38.3 7.0 %collective-permute-done.3.refs_3_ = bf16[528,256]{1,0:T(8,128)(2,1)S(1)} collective-permute-done((bf16[528,256]{1,0:T(8,128)(2,1)}, bf16[528,256]{1,0:T(8,128)(2,1)S(1)}, u32[]{:S(2)}, u32[]{:S(2)}) %collective-permute-start.3) | collective-permute-done | bytes 270368 | tf_op jit(solution)/shard_map/ppermute | solution.py:553
  45.3 0.0 collective-permute-start.6
  45.3 4.3 %collective-permute-done.4.refs_4_ = bf16[528,256]{1,0:T(8,128)(2,1)S(1)} collective-permute-done((bf16[528,256]{1,0:T(8,128)(2,1)}, bf16[528,256]{1,0:T(8,128)(2,1)S(1)}, u32[]{:S(2)}, u32[]{:S(2)}) %collective-permute-start.4) | collective-permute-done | bytes 270368 | tf_op jit(solution)/shard_map/ppermute | solution.py:553
  49.7 0.0 collective-permute-start.7
  49.7 0.1 collective-permute-done.5.refs_5_
  49.7 0.4 collective-permute-start.8
  50.2 0.0 collective-permute-done.1.held
  50.2 0.0 all-to-all-done
  50.2 0.0 copy-start
  50.2 7.4 %route.1 = (f32[32,2048]{1,0:T(8,128)S(1)}, bf16[32,640]{1,0:T(8,128)(2,1)S(1)}, f32[1,32]{1,0:T(1,128)S(1)}, bf16[528,256]{1,0:T(8,128)(2,1)S(1)}) custom-call(bf16[512,512]{1,0:T(8,128)(2,1)S(1)} %bitcast.12, bf16[512,2048]{1,0:T(8,128)(2,1)S(1)} %get-tuple-element.15.w_in_ref, f32[1,2048]{1,0:T(1,128)} %bitcast.14, bf16[2048,512]{1,0:T(8,128)(2,1)} %w_out.3, ...), custom_call_target="tpu_custom_call" | custom-call | tf_op jit(solution)/shard_map/route/pallas_call | solution.py:484
  57.6 0.1 collective-permute-start.2
  57.6 0.0 collective-permute-done.6.refs_7_
  57.6 0.0 collective-permute-done.7.refs_8_
  57.7 0.0 collective-permute-done.8.refs_9_
  57.7 4.0 %collective-permute-done.2.refs_1_ = bf16[32,640]{1,0:T(8,128)(2,1)S(1)} collective-permute-done((bf16[32,640]{1,0:T(8,128)(2,1)S(1)}, bf16[32,640]{1,0:T(8,128)(2,1)S(1)}, u32[]{:S(2)}, u32[]{:S(2)}) %collective-permute-start.2) | collective-permute-done | bytes 40992 | tf_op jit(solution)/shard_map/ppermute | solution.py:536
  61.6 0.0 copy-done
  61.6 1.8 %negative_sums.1 = (f32[1,32]{1,0:T(1,128)S(1)}, f32[1,32]{1,0:T(1,128)S(1)}) custom-call(bf16[32,640]{1,0:T(8,128)(2,1)S(1)} %get-tuple-element.22.refs_0_, bf16[32,640]{1,0:T(8,128)(2,1)S(1)} %collective-permute-done.2.refs_1_, bf16[528,256]{1,0:T(8,128)(2,1)S(1)} %copy-done, bf16[528,256]{1,0:T(8,128)(2,1)S(1)} %collective-permute-done.3.refs_3_, ...), custom_call_target="tpu_custom_call" | custom-call | tf_op jit(solution)/shard_map/negative_sums/pallas_call | solution.py:527
  63.4 0.0 collective-permute-start.9
  63.4 0.7 %copy.17 = f32[32,2048]{1,0:T(8,128)} copy(f32[32,2048]{1,0:T(8,128)S(1)} %get-tuple-element.26) | data formatting | bytes 524288
  64.1 2.9 %collective-permute-done.9 = f32[1,32]{1,0:T(1,128)S(1)} collective-permute-done((f32[1,32]{1,0:T(1,128)S(1)}, f32[1,32]{1,0:T(1,128)S(1)}, u32[]{:S(2)}, u32[]{:S(2)}) %collective-permute-start.9) | collective-permute-done | bytes 160 | tf_op jit(solution)/shard_map/ppermute | solution.py:536
  67.0 0.5 subtract_bitcast_fusion
Async XLA Ops:
  3.0 47.2 %all-to-all-start = ((bf16[32,16,512]{2,1,0:T(8,128)(2,1)}), bf16[32,16,512]{2,1,0:T(8,128)(2,1)S(1)}, u32[]{:S(2)}, u32[]{:S(2)}) async-start(bf16[32,16,512]{2,1,0:T(8,128)(2,1)} %bitcast.3), calls=%async_computation | async-start | bytes 1048576 | tf_op jit(solution)/shard_map/all_to_all | solution.py:594
  10.3 21.3 %collective-permute-start = (bf16[144,512]{1,0:T(8,128)(2,1)S(1)}, bf16[144,512]{1,0:T(8,128)(2,1)S(1)}, u32[]{:S(2)}, u32[]{:S(2)}) collective-permute-start(bf16[144,512]{1,0:T(8,128)(2,1)S(1)} %get-tuple-element.19.own_ref), channel_id=1, source_target_pairs={{0,4},{1,5},{2,6},{3,7},{4,0},{5,1},{6,2},{7,3},{8,12},{9,13},{10,... | collective-permute-start | bytes 442376 | tf_op jit(solution)/shard_map/ppermute | solution.py:536
  34.8 10.6 %collective-permute-start.3 = (bf16[528,256]{1,0:T(8,128)(2,1)}, bf16[528,256]{1,0:T(8,128)(2,1)S(1)}, u32[]{:S(2)}, u32[]{:S(2)}) collective-permute-start(bf16[528,256]{1,0:T(8,128)(2,1)} %neg_tower.1.refs_2_), channel_id=1, source_target_pairs={{0,17},{1,16},{2,19},{3,18},{4,21},{5,20},{6,23},{7,22},{8,25},{9,... | collective-permute-start | bytes 811016 | tf_op jit(solution)/shard_map/ppermute | solution.py:553
  37.2 12.4 %collective-permute-start.4 = (bf16[528,256]{1,0:T(8,128)(2,1)}, bf16[528,256]{1,0:T(8,128)(2,1)S(1)}, u32[]{:S(2)}, u32[]{:S(2)}) collective-permute-start(bf16[528,256]{1,0:T(8,128)(2,1)} %neg_tower.1.refs_2_), channel_id=1, source_target_pairs={{0,16},{1,17},{2,18},{3,19},{4,20},{5,21},{6,22},{7,23},{8,24},{9,... | collective-permute-start | bytes 811016 | tf_op jit(solution)/shard_map/ppermute | solution.py:553
  37.8 12.0 %collective-permute-start.5 = (bf16[528,256]{1,0:T(8,128)(2,1)}, bf16[528,256]{1,0:T(8,128)(2,1)S(1)}, u32[]{:S(2)}, u32[]{:S(2)}) collective-permute-start(bf16[528,256]{1,0:T(8,128)(2,1)} %neg_tower.1.refs_2_), channel_id=1, source_target_pairs={{0,1},{1,0},{2,3},{3,2},{4,5},{5,4},{6,7},{7,6},{8,9},{9,8},{10,11... | collective-permute-start | bytes 811016 | tf_op jit(solution)/shard_map/ppermute | solution.py:553
  38.3 11.9 %collective-permute-start.1 = (bf16[528,256]{1,0:T(8,128)(2,1)}, bf16[528,256]{1,0:T(8,128)(2,1)}, u32[]{:S(2)}, u32[]{:S(2)}) collective-permute-start(bf16[528,256]{1,0:T(8,128)(2,1)} %neg_tower.1.refs_2_), channel_id=1, source_target_pairs={{0,8},{8,0},{16,24},{24,16},{1,9},{9,1},{17,25},{25,17},{2,10},{10... | collective-permute-start | bytes 811016 | tf_op jit(solution)/shard_map/ppermute | solution.py:544
  45.3 12.3 %collective-permute-start.6 = (bf16[528,256]{1,0:T(8,128)(2,1)S(1)}, bf16[528,256]{1,0:T(8,128)(2,1)}, u32[]{:S(2)}, u32[]{:S(2)}) collective-permute-start(bf16[528,256]{1,0:T(8,128)(2,1)S(1)} %collective-permute-done.3.refs_3_), channel_id=1, source_target_pairs={{0,8},{8,0},{16,24},{24,16},{1,9},{9,1},{17,25},{25,17},{2,10},{10... | collective-permute-start | bytes 811016 | tf_op jit(solution)/shard_map/ppermute | solution.py:544
  49.7 8.0 %collective-permute-start.7 = (bf16[528,256]{1,0:T(8,128)(2,1)S(1)}, bf16[528,256]{1,0:T(8,128)(2,1)}, u32[]{:S(2)}, u32[]{:S(2)}) collective-permute-start(bf16[528,256]{1,0:T(8,128)(2,1)S(1)} %collective-permute-done.4.refs_4_), channel_id=1, source_target_pairs={{0,8},{8,0},{16,24},{24,16},{1,9},{9,1},{17,25},{25,17},{2,10},{10... | collective-permute-start | bytes 811016 | tf_op jit(solution)/shard_map/ppermute | solution.py:544
  49.7 7.9 %collective-permute-start.8 = (bf16[528,256]{1,0:T(8,128)(2,1)S(1)}, bf16[528,256]{1,0:T(8,128)(2,1)}, u32[]{:S(2)}, u32[]{:S(2)}) collective-permute-start(bf16[528,256]{1,0:T(8,128)(2,1)S(1)} %collective-permute-done.5.refs_5_), channel_id=1, source_target_pairs={{0,8},{8,0},{16,24},{24,16},{1,9},{9,1},{17,25},{25,17},{2,10},{10... | collective-permute-start | bytes 811016 | tf_op jit(solution)/shard_map/ppermute | solution.py:544
  50.2 11.4 %copy-start = (bf16[528,256]{1,0:T(8,128)(2,1)S(1)}, bf16[528,256]{1,0:T(8,128)(2,1)}, u32[]{:S(2)}) copy-start(bf16[528,256]{1,0:T(8,128)(2,1)} %neg_tower.1.refs_2_) | copy-start | bytes 811012
  57.6 4.1 %collective-permute-start.2 = (bf16[32,640]{1,0:T(8,128)(2,1)S(1)}, bf16[32,640]{1,0:T(8,128)(2,1)S(1)}, u32[]{:S(2)}, u32[]{:S(2)}) collective-permute-start(bf16[32,640]{1,0:T(8,128)(2,1)S(1)} %get-tuple-element.22.refs_0_), channel_id=1, source_target_pairs={{0,2},{1,3},{2,0},{3,1},{4,6},{5,7},{6,4},{7,5},{8,10},{9,11},{10,... | collective-permute-start | bytes 122888 | tf_op jit(solution)/shard_map/ppermute | solution.py:536
  63.4 3.6 %collective-permute-start.9 = (f32[1,32]{1,0:T(1,128)S(1)}, f32[1,32]{1,0:T(1,128)S(1)}, u32[]{:S(2)}, u32[]{:S(2)}) collective-permute-start(f32[1,32]{1,0:T(1,128)S(1)} %get-tuple-element.25), channel_id=1, source_target_pairs={{0,2},{1,3},{2,0},{3,1},{4,6},{5,7},{6,4},{7,5},{8,10},{9,11},{10,... | collective-permute-start | bytes 392 | tf_op jit(solution)/shard_map/ppermute | solution.py:536
